TPU v7x, 32 devices: a whole 2x2x4 slice. The times are simulated.
32 devices in a mesh: image: 8 (over z, core), band: 4 (over y, x).
Axes of the slice: x: 2, y: 2, z: 4, core: 2. Of those that a mesh axis runs over, the one named last changes fastest.
Arguments:
- images: float32 [8, 128, 16, 128], P('image', None, 'band'), may hold values from -60 to 60, as said below
- cotangent: float32 [8, 128, 16, 128], P('image', None, 'band'), may hold values from -6 to 6
- filters: float32 [2, 1152, 128], replicated, may hold values from -6 to 6
- rates: float32 [2], replicated, may hold values from 0.002 to 0.008
Outputs:
- new_filters: float32 [8, 2, 1152, 128], P('image')
Inputs may be any that keep to these rules, and one draw needn't show every extreme that they name: `images`: Real-valued feature maps whose channels differ in scale.
All inputs are finite; a program needn't handle non-finite values.
Results may differ from a plain program's by a relative error of at most 0.0001.
Values sent between devices are 32-bit elements; how exact they have to be, the bound alone decides.
No kernel may reach another device: no remote copies, remote signals or barrier semaphores. Data moves between devices by JAX's collectives and lax.ppermute only.
A program may use at most 64 MiB of HBM per device.

v0:
```python
import jax
import jax.numpy as jnp
from jax import lax
from jax.sharding import PartitionSpec as P

HIGH = lax.Precision.HIGHEST


def extended_2(block, sides, width):
    for axis, dim in sides:
        count = lax.axis_size(axis)
        forward = [(i, i + 1) for i in range(count - 1)]
        backward = [(target, source) for source, target in forward]
        low = lax.ppermute(
            lax.slice_in_dim(block, block.shape[dim] - width, None, axis=dim), axis, forward
        )
        high = lax.ppermute(lax.slice_in_dim(block, 0, width, axis=dim), axis, backward)
        block = jnp.concatenate([low, block, high], axis=dim)
    return block


def partner(block, axis, apart):
    count = lax.axis_size(axis)
    route = []
    for low in range(count):
        high = low | 1 << apart
        if high != low and high < count:
            route += [(low, high), (high, low)]
    return lax.ppermute(block, axis, route)


def taps(padded, rows, cols):
    chans = padded.shape[0]
    pieces = [padded[:, dr : dr + rows, dc : dc + cols] for dr in range(3) for dc in range(3)]
    return jnp.stack(pieces, axis=1).reshape(chans * 9, rows * cols)


def flipped(padded, rows, cols):
    chans = padded.shape[0]
    pieces = [
        padded[:, 2 - dr : 2 - dr + rows, 2 - dc : 2 - dc + cols]
        for dr in range(3)
        for dc in range(3)
    ]
    return jnp.stack(pieces, axis=1).reshape(chans, 9, rows * cols)


def with_rims(field):
    extended = extended_2(field, (("band", 1),), 1)
    return jnp.pad(extended, ((0, 0), (0, 0), (1, 1)))


def combine(own, other, inner, own_sq, other_sq):
    coef_own = (1.0 - inner / (2.0 * (own_sq + 1e-06)))[:, None, None]
    coef_other = (1.0 - inner / (2.0 * (other_sq + 1e-06)))[:, None, None]
    return coef_own * own + coef_other * other


def local(images, cotangent, filters, rates):
    feats = images[0]
    cot = cotangent[0]
    chans = feats.shape[0]
    rows = feats.shape[1]
    cols = feats.shape[2]
    scale = (9 * chans) ** (-0.5)
    patch_one = taps(with_rims(feats), rows, cols)
    pre = scale * jnp.einsum("kc,kp->cp", filters[0], patch_one, precision=HIGH)
    hidden = jax.nn.silu(pre).reshape(chans, rows, cols)
    patch_two = taps(with_rims(hidden), rows, cols)
    back = flipped(with_rims(cot), rows, cols)
    flat_cot = cot.reshape(chans, rows * cols)
    grad_two = scale * jnp.einsum("kp,cp->kc", patch_two, flat_cot, precision=HIGH)
    weight_two = filters[1].reshape(chans, 9, chans)
    dhidden = scale * jnp.einsum("itc,ctp->ip", weight_two, back, precision=HIGH)
    sig = jax.nn.sigmoid(pre)
    dpre = dhidden * sig * (1.0 + pre * (1.0 - sig))
    grad_one = scale * jnp.einsum("kp,cp->kc", patch_one, dpre, precision=HIGH)
    grads = jnp.stack([grad_one, grad_two])
    levels = lax.axis_size("image").bit_length() - 1
    block = lax.psum_scatter(grads, "band", scatter_dimension=1, tiled=True)
    for level in range(levels):
        other = partner(block, "image", level)
        inner, own_sq, other_sq = lax.psum(
            (
                jnp.sum(block * other, axis=(1, 2)),
                jnp.sum(block * block, axis=(1, 2)),
                jnp.sum(other * other, axis=(1, 2)),
            ),
            "band",
        )
        block = combine(block, other, inner, own_sq, other_sq)
    height = block.shape[1]
    start = lax.axis_index("band") * height
    mine = lax.dynamic_slice_in_dim(filters, start, height, 1)
    fresh = (mine - rates[:, None, None] * block)[None]
    return lax.all_gather(fresh, "band", axis=2, tiled=True)


def solution(mesh):
    in_specs = (P("image", None, "band", None), P("image", None, "band", None), P(), P())
    out_specs = P("image", None, None, None)
    return jax.shard_map(local, mesh=mesh, in_specs=in_specs, out_specs=out_specs, check_vma=False)
```

profile of v0, /device:TPU:0, one launch (start us, length us, event | category | flops | bytes accessed | tf_op | source)
XLA Modules:
  0.0 191.5 jit_solution(15602402099793860549)
XLA Ops:
  6.5 1.2 fusion.53
  7.8 4.9 %collective-permute-start.2 = (f32[128,1,128]{2,1,0:T(1,128)S(1)}, f32[128,1,128]{2,1,0:T(1,128)S(1)}, u32[]{:S(2)}, u32[]{:S(2)}) collective-permute-start(f32[128,1,128]{2,1,0:T(1,128)S(1)} %get-tuple-element.31), channel_id=1, source_target_pairs={{0,1},{1,2},{2,3},{4,5},{5,6},{6,7},{8,9},{9,10},{10,11},{12,13},{... | collective-permute-start | bytes 196616 | tf_op jit(solution)/shard_map/ppermute | solution.py:14
  12.6 1.3 collective-permute-start.3
  13.9 1.1 fusion.55
  15.1 4.5 %collective-permute-start = (f32[128,1,128]{2,1,0:T(1,128)S(1)}, f32[128,1,128]{2,1,0:T(1,128)S(1)}, u32[]{:S(2)}, u32[]{:S(2)}) collective-permute-start(f32[128,1,128]{2,1,0:T(1,128)S(1)} %get-tuple-element.35), channel_id=1, source_target_pairs={{0,1},{1,2},{2,3},{4,5},{5,6},{6,7},{8,9},{9,10},{10,11},{12,13},{... | collective-permute-start | bytes 196616 | tf_op jit(solution)/shard_map/ppermute | solution.py:14
  19.7 1.3 collective-permute-start.1
  21.0 1.8 stack.113
  22.7 1.0 reshape_squeeze.6
  24.0 0.8 stack.116
  24.8 0.8 stack.110
  25.6 0.9 select_maximum_fusion.2
  27.1 0.8 stack.117
  27.9 0.8 stack.115
  28.7 0.8 stack.114
  29.5 0.8 stack.112
  30.3 0.8 stack.111
  32.0 0.9 select_maximum_fusion.4
  34.7 0.8 copy-done.3
  35.5 4.6 %fusion.45 = (f32[128,512]{0,1:T(8,128)S(1)}, f32[128,512]{0,1:T(8,128)}) fusion(f32[2,1152,128]{2,1,0:T(8,128)S(1)} %copy-done.3, f32[144,8,4,128]{3,2,1,0:T(4,128)S(1)} %bitcast.133), kind=kOutput, calls=%fused_computation.85 | convolution fusion | flops 906297344 | bytes 3473408 | tf_op jit(solution)/shard_map/kc,kp->cp/dot_general | solution.py:67
  40.3 0.8 fusion.54
  41.1 5.5 %collective-permute-start.4 = (f32[128,1,128]{2,1,0:T(1,128)}, f32[128,1,128]{2,1,0:T(1,128)}, u32[]{:S(2)}, u32[]{:S(2)}) collective-permute-start(f32[128,1,128]{2,1,0:T(1,128)} %get-tuple-element.33), channel_id=1, source_target_pairs={{0,1},{1,2},{2,3},{4,5},{5,6},{6,7},{8,9},{9,10},{10,11},{12,13},{... | collective-permute-start | bytes 196616 | tf_op jit(solution)/shard_map/ppermute | solution.py:14
  46.6 1.5 collective-permute-start.5
  48.1 1.7 constant_dynamic-update-slice_fusion.7
  49.8 1.7 constant_dynamic-update-slice_fusion.6
  51.4 1.7 constant_dynamic-update-slice_fusion.5
  53.1 0.7 constant_dynamic-update-slice_fusion.4
  55.3 0.7 constant_dynamic-update-slice_fusion.1
  56.7 5.7 %fusion.18 = f32[128,512]{0,1:T(8,128)S(1)} fusion(f32[128,9,512]{2,0,1:T(8,128)} %constant_dynamic-update-slice_fusion, f32[128,9,128]{2,1,0:T(8,128)S(1)} %copy-done.2, f32[128,512]{0,1:T(8,128)S(1)} %copy-done.11), kind=kOutput, calls=%fused_computation.20 | convolution fusion | flops 906559488 | bytes 3473408 | tf_op jit(solution)/shard_map/itc,ctp->ip/dot_general | solution.py:74
  62.4 2.0 %fusion = f32[1,1152,128]{2,1,0:T(8,128)S(1)} fusion(f32[128,512]{0,1:T(8,128)S(1)} %fusion.18, f32[144,8,4,128]{3,2,1,0:T(4,128)S(1)} %bitcast.134), kind=kOutput, calls=%fused_computation.2 | convolution fusion | flops 906117120 | bytes 3211264 | tf_op jit(solution)/shard_map/kp,cp->kc/dot_general | solution.py:77
  64.4 1.1 copy.14
  65.5 1.7 select_maximum_fusion
  67.3 1.0 fusion.33
  69.6 2.0 %fusion.1 = f32[1,1152,128]{2,1,0:T(8,128)S(1)} fusion(f32[144,8,4,128]{3,2,1,0:T(4,128)S(1)} %bitcast.143, f32[16,8,4,128]{3,2,1,0:T(4,128)S(1)} %bitcast.138), kind=kOutput, calls=%fused_computation.3 | convolution fusion | flops 906117120 | bytes 3211264 | tf_op jit(solution)/shard_map/kp,cp->kc/dot_general | solution.py:72
  71.6 1.1 pad_maximum_fusion
  72.8 32.0 %reduce-scatter.2.cloned.1.call-done = f32[2,288,128]{2,1,0:T(8,128)} async-done(((f32[2,1152,128]{2,1,0:T(8,128)}), f32[2,288,128]{2,1,0:T(8,128)}) %reduce-scatter.2.cloned.1.call-update) | async-done | bytes 294928 | tf_op jit(solution)/shard_map/reduce_scatter | solution.py:80
  104.8 1.8 collective-permute-done.6
  106.6 1.1 multiply_reduce_fusion.7
  107.7 8.9 %all-reduce.5 = (f32[2]{0:T(128)S(1)}, f32[2]{0:T(128)S(1)}, f32[2]{0:T(128)S(1)}) all-reduce(f32[2]{0:T(128)S(1)} %get-tuple-element.12, f32[2]{0:T(128)S(1)} %get-tuple-element.13, f32[2]{0:T(128)S(1)} %get-tuple-element.11), channel_id=1, replica_groups=mesh['image'=8,'band'=4] {'band'}, use_global_device_ids=true, to_apply=%region_2.3 | all-reduce | flops 6 | bytes 48 | tf_op jit(solution)/shard_map/psum | solution.py:83
  116.7 1.1 multiply_add_fusion.1
  117.7 1.5 collective-permute-start.7
  119.3 5.6 %collective-permute-done.7 = f32[2,288,128]{2,1,0:T(8,128)S(1)} collective-permute-done((f32[2,288,128]{2,1,0:T(8,128)S(1)}, f32[2,288,128]{2,1,0:T(8,128)S(1)}, u32[]{:S(2)}, u32[]{:S(2)}) %collective-permute-start.7) | collective-permute-done | bytes 294944 | tf_op jit(solution)/shard_map/ppermute | solution.py:29
  125.0 8.9 %all-reduce.4 = (f32[2]{0:T(128)S(1)}, f32[2]{0:T(128)S(1)}, f32[2]{0:T(128)S(1)}) all-reduce(f32[2]{0:T(128)S(1)} %get-tuple-element.9, f32[2]{0:T(128)S(1)} %get-tuple-element.10, f32[2]{0:T(128)S(1)} %get-tuple-element.8), channel_id=1, replica_groups=mesh['image'=8,'band'=4] {'band'}, use_global_device_ids=true, to_apply=%region_8.9 | all-reduce | flops 6 | bytes 48 | tf_op jit(solution)/shard_map/psum | solution.py:83
  134.0 2.5 %collective-permute-start.8 = (f32[2,288,128]{2,1,0:T(8,128)S(1)}, f32[2,288,128]{2,1,0:T(8,128)S(1)}, u32[]{:S(2)}, u32[]{:S(2)}) collective-permute-start(f32[2,288,128]{2,1,0:T(8,128)S(1)} %multiply_add_fusion), channel_id=1, source_target_pairs={{0,16},{16,0},{4,20},{20,4},{8,24},{24,8},{12,28},{28,12},{1,17},{... | collective-permute-start | bytes 884744 | tf_op jit(solution)/shard_map/ppermute | solution.py:29
  136.5 9.0 %collective-permute-done.8 = f32[2,288,128]{2,1,0:T(8,128)S(1)} collective-permute-done((f32[2,288,128]{2,1,0:T(8,128)S(1)}, f32[2,288,128]{2,1,0:T(8,128)S(1)}, u32[]{:S(2)}, u32[]{:S(2)}) %collective-permute-start.8) | collective-permute-done | bytes 294944 | tf_op jit(solution)/shard_map/ppermute | solution.py:29
  145.6 8.9 %all-reduce.3 = (f32[2]{0:T(128)S(1)}, f32[2]{0:T(128)S(1)}, f32[2]{0:T(128)S(1)}) all-reduce(f32[2]{0:T(128)S(1)} %get-tuple-element.6, f32[2]{0:T(128)S(1)} %get-tuple-element.7, f32[2]{0:T(128)S(1)} %get-tuple-element.5), channel_id=1, replica_groups=mesh['image'=8,'band'=4] {'band'}, use_global_device_ids=true, to_apply=%region_14.15 | all-reduce | flops 6 | bytes 48 | tf_op jit(solution)/shard_map/psum | solution.py:83
  154.6 0.8 multiply_subtract_fusion
  155.4 26.8 %all-gather.3.cloned.1.call-done = f32[2,1152,128]{2,1,0:T(8,128)} async-done(((f32[2,288,128]{2,1,0:T(8,128)}), f32[2,1152,128]{2,1,0:T(8,128)}) %all-gather.3.cloned.1.call-update) | async-done | bytes 1179664 | tf_op jit(solution)/shard_map/all_gather | solution.py:96
  182.3 2.4 %copy.70 = f32[1,2,1152,128]{3,2,1,0:T(8,128)} copy(f32[1,2,1152,128]{3,2,1,0:T(8,128)} %bitcast.146) | data formatting | bytes 2359296
  (70 shorter events, 7.6 us)
Async XLA Ops:
  6.5 17.2 %copy-start = (f32[1,128,4,128]{3,2,1,0:T(4,128)S(1)}, f32[1,128,4,128]{3,2,1,0:T(4,128)}, u32[]{:S(2)}) copy-start(f32[1,128,4,128]{3,2,1,0:T(4,128)} %param.5) | copy-start | bytes 786436
  6.5 16.2 %slice-start = ((f32[2,1152,128]{2,1,0:T(8,128)}), f32[1,1152,128]{2,1,0:T(8,128)S(1)}, s32[]{:S(2)}) async-start(f32[2,1152,128]{2,1,0:T(8,128)} %param.6), calls=%async_computation.3 | async-start | bytes 1179648 | tf_op jit(solution)/shard_map/slice | solution.py:73
  6.5 98.3 %reduce-scatter.2.cloned.1.call-start = ((), (), s32[]{:S(2)}) async-start(), calls=%async_computation.1 | async-start | bytes 1474560 | tf_op jit(solution)/shard_map/reduce_scatter | solution.py:80
  7.8 16.0 %collective-permute-start.2 = (f32[128,1,128]{2,1,0:T(1,128)S(1)}, f32[128,1,128]{2,1,0:T(1,128)S(1)}, u32[]{:S(2)}, u32[]{:S(2)}) collective-permute-start(f32[128,1,128]{2,1,0:T(1,128)S(1)} %get-tuple-element.31), channel_id=1, source_target_pairs={{0,1},{1,2},{2,3},{4,5},{5,6},{6,7},{8,9},{9,10},{10,11},{12,13},{... | collective-permute-start | bytes 196616 | tf_op jit(solution)/shard_map/ppermute | solution.py:14
  12.6 11.1 %collective-permute-start.3 = (f32[128,1,128]{2,1,0:T(1,128)S(1)}, f32[128,1,128]{2,1,0:T(1,128)S(1)}, u32[]{:S(2)}, u32[]{:S(2)}) collective-permute-start(f32[128,1,128]{2,1,0:T(1,128)S(1)} %get-tuple-element.32), channel_id=1, source_target_pairs={{1,0},{2,1},{3,2},{5,4},{6,5},{7,6},{9,8},{10,9},{11,10},{13,12},{... | collective-permute-start | bytes 196616 | tf_op jit(solution)/shard_map/ppermute | solution.py:17
  15.1 16.9 %collective-permute-start = (f32[128,1,128]{2,1,0:T(1,128)S(1)}, f32[128,1,128]{2,1,0:T(1,128)S(1)}, u32[]{:S(2)}, u32[]{:S(2)}) collective-permute-start(f32[128,1,128]{2,1,0:T(1,128)S(1)} %get-tuple-element.35), channel_id=1, source_target_pairs={{0,1},{1,2},{2,3},{4,5},{5,6},{6,7},{8,9},{9,10},{10,11},{12,13},{... | collective-permute-start | bytes 196616 | tf_op jit(solution)/shard_map/ppermute | solution.py:14
  19.7 12.3 %collective-permute-start.1 = (f32[128,1,128]{2,1,0:T(1,128)S(1)}, f32[128,1,128]{2,1,0:T(1,128)S(1)}, u32[]{:S(2)}, u32[]{:S(2)}) collective-permute-start(f32[128,1,128]{2,1,0:T(1,128)S(1)} %get-tuple-element.36), channel_id=1, source_target_pairs={{1,0},{2,1},{3,2},{5,4},{6,5},{7,6},{9,8},{10,9},{11,10},{13,12},{... | collective-permute-start | bytes 196616 | tf_op jit(solution)/shard_map/ppermute | solution.py:17
  27.1 4.9 %copy-start.1 = (f32[1,128,4,128]{3,2,1,0:T(4,128)S(1)}, f32[1,128,4,128]{3,2,1,0:T(4,128)}, u32[]{:S(2)}) copy-start(f32[1,128,4,128]{3,2,1,0:T(4,128)} %param.4) | copy-start | bytes 786436
  34.3 1.3 copy-start.3
  35.5 17.6 %copy-start.6 = (f32[128,1,512]{2,0,1:T(8,128)S(1)}, f32[128,1,512]{2,0,1:T(8,128)}, u32[]{:S(2)}) copy-start(f32[128,1,512]{2,0,1:T(8,128)} %stack.113) | copy-start | bytes 786436
  40.1 16.6 %copy-start.5 = (f32[128,512]{0,1:T(8,128)}, f32[128,512]{0,1:T(8,128)S(1)}, u32[]{:S(2)}) copy-start(f32[128,512]{0,1:T(8,128)S(1)} %get-tuple-element.43) | copy-start | bytes 786436
  40.3 13.6 %copy-start.10 = (f32[128,1,512]{2,0,1:T(8,128)S(1)}, f32[128,1,512]{2,0,1:T(8,128)}, u32[]{:S(2)}) copy-start(f32[128,1,512]{2,0,1:T(8,128)} %stack.114) | copy-start | bytes 786436
  40.3 14.3 %copy-start.9 = (f32[128,1,512]{2,0,1:T(8,128)S(1)}, f32[128,1,512]{2,0,1:T(8,128)}, u32[]{:S(2)}) copy-start(f32[128,1,512]{2,0,1:T(8,128)} %stack.115) | copy-start | bytes 786436
  40.3 15.0 %copy-start.7 = (f32[128,1,512]{2,0,1:T(8,128)S(1)}, f32[128,1,512]{2,0,1:T(8,128)}, u32[]{:S(2)}) copy-start(f32[128,1,512]{2,0,1:T(8,128)} %stack.116) | copy-start | bytes 786436
  40.3 15.7 %copy-start.8 = (f32[128,1,512]{2,0,1:T(8,128)S(1)}, f32[128,1,512]{2,0,1:T(8,128)}, u32[]{:S(2)}) copy-start(f32[128,1,512]{2,0,1:T(8,128)} %stack.117) | copy-start | bytes 786436
  40.3 16.4 %copy-start.2 = (f32[128,9,128]{2,1,0:T(8,128)S(1)}, f32[128,9,128]{2,1,0:T(8,128)}, u32[]{:S(2)}) copy-start(f32[128,9,128]{2,1,0:T(8,128)} %reshape_squeeze.6) | copy-start | bytes 1769476
  40.3 16.4 %copy-start.11 = (f32[128,512]{0,1:T(8,128)S(1)}, f32[128,512]{0,1:T(8,128)}, u32[]{:S(2)}) copy-start(f32[128,512]{0,1:T(8,128)} %get-tuple-element.44) | copy-start | bytes 786436
  41.1 24.4 %collective-permute-start.4 = (f32[128,1,128]{2,1,0:T(1,128)}, f32[128,1,128]{2,1,0:T(1,128)}, u32[]{:S(2)}, u32[]{:S(2)}) collective-permute-start(f32[128,1,128]{2,1,0:T(1,128)} %get-tuple-element.33), channel_id=1, source_target_pairs={{0,1},{1,2},{2,3},{4,5},{5,6},{6,7},{8,9},{9,10},{10,11},{12,13},{... | collective-permute-start | bytes 196616 | tf_op jit(solution)/shard_map/ppermute | solution.py:14
  46.6 18.9 %collective-permute-start.5 = (f32[128,1,128]{2,1,0:T(1,128)}, f32[128,1,128]{2,1,0:T(1,128)S(1)}, u32[]{:S(2)}, u32[]{:S(2)}) collective-permute-start(f32[128,1,128]{2,1,0:T(1,128)} %get-tuple-element.34), channel_id=1, source_target_pairs={{1,0},{2,1},{3,2},{5,4},{6,5},{7,6},{9,8},{10,9},{11,10},{13,12},{... | collective-permute-start | bytes 196616 | tf_op jit(solution)/shard_map/ppermute | solution.py:17
  72.7 81.8 %copy-start.4 = (f32[2,1152,128]{2,1,0:T(8,128)S(1)}, f32[2,1152,128]{2,1,0:T(8,128)}, u32[]{:S(2)}) copy-start(f32[2,1152,128]{2,1,0:T(8,128)} %param.6) | copy-start | bytes 3538948
  72.7 81.8 %copy-start.12 = (f32[2]{0:T(128)S(1)}, f32[2]{0:T(128)}, u32[]{:S(2)}) copy-start(f32[2]{0:T(128)} %param.7) | copy-start | bytes 28
  72.7 109.5 %all-gather.3.cloned.1.call-start = ((), (), s32[]{:S(2)}) async-start(), calls=%async_computation.2 | async-start | bytes 1474560 | tf_op jit(solution)/shard_map/all_gather | solution.py:96
  104.8 1.8 collective-permute-start.6
  117.7 7.1 %collective-permute-start.7 = (f32[2,288,128]{2,1,0:T(8,128)S(1)}, f32[2,288,128]{2,1,0:T(8,128)S(1)}, u32[]{:S(2)}, u32[]{:S(2)}) collective-permute-start(f32[2,288,128]{2,1,0:T(8,128)S(1)} %multiply_add_fusion.1), channel_id=1, source_target_pairs={{0,8},{8,0},{4,12},{12,4},{16,24},{24,16},{20,28},{28,20},{1,9},{9... | collective-permute-start | bytes 884744 | tf_op jit(solution)/shard_map/ppermute | solution.py:29
  134.0 11.4 %collective-permute-start.8 = (f32[2,288,128]{2,1,0:T(8,128)S(1)}, f32[2,288,128]{2,1,0:T(8,128)S(1)}, u32[]{:S(2)}, u32[]{:S(2)}) collective-permute-start(f32[2,288,128]{2,1,0:T(8,128)S(1)} %multiply_add_fusion), channel_id=1, source_target_pairs={{0,16},{16,0},{4,20},{20,4},{8,24},{24,8},{12,28},{28,12},{1,17},{... | collective-permute-start | bytes 884744 | tf_op jit(solution)/shard_map/ppermute | solution.py:29
Sparse Core Ops, SparseCore 0:
  72.9 31.8 reduce-scatter.1
  155.6 26.6 all-gather.2
where the time goes:
time: 192 us; the launch traced here: 191 us
  waiting for transfers between devices  75.2 us (39%)
  local copies, waits for them, and re-layouts  28.6 us (15%)
  blocking collectives  26.7 us (14%)
  starting transfers between devices  23.1 us (12%)
  matrix products  14.3 us (7%)
  between operations  13.7 us (7%)
  other arithmetic  9.83 us (5%)
    reduce_scatter x1, waiting for transfers between devices, local(): block = lax.psum_scatter(grads, 'band', scatter_dimension=1, tiled=True)  32 us
    all_gather x1, waiting for transfers between devices, local(): return lax.all_gather(fresh, 'band', axis=2, tiled=True)  26.8 us
    psum x3, blocking collectives, local(): lax.psum((jnp.sum(block * other, axis=(1, 2)), jnp.sum(block * block, axi...  26.7 us
    ppermute x3, waiting for transfers between devices, partner(): return lax.ppermute(block, axis, route)  16.3 us
    ppermute x3, starting transfers between devices, extended_2(): lax.ppermute(lax.slice_in_dim(block, block.shape[dim] - width, None, axis...  15 us
    unnamed x47, local copies, waits for them, and re-layouts  13.5 us
    another operation x10, local copies, waits for them, and re-layouts, flipped(): return jnp.stack(pieces, axis=1).reshape(chans, 9, rows * cols)  8.26 us
    dot_general x1, matrix products, local(): jnp.einsum('itc,ctp->ip', weight_two, back, precision=HIGH)  5.67 us
  transfers between devices with their start and end apart: 11, of which 5 were waited for; matrix products, arithmetic and copies ran while one was open for 15% of the time, Pallas kernels for 0%

commit v1 on v0

v1 whole, which is shorter than its diff:
```python
import functools

import jax
import jax.numpy as jnp
from jax import lax
from jax.experimental import pallas as pl
from jax.experimental.pallas import tpu as pltpu
from jax.sharding import PartitionSpec as P

HIGH = lax.Precision.HIGHEST
F32 = jnp.float32
BF16 = jnp.bfloat16


def call(body, outs, scratch=(), flops=0, nbytes=0):
    return pl.pallas_call(
        body,
        out_shape=[jax.ShapeDtypeStruct(s, F32) for s in outs],
        scratch_shapes=list(scratch),
        cost_estimate=pl.CostEstimate(
            flops=flops, bytes_accessed=nbytes, transcendentals=0
        ),
        compiler_params=pltpu.CompilerParams(vmem_limit_bytes=48 * 2**20),
    )


def edges_kernel(rows, x_ref, c_ref, down_ref, up_ref):
    chans = x_ref.shape[0] // rows
    for slot, ref in enumerate((x_ref, c_ref)):
        at = slice(slot * chans, (slot + 1) * chans)
        up_ref[at, :] = ref[pl.ds(0, chans, stride=rows), :]
        down_ref[at, :] = ref[pl.ds(rows - 1, chans, stride=rows), :]


def halves(value):
    high = value.astype(BF16)
    return high, (value - high.astype(F32)).astype(BF16)


def dot3(ah, al, bh, bl, dims):
    def one(a, b):
        return lax.dot_general(a, b, (dims, ((), ())), preferred_element_type=F32)

    return one(ah, bh) + (one(ah, bl) + one(al, bh))


def moved(value, step):
    cols = value.shape[-1]
    col = lax.broadcasted_iota(jnp.int32, value.shape, value.ndim - 1)
    if step > 0:
        return jnp.where(col == cols - 1, 0.0, pltpu.roll(value, cols - 1, 1))
    return jnp.where(col == 0, 0.0, pltpu.roll(value, 1, 1))


def grads_kernel(
    rows, scale, n_band, x_ref, c_ref, prev_ref, next_ref, f_ref, *rest
):
    outs = rest[:n_band]
    g_ref, xh, xl, ch, cl, fh, fl, dh, dl = rest[n_band:]
    chans = x_ref.shape[0] // rows
    cols = x_ref.shape[1]

    def row_of(ref, slot, row):
        if row < 0:
            return prev_ref[slot * chans : (slot + 1) * chans, :]
        if row == rows:
            return next_ref[slot * chans : (slot + 1) * chans, :]
        return ref[pl.ds(row, chans, stride=rows), :]

    def put(high_ref, low_ref, at, row, value):
        high, low = halves(value)
        part = (slice(at * chans, (at + 1) * chans), slice(row * cols, (row + 1) * cols))
        high_ref[part] = high
        low_ref[part] = low

    for row in range(-1, rows + 1):
        value = row_of(x_ref, 0, row)
        other = row_of(c_ref, 1, row)
        for a in range(3):
            if 0 <= row - a + 1 < rows:
                put(xh, xl, a, row - a + 1, value)
            if 0 <= row + a - 1 < rows:
                put(ch, cl, a, row + a - 1, other)
    for a in range(3):
        for b in range(3):
            tap = f_ref[0, pl.ds(3 * a + b, chans, stride=9), :]
            put(fh, fl, b, a, tap.T)
    pre3 = dot3(fh[...], fl[...], xh[...], xl[...], ((1,), (0,)))
    for a in range(3):
        for b in range(3):
            put(fh, fl, b, a, f_ref[1, pl.ds(3 * a + b, chans, stride=9), :])
    back3 = dot3(fh[...], fl[...], ch[...], cl[...], ((1,), (0,)))
    dpres = []
    for row in range(rows):
        at = slice(row * cols, (row + 1) * cols)
        pre = scale * (
            pre3[chans : 2 * chans, at]
            + moved(pre3[:chans, at], -1)
            + moved(pre3[2 * chans :, at], 1)
        )
        dhidden = scale * (
            back3[chans : 2 * chans, at]
            + moved(back3[:chans, at], 1)
            + moved(back3[2 * chans :, at], -1)
        )
        sig = jax.nn.sigmoid(pre)
        hidden = pre * sig
        dpre = dhidden * sig * (1.0 + pre * (1.0 - sig))
        dpres.append(dpre)
        for b, value in enumerate((moved(hidden, -1), hidden, moved(hidden, 1))):
            put(dh, dl, b, row, value)
    grad2 = dot3(dh[...], dl[...], ch[...], cl[...], ((1,), (1,)))
    for a in range(3):
        for b in range(3):
            t = 3 * a + b
            g_ref[1, t * chans : (t + 1) * chans, :] = (
                scale * grad2[b * chans : (b + 1) * chans, a * chans : (a + 1) * chans]
            )
    for row, dpre in enumerate(dpres):
        for b, value in enumerate((moved(dpre, 1), dpre, moved(dpre, -1))):
            put(dh, dl, b, row, value)
    grad1 = dot3(xh[...], xl[...], dh[...], dl[...], ((1,), (1,)))
    for a in range(3):
        for b in range(3):
            t = 3 * a + b
            g_ref[0, t * chans : (t + 1) * chans, :] = (
                scale * grad1[a * chans : (a + 1) * chans, b * chans : (b + 1) * chans]
            )
    band = lax.axis_index("band")
    size = g_ref.shape[1] // n_band
    for k, out in enumerate(outs):
        start = pl.multiple_of(lax.bitwise_xor(band, k) * size, 8)
        for layer in range(2):
            out[layer] = g_ref[layer, pl.ds(start, size), :]


def sum_kernel(n_band, *refs):
    parts, (keep_ref, give_ref) = refs[:n_band], refs[n_band:]
    mine = lax.axis_index("image") % 2
    for out, layer in ((keep_ref, mine), (give_ref, 1 - mine)):
        total = parts[0][layer]
        for part in parts[1:]:
            total = total + part[layer]
        out[...] = total


def pack_kernel(n_pair, keep_ref, other_ref, *outs):
    image = lax.axis_index("image")
    mine = image % 2
    pair = image // 2
    size = keep_ref.shape[0] // n_pair
    for k, out in enumerate(outs):
        start = pl.multiple_of(lax.bitwise_xor(pair, k) * size, 8)
        out[mine] = keep_ref[pl.ds(start, size), :]
        out[1 - mine] = other_ref[pl.ds(start, size), :]


def gram_kernel(n_pair, *refs):
    parts, out = refs[:n_pair], refs[n_pair]
    held = refs[n_pair + 1]
    pair = lax.axis_index("image") // 2
    for k, part in enumerate(parts):
        at = lax.bitwise_xor(pair, k) * 2
        held[at] = part[0]
        held[at + 1] = part[1]
    count = 2 * n_pair
    row = lax.broadcasted_iota(jnp.int32, out.shape, 0)
    col = lax.broadcasted_iota(jnp.int32, out.shape, 1)
    total = jnp.zeros(out.shape, F32)
    for i in range(count):
        for j in range(i, count):
            value = jnp.sum(held[i] * held[j], keepdims=True)
            here = ((row == i) & (col == j)) | ((row == j) & (col == i))
            total = jnp.where(here, value, total)
    out[...] = total


def merge_kernel(n_pair, n_band, sums_ref, *refs):
    parts, out = refs[:n_pair], refs[n_pair]
    image = lax.axis_index("image")
    mine = image % 2
    pair = image // 2
    count = 2 * n_pair
    gram = jnp.zeros(sums_ref.shape[1:], F32)
    for half in range(n_pair):
        for at in range(n_band):
            gram = gram + sums_ref[(2 * half + mine) * n_band + at]
    row = lax.broadcasted_iota(jnp.int32, gram.shape, 0)
    col = lax.broadcasted_iota(jnp.int32, gram.shape, 1)

    def swap(value, axis, step):
        size = value.shape[axis]
        index = row if axis == 0 else col
        return jnp.where(
            (index & step) != 0,
            pltpu.roll(value, step, axis),
            pltpu.roll(value, size - step, axis),
        )

    weight = jnp.ones((count, 1), F32)
    step = 1
    while step < count:
        own = jnp.where(row == col, gram, 0.0)
        cross = jnp.where((row ^ step) == col, gram, 0.0)
        down = 1.0 - jnp.sum(cross, 1, keepdims=True) / (
            2.0 * (jnp.sum(own, 1, keepdims=True) + 1e-06)
        )
        along = 1.0 - jnp.sum(cross, 0, keepdims=True) / (
            2.0 * (jnp.sum(own, 0, keepdims=True) + 1e-06)
        )
        weight = weight * down
        gram = gram * down * along
        gram = gram + swap(gram, 0, step)
        gram = gram + swap(gram, 1, step)
        step *= 2
    place = lax.broadcasted_iota(jnp.int32, weight.shape, 0)
    total = jnp.zeros(out.shape, F32)
    for k, part in enumerate(parts):
        at = lax.bitwise_xor(pair, k) * 2
        for j in range(2):
            factor = jnp.sum(jnp.where(place == at + j, weight, 0.0), keepdims=True)
            total = total + factor * part[j]
    out[...] = total


def gather_kernel(n_pair, *refs):
    parts, out = refs[:n_pair], refs[n_pair]
    pair = lax.axis_index("image") // 2
    size = parts[0].shape[0]
    for k, part in enumerate(parts):
        start = pl.multiple_of(lax.bitwise_xor(pair, k) * size, 8)
        out[pl.ds(start, size), :] = part[...]


def final_kernel(n_band, chans, rates_ref, f_ref, *refs):
    own, others = refs[:n_band], refs[n_band : 2 * n_band]
    out = refs[2 * n_band]
    held = refs[2 * n_band + 1]
    mine = lax.axis_index("image") % 2
    band = lax.axis_index("band")
    size = own[0].shape[0]
    for k in range(n_band):
        start = pl.multiple_of(lax.bitwise_xor(band, k) * size, 8)
        held[mine, pl.ds(start, size), :] = own[k][...]
        held[1 - mine, pl.ds(start, size), :] = others[k][...]
    for layer in range(2):
        rate = rates_ref[layer]
        for t in range(9):
            at = pl.ds(t, chans, stride=9)
            out[0, layer, at, :] = (
                f_ref[layer, at, :] - rate * held[layer, t * chans : (t + 1) * chans, :]
            )


def xor_route(count, k):
    return [(i, i ^ k) for i in range(count)]


def fast(images, cotangent, filters, rates):
    _, chans, rows, cols = images.shape
    n_band = lax.axis_size("band")
    n_image = lax.axis_size("image")
    n_pair = n_image // 2
    kdim = filters.shape[1]
    block = kdim // n_band
    slot = block // n_pair
    scale = kdim ** (-0.5)
    x = images.reshape(chans * rows, cols)
    cot = cotangent.reshape(chans * rows, cols)
    down, up = call(functools.partial(edges_kernel, rows), [(2 * chans, cols)] * 2)(x, cot)
    fwd = [(i, i + 1) for i in range(n_band - 1)]
    bwd = [(j, i) for i, j in fwd]
    before = lax.ppermute(down, "band", fwd)
    after = lax.ppermute(up, "band", bwd)
    wide = (3 * chans, rows * cols)
    parts = call(
        functools.partial(grads_kernel, rows, scale, n_band),
        [(2, block, chans)] * n_band,
        [pltpu.VMEM((2, kdim, chans), F32)]
        + [pltpu.VMEM(wide, BF16)] * 4
        + [pltpu.VMEM((3 * chans, 3 * chans), BF16)] * 2
        + [pltpu.VMEM(wide, BF16)] * 2,
        flops=24 * kdim * chans * rows * cols,
        nbytes=4 * (2 * chans * rows * cols + 4 * kdim * chans),
    )(x, cot, before, after, filters)
    parts = [parts[0]] + [
        lax.ppermute(parts[k], "band", xor_route(n_band, k)) for k in range(1, n_band)
    ]
    keep, give = call(functools.partial(sum_kernel, n_band), [(block, chans)] * 2)(*parts)
    other = lax.ppermute(give, "image", xor_route(n_image, 1))
    parts = call(functools.partial(pack_kernel, n_pair), [(2, slot, chans)] * n_pair)(keep, other)
    parts = [parts[0]] + [
        lax.ppermute(parts[k], "image", xor_route(n_image, 2 * k)) for k in range(1, n_pair)
    ]
    (gram,) = call(
        functools.partial(gram_kernel, n_pair),
        [(n_image, 128)],
        [pltpu.VMEM((n_image, slot, chans), F32)],
    )(*parts)
    sums = jnp.broadcast_to(gram[None], (n_image * n_band,) + gram.shape)
    sums = lax.all_to_all(sums, ("image", "band"), 0, 0, tiled=True)
    (mine,) = call(functools.partial(merge_kernel, n_pair, n_band), [(slot, chans)])(sums, *parts)
    pieces = [mine] + [
        lax.ppermute(mine, "image", xor_route(n_image, 2 * k)) for k in range(1, n_pair)
    ]
    (mine,) = call(functools.partial(gather_kernel, n_pair), [(block, chans)])(*pieces)
    own = [mine] + [
        lax.ppermute(mine, "band", xor_route(n_band, k)) for k in range(1, n_band)
    ]
    others = [lax.ppermute(piece, "image", xor_route(n_image, 1)) for piece in own]
    out = pl.pallas_call(
        functools.partial(final_kernel, n_band, chans),
        out_shape=jax.ShapeDtypeStruct((1,) + filters.shape, F32),
        in_specs=[pl.BlockSpec(memory_space=pltpu.SMEM)]
        + [pl.BlockSpec(memory_space=pltpu.VMEM)] * (1 + 2 * n_band),
        scratch_shapes=[pltpu.VMEM(filters.shape, F32)],
        compiler_params=pltpu.CompilerParams(vmem_limit_bytes=48 * 2**20),
    )(rates, filters, *own, *others)
    return out


def with_rims(field):
    count = lax.axis_size("band")
    forward = [(i, i + 1) for i in range(count - 1)]
    backward = [(target, source) for source, target in forward]
    low = lax.ppermute(field[:, -1:], "band", forward)
    high = lax.ppermute(field[:, :1], "band", backward)
    extended = jnp.concatenate([low, field, high], axis=1)
    return jnp.pad(extended, ((0, 0), (0, 0), (1, 1)))


def taps(padded, rows, cols, flip=False):
    chans = padded.shape[0]
    at = (2, 1, 0) if flip else (0, 1, 2)
    pieces = [padded[:, dr : dr + rows, dc : dc + cols] for dr in at for dc in at]
    return jnp.stack(pieces, axis=1).reshape(chans, 9, rows * cols)


def plain(images, cotangent, filters, rates):
    feats, cot = images[0], cotangent[0]
    chans, rows, cols = feats.shape
    scale = (9 * chans) ** (-0.5)
    patch_one = taps(with_rims(feats), rows, cols).reshape(9 * chans, rows * cols)
    pre = scale * jnp.einsum("kc,kp->cp", filters[0], patch_one, precision=HIGH)
    hidden = jax.nn.silu(pre).reshape(chans, rows, cols)
    patch_two = taps(with_rims(hidden), rows, cols).reshape(9 * chans, rows * cols)
    back = taps(with_rims(cot), rows, cols, flip=True)
    flat_cot = cot.reshape(chans, rows * cols)
    grad_two = scale * jnp.einsum("kp,cp->kc", patch_two, flat_cot, precision=HIGH)
    weight_two = filters[1].reshape(chans, 9, chans)
    dhidden = scale * jnp.einsum("itc,ctp->ip", weight_two, back, precision=HIGH)
    sig = jax.nn.sigmoid(pre)
    dpre = dhidden * sig * (1.0 + pre * (1.0 - sig))
    grad_one = scale * jnp.einsum("kp,cp->kc", patch_one, dpre, precision=HIGH)
    block = lax.psum_scatter(
        jnp.stack([grad_one, grad_two]), "band", scatter_dimension=1, tiled=True
    )
    count = lax.axis_size("image")
    for level in range(count.bit_length() - 1):
        other = lax.ppermute(block, "image", xor_route(count, 1 << level))
        inner, own_sq, other_sq = lax.psum(
            tuple(jnp.sum(v, axis=(1, 2)) for v in (block * other, block * block, other * other)),
            "band",
        )
        low = (1.0 - inner / (2.0 * (own_sq + 1e-06)))[:, None, None]
        high = (1.0 - inner / (2.0 * (other_sq + 1e-06)))[:, None, None]
        block = low * block + high * other
    height = block.shape[1]
    mine = lax.dynamic_slice_in_dim(filters, lax.axis_index("band") * height, height, 1)
    fresh = (mine - rates[:, None, None] * block)[None]
    return lax.all_gather(fresh, "band", axis=2, tiled=True)


def local(images, cotangent, filters, rates):
    n_band = lax.axis_size("band")
    n_image = lax.axis_size("image")
    kdim = filters.shape[1]
    fits = (
        n_image >= 4
        and n_image & (n_image - 1) == 0
        and n_band & (n_band - 1) == 0
        and kdim % (n_band * (n_image // 2) * 8) == 0
    )
    return (fast if fits else plain)(images, cotangent, filters, rates)


def solution(mesh):
    in_specs = (P("image", None, "band", None), P("image", None, "band", None), P(), P())
    out_specs = P("image", None, None, None)
    return jax.shard_map(local, mesh=mesh, in_specs=in_specs, out_specs=out_specs, check_vma=False)
```

time: 192 us -> 77.6 us (0.40)
  waiting for transfers between devices: 75.2 us -> 34.3 us
  local copies, waits for them, and re-layouts: 28.6 us -> 3.19 us
  blocking collectives: 26.7 us -> 11.7 us
  matrix products: 14.3 us -> 0 us
  between operations: 13.7 us -> 0.11 us
  other arithmetic: 9.83 us -> 0 us
  Pallas kernels: 0 us -> 5.75 us
    reduce_scatter x1 -> x0, waiting for transfers between devices: 32 us -> none  [local(): block = lax.psum_scatter(grads, 'band', scatter_dimension=1, tiled=True)]
    all_gather x1 -> x0, waiting for transfers between devices: 26.8 us -> none  [local(): return lax.all_gather(fresh, 'band', axis=2, tiled=True)]
    psum x3 -> x0, blocking collectives: 26.7 us -> none  [local(): lax.psum((jnp.sum(block * other, axis=(1, 2)), jnp.sum(block * block, axi...]
    ppermute x9 -> x19, waiting for transfers between devices: 16.3 us -> 34.3 us  [the longest x3 11.6 us: fast(): lax.ppermute(parts[k], 'band', xor_route(n_band, k))]
    dot_general x4 -> x0, matrix products: 14.3 us -> none  [the longest x1 5.67 us: local(): jnp.einsum('itc,ctp->ip', weight_two, back, precision=HIGH)]
    all_to_all x0 -> x1, blocking collectives: none -> 11.7 us  [fast(): sums = lax.all_to_all(sums, ('image', 'band'), 0, 0, tiled=True)]
    another operation x15 -> x0, local copies, waits for them, and re-layouts: 11.3 us -> none  [the longest x10 8.26 us: flipped(): return jnp.stack(pieces, axis=1).reshape(chans, 9, rows * cols)]
    unnamed x47 -> x10, local copies, waits for them, and re-layouts: 13.5 us -> 3.18 us
  transfers between devices with their start and end apart: 11 -> 19, of which waited for: 5 -> 14; matrix products, arithmetic and copies ran while one was open for 15% -> 0% of each run, Pallas kernels for 0% -> 0%
where the time goes in v1:
time: 77.6 us; the launch traced here: 77.3 us
  waiting for transfers between devices  34.3 us (44%)
  starting transfers between devices  22.3 us (29%)
  blocking collectives  11.7 us (15%)
  Pallas kernels  5.75 us (7%)
  local copies, waits for them, and re-layouts  3.19 us (4%)
    all_to_all x1, blocking collectives, fast(): sums = lax.all_to_all(sums, ('image', 'band'), 0, 0, tiled=True)  11.7 us
    ppermute x3, waiting for transfers between devices, fast(): lax.ppermute(parts[k], 'band', xor_route(n_band, k))  11.6 us
    ppermute x3, waiting for transfers between devices, fast(): lax.ppermute(parts[k], 'image', xor_route(n_image, 2 * k))  6.03 us
    ppermute x3, waiting for transfers between devices, fast(): lax.ppermute(mine, 'band', xor_route(n_band, k))  5.34 us
    ppermute x1, starting transfers between devices, fast(): before = lax.ppermute(down, 'band', fwd)  4.88 us
    ppermute x1, waiting for transfers between devices, fast(): after = lax.ppermute(up, 'band', bwd)  4.75 us
    ppermute x3, starting transfers between devices, fast(): lax.ppermute(mine, 'image', xor_route(n_image, 2 * k))  4.45 us
    ppermute x3, starting transfers between devices, fast(): lax.ppermute(parts[k], 'image', xor_route(n_image, 2 * k))  4.45 us
  transfers between devices with their start and end apart: 19, of which 14 were waited for; matrix products, arithmetic and copies ran while one was open for 0% of the time, Pallas kernels for 0%

profile of v1, /device:TPU:0, one launch (start us, length us, event | category | flops | bytes accessed | tf_op | source)
XLA Modules:
  0.0 77.3 jit_solution(3112099979812696935)
XLA Ops:
  0.0 0.9 %copy-done.2 = f32[1,128,4,128]{3,2,1,0:T(4,128)S(1)} copy-done((f32[1,128,4,128]{3,2,1,0:T(4,128)S(1)}, f32[1,128,4,128]{3,2,1,0:T(4,128)}, u32[]{:S(2)}) %copy-start.2) | copy-done | bytes 262168
  1.0 0.9 %copy-done.3 = f32[1,128,4,128]{3,2,1,0:T(4,128)S(1)} copy-done((f32[1,128,4,128]{3,2,1,0:T(4,128)S(1)}, f32[1,128,4,128]{3,2,1,0:T(4,128)}, u32[]{:S(2)}) %copy-start.3) | copy-done | bytes 262168
  1.9 4.9 %collective-permute-start = (f32[256,128]{1,0:T(8,128)S(1)}, f32[256,128]{1,0:T(8,128)S(1)}, u32[]{:S(2)}, u32[]{:S(2)}) collective-permute-start(f32[256,128]{1,0:T(8,128)S(1)} %get-tuple-element.17), channel_id=1, source_target_pairs={{0,1},{1,2},{2,3},{4,5},{5,6},{6,7},{8,9},{9,10},{10,11},{12,13},{... | collective-permute-start | bytes 393224 | tf_op jit(solution)/shard_map/ppermute | solution.py:273
  6.8 1.3 %collective-permute-start.1 = (f32[256,128]{1,0:T(8,128)S(1)}, f32[256,128]{1,0:T(8,128)S(1)}, u32[]{:S(2)}, u32[]{:S(2)}) collective-permute-start(f32[256,128]{1,0:T(8,128)S(1)} %get-tuple-element.18), channel_id=1, source_target_pairs={{1,0},{2,1},{3,2},{5,4},{6,5},{7,6},{9,8},{10,9},{11,10},{13,12},{... | collective-permute-start | bytes 393224 | tf_op jit(solution)/shard_map/ppermute | solution.py:274
  8.1 1.4 %collective-permute-done.prev_ref = f32[256,128]{1,0:T(8,128)S(1)} collective-permute-done((f32[256,128]{1,0:T(8,128)S(1)}, f32[256,128]{1,0:T(8,128)S(1)}, u32[]{:S(2)}, u32[]{:S(2)}) %collective-permute-start) | collective-permute-done | bytes 131104 | tf_op jit(solution)/shard_map/ppermute | solution.py:273
  9.5 4.8 %collective-permute-done.1.next_ref = f32[256,128]{1,0:T(8,128)S(1)} collective-permute-done((f32[256,128]{1,0:T(8,128)S(1)}, f32[256,128]{1,0:T(8,128)S(1)}, u32[]{:S(2)}, u32[]{:S(2)}) %collective-permute-start.1) | collective-permute-done | bytes 131104 | tf_op jit(solution)/shard_map/ppermute | solution.py:274
  14.3 1.3 %copy-done = f32[2,1152,128]{2,1,0:T(8,128)S(1)} copy-done((f32[2,1152,128]{2,1,0:T(8,128)S(1)}, f32[2,1152,128]{2,1,0:T(8,128)}, u32[]{:S(2)}) %copy-start) | copy-done | bytes 1179672
  15.6 3.0 %shard_map.47 = (f32[2,288,128]{2,1,0:T(8,128)S(1)}, f32[2,288,128]{2,1,0:T(8,128)S(1)}, f32[2,288,128]{2,1,0:T(8,128)S(1)}, f32[2,288,128]{2,1,0:T(8,128)S(1)}) custom-call(f32[512,128]{1,0:T(8,128)S(1)} %bitcast.3, f32[512,128]{1,0:T(8,128)S(1)} %bitcast.5, f32[256,128]{1,0:T(8,128)S(1)} %collective-permute-done.prev_ref, ...), custom_call_target="tpu_custom_call" | custom-call | flops 1811939328 | bytes 2883584 | tf_op jit(solution)/shard_map/pallas_call | solution.py:276
  18.6 1.8 %collective-permute-start.2 = (f32[2,288,128]{2,1,0:T(8,128)S(1)}, f32[2,288,128]{2,1,0:T(8,128)S(1)}, u32[]{:S(2)}, u32[]{:S(2)}) collective-permute-start(f32[2,288,128]{2,1,0:T(8,128)S(1)} %get-tuple-element.20), channel_id=1, source_target_pairs={{0,1},{1,0},{2,3},{3,2},{4,5},{5,4},{6,7},{7,6},{8,9},{9,8},{10,11... | collective-permute-start | bytes 884744 | tf_op jit(solution)/shard_map/ppermute | solution.py:287
  20.4 0.0 collective-permute-start.3
  20.4 1.7 %collective-permute-start.4 = (f32[2,288,128]{2,1,0:T(8,128)S(1)}, f32[2,288,128]{2,1,0:T(8,128)S(1)}, u32[]{:S(2)}, u32[]{:S(2)}) collective-permute-start(f32[2,288,128]{2,1,0:T(8,128)S(1)} %get-tuple-element.22), channel_id=1, source_target_pairs={{0,3},{1,2},{2,1},{3,0},{4,7},{5,6},{6,5},{7,4},{8,11},{9,10},{10,... | collective-permute-start | bytes 884744 | tf_op jit(solution)/shard_map/ppermute | solution.py:287
  22.1 6.4 %collective-permute-done.2.refs_1_ = f32[2,288,128]{2,1,0:T(8,128)S(1)} collective-permute-done((f32[2,288,128]{2,1,0:T(8,128)S(1)}, f32[2,288,128]{2,1,0:T(8,128)S(1)}, u32[]{:S(2)}, u32[]{:S(2)}) %collective-permute-start.2) | collective-permute-done | bytes 294944 | tf_op jit(solution)/shard_map/ppermute | solution.py:287
  28.5 5.2 %collective-permute-done.3.refs_2_ = f32[2,288,128]{2,1,0:T(8,128)S(1)} collective-permute-done((f32[2,288,128]{2,1,0:T(8,128)S(1)}, f32[2,288,128]{2,1,0:T(8,128)S(1)}, u32[]{:S(2)}, u32[]{:S(2)}) %collective-permute-start.3) | collective-permute-done | bytes 294944 | tf_op jit(solution)/shard_map/ppermute | solution.py:287
  33.8 0.0 collective-permute-done.4.refs_3_
  33.8 0.1 shard_map.48
  33.9 0.1 collective-permute-start.5
  33.9 1.4 %collective-permute-done.5.other_ref = f32[288,128]{1,0:T(8,128)S(1)} collective-permute-done((f32[288,128]{1,0:T(8,128)S(1)}, f32[288,128]{1,0:T(8,128)S(1)}, u32[]{:S(2)}, u32[]{:S(2)}) %collective-permute-start.5) | collective-permute-done | bytes 147488 | tf_op jit(solution)/shard_map/ppermute | solution.py:290
  35.3 1.6 %collective-permute-start.6 = (f32[2,72,128]{2,1,0:T(8,128)S(1)}, f32[2,72,128]{2,1,0:T(8,128)S(1)}, u32[]{:S(2)}, u32[]{:S(2)}) collective-permute-start(f32[2,72,128]{2,1,0:T(8,128)S(1)} %get-tuple-element.26), channel_id=1, source_target_pairs={{0,8},{4,12},{8,0},{12,4},{16,24},{20,28},{24,16},{28,20},{1,9},{5... | collective-permute-start | bytes 221192 | tf_op jit(solution)/shard_map/ppermute | solution.py:293
  37.0 2.6 %collective-permute-start.7 = (f32[2,72,128]{2,1,0:T(8,128)S(1)}, f32[2,72,128]{2,1,0:T(8,128)S(1)}, u32[]{:S(2)}, u32[]{:S(2)}) collective-permute-start(f32[2,72,128]{2,1,0:T(8,128)S(1)} %get-tuple-element.27), channel_id=1, source_target_pairs={{0,16},{4,20},{8,24},{12,28},{16,0},{20,4},{24,8},{28,12},{1,17},{... | collective-permute-start | bytes 221192 | tf_op jit(solution)/shard_map/ppermute | solution.py:293
  39.6 0.2 collective-permute-start.8
  39.8 0.0 collective-permute-done.6.refs_1_
  39.8 5.2 %collective-permute-done.7.refs_2_ = f32[2,72,128]{2,1,0:T(8,128)S(1)} collective-permute-done((f32[2,72,128]{2,1,0:T(8,128)S(1)}, f32[2,72,128]{2,1,0:T(8,128)S(1)}, u32[]{:S(2)}, u32[]{:S(2)}) %collective-permute-start.7) | collective-permute-done | bytes 73760 | tf_op jit(solution)/shard_map/ppermute | solution.py:293
  45.0 0.8 %collective-permute-done.8.refs_3_ = f32[2,72,128]{2,1,0:T(8,128)S(1)} collective-permute-done((f32[2,72,128]{2,1,0:T(8,128)S(1)}, f32[2,72,128]{2,1,0:T(8,128)S(1)}, u32[]{:S(2)}, u32[]{:S(2)}) %collective-permute-start.8) | collective-permute-done | bytes 73760 | tf_op jit(solution)/shard_map/ppermute | solution.py:293
  45.8 0.3 shard_map.50
  46.1 11.7 %all_to_all.5.sums_ref = f32[32,8,128]{2,1,0:T(8,128)S(1)} all-to-all(f32[32,8,128]{2,1,0:T(8,128)S(1)} %broadcast_in_dim.2), channel_id=1, replica_groups=mesh['image'=8,'band'=4] {'image','band'}, dimensions={0} | all-to-all | bytes 262144 | tf_op jit(solution)/shard_map/all_to_all | solution.py:301
  57.8 0.6 shard_map.51.refs_0_
  58.4 1.4 %collective-permute-start.11 = (f32[72,128]{1,0:T(8,128)S(1)}, f32[72,128]{1,0:T(8,128)S(1)}, u32[]{:S(2)}, u32[]{:S(2)}) collective-permute-start(f32[72,128]{1,0:T(8,128)S(1)} %shard_map.51.refs_0_), channel_id=1, source_target_pairs={{0,24},{4,28},{8,16},{12,20},{16,8},{20,12},{24,0},{28,4},{1,25},{... | collective-permute-start | bytes 110600 | tf_op jit(solution)/shard_map/ppermute | solution.py:304
  59.8 0.8 %collective-permute-start.10 = (f32[72,128]{1,0:T(8,128)S(1)}, f32[72,128]{1,0:T(8,128)S(1)}, u32[]{:S(2)}, u32[]{:S(2)}) collective-permute-start(f32[72,128]{1,0:T(8,128)S(1)} %shard_map.51.refs_0_), channel_id=1, source_target_pairs={{0,16},{4,20},{8,24},{12,28},{16,0},{20,4},{24,8},{28,12},{1,17},{... | collective-permute-start | bytes 110600 | tf_op jit(solution)/shard_map/ppermute | solution.py:304
  60.5 2.3 %collective-permute-start.9 = (f32[72,128]{1,0:T(8,128)S(1)}, f32[72,128]{1,0:T(8,128)S(1)}, u32[]{:S(2)}, u32[]{:S(2)}) collective-permute-start(f32[72,128]{1,0:T(8,128)S(1)} %shard_map.51.refs_0_), channel_id=1, source_target_pairs={{0,8},{4,12},{8,0},{12,4},{16,24},{20,28},{24,16},{28,20},{1,9},{5... | collective-permute-start | bytes 110600 | tf_op jit(solution)/shard_map/ppermute | solution.py:304
  62.8 1.7 %collective-permute-done.11.refs_3_ = f32[72,128]{1,0:T(8,128)S(1)} collective-permute-done((f32[72,128]{1,0:T(8,128)S(1)}, f32[72,128]{1,0:T(8,128)S(1)}, u32[]{:S(2)}, u32[]{:S(2)}) %collective-permute-start.11) | collective-permute-done | bytes 36896 | tf_op jit(solution)/shard_map/ppermute | solution.py:304
  64.5 0.7 collective-permute-done.10.refs_2_
  65.2 0.0 collective-permute-done.9.refs_1_
  65.2 0.7 collective-permute-start.14
  65.9 1.4 %collective-permute-start.13 = (f32[288,128]{1,0:T(8,128)S(1)}, f32[288,128]{1,0:T(8,128)S(1)}, u32[]{:S(2)}, u32[]{:S(2)}) collective-permute-start(f32[288,128]{1,0:T(8,128)S(1)} %shard_map.52.refs_0_), channel_id=1, source_target_pairs={{0,2},{1,3},{2,0},{3,1},{4,6},{5,7},{6,4},{7,5},{8,10},{9,11},{10,... | collective-permute-start | bytes 442376 | tf_op jit(solution)/shard_map/ppermute | solution.py:308
  67.3 1.5 %collective-permute-start.12 = (f32[288,128]{1,0:T(8,128)S(1)}, f32[288,128]{1,0:T(8,128)S(1)}, u32[]{:S(2)}, u32[]{:S(2)}) collective-permute-start(f32[288,128]{1,0:T(8,128)S(1)} %shard_map.52.refs_0_), channel_id=1, source_target_pairs={{0,1},{1,0},{2,3},{3,2},{4,5},{5,4},{6,7},{7,6},{8,9},{9,8},{10,11... | collective-permute-start | bytes 442376 | tf_op jit(solution)/shard_map/ppermute | solution.py:308
  68.8 0.0 collective-permute-start.15
  68.8 3.4 %collective-permute-done.14.refs_3_ = f32[288,128]{1,0:T(8,128)S(1)} collective-permute-done((f32[288,128]{1,0:T(8,128)S(1)}, f32[288,128]{1,0:T(8,128)S(1)}, u32[]{:S(2)}, u32[]{:S(2)}) %collective-permute-start.14) | collective-permute-done | bytes 147488 | tf_op jit(solution)/shard_map/ppermute | solution.py:308
  72.2 0.0 collective-permute-start.18
  72.2 1.1 %collective-permute-done.13.refs_2_ = f32[288,128]{1,0:T(8,128)S(1)} collective-permute-done((f32[288,128]{1,0:T(8,128)S(1)}, f32[288,128]{1,0:T(8,128)S(1)}, u32[]{:S(2)}, u32[]{:S(2)}) %collective-permute-start.13) | collective-permute-done | bytes 147488 | tf_op jit(solution)/shard_map/ppermute | solution.py:308
  73.3 0.0 collective-permute-start.17
  73.3 0.8 %collective-permute-done.12.refs_1_ = f32[288,128]{1,0:T(8,128)S(1)} collective-permute-done((f32[288,128]{1,0:T(8,128)S(1)}, f32[288,128]{1,0:T(8,128)S(1)}, u32[]{:S(2)}, u32[]{:S(2)}) %collective-permute-start.12) | collective-permute-done | bytes 147488 | tf_op jit(solution)/shard_map/ppermute | solution.py:308
  74.1 0.0 collective-permute-start.16
  74.1 0.0 collective-permute-done.15.refs_4_
  74.1 0.0 collective-permute-done.18.refs_7_
  74.2 0.5 collective-permute-done.17.refs_6_
  74.7 0.8 %collective-permute-done.16.refs_5_ = f32[288,128]{1,0:T(8,128)S(1)} collective-permute-done((f32[288,128]{1,0:T(8,128)S(1)}, f32[288,128]{1,0:T(8,128)S(1)}, u32[]{:S(2)}, u32[]{:S(2)}) %collective-permute-start.16) | collective-permute-done | bytes 147488 | tf_op jit(solution)/shard_map/ppermute | solution.py:310
  75.5 0.0 copy-done.1
  75.5 1.8 %shard_map.53 = f32[1,2,1152,128]{3,2,1,0:T(8,128)} custom-call(f32[2]{0:T(128)S(1)} %copy-done.4, f32[2,1152,128]{2,1,0:T(8,128)S(1)} %copy-done.1, f32[288,128]{1,0:T(8,128)S(1)} %shard_map.52.refs_0_, f32[288,128]{1,0:T(8,128)S(1)} %collective-permute-done.12.refs_1_, f32[288,128]{1,0:T(8,128)S(1)} %collective-permute-done.13.refs_2_, ...), custom_call_target="tpu_custom_call" | custom-call | tf_op jit(solution)/shard_map/pallas_call | solution.py:311
  (10 shorter events, 0.1 us)
Async XLA Ops:
  0.0 0.9 %copy-start.2 = (f32[1,128,4,128]{3,2,1,0:T(4,128)S(1)}, f32[1,128,4,128]{3,2,1,0:T(4,128)}, u32[]{:S(2)}) copy-start(f32[1,128,4,128]{3,2,1,0:T(4,128)} %param.4) | copy-start | bytes 786436
  1.0 0.9 %copy-start.3 = (f32[1,128,4,128]{3,2,1,0:T(4,128)S(1)}, f32[1,128,4,128]{3,2,1,0:T(4,128)}, u32[]{:S(2)}) copy-start(f32[1,128,4,128]{3,2,1,0:T(4,128)} %param.5) | copy-start | bytes 786436
  1.9 7.6 %collective-permute-start = (f32[256,128]{1,0:T(8,128)S(1)}, f32[256,128]{1,0:T(8,128)S(1)}, u32[]{:S(2)}, u32[]{:S(2)}) collective-permute-start(f32[256,128]{1,0:T(8,128)S(1)} %get-tuple-element.17), channel_id=1, source_target_pairs={{0,1},{1,2},{2,3},{4,5},{5,6},{6,7},{8,9},{9,10},{10,11},{12,13},{... | collective-permute-start | bytes 393224 | tf_op jit(solution)/shard_map/ppermute | solution.py:273
  6.8 7.5 %collective-permute-start.1 = (f32[256,128]{1,0:T(8,128)S(1)}, f32[256,128]{1,0:T(8,128)S(1)}, u32[]{:S(2)}, u32[]{:S(2)}) collective-permute-start(f32[256,128]{1,0:T(8,128)S(1)} %get-tuple-element.18), channel_id=1, source_target_pairs={{1,0},{2,1},{3,2},{5,4},{6,5},{7,6},{9,8},{10,9},{11,10},{13,12},{... | collective-permute-start | bytes 393224 | tf_op jit(solution)/shard_map/ppermute | solution.py:274
  14.3 1.3 %copy-start = (f32[2,1152,128]{2,1,0:T(8,128)S(1)}, f32[2,1152,128]{2,1,0:T(8,128)}, u32[]{:S(2)}) copy-start(f32[2,1152,128]{2,1,0:T(8,128)} %f_ref.3) | copy-start | bytes 3538948
  18.6 9.9 %collective-permute-start.2 = (f32[2,288,128]{2,1,0:T(8,128)S(1)}, f32[2,288,128]{2,1,0:T(8,128)S(1)}, u32[]{:S(2)}, u32[]{:S(2)}) collective-permute-start(f32[2,288,128]{2,1,0:T(8,128)S(1)} %get-tuple-element.20), channel_id=1, source_target_pairs={{0,1},{1,0},{2,3},{3,2},{4,5},{5,4},{6,7},{7,6},{8,9},{9,8},{10,11... | collective-permute-start | bytes 884744 | tf_op jit(solution)/shard_map/ppermute | solution.py:287
  20.4 13.4 %collective-permute-start.3 = (f32[2,288,128]{2,1,0:T(8,128)S(1)}, f32[2,288,128]{2,1,0:T(8,128)S(1)}, u32[]{:S(2)}, u32[]{:S(2)}) collective-permute-start(f32[2,288,128]{2,1,0:T(8,128)S(1)} %get-tuple-element.21), channel_id=1, source_target_pairs={{0,2},{1,3},{2,0},{3,1},{4,6},{5,7},{6,4},{7,5},{8,10},{9,11},{10,... | collective-permute-start | bytes 884744 | tf_op jit(solution)/shard_map/ppermute | solution.py:287
  20.4 13.4 %collective-permute-start.4 = (f32[2,288,128]{2,1,0:T(8,128)S(1)}, f32[2,288,128]{2,1,0:T(8,128)S(1)}, u32[]{:S(2)}, u32[]{:S(2)}) collective-permute-start(f32[2,288,128]{2,1,0:T(8,128)S(1)} %get-tuple-element.22), channel_id=1, source_target_pairs={{0,3},{1,2},{2,1},{3,0},{4,7},{5,6},{6,5},{7,4},{8,11},{9,10},{10,... | collective-permute-start | bytes 884744 | tf_op jit(solution)/shard_map/ppermute | solution.py:287
  33.8 41.7 %copy-start.1 = (f32[2,1152,128]{2,1,0:T(8,128)S(1)}, f32[2,1152,128]{2,1,0:T(8,128)}, u32[]{:S(2)}) copy-start(f32[2,1152,128]{2,1,0:T(8,128)} %f_ref.3) | copy-start | bytes 3538948
  33.8 41.7 %copy-start.4 = (f32[2]{0:T(128)S(1)}, f32[2]{0:T(128)}, u32[]{:S(2)}) copy-start(f32[2]{0:T(128)} %rates_ref.1) | copy-start | bytes 28
  33.9 1.4 %collective-permute-start.5 = (f32[288,128]{1,0:T(8,128)S(1)}, f32[288,128]{1,0:T(8,128)S(1)}, u32[]{:S(2)}, u32[]{:S(2)}) collective-permute-start(f32[288,128]{1,0:T(8,128)S(1)} %get-tuple-element.24), channel_id=1, source_target_pairs={{0,4},{4,0},{8,12},{12,8},{16,20},{20,16},{24,28},{28,24},{1,5},{5... | collective-permute-start | bytes 442376 | tf_op jit(solution)/shard_map/ppermute | solution.py:290
  35.3 4.5 %collective-permute-start.6 = (f32[2,72,128]{2,1,0:T(8,128)S(1)}, f32[2,72,128]{2,1,0:T(8,128)S(1)}, u32[]{:S(2)}, u32[]{:S(2)}) collective-permute-start(f32[2,72,128]{2,1,0:T(8,128)S(1)} %get-tuple-element.26), channel_id=1, source_target_pairs={{0,8},{4,12},{8,0},{12,4},{16,24},{20,28},{24,16},{28,20},{1,9},{5... | collective-permute-start | bytes 221192 | tf_op jit(solution)/shard_map/ppermute | solution.py:293
  37.0 8.1 %collective-permute-start.7 = (f32[2,72,128]{2,1,0:T(8,128)S(1)}, f32[2,72,128]{2,1,0:T(8,128)S(1)}, u32[]{:S(2)}, u32[]{:S(2)}) collective-permute-start(f32[2,72,128]{2,1,0:T(8,128)S(1)} %get-tuple-element.27), channel_id=1, source_target_pairs={{0,16},{4,20},{8,24},{12,28},{16,0},{20,4},{24,8},{28,12},{1,17},{... | collective-permute-start | bytes 221192 | tf_op jit(solution)/shard_map/ppermute | solution.py:293
  39.6 6.3 %collective-permute-start.8 = (f32[2,72,128]{2,1,0:T(8,128)S(1)}, f32[2,72,128]{2,1,0:T(8,128)S(1)}, u32[]{:S(2)}, u32[]{:S(2)}) collective-permute-start(f32[2,72,128]{2,1,0:T(8,128)S(1)} %get-tuple-element.28), channel_id=1, source_target_pairs={{0,24},{4,28},{8,16},{12,20},{16,8},{20,12},{24,0},{28,4},{1,25},{... | collective-permute-start | bytes 221192 | tf_op jit(solution)/shard_map/ppermute | solution.py:293
  58.4 6.1 %collective-permute-start.11 = (f32[72,128]{1,0:T(8,128)S(1)}, f32[72,128]{1,0:T(8,128)S(1)}, u32[]{:S(2)}, u32[]{:S(2)}) collective-permute-start(f32[72,128]{1,0:T(8,128)S(1)} %shard_map.51.refs_0_), channel_id=1, source_target_pairs={{0,24},{4,28},{8,16},{12,20},{16,8},{20,12},{24,0},{28,4},{1,25},{... | collective-permute-start | bytes 110600 | tf_op jit(solution)/shard_map/ppermute | solution.py:304
  59.8 5.4 %collective-permute-start.10 = (f32[72,128]{1,0:T(8,128)S(1)}, f32[72,128]{1,0:T(8,128)S(1)}, u32[]{:S(2)}, u32[]{:S(2)}) collective-permute-start(f32[72,128]{1,0:T(8,128)S(1)} %shard_map.51.refs_0_), channel_id=1, source_target_pairs={{0,16},{4,20},{8,24},{12,28},{16,0},{20,4},{24,8},{28,12},{1,17},{... | collective-permute-start | bytes 110600 | tf_op jit(solution)/shard_map/ppermute | solution.py:304
  60.5 4.7 %collective-permute-start.9 = (f32[72,128]{1,0:T(8,128)S(1)}, f32[72,128]{1,0:T(8,128)S(1)}, u32[]{:S(2)}, u32[]{:S(2)}) collective-permute-start(f32[72,128]{1,0:T(8,128)S(1)} %shard_map.51.refs_0_), channel_id=1, source_target_pairs={{0,8},{4,12},{8,0},{12,4},{16,24},{20,28},{24,16},{28,20},{1,9},{5... | collective-permute-start | bytes 110600 | tf_op jit(solution)/shard_map/ppermute | solution.py:304
  65.2 7.0 %collective-permute-start.14 = (f32[288,128]{1,0:T(8,128)S(1)}, f32[288,128]{1,0:T(8,128)S(1)}, u32[]{:S(2)}, u32[]{:S(2)}) collective-permute-start(f32[288,128]{1,0:T(8,128)S(1)} %shard_map.52.refs_0_), channel_id=1, source_target_pairs={{0,3},{1,2},{2,1},{3,0},{4,7},{5,6},{6,5},{7,4},{8,11},{9,10},{10,... | collective-permute-start | bytes 442376 | tf_op jit(solution)/shard_map/ppermute | solution.py:308
  65.9 7.4 %collective-permute-start.13 = (f32[288,128]{1,0:T(8,128)S(1)}, f32[288,128]{1,0:T(8,128)S(1)}, u32[]{:S(2)}, u32[]{:S(2)}) collective-permute-start(f32[288,128]{1,0:T(8,128)S(1)} %shard_map.52.refs_0_), channel_id=1, source_target_pairs={{0,2},{1,3},{2,0},{3,1},{4,6},{5,7},{6,4},{7,5},{8,10},{9,11},{10,... | collective-permute-start | bytes 442376 | tf_op jit(solution)/shard_map/ppermute | solution.py:308
  67.3 6.8 %collective-permute-start.12 = (f32[288,128]{1,0:T(8,128)S(1)}, f32[288,128]{1,0:T(8,128)S(1)}, u32[]{:S(2)}, u32[]{:S(2)}) collective-permute-start(f32[288,128]{1,0:T(8,128)S(1)} %shard_map.52.refs_0_), channel_id=1, source_target_pairs={{0,1},{1,0},{2,3},{3,2},{4,5},{5,4},{6,7},{7,6},{8,9},{9,8},{10,11... | collective-permute-start | bytes 442376 | tf_op jit(solution)/shard_map/ppermute | solution.py:308
  68.8 5.4 %collective-permute-start.15 = (f32[288,128]{1,0:T(8,128)S(1)}, f32[288,128]{1,0:T(8,128)S(1)}, u32[]{:S(2)}, u32[]{:S(2)}) collective-permute-start(f32[288,128]{1,0:T(8,128)S(1)} %shard_map.52.refs_0_), channel_id=1, source_target_pairs={{0,4},{4,0},{8,12},{12,8},{16,20},{20,16},{24,28},{28,24},{1,5},{5... | collective-permute-start | bytes 442376 | tf_op jit(solution)/shard_map/ppermute | solution.py:310
  72.2 1.9 %collective-permute-start.18 = (f32[288,128]{1,0:T(8,128)S(1)}, f32[288,128]{1,0:T(8,128)S(1)}, u32[]{:S(2)}, u32[]{:S(2)}) collective-permute-start(f32[288,128]{1,0:T(8,128)S(1)} %collective-permute-done.14.refs_3_), channel_id=1, source_target_pairs={{0,4},{4,0},{8,12},{12,8},{16,20},{20,16},{24,28},{28,24},{1,5},{5... | collective-permute-start | bytes 442376 | tf_op jit(solution)/shard_map/ppermute | solution.py:310
  73.3 1.4 %collective-permute-start.17 = (f32[288,128]{1,0:T(8,128)S(1)}, f32[288,128]{1,0:T(8,128)S(1)}, u32[]{:S(2)}, u32[]{:S(2)}) collective-permute-start(f32[288,128]{1,0:T(8,128)S(1)} %collective-permute-done.13.refs_2_), channel_id=1, source_target_pairs={{0,4},{4,0},{8,12},{12,8},{16,20},{20,16},{24,28},{28,24},{1,5},{5... | collective-permute-start | bytes 442376 | tf_op jit(solution)/shard_map/ppermute | solution.py:310
  74.1 1.4 %collective-permute-start.16 = (f32[288,128]{1,0:T(8,128)S(1)}, f32[288,128]{1,0:T(8,128)S(1)}, u32[]{:S(2)}, u32[]{:S(2)}) collective-permute-start(f32[288,128]{1,0:T(8,128)S(1)} %collective-permute-done.12.refs_1_), channel_id=1, source_target_pairs={{0,4},{4,0},{8,12},{12,8},{16,20},{20,16},{24,28},{28,24},{1,5},{5... | collective-permute-start | bytes 442376 | tf_op jit(solution)/shard_map/ppermute | solution.py:310

commit v2 on v1

--- a/solution.py
+++ b/solution.py
@@ -6,6 +6,7 @@
 from jax.experimental import pallas as pl
 from jax.experimental.pallas import tpu as pltpu
 from jax.sharding import PartitionSpec as P
+
 
 HIGH = lax.Precision.HIGHEST
 F32 = jnp.float32
@@ -24,9 +25,17 @@
     )
 
 
-def edges_kernel(rows, x_ref, c_ref, down_ref, up_ref):
-    chans = x_ref.shape[0] // rows
+def edges_kernel(x_hbm, c_hbm, down_ref, up_ref, x_ref, c_ref, sems):
+    copies = [
+        pltpu.make_async_copy(x_hbm, x_ref, sems.at[0]),
+        pltpu.make_async_copy(c_hbm, c_ref, sems.at[1]),
+    ]
+    for copy in copies:
+        copy.start()
+    chans = down_ref.shape[0] // 2
+    rows = x_ref.shape[0] // chans
     for slot, ref in enumerate((x_ref, c_ref)):
+        copies[slot].wait()
         at = slice(slot * chans, (slot + 1) * chans)
         up_ref[at, :] = ref[pl.ds(0, chans, stride=rows), :]
         down_ref[at, :] = ref[pl.ds(rows - 1, chans, stride=rows), :]
@@ -52,30 +61,24 @@
     return jnp.where(col == 0, 0.0, pltpu.roll(value, 1, 1))
 
 
-def grads_kernel(
-    rows, scale, n_band, x_ref, c_ref, prev_ref, next_ref, f_ref, *rest
-):
-    outs = rest[:n_band]
-    g_ref, xh, xl, ch, cl, fh, fl, dh, dl = rest[n_band:]
+def put(high_ref, low_ref, at, row, value):
+    high, low = halves(value)
+    rows, cols = value.shape
+    part = (slice(at * rows, (at + 1) * rows), slice(row * cols, (row + 1) * cols))
+    high_ref[part] = high
+    low_ref[part] = low
+
+
+def inner_kernel(rows, x_ref, c_ref, f_ref, *refs):
+    xh, xl, ch, cl, fh, fl, gh, gl, pre_ref, back_ref = refs
     chans = x_ref.shape[0] // rows
     cols = x_ref.shape[1]
-
-    def row_of(ref, slot, row):
-        if row < 0:
-            return prev_ref[slot * chans : (slot + 1) * chans, :]
-        if row == rows:
-            return next_ref[slot * chans : (slot + 1) * chans, :]
-        return ref[pl.ds(row, chans, stride=rows), :]
-
-    def put(high_ref, low_ref, at, row, value):
-        high, low = halves(value)
-        part = (slice(at * chans, (at + 1) * chans), slice(row * cols, (row + 1) * cols))
-        high_ref[part] = high
-        low_ref[part] = low
-
+    blank = jnp.zeros((chans, cols), F32)
     for row in range(-1, rows + 1):
-        value = row_of(x_ref, 0, row)
-        other = row_of(c_ref, 1, row)
+        inside = 0 <= row < rows
+        at = pl.ds(row, chans, stride=rows)
+        value = x_ref[at, :] if inside else blank
+        other = c_ref[at, :] if inside else blank
         for a in range(3):
             if 0 <= row - a + 1 < rows:
                 put(xh, xl, a, row - a + 1, value)
@@ -83,55 +86,83 @@
                 put(ch, cl, a, row + a - 1, other)
     for a in range(3):
         for b in range(3):
-            tap = f_ref[0, pl.ds(3 * a + b, chans, stride=9), :]
-            put(fh, fl, b, a, tap.T)
-    pre3 = dot3(fh[...], fl[...], xh[...], xl[...], ((1,), (0,)))
-    for a in range(3):
-        for b in range(3):
-            put(fh, fl, b, a, f_ref[1, pl.ds(3 * a + b, chans, stride=9), :])
-    back3 = dot3(fh[...], fl[...], ch[...], cl[...], ((1,), (0,)))
+            at = pl.ds(3 * a + b, chans, stride=9)
+            put(fh, fl, b, a, f_ref[0, at, :].T)
+            put(gh, gl, b, a, f_ref[1, at, :])
+    pre_ref[...] = dot3(fh[...], fl[...], xh[...], xl[...], ((1,), (0,)))
+    back_ref[...] = dot3(gh[...], gl[...], ch[...], cl[...], ((1,), (0,)))
+
+
+def grads_kernel(rows, scale, n_band, cuts, *refs):
+    prev_ref, next_ref, xh, xl, ch, cl, fh, fl, gh, gl, pre_ref, back_ref = refs[:12]
+    outs, (g_ref, dh, dl) = refs[12:-3], refs[-3:]
+    chans = prev_ref.shape[0] // 2
+    cols = prev_ref.shape[1]
+    last = rows - 1
+    mm, nt = ((1,), (0,)), ((1,), (1,))
+    tall = [slice(k * chans, (k + 1) * chans) for k in range(3)]
+    x_rim = {0: (0, halves(prev_ref[:chans, :])), 2: (last, halves(next_ref[:chans, :]))}
+    c_rim = {2: (0, halves(prev_ref[chans:, :])), 0: (last, halves(next_ref[chans:, :]))}
+    pre_rim = {
+        row: dot3(fh[:, tall[a]], fl[:, tall[a]], *rim, mm) for a, (row, rim) in x_rim.items()
+    }
+    back_rim = {
+        row: dot3(gh[:, tall[a]], gl[:, tall[a]], *rim, mm) for a, (row, rim) in c_rim.items()
+    }
     dpres = []
     for row in range(rows):
-        at = slice(row * cols, (row + 1) * cols)
+        wide = slice(row * cols, (row + 1) * cols)
+
+        def summed(ref, rim, k):
+            value = ref[tall[k], wide]
+            return value + rim[row][tall[k], :] if row in rim else value
+
         pre = scale * (
-            pre3[chans : 2 * chans, at]
-            + moved(pre3[:chans, at], -1)
-            + moved(pre3[2 * chans :, at], 1)
+            summed(pre_ref, pre_rim, 1)
+            + moved(summed(pre_ref, pre_rim, 0), -1)
+            + moved(summed(pre_ref, pre_rim, 2), 1)
         )
         dhidden = scale * (
-            back3[chans : 2 * chans, at]
-            + moved(back3[:chans, at], 1)
-            + moved(back3[2 * chans :, at], -1)
+            summed(back_ref, back_rim, 1)
+            + moved(summed(back_ref, back_rim, 0), 1)
+            + moved(summed(back_ref, back_rim, 2), -1)
         )
         sig = jax.nn.sigmoid(pre)
         hidden = pre * sig
-        dpre = dhidden * sig * (1.0 + pre * (1.0 - sig))
-        dpres.append(dpre)
+        dpres.append(dhidden * sig * (1.0 + pre * (1.0 - sig)))
         for b, value in enumerate((moved(hidden, -1), hidden, moved(hidden, 1))):
             put(dh, dl, b, row, value)
-    grad2 = dot3(dh[...], dl[...], ch[...], cl[...], ((1,), (1,)))
+    grad2 = dot3(dh[...], dl[...], ch[...], cl[...], nt)
     for a in range(3):
+        part = grad2[:, tall[a]]
+        if a in c_rim:
+            row, rim = c_rim[a]
+            wide = slice(row * cols, (row + 1) * cols)
+            part = part + dot3(dh[:, wide], dl[:, wide], *rim, nt)
         for b in range(3):
             t = 3 * a + b
-            g_ref[1, t * chans : (t + 1) * chans, :] = (
-                scale * grad2[b * chans : (b + 1) * chans, a * chans : (a + 1) * chans]
-            )
+            g_ref[1, t * chans : (t + 1) * chans, :] = scale * part[tall[b], :]
     for row, dpre in enumerate(dpres):
         for b, value in enumerate((moved(dpre, 1), dpre, moved(dpre, -1))):
             put(dh, dl, b, row, value)
-    grad1 = dot3(xh[...], xl[...], dh[...], dl[...], ((1,), (1,)))
+    grad1 = dot3(xh[...], xl[...], dh[...], dl[...], nt)
     for a in range(3):
+        part = grad1[tall[a], :]
+        if a in x_rim:
+            row, rim = x_rim[a]
+            wide = slice(row * cols, (row + 1) * cols)
+            part = part + dot3(*rim, dh[:, wide], dl[:, wide], nt)
         for b in range(3):
             t = 3 * a + b
-            g_ref[0, t * chans : (t + 1) * chans, :] = (
-                scale * grad1[a * chans : (a + 1) * chans, b * chans : (b + 1) * chans]
-            )
+            g_ref[0, t * chans : (t + 1) * chans, :] = scale * part[:, tall[b]]
     band = lax.axis_index("band")
     size = g_ref.shape[1] // n_band
-    for k, out in enumerate(outs):
-        start = pl.multiple_of(lax.bitwise_xor(band, k) * size, 8)
-        for layer in range(2):
-            out[layer] = g_ref[layer, pl.ds(start, size), :]
+    for k in range(n_band):
+        start = lax.bitwise_xor(band, k) * size
+        for c, (off, height) in enumerate(cuts):
+            at = pl.ds(pl.multiple_of(start + off, 8), height)
+            for layer in range(2):
+                outs[c * n_band + k][layer] = g_ref[layer, at, :]
 
 
 def sum_kernel(n_band, *refs):
@@ -155,38 +186,42 @@
         out[1 - mine] = other_ref[pl.ds(start, size), :]
 
 
-def gram_kernel(n_pair, *refs):
-    parts, out = refs[:n_pair], refs[n_pair]
-    held = refs[n_pair + 1]
+def gram_kernel(n_pair, cuts, *refs):
+    parts, (out, held) = refs[:-2], refs[-2:]
     pair = lax.axis_index("image") // 2
-    for k, part in enumerate(parts):
-        at = lax.bitwise_xor(pair, k) * 2
-        held[at] = part[0]
-        held[at + 1] = part[1]
+    for c, (off, height) in enumerate(cuts):
+        for k in range(n_pair):
+            at = lax.bitwise_xor(pair, k) * 2
+            for j in range(2):
+                held[at + j, off : off + height, :] = parts[c * n_pair + k][j]
     count = 2 * n_pair
-    row = lax.broadcasted_iota(jnp.int32, out.shape, 0)
     col = lax.broadcasted_iota(jnp.int32, out.shape, 1)
     total = jnp.zeros(out.shape, F32)
     for i in range(count):
         for j in range(i, count):
             value = jnp.sum(held[i] * held[j], keepdims=True)
-            here = ((row == i) & (col == j)) | ((row == j) & (col == i))
-            total = jnp.where(here, value, total)
+            total = jnp.where((col == i * count + j) | (col == j * count + i), value, total)
     out[...] = total
 
 
-def merge_kernel(n_pair, n_band, sums_ref, *refs):
-    parts, out = refs[:n_pair], refs[n_pair]
+def merge_kernel(n_pair, n_band, cuts, sums_ref, *refs):
+    parts, out = refs[:-1], refs[-1]
     image = lax.axis_index("image")
     mine = image % 2
     pair = image // 2
     count = 2 * n_pair
-    gram = jnp.zeros(sums_ref.shape[1:], F32)
-    for half in range(n_pair):
-        for at in range(n_band):
-            gram = gram + sums_ref[(2 * half + mine) * n_band + at]
-    row = lax.broadcasted_iota(jnp.int32, gram.shape, 0)
-    col = lax.broadcasted_iota(jnp.int32, gram.shape, 1)
+    sums = sums_ref[...]
+    lanes = sums.shape[1]
+    device = lax.broadcasted_iota(jnp.int32, sums.shape, 0)
+    same = ((device // n_band) % 2) == mine
+    flat = jnp.sum(jnp.where(same, sums, 0.0), 0, keepdims=True)
+    row = lax.broadcasted_iota(jnp.int32, (count, lanes), 0)
+    col = lax.broadcasted_iota(jnp.int32, (count, lanes), 1)
+    gram = jnp.broadcast_to(flat, (count, lanes))
+    wide = gram
+    for i in range(1, count):
+        gram = jnp.where(row == i, pltpu.roll(wide, lanes - i * count, 1), gram)
+    gram = jnp.where(col < count, gram, 0.0)
 
     def swap(value, axis, step):
         size = value.shape[axis]
@@ -214,22 +249,26 @@
         gram = gram + swap(gram, 1, step)
         step *= 2
     place = lax.broadcasted_iota(jnp.int32, weight.shape, 0)
-    total = jnp.zeros(out.shape, F32)
-    for k, part in enumerate(parts):
+    factors = {}
+    for k in range(n_pair):
         at = lax.bitwise_xor(pair, k) * 2
         for j in range(2):
-            factor = jnp.sum(jnp.where(place == at + j, weight, 0.0), keepdims=True)
-            total = total + factor * part[j]
-    out[...] = total
-
-
-def gather_kernel(n_pair, *refs):
+            factors[k, j] = jnp.sum(jnp.where(place == at + j, weight, 0.0), keepdims=True)
+    for c, (off, height) in enumerate(cuts):
+        total = jnp.zeros((height, out.shape[1]), F32)
+        for k in range(n_pair):
+            for j in range(2):
+                total = total + factors[k, j] * parts[c * n_pair + k][j]
+        out[off : off + height, :] = total
+
+
+def gather_kernel(n_pair, cuts, *refs):
     parts, out = refs[:n_pair], refs[n_pair]
     pair = lax.axis_index("image") // 2
-    size = parts[0].shape[0]
-    for k, part in enumerate(parts):
-        start = pl.multiple_of(lax.bitwise_xor(pair, k) * size, 8)
-        out[pl.ds(start, size), :] = part[...]
+    for off, height in cuts:
+        for k, part in enumerate(parts):
+            start = off * n_pair + lax.bitwise_xor(pair, k) * height
+            out[pl.ds(pl.multiple_of(start, 8), height), :] = part[off : off + height, :]
 
 
 def final_kernel(n_band, chans, rates_ref, f_ref, *refs):
@@ -256,6 +295,10 @@
     return [(i, i ^ k) for i in range(count)]
 
 
+def swapped(value, axis, k):
+    return lax.ppermute(value, axis, xor_route(lax.axis_size(axis), k))
+
+
 def fast(images, cotangent, filters, rates):
     _, chans, rows, cols = images.shape
     n_band = lax.axis_size("band")
@@ -267,43 +310,67 @@
     scale = kdim ** (-0.5)
     x = images.reshape(chans * rows, cols)
     cot = cotangent.reshape(chans * rows, cols)
-    down, up = call(functools.partial(edges_kernel, rows), [(2 * chans, cols)] * 2)(x, cot)
+    down, up = pl.pallas_call(
+        edges_kernel,
+        out_shape=[jax.ShapeDtypeStruct((2 * chans, cols), F32)] * 2,
+        in_specs=[pl.BlockSpec(memory_space=pl.ANY)] * 2,
+        scratch_shapes=[pltpu.VMEM(x.shape, F32)] * 2 + [pltpu.SemaphoreType.DMA((2,))],
+        compiler_params=pltpu.CompilerParams(vmem_limit_bytes=60 * 2**20),
+    )(x, cot)
     fwd = [(i, i + 1) for i in range(n_band - 1)]
     bwd = [(j, i) for i, j in fwd]
     before = lax.ppermute(down, "band", fwd)
     after = lax.ppermute(up, "band", bwd)
-    wide = (3 * chans, rows * cols)
+    tall, wide = 3 * chans, rows * cols
+    inner = pl.pallas_call(
+        functools.partial(inner_kernel, rows),
+        out_shape=[jax.ShapeDtypeStruct((tall, wide), BF16)] * 4
+        + [jax.ShapeDtypeStruct((tall, tall), BF16)] * 4
+        + [jax.ShapeDtypeStruct((tall, wide), F32)] * 2,
+        cost_estimate=pl.CostEstimate(
+            flops=12 * tall * tall * wide, bytes_accessed=8 * kdim * chans, transcendentals=0
+        ),
+        compiler_params=pltpu.CompilerParams(vmem_limit_bytes=40 * 2**20),
+    )(x, cot, filters)
+    tiles = slot // 8
+    first = 8 * ((tiles + 1) // 2)
+    slots = [(0, first)] + ([(first, slot - first)] if first < slot else [])
+    cuts = [(off * n_pair, height * n_pair) for off, height in slots]
     parts = call(
-        functools.partial(grads_kernel, rows, scale, n_band),
-        [(2, block, chans)] * n_band,
-        [pltpu.VMEM((2, kdim, chans), F32)]
-        + [pltpu.VMEM(wide, BF16)] * 4
-        + [pltpu.VMEM((3 * chans, 3 * chans), BF16)] * 2
-        + [pltpu.VMEM(wide, BF16)] * 2,
-        flops=24 * kdim * chans * rows * cols,
-        nbytes=4 * (2 * chans * rows * cols + 4 * kdim * chans),
-    )(x, cot, before, after, filters)
-    parts = [parts[0]] + [
-        lax.ppermute(parts[k], "band", xor_route(n_band, k)) for k in range(1, n_band)
-    ]
-    keep, give = call(functools.partial(sum_kernel, n_band), [(block, chans)] * 2)(*parts)
-    other = lax.ppermute(give, "image", xor_route(n_image, 1))
-    parts = call(functools.partial(pack_kernel, n_pair), [(2, slot, chans)] * n_pair)(keep, other)
-    parts = [parts[0]] + [
-        lax.ppermute(parts[k], "image", xor_route(n_image, 2 * k)) for k in range(1, n_pair)
-    ]
+        functools.partial(grads_kernel, rows, scale, n_band, cuts),
+        [(2, height, chans) for _, height in cuts for _ in range(n_band)],
+        [
+            pltpu.VMEM((2, kdim, chans), F32),
+            pltpu.VMEM((tall, wide), BF16),
+            pltpu.VMEM((tall, wide), BF16),
+        ],
+    )(before, after, *inner)
+    sent = []
+    for c in range(len(cuts)):
+        mine = parts[c * n_band : (c + 1) * n_band]
+        sent.append([mine[0]] + [swapped(mine[k], "band", k) for k in range(1, n_band)])
+    slices = []
+    for c, (_, height) in enumerate(cuts):
+        keep, give = call(functools.partial(sum_kernel, n_band), [(height, chans)] * 2)(*sent[c])
+        other = swapped(give, "image", 1)
+        packed = call(
+            functools.partial(pack_kernel, n_pair), [(2, height // n_pair, chans)] * n_pair
+        )(keep, other)
+        slices += [packed[0]] + [swapped(packed[k], "image", 2 * k) for k in range(1, n_pair)]
     (gram,) = call(
-        functools.partial(gram_kernel, n_pair),
-        [(n_image, 128)],
+        functools.partial(gram_kernel, n_pair, slots),
+        [(1, 128)],
         [pltpu.VMEM((n_image, slot, chans), F32)],
-    )(*parts)
-    sums = jnp.broadcast_to(gram[None], (n_image * n_band,) + gram.shape)
+    )(*slices)
+    sums = jnp.broadcast_to(gram, (n_image * n_band, gram.shape[1]))
     sums = lax.all_to_all(sums, ("image", "band"), 0, 0, tiled=True)
-    (mine,) = call(functools.partial(merge_kernel, n_pair, n_band), [(slot, chans)])(sums, *parts)
+    (mine,) = call(
+        functools.partial(merge_kernel, n_pair, n_band, slots), [(slot, chans)]
+    )(sums, *slices)
     pieces = [mine] + [
         lax.ppermute(mine, "image", xor_route(n_image, 2 * k)) for k in range(1, n_pair)
     ]
-    (mine,) = call(functools.partial(gather_kernel, n_pair), [(block, chans)])(*pieces)
+    (mine,) = call(functools.partial(gather_kernel, n_pair, slots), [(block, chans)])(*pieces)
     own = [mine] + [
         lax.ppermute(mine, "band", xor_route(n_band, k)) for k in range(1, n_band)
     ]
@@ -376,7 +443,7 @@
     n_image = lax.axis_size("image")
     kdim = filters.shape[1]
     fits = (
-        n_image >= 4
+        4 <= n_image and n_image**2 <= 128
         and n_image & (n_image - 1) == 0
         and n_band & (n_band - 1) == 0
         and kdim % (n_band * (n_image // 2) * 8) == 0

time: 77.6 us -> 77.5 us (level)
  waiting for transfers between devices: 34.3 us -> 22.9 us
  starting transfers between devices: 22.3 us -> 32 us
  Pallas kernels: 5.75 us -> 8.53 us
  blocking collectives: 11.7 us -> 10.4 us
    ppermute x7 -> x14, starting transfers between devices: 8.08 us -> 17.3 us  [swapped(): return lax.ppermute(value, axis, xor_route(lax.axis_size(axis), k))]
    ppermute x7 -> x14, waiting for transfers between devices: 19 us -> 13.6 us  [swapped(): return lax.ppermute(value, axis, xor_route(lax.axis_size(axis), k))]
    ppermute x1, waiting for transfers between devices: 4.75 us -> 1.68 us  [fast(): after = lax.ppermute(up, 'band', bwd)]
    pallas_call x7 -> x10, Pallas kernels: 3.97 us -> 6.75 us  [the longest x1 2.41 us: fast(): call(functools.partial(grads_kernel, rows, scale, n_band, cuts), [(2, hei...]
    ppermute x1, waiting for transfers between devices: 1.43 us -> 0.01 us  [fast(): before = lax.ppermute(down, 'band', fwd)]
    all_to_all x1, blocking collectives: 11.7 us -> 10.4 us  [fast(): sums = lax.all_to_all(sums, ('image', 'band'), 0, 0, tiled=True)]
    ppermute x3, waiting for transfers between devices: 5.34 us -> 4.46 us  [fast(): lax.ppermute(mine, 'band', xor_route(n_band, k))]
  transfers between devices with their start and end apart: 19 -> 26, of which waited for: 14 -> 13; matrix products, arithmetic and copies ran while one was open for 0% -> 0% of each run, Pallas kernels for 0% -> 2%
where the time goes in v2:
time: 77.5 us; the launch traced here: 77.2 us
  starting transfers between devices  32 us (41%)
  waiting for transfers between devices  22.9 us (30%)
  blocking collectives  10.4 us (13%)
  Pallas kernels  8.53 us (11%)
  local copies, waits for them, and re-layouts  3.18 us (4%)
    ppermute x14, starting transfers between devices, swapped(): return lax.ppermute(value, axis, xor_route(lax.axis_size(axis), k))  17.3 us
    ppermute x14, waiting for transfers between devices, swapped(): return lax.ppermute(value, axis, xor_route(lax.axis_size(axis), k))  13.6 us
    all_to_all x1, blocking collectives, fast(): sums = lax.all_to_all(sums, ('image', 'band'), 0, 0, tiled=True)  10.4 us
    ppermute x1, starting transfers between devices, fast(): before = lax.ppermute(down, 'band', fwd)  4.88 us
    ppermute x3, waiting for transfers between devices, fast(): lax.ppermute(mine, 'band', xor_route(n_band, k))  4.46 us
    ppermute x3, starting transfers between devices, fast(): lax.ppermute(mine, 'image', xor_route(n_image, 2 * k))  4.45 us
    ppermute x3, starting transfers between devices, fast(): lax.ppermute(mine, 'band', xor_route(n_band, k))  3.55 us
    unnamed x10, local copies, waits for them, and re-layouts  3.17 us
  transfers between devices with their start and end apart: 26, of which 13 were waited for; matrix products, arithmetic and copies ran while one was open for 0% of the time, Pallas kernels for 2%

profile of v2, /device:TPU:0, one launch (start us, length us, event | category | flops | bytes accessed | tf_op | source)
XLA Modules:
  0.0 77.2 jit_solution(12201460952525401432)
XLA Ops:
  0.0 1.8 %shard_map.46 = (f32[256,128]{1,0:T(8,128)}, f32[256,128]{1,0:T(8,128)}) custom-call(f32[512,128]{1,0:T(8,128)} %bitcast.4, f32[512,128]{1,0:T(8,128)} %bitcast.6), custom_call_target="tpu_custom_call" | custom-call | tf_op jit(solution)/shard_map/pallas_call | solution.py:313
  1.8 4.9 %collective-permute-start = (f32[256,128]{1,0:T(8,128)}, f32[256,128]{1,0:T(8,128)S(1)}, u32[]{:S(2)}, u32[]{:S(2)}) collective-permute-start(f32[256,128]{1,0:T(8,128)} %get-tuple-element.37), channel_id=1, source_target_pairs={{0,1},{1,2},{2,3},{4,5},{5,6},{6,7},{8,9},{9,10},{10,11},{12,13},{... | collective-permute-start | bytes 393224 | tf_op jit(solution)/shard_map/ppermute | solution.py:322
  6.6 1.3 %collective-permute-start.1 = (f32[256,128]{1,0:T(8,128)}, f32[256,128]{1,0:T(8,128)S(1)}, u32[]{:S(2)}, u32[]{:S(2)}) collective-permute-start(f32[256,128]{1,0:T(8,128)} %get-tuple-element.38), channel_id=1, source_target_pairs={{1,0},{2,1},{3,2},{5,4},{6,5},{7,6},{9,8},{10,9},{11,10},{13,12},{... | collective-permute-start | bytes 393224 | tf_op jit(solution)/shard_map/ppermute | solution.py:323
  7.9 0.0 copy-start
  8.0 1.3 %copy-done = f32[2,1152,128]{2,1,0:T(8,128)S(1)} copy-done((f32[2,1152,128]{2,1,0:T(8,128)S(1)}, f32[2,1152,128]{2,1,0:T(8,128)}, u32[]{:S(2)}) %copy-start) | copy-done | bytes 1179672
  9.2 0.9 %copy-done.2 = f32[1,128,4,128]{3,2,1,0:T(4,128)S(1)} copy-done((f32[1,128,4,128]{3,2,1,0:T(4,128)S(1)}, f32[1,128,4,128]{3,2,1,0:T(4,128)}, u32[]{:S(2)}) %copy-start.2) | copy-done | bytes 262168
  10.2 0.9 %copy-done.3 = f32[1,128,4,128]{3,2,1,0:T(4,128)S(1)} copy-done((f32[1,128,4,128]{3,2,1,0:T(4,128)S(1)}, f32[1,128,4,128]{3,2,1,0:T(4,128)}, u32[]{:S(2)}) %copy-start.3) | copy-done | bytes 262168
  11.1 1.5 %shard_map.47 = (bf16[384,512]{1,0:T(8,128)(2,1)S(1)}, bf16[384,512]{1,0:T(8,128)(2,1)S(1)}, bf16[384,512]{1,0:T(8,128)(2,1)S(1)}, bf16[384,512]{1,0:T(8,128)(2,...) custom-call(f32[512,128]{1,0:T(8,128)S(1)} %bitcast.5, ...), custom_call_target="tpu_custom_call" | custom-call | flops 905969664 | bytes 1179648 | tf_op jit(solution)/shard_map/pallas_call | solution.py:325
  12.7 1.7 %collective-permute-done.1.refs_1_ = f32[256,128]{1,0:T(8,128)S(1)} collective-permute-done((f32[256,128]{1,0:T(8,128)}, f32[256,128]{1,0:T(8,128)S(1)}, u32[]{:S(2)}, u32[]{:S(2)}) %collective-permute-start.1) | collective-permute-done | bytes 131104 | tf_op jit(solution)/shard_map/ppermute | solution.py:323
  14.3 2.4 %shard_map.48 = (f32[2,160,128]{2,1,0:T(8,128)S(1)}, f32[2,160,128]{2,1,0:T(8,128)S(1)}, f32[2,160,128]{2,1,0:T(8,128)S(1)}, f32[2,160,128]{2,1,0:T(8,128)S(1)},...) custom-call(f32[256,128]{1,0:T(8,128)S(1)} %collective-permute-done., ...), custom_call_target="tpu_custom_call" | custom-call | tf_op jit(solution)/shard_map/pallas_call | solution.py:339
  16.8 1.8 %collective-permute-start.9 = (f32[2,128,128]{2,1,0:T(8,128)S(1)}, f32[2,128,128]{2,1,0:T(8,128)S(1)}, u32[]{:S(2)}, u32[]{:S(2)}) collective-permute-start(f32[2,128,128]{2,1,0:T(8,128)S(1)} %get-tuple-element.60), channel_id=1, source_target_pairs={{0,1},{1,0},{2,3},{3,2},{4,5},{5,4},{6,7},{7,6},{8,9},{9,8},{10,11... | collective-permute-start | bytes 393224 | tf_op jit(solution)/shard_map/ppermute | solution.py:299
  18.6 0.3 collective-permute-start.2
  18.9 1.9 %collective-permute-start.3 = (f32[2,160,128]{2,1,0:T(8,128)S(1)}, f32[2,160,128]{2,1,0:T(8,128)S(1)}, u32[]{:S(2)}, u32[]{:S(2)}) collective-permute-start(f32[2,160,128]{2,1,0:T(8,128)S(1)} %get-tuple-element.51), channel_id=1, source_target_pairs={{0,2},{1,3},{2,0},{3,1},{4,6},{5,7},{6,4},{7,5},{8,10},{9,11},{10,... | collective-permute-start | bytes 491528 | tf_op jit(solution)/shard_map/ppermute | solution.py:299
  20.8 1.3 %collective-permute-start.4 = (f32[2,160,128]{2,1,0:T(8,128)S(1)}, f32[2,160,128]{2,1,0:T(8,128)S(1)}, u32[]{:S(2)}, u32[]{:S(2)}) collective-permute-start(f32[2,160,128]{2,1,0:T(8,128)S(1)} %get-tuple-element.52), channel_id=1, source_target_pairs={{0,3},{1,2},{2,1},{3,0},{4,7},{5,6},{6,5},{7,4},{8,11},{9,10},{10,... | collective-permute-start | bytes 491528 | tf_op jit(solution)/shard_map/ppermute | solution.py:299
  22.1 0.8 collective-permute-start.10
  22.8 0.4 collective-permute-done.9.refs_1_
  23.2 2.0 %collective-permute-start.11 = (f32[2,128,128]{2,1,0:T(8,128)S(1)}, f32[2,128,128]{2,1,0:T(8,128)S(1)}, u32[]{:S(2)}, u32[]{:S(2)}) collective-permute-start(f32[2,128,128]{2,1,0:T(8,128)S(1)} %get-tuple-element.62), channel_id=1, source_target_pairs={{0,3},{1,2},{2,1},{3,0},{4,7},{5,6},{6,5},{7,4},{8,11},{9,10},{10,... | collective-permute-start | bytes 393224 | tf_op jit(solution)/shard_map/ppermute | solution.py:299
  25.2 7.8 %collective-permute-done.10.refs_2_ = f32[2,128,128]{2,1,0:T(8,128)S(1)} collective-permute-done((f32[2,128,128]{2,1,0:T(8,128)S(1)}, f32[2,128,128]{2,1,0:T(8,128)S(1)}, u32[]{:S(2)}, u32[]{:S(2)}) %collective-permute-start.10) | collective-permute-done | bytes 131104 | tf_op jit(solution)/shard_map/ppermute | solution.py:299
  33.0 0.1 collective-permute-start.12
  33.1 0.1 shard_map.49
  33.2 0.5 collective-permute-start.5
  33.8 0.6 collective-permute-done.12.other_ref
  34.4 1.6 %collective-permute-start.13 = (f32[2,32,128]{2,1,0:T(8,128)S(1)}, f32[2,32,128]{2,1,0:T(8,128)S(1)}, u32[]{:S(2)}, u32[]{:S(2)}) collective-permute-start(f32[2,32,128]{2,1,0:T(8,128)S(1)} %get-tuple-element.66), channel_id=1, source_target_pairs={{0,8},{4,12},{8,0},{12,4},{16,24},{20,28},{24,16},{28,20},{1,9},{5... | collective-permute-start | bytes 98312 | tf_op jit(solution)/shard_map/ppermute | solution.py:299
  36.0 0.5 collective-permute-start.6
  36.5 2.6 %collective-permute-start.7 = (f32[2,40,128]{2,1,0:T(8,128)S(1)}, f32[2,40,128]{2,1,0:T(8,128)S(1)}, u32[]{:S(2)}, u32[]{:S(2)}) collective-permute-start(f32[2,40,128]{2,1,0:T(8,128)S(1)} %get-tuple-element.57), channel_id=1, source_target_pairs={{0,16},{4,20},{8,24},{12,28},{16,0},{20,4},{24,8},{28,12},{1,17},{... | collective-permute-start | bytes 122888 | tf_op jit(solution)/shard_map/ppermute | solution.py:299
  39.1 1.3 %collective-permute-start.8 = (f32[2,40,128]{2,1,0:T(8,128)S(1)}, f32[2,40,128]{2,1,0:T(8,128)S(1)}, u32[]{:S(2)}, u32[]{:S(2)}) collective-permute-start(f32[2,40,128]{2,1,0:T(8,128)S(1)} %get-tuple-element.58), channel_id=1, source_target_pairs={{0,24},{4,28},{8,16},{12,20},{16,8},{20,12},{24,0},{28,4},{1,25},{... | collective-permute-start | bytes 122888 | tf_op jit(solution)/shard_map/ppermute | solution.py:299
  40.5 1.7 %collective-permute-start.14 = (f32[2,32,128]{2,1,0:T(8,128)S(1)}, f32[2,32,128]{2,1,0:T(8,128)S(1)}, u32[]{:S(2)}, u32[]{:S(2)}) collective-permute-start(f32[2,32,128]{2,1,0:T(8,128)S(1)} %get-tuple-element.67), channel_id=1, source_target_pairs={{0,16},{4,20},{8,24},{12,28},{16,0},{20,4},{24,8},{28,12},{1,17},{... | collective-permute-start | bytes 98312 | tf_op jit(solution)/shard_map/ppermute | solution.py:299
  42.2 0.9 %collective-permute-start.15 = (f32[2,32,128]{2,1,0:T(8,128)S(1)}, f32[2,32,128]{2,1,0:T(8,128)S(1)}, u32[]{:S(2)}, u32[]{:S(2)}) collective-permute-start(f32[2,32,128]{2,1,0:T(8,128)S(1)} %get-tuple-element.68), channel_id=1, source_target_pairs={{0,24},{4,28},{8,16},{12,20},{16,8},{20,12},{24,0},{28,4},{1,25},{... | collective-permute-start | bytes 98312 | tf_op jit(solution)/shard_map/ppermute | solution.py:299
  43.1 3.4 %collective-permute-done.14.refs_6_ = f32[2,32,128]{2,1,0:T(8,128)S(1)} collective-permute-done((f32[2,32,128]{2,1,0:T(8,128)S(1)}, f32[2,32,128]{2,1,0:T(8,128)S(1)}, u32[]{:S(2)}, u32[]{:S(2)}) %collective-permute-start.14) | collective-permute-done | bytes 32800 | tf_op jit(solution)/shard_map/ppermute | solution.py:299
  46.4 1.5 %collective-permute-done.15.refs_7_ = f32[2,32,128]{2,1,0:T(8,128)S(1)} collective-permute-done((f32[2,32,128]{2,1,0:T(8,128)S(1)}, f32[2,32,128]{2,1,0:T(8,128)S(1)}, u32[]{:S(2)}, u32[]{:S(2)}) %collective-permute-start.15) | collective-permute-done | bytes 32800 | tf_op jit(solution)/shard_map/ppermute | solution.py:299
  47.9 0.3 shard_map.53
  48.2 10.4 %all_to_all.8 = f32[32,1,128]{2,1,0:T(1,128)S(1)} all-to-all(f32[32,1,128]{2,1,0:T(1,128)S(1)} %broadcast_in_dim.2), channel_id=1, replica_groups=mesh['image'=8,'band'=4] {'image','band'}, dimensions={0} | all-to-all | bytes 32768 | tf_op jit(solution)/shard_map/all_to_all | solution.py:366
  58.6 0.6 shard_map.54.refs_0_
  59.3 0.6 collective-permute-start.18
  59.9 1.5 %collective-permute-start.17 = (f32[72,128]{1,0:T(8,128)S(1)}, f32[72,128]{1,0:T(8,128)S(1)}, u32[]{:S(2)}, u32[]{:S(2)}) collective-permute-start(f32[72,128]{1,0:T(8,128)S(1)} %shard_map.54.refs_0_), channel_id=1, source_target_pairs={{0,16},{4,20},{8,24},{12,28},{16,0},{20,4},{24,8},{28,12},{1,17},{... | collective-permute-start | bytes 110600 | tf_op jit(solution)/shard_map/ppermute | solution.py:371
  61.4 2.4 %collective-permute-start.16 = (f32[72,128]{1,0:T(8,128)S(1)}, f32[72,128]{1,0:T(8,128)S(1)}, u32[]{:S(2)}, u32[]{:S(2)}) collective-permute-start(f32[72,128]{1,0:T(8,128)S(1)} %shard_map.54.refs_0_), channel_id=1, source_target_pairs={{0,8},{4,12},{8,0},{12,4},{16,24},{20,28},{24,16},{28,20},{1,9},{5... | collective-permute-start | bytes 110600 | tf_op jit(solution)/shard_map/ppermute | solution.py:371
  63.7 1.4 %collective-permute-done.18.refs_3_ = f32[72,128]{1,0:T(8,128)S(1)} collective-permute-done((f32[72,128]{1,0:T(8,128)S(1)}, f32[72,128]{1,0:T(8,128)S(1)}, u32[]{:S(2)}, u32[]{:S(2)}) %collective-permute-start.18) | collective-permute-done | bytes 36896 | tf_op jit(solution)/shard_map/ppermute | solution.py:371
  65.1 0.5 collective-permute-done.17.refs_2_
  65.6 0.2 collective-permute-done.16.refs_1_
  65.8 0.7 collective-permute-start.21
  66.5 1.4 %collective-permute-start.20 = (f32[288,128]{1,0:T(8,128)S(1)}, f32[288,128]{1,0:T(8,128)S(1)}, u32[]{:S(2)}, u32[]{:S(2)}) collective-permute-start(f32[288,128]{1,0:T(8,128)S(1)} %shard_map.55.refs_0_), channel_id=1, source_target_pairs={{0,2},{1,3},{2,0},{3,1},{4,6},{5,7},{6,4},{7,5},{8,10},{9,11},{10,... | collective-permute-start | bytes 442376 | tf_op jit(solution)/shard_map/ppermute | solution.py:375
  67.8 1.5 %collective-permute-start.19 = (f32[288,128]{1,0:T(8,128)S(1)}, f32[288,128]{1,0:T(8,128)S(1)}, u32[]{:S(2)}, u32[]{:S(2)}) collective-permute-start(f32[288,128]{1,0:T(8,128)S(1)} %shard_map.55.refs_0_), channel_id=1, source_target_pairs={{0,1},{1,0},{2,3},{3,2},{4,5},{5,4},{6,7},{7,6},{8,9},{9,8},{10,11... | collective-permute-start | bytes 442376 | tf_op jit(solution)/shard_map/ppermute | solution.py:375
  69.4 3.6 %collective-permute-done.21.refs_3_ = f32[288,128]{1,0:T(8,128)S(1)} collective-permute-done((f32[288,128]{1,0:T(8,128)S(1)}, f32[288,128]{1,0:T(8,128)S(1)}, u32[]{:S(2)}, u32[]{:S(2)}) %collective-permute-start.21) | collective-permute-done | bytes 147488 | tf_op jit(solution)/shard_map/ppermute | solution.py:375
  72.9 0.9 %collective-permute-done.20.refs_2_ = f32[288,128]{1,0:T(8,128)S(1)} collective-permute-done((f32[288,128]{1,0:T(8,128)S(1)}, f32[288,128]{1,0:T(8,128)S(1)}, u32[]{:S(2)}, u32[]{:S(2)}) %collective-permute-start.20) | collective-permute-done | bytes 147488 | tf_op jit(solution)/shard_map/ppermute | solution.py:375
  73.8 0.5 collective-permute-start.23
  74.3 0.9 %collective-permute-done.24.refs_6_ = f32[288,128]{1,0:T(8,128)S(1)} collective-permute-done((f32[288,128]{1,0:T(8,128)S(1)}, f32[288,128]{1,0:T(8,128)S(1)}, u32[]{:S(2)}, u32[]{:S(2)}) %collective-permute-start.24) | collective-permute-done | bytes 147488 | tf_op jit(solution)/shard_map/ppermute | solution.py:377
  75.2 0.2 collective-permute-done.23.refs_5_
  75.4 1.8 %shard_map.56 = f32[1,2,1152,128]{3,2,1,0:T(8,128)} custom-call(f32[2]{0:T(128)S(1)} %copy-done.4, f32[2,1152,128]{2,1,0:T(8,128)S(1)} %copy-done.1, f32[288,128]{1,0:T(8,128)S(1)} %shard_map.55.refs_0_, f32[288,128]{1,0:T(8,128)S(1)} %collective-permute-done.19.refs_1_, f32[288,128]{1,0:T(8,128)S(1)} %collective-permute-done.20.refs_2_, ...), custom_call_target="tpu_custom_call" | custom-call | tf_op jit(solution)/shard_map/pallas_call | solution.py:378
  (27 shorter events, 0.1 us)
Async XLA Ops:
  1.8 10.9 %collective-permute-start = (f32[256,128]{1,0:T(8,128)}, f32[256,128]{1,0:T(8,128)S(1)}, u32[]{:S(2)}, u32[]{:S(2)}) collective-permute-start(f32[256,128]{1,0:T(8,128)} %get-tuple-element.37), channel_id=1, source_target_pairs={{0,1},{1,2},{2,3},{4,5},{5,6},{6,7},{8,9},{9,10},{10,11},{12,13},{... | collective-permute-start | bytes 393224 | tf_op jit(solution)/shard_map/ppermute | solution.py:322
  6.6 7.7 %collective-permute-start.1 = (f32[256,128]{1,0:T(8,128)}, f32[256,128]{1,0:T(8,128)S(1)}, u32[]{:S(2)}, u32[]{:S(2)}) collective-permute-start(f32[256,128]{1,0:T(8,128)} %get-tuple-element.38), channel_id=1, source_target_pairs={{1,0},{2,1},{3,2},{5,4},{6,5},{7,6},{9,8},{10,9},{11,10},{13,12},{... | collective-permute-start | bytes 393224 | tf_op jit(solution)/shard_map/ppermute | solution.py:323
  7.9 1.3 %copy-start = (f32[2,1152,128]{2,1,0:T(8,128)S(1)}, f32[2,1152,128]{2,1,0:T(8,128)}, u32[]{:S(2)}) copy-start(f32[2,1152,128]{2,1,0:T(8,128)} %f_ref.3) | copy-start | bytes 3538948
  9.2 0.9 %copy-start.2 = (f32[1,128,4,128]{3,2,1,0:T(4,128)S(1)}, f32[1,128,4,128]{3,2,1,0:T(4,128)}, u32[]{:S(2)}) copy-start(f32[1,128,4,128]{3,2,1,0:T(4,128)} %param.4) | copy-start | bytes 786436
  10.2 0.9 %copy-start.3 = (f32[1,128,4,128]{3,2,1,0:T(4,128)S(1)}, f32[1,128,4,128]{3,2,1,0:T(4,128)}, u32[]{:S(2)}) copy-start(f32[1,128,4,128]{3,2,1,0:T(4,128)} %param.5) | copy-start | bytes 786436
  16.8 6.4 %collective-permute-start.9 = (f32[2,128,128]{2,1,0:T(8,128)S(1)}, f32[2,128,128]{2,1,0:T(8,128)S(1)}, u32[]{:S(2)}, u32[]{:S(2)}) collective-permute-start(f32[2,128,128]{2,1,0:T(8,128)S(1)} %get-tuple-element.60), channel_id=1, source_target_pairs={{0,1},{1,0},{2,3},{3,2},{4,5},{5,4},{6,7},{7,6},{8,9},{9,8},{10,11... | collective-permute-start | bytes 393224 | tf_op jit(solution)/shard_map/ppermute | solution.py:299
  18.6 14.5 %collective-permute-start.2 = (f32[2,160,128]{2,1,0:T(8,128)S(1)}, f32[2,160,128]{2,1,0:T(8,128)S(1)}, u32[]{:S(2)}, u32[]{:S(2)}) collective-permute-start(f32[2,160,128]{2,1,0:T(8,128)S(1)} %get-tuple-element.50), channel_id=1, source_target_pairs={{0,1},{1,0},{2,3},{3,2},{4,5},{5,4},{6,7},{7,6},{8,9},{9,8},{10,11... | collective-permute-start | bytes 491528 | tf_op jit(solution)/shard_map/ppermute | solution.py:299
  18.9 14.3 %collective-permute-start.3 = (f32[2,160,128]{2,1,0:T(8,128)S(1)}, f32[2,160,128]{2,1,0:T(8,128)S(1)}, u32[]{:S(2)}, u32[]{:S(2)}) collective-permute-start(f32[2,160,128]{2,1,0:T(8,128)S(1)} %get-tuple-element.51), channel_id=1, source_target_pairs={{0,2},{1,3},{2,0},{3,1},{4,6},{5,7},{6,4},{7,5},{8,10},{9,11},{10,... | collective-permute-start | bytes 491528 | tf_op jit(solution)/shard_map/ppermute | solution.py:299
  20.8 12.4 %collective-permute-start.4 = (f32[2,160,128]{2,1,0:T(8,128)S(1)}, f32[2,160,128]{2,1,0:T(8,128)S(1)}, u32[]{:S(2)}, u32[]{:S(2)}) collective-permute-start(f32[2,160,128]{2,1,0:T(8,128)S(1)} %get-tuple-element.52), channel_id=1, source_target_pairs={{0,3},{1,2},{2,1},{3,0},{4,7},{5,6},{6,5},{7,4},{8,11},{9,10},{10,... | collective-permute-start | bytes 491528 | tf_op jit(solution)/shard_map/ppermute | solution.py:299
  22.1 10.9 %collective-permute-start.10 = (f32[2,128,128]{2,1,0:T(8,128)S(1)}, f32[2,128,128]{2,1,0:T(8,128)S(1)}, u32[]{:S(2)}, u32[]{:S(2)}) collective-permute-start(f32[2,128,128]{2,1,0:T(8,128)S(1)} %get-tuple-element.61), channel_id=1, source_target_pairs={{0,2},{1,3},{2,0},{3,1},{4,6},{5,7},{6,4},{7,5},{8,10},{9,11},{10,... | collective-permute-start | bytes 393224 | tf_op jit(solution)/shard_map/ppermute | solution.py:299
  23.2 9.8 %collective-permute-start.11 = (f32[2,128,128]{2,1,0:T(8,128)S(1)}, f32[2,128,128]{2,1,0:T(8,128)S(1)}, u32[]{:S(2)}, u32[]{:S(2)}) collective-permute-start(f32[2,128,128]{2,1,0:T(8,128)S(1)} %get-tuple-element.62), channel_id=1, source_target_pairs={{0,3},{1,2},{2,1},{3,0},{4,7},{5,6},{6,5},{7,4},{8,11},{9,10},{10,... | collective-permute-start | bytes 393224 | tf_op jit(solution)/shard_map/ppermute | solution.py:299
  33.0 42.4 %copy-start.1 = (f32[2,1152,128]{2,1,0:T(8,128)S(1)}, f32[2,1152,128]{2,1,0:T(8,128)}, u32[]{:S(2)}) copy-start(f32[2,1152,128]{2,1,0:T(8,128)} %f_ref.3) | copy-start | bytes 3538948
  33.0 42.4 %copy-start.4 = (f32[2]{0:T(128)S(1)}, f32[2]{0:T(128)}, u32[]{:S(2)}) copy-start(f32[2]{0:T(128)} %rates_ref.1) | copy-start | bytes 28
  33.0 1.3 %collective-permute-start.12 = (f32[128,128]{1,0:T(8,128)S(1)}, f32[128,128]{1,0:T(8,128)S(1)}, u32[]{:S(2)}, u32[]{:S(2)}) collective-permute-start(f32[128,128]{1,0:T(8,128)S(1)} %get-tuple-element.64), channel_id=1, source_target_pairs={{0,4},{4,0},{8,12},{12,8},{16,20},{20,16},{24,28},{28,24},{1,5},{5... | collective-permute-start | bytes 196616 | tf_op jit(solution)/shard_map/ppermute | solution.py:299
  33.2 2.8 %collective-permute-start.5 = (f32[160,128]{1,0:T(8,128)S(1)}, f32[160,128]{1,0:T(8,128)S(1)}, u32[]{:S(2)}, u32[]{:S(2)}) collective-permute-start(f32[160,128]{1,0:T(8,128)S(1)} %get-tuple-element.54), channel_id=1, source_target_pairs={{0,4},{4,0},{8,12},{12,8},{16,20},{20,16},{24,28},{28,24},{1,5},{5... | collective-permute-start | bytes 245768 | tf_op jit(solution)/shard_map/ppermute | solution.py:299
  34.4 7.8 %collective-permute-start.13 = (f32[2,32,128]{2,1,0:T(8,128)S(1)}, f32[2,32,128]{2,1,0:T(8,128)S(1)}, u32[]{:S(2)}, u32[]{:S(2)}) collective-permute-start(f32[2,32,128]{2,1,0:T(8,128)S(1)} %get-tuple-element.66), channel_id=1, source_target_pairs={{0,8},{4,12},{8,0},{12,4},{16,24},{20,28},{24,16},{28,20},{1,9},{5... | collective-permute-start | bytes 98312 | tf_op jit(solution)/shard_map/ppermute | solution.py:299
  36.0 11.9 %collective-permute-start.6 = (f32[2,40,128]{2,1,0:T(8,128)S(1)}, f32[2,40,128]{2,1,0:T(8,128)S(1)}, u32[]{:S(2)}, u32[]{:S(2)}) collective-permute-start(f32[2,40,128]{2,1,0:T(8,128)S(1)} %get-tuple-element.56), channel_id=1, source_target_pairs={{0,8},{4,12},{8,0},{12,4},{16,24},{20,28},{24,16},{28,20},{1,9},{5... | collective-permute-start | bytes 122888 | tf_op jit(solution)/shard_map/ppermute | solution.py:299
  36.5 11.4 %collective-permute-start.7 = (f32[2,40,128]{2,1,0:T(8,128)S(1)}, f32[2,40,128]{2,1,0:T(8,128)S(1)}, u32[]{:S(2)}, u32[]{:S(2)}) collective-permute-start(f32[2,40,128]{2,1,0:T(8,128)S(1)} %get-tuple-element.57), channel_id=1, source_target_pairs={{0,16},{4,20},{8,24},{12,28},{16,0},{20,4},{24,8},{28,12},{1,17},{... | collective-permute-start | bytes 122888 | tf_op jit(solution)/shard_map/ppermute | solution.py:299
  39.1 8.8 %collective-permute-start.8 = (f32[2,40,128]{2,1,0:T(8,128)S(1)}, f32[2,40,128]{2,1,0:T(8,128)S(1)}, u32[]{:S(2)}, u32[]{:S(2)}) collective-permute-start(f32[2,40,128]{2,1,0:T(8,128)S(1)} %get-tuple-element.58), channel_id=1, source_target_pairs={{0,24},{4,28},{8,16},{12,20},{16,8},{20,12},{24,0},{28,4},{1,25},{... | collective-permute-start | bytes 122888 | tf_op jit(solution)/shard_map/ppermute | solution.py:299
  40.5 6.0 %collective-permute-start.14 = (f32[2,32,128]{2,1,0:T(8,128)S(1)}, f32[2,32,128]{2,1,0:T(8,128)S(1)}, u32[]{:S(2)}, u32[]{:S(2)}) collective-permute-start(f32[2,32,128]{2,1,0:T(8,128)S(1)} %get-tuple-element.67), channel_id=1, source_target_pairs={{0,16},{4,20},{8,24},{12,28},{16,0},{20,4},{24,8},{28,12},{1,17},{... | collective-permute-start | bytes 98312 | tf_op jit(solution)/shard_map/ppermute | solution.py:299
  42.2 5.7 %collective-permute-start.15 = (f32[2,32,128]{2,1,0:T(8,128)S(1)}, f32[2,32,128]{2,1,0:T(8,128)S(1)}, u32[]{:S(2)}, u32[]{:S(2)}) collective-permute-start(f32[2,32,128]{2,1,0:T(8,128)S(1)} %get-tuple-element.68), channel_id=1, source_target_pairs={{0,24},{4,28},{8,16},{12,20},{16,8},{20,12},{24,0},{28,4},{1,25},{... | collective-permute-start | bytes 98312 | tf_op jit(solution)/shard_map/ppermute | solution.py:299
  59.3 5.8 %collective-permute-start.18 = (f32[72,128]{1,0:T(8,128)S(1)}, f32[72,128]{1,0:T(8,128)S(1)}, u32[]{:S(2)}, u32[]{:S(2)}) collective-permute-start(f32[72,128]{1,0:T(8,128)S(1)} %shard_map.54.refs_0_), channel_id=1, source_target_pairs={{0,24},{4,28},{8,16},{12,20},{16,8},{20,12},{24,0},{28,4},{1,25},{... | collective-permute-start | bytes 110600 | tf_op jit(solution)/shard_map/ppermute | solution.py:371
  59.9 5.8 %collective-permute-start.17 = (f32[72,128]{1,0:T(8,128)S(1)}, f32[72,128]{1,0:T(8,128)S(1)}, u32[]{:S(2)}, u32[]{:S(2)}) collective-permute-start(f32[72,128]{1,0:T(8,128)S(1)} %shard_map.54.refs_0_), channel_id=1, source_target_pairs={{0,16},{4,20},{8,24},{12,28},{16,0},{20,4},{24,8},{28,12},{1,17},{... | collective-permute-start | bytes 110600 | tf_op jit(solution)/shard_map/ppermute | solution.py:371
  61.4 4.4 %collective-permute-start.16 = (f32[72,128]{1,0:T(8,128)S(1)}, f32[72,128]{1,0:T(8,128)S(1)}, u32[]{:S(2)}, u32[]{:S(2)}) collective-permute-start(f32[72,128]{1,0:T(8,128)S(1)} %shard_map.54.refs_0_), channel_id=1, source_target_pairs={{0,8},{4,12},{8,0},{12,4},{16,24},{20,28},{24,16},{28,20},{1,9},{5... | collective-permute-start | bytes 110600 | tf_op jit(solution)/shard_map/ppermute | solution.py:371
  65.8 7.2 %collective-permute-start.21 = (f32[288,128]{1,0:T(8,128)S(1)}, f32[288,128]{1,0:T(8,128)S(1)}, u32[]{:S(2)}, u32[]{:S(2)}) collective-permute-start(f32[288,128]{1,0:T(8,128)S(1)} %shard_map.55.refs_0_), channel_id=1, source_target_pairs={{0,3},{1,2},{2,1},{3,0},{4,7},{5,6},{6,5},{7,4},{8,11},{9,10},{10,... | collective-permute-start | bytes 442376 | tf_op jit(solution)/shard_map/ppermute | solution.py:375
  66.5 7.3 %collective-permute-start.20 = (f32[288,128]{1,0:T(8,128)S(1)}, f32[288,128]{1,0:T(8,128)S(1)}, u32[]{:S(2)}, u32[]{:S(2)}) collective-permute-start(f32[288,128]{1,0:T(8,128)S(1)} %shard_map.55.refs_0_), channel_id=1, source_target_pairs={{0,2},{1,3},{2,0},{3,1},{4,6},{5,7},{6,4},{7,5},{8,10},{9,11},{10,... | collective-permute-start | bytes 442376 | tf_op jit(solution)/shard_map/ppermute | solution.py:375
  67.8 6.0 %collective-permute-start.19 = (f32[288,128]{1,0:T(8,128)S(1)}, f32[288,128]{1,0:T(8,128)S(1)}, u32[]{:S(2)}, u32[]{:S(2)}) collective-permute-start(f32[288,128]{1,0:T(8,128)S(1)} %shard_map.55.refs_0_), channel_id=1, source_target_pairs={{0,1},{1,0},{2,3},{3,2},{4,5},{5,4},{6,7},{7,6},{8,9},{9,8},{10,11... | collective-permute-start | bytes 442376 | tf_op jit(solution)/shard_map/ppermute | solution.py:375
  69.3 5.0 %collective-permute-start.22 = (f32[288,128]{1,0:T(8,128)S(1)}, f32[288,128]{1,0:T(8,128)S(1)}, u32[]{:S(2)}, u32[]{:S(2)}) collective-permute-start(f32[288,128]{1,0:T(8,128)S(1)} %shard_map.55.refs_0_), channel_id=1, source_target_pairs={{0,4},{4,0},{8,12},{12,8},{16,20},{20,16},{24,28},{28,24},{1,5},{5... | collective-permute-start | bytes 442376 | tf_op jit(solution)/shard_map/ppermute | solution.py:377
  72.9 1.4 %collective-permute-start.25 = (f32[288,128]{1,0:T(8,128)S(1)}, f32[288,128]{1,0:T(8,128)S(1)}, u32[]{:S(2)}, u32[]{:S(2)}) collective-permute-start(f32[288,128]{1,0:T(8,128)S(1)} %collective-permute-done.21.refs_3_), channel_id=1, source_target_pairs={{0,4},{4,0},{8,12},{12,8},{16,20},{20,16},{24,28},{28,24},{1,5},{5... | collective-permute-start | bytes 442376 | tf_op jit(solution)/shard_map/ppermute | solution.py:377
  73.8 1.4 %collective-permute-start.24 = (f32[288,128]{1,0:T(8,128)S(1)}, f32[288,128]{1,0:T(8,128)S(1)}, u32[]{:S(2)}, u32[]{:S(2)}) collective-permute-start(f32[288,128]{1,0:T(8,128)S(1)} %collective-permute-done.20.refs_2_), channel_id=1, source_target_pairs={{0,4},{4,0},{8,12},{12,8},{16,20},{20,16},{24,28},{28,24},{1,5},{5... | collective-permute-start | bytes 442376 | tf_op jit(solution)/shard_map/ppermute | solution.py:377
  73.8 1.6 %collective-permute-start.23 = (f32[288,128]{1,0:T(8,128)S(1)}, f32[288,128]{1,0:T(8,128)S(1)}, u32[]{:S(2)}, u32[]{:S(2)}) collective-permute-start(f32[288,128]{1,0:T(8,128)S(1)} %collective-permute-done.19.refs_1_), channel_id=1, source_target_pairs={{0,4},{4,0},{8,12},{12,8},{16,20},{20,16},{24,28},{28,24},{1,5},{5... | collective-permute-start | bytes 442376 | tf_op jit(solution)/shard_map/ppermute | solution.py:377

commit v3 on v0

v3 whole, which is shorter than its diff:
```python
import functools

import jax
import jax.numpy as jnp
from jax import lax
from jax.experimental import pallas as pl
from jax.experimental.pallas import tpu as pltpu
from jax.sharding import PartitionSpec as P


HIGH = lax.Precision.HIGHEST
F32 = jnp.float32
BF16 = jnp.bfloat16


AXES = ("pair", "core", "half", "lo")


def call(body, outs, scratch=(), flops=0):
    outs = [o if isinstance(o, jax.ShapeDtypeStruct) else jax.ShapeDtypeStruct(o, F32) for o in outs]
    return pl.pallas_call(
        body,
        out_shape=outs,
        scratch_shapes=list(scratch),
        cost_estimate=pl.CostEstimate(flops=flops, bytes_accessed=flops // 500, transcendentals=0),
        compiler_params=pltpu.CompilerParams(vmem_limit_bytes=40 * 2**20),
    )


def halves(value):
    high = value.astype(BF16)
    return high, (value - high.astype(F32)).astype(BF16)


def dot3(ah, al, bh, bl, dims):
    def one(a, b):
        return lax.dot_general(a, b, (dims, ((), ())), preferred_element_type=F32)

    return one(ah, bh) + (one(ah, bl) + one(al, bh))


def moved(value, step):
    cols = value.shape[-1]
    col = lax.broadcasted_iota(jnp.int32, value.shape, value.ndim - 1)
    if step > 0:
        return jnp.where(col == cols - 1, 0.0, pltpu.roll(value, cols - 1, 1))
    return jnp.where(col == 0, 0.0, pltpu.roll(value, 1, 1))


def put(high_ref, low_ref, at, row, value):
    high, low = halves(value)
    rows, cols = value.shape
    part = (slice(at * rows, (at + 1) * rows), slice(row * cols, (row + 1) * cols))
    high_ref[part] = high
    low_ref[part] = low


def filter_kernel(f_ref, fh, fl, gh, gl, taps_ref):
    lo = lax.axis_index("lo")
    chans = f_ref.shape[2]
    mine = fh.shape[0] // 3
    rows = pl.ds(pl.multiple_of(lo * mine, 8), mine)
    for a in range(3):
        for b in range(3):
            t = 3 * a + b
            at = pl.ds(t, chans, stride=9)
            taps_ref[0, t] = f_ref[0, at, :].T
            taps_ref[1, t] = f_ref[1, at, :]
            put(fh, fl, b, a, taps_ref[0, t, rows, :])
            put(gh, gl, b, a, taps_ref[1, t, rows, :])


def edge_kernel(own_ref, *refs):
    parts, out = refs[:-1], refs[-1]
    core, lo = lax.axis_index("core"), lax.axis_index("lo")
    kept = core == lax.axis_index("half")
    count = len(parts)
    chans = out.shape[0]
    rows = own_ref.shape[0] // chans
    place = jnp.where(core == 0, count - 1, 0)
    for k, part in enumerate(parts):
        for c, row in ((0, rows - 1), (1, 0)):
            here = (lax.bitwise_xor(lo, k) == place) & (core == c)
            at = pl.ds(row, chans, stride=rows)
            if k == 0:

                @pl.when(here & kept)
                def _():
                    out[...] = own_ref[at, :]

                here = here & jnp.logical_not(kept)

            @pl.when(here)
            def _():
                out[...] = part[at, :]


def rows_kernel(flip, own_ref, *refs):
    parts, (fh, fl, vh, vl, out, raw) = refs[:-6], refs[-6:]
    lo = lax.axis_index("lo")
    kept = lax.axis_index("core") == lax.axis_index("half")
    chans = raw.shape[1]
    cols = raw.shape[2]
    rows = own_ref.shape[0] // chans
    total = raw.shape[0]

    def take(ref, at):
        for row in range(rows):
            raw[at + row] = ref[pl.ds(row, chans, stride=rows), :]

    for k, part in enumerate(parts):
        at = lax.bitwise_xor(lo, k) * rows
        if k:
            take(part, at)
            continue

        @pl.when(kept)
        def _():
            take(own_ref, at)

        @pl.when(jnp.logical_not(kept))
        def _():
            take(part, at)

    for a in range(3):
        step = 1 - a if flip else a - 1
        for row in range(total):
            value = raw[row + step] if 0 <= row + step < total else jnp.zeros((chans, cols), F32)
            put(vh, vl, a, row, value)
    out[...] = dot3(fh[...], fl[...], vh[...], vl[...], ((1,), (0,)))


def grads_kernel(total, scale, *refs):
    x_edge, c_edge, xh, xl, ch, cl, fh, fl, gh, gl, pre_ref, back_ref = refs[:12]
    (keep_ref, give_ref), (g_ref, dh, dl) = refs[12:14], refs[14:]
    chans, cols = x_edge.shape
    mine = fh.shape[0] // 3
    core = lax.axis_index("core")
    last = total - 1
    mm, nt = ((1,), (0,)), ((1,), (1,))
    tall = [slice(k * chans, (k + 1) * chans) for k in range(3)]
    part_of = [slice(k * mine, (k + 1) * mine) for k in range(3)]

    def rims(edge, first, final):
        before = halves(jnp.where(core == 1, edge[...], 0.0))
        after = halves(jnp.where(core == 0, edge[...], 0.0))
        return {first: (0, before), final: (last, after)}

    x_rim = rims(x_edge, 0, 2)
    c_rim = rims(c_edge, 2, 0)
    pre_rim = {
        row: dot3(fh[:, tall[a]], fl[:, tall[a]], *rim, mm) for a, (row, rim) in x_rim.items()
    }
    back_rim = {
        row: dot3(gh[:, tall[a]], gl[:, tall[a]], *rim, mm) for a, (row, rim) in c_rim.items()
    }
    for row in range(total):
        wide = slice(row * cols, (row + 1) * cols)

        def summed(ref, rim, k):
            value = ref[part_of[k], wide]
            return value + rim[row][part_of[k], :] if row in rim else value

        pre = scale * (
            summed(pre_ref, pre_rim, 1)
            + moved(summed(pre_ref, pre_rim, 0), -1)
            + moved(summed(pre_ref, pre_rim, 2), 1)
        )
        dhidden = scale * (
            summed(back_ref, back_rim, 1)
            + moved(summed(back_ref, back_rim, 0), 1)
            + moved(summed(back_ref, back_rim, 2), -1)
        )
        sig = jax.nn.sigmoid(pre)
        hidden = pre * sig
        dpre = dhidden * sig * (1.0 + pre * (1.0 - sig))
        for b, value in enumerate((moved(dpre, 1), dpre, moved(dpre, -1))):
            put(dh.at[0], dl.at[0], b, row, value)
        for b, value in enumerate((moved(hidden, -1), hidden, moved(hidden, 1))):
            put(dh.at[1], dl.at[1], b, row, value)
    for layer, (vh, vl, rim_of) in enumerate(((xh, xl, x_rim), (ch, cl, c_rim))):
        grad = dot3(dh[layer], dl[layer], vh[...], vl[...], nt)
        for a in range(3):
            part = grad[:, tall[a]]
            if a in rim_of:
                row, rim = rim_of[a]
                wide = slice(row * cols, (row + 1) * cols)
                part = part + dot3(dh[layer, :, wide], dl[layer, :, wide], *rim, nt)
            for b in range(3):
                t = 3 * a + b
                g_ref[layer, t * mine : (t + 1) * mine, :] = scale * part[part_of[b], :]
    keep_ref[...] = g_ref[core]
    give_ref[...] = g_ref[1 - core]


def gram_kernel(v_ref, out):
    count = v_ref.shape[0]
    col = lax.broadcasted_iota(jnp.int32, out.shape, 1)
    total = jnp.zeros(out.shape, F32)
    for i in range(count):
        for j in range(i, count):
            value = jnp.sum(v_ref[i] * v_ref[j], keepdims=True)
            total = jnp.where((col == i * count + j) | (col == j * count + i), value, total)
    out[...] = total


def merge_kernel(n_band, sums_ref, v_ref, out):
    core = lax.axis_index("core")
    count = v_ref.shape[0]
    sums = sums_ref[...]
    lanes = sums.shape[1]
    device = lax.broadcasted_iota(jnp.int32, sums.shape, 0)
    same = ((device // n_band) % 2) == core
    flat = jnp.sum(jnp.where(same, sums, 0.0), 0, keepdims=True)
    row = lax.broadcasted_iota(jnp.int32, (count, lanes), 0)
    col = lax.broadcasted_iota(jnp.int32, (count, lanes), 1)
    gram = jnp.broadcast_to(flat, (count, lanes))
    wide = gram
    for i in range(1, count):
        gram = jnp.where(row == i, pltpu.roll(wide, lanes - i * count, 1), gram)
    gram = jnp.where(col < count, gram, 0.0)

    def swap(value, axis, step):
        size = value.shape[axis]
        index = row if axis == 0 else col
        return jnp.where(
            (index & step) != 0,
            pltpu.roll(value, step, axis),
            pltpu.roll(value, size - step, axis),
        )

    weight = jnp.ones((count, 1), F32)
    step = 1
    while step < count:
        own = jnp.where(row == col, gram, 0.0)
        cross = jnp.where((row ^ step) == col, gram, 0.0)
        down = 1.0 - jnp.sum(cross, 1, keepdims=True) / (
            2.0 * (jnp.sum(own, 1, keepdims=True) + 1e-06)
        )
        along = 1.0 - jnp.sum(cross, 0, keepdims=True) / (
            2.0 * (jnp.sum(own, 0, keepdims=True) + 1e-06)
        )
        weight = weight * down
        gram = gram * down * along
        gram = gram + swap(gram, 0, step)
        gram = gram + swap(gram, 1, step)
        step *= 2
    total = jnp.zeros(out.shape, F32)
    for i in range(count):
        total = total + weight[i : i + 1, :] * v_ref[i]
    out[...] = total


def gather_kernel(*refs):
    parts, out = refs[:-1], refs[-1]
    pair = lax.axis_index("pair")
    size = parts[0].shape[0]
    for k, part in enumerate(parts):
        start = pl.multiple_of(lax.bitwise_xor(pair, k) * size, 8)
        out[pl.ds(start, size), :] = part[...]


def final_kernel(n_pair, n_lo, rates_ref, f_ref, *refs):
    n_band = 2 * n_lo
    own, others = refs[:n_band], refs[n_band : 2 * n_band]
    out, held = refs[2 * n_band :]
    core = lax.axis_index("core")
    band = lax.axis_index("half") * n_lo + lax.axis_index("lo")
    size = own[0].shape[0] // n_pair
    chans = f_ref.shape[2]
    mine = chans // n_lo
    for k in range(n_band):
        place = lax.bitwise_xor(band, k)
        half, lo = place // n_lo, place % n_lo
        for p in range(n_pair):
            to = pl.ds(pl.multiple_of((2 * p + half) * size, 8), size)
            at = slice(p * size, (p + 1) * size)
            held[core, lo, to, :] = own[k][at, :]
            held[1 - core, lo, to, :] = others[k][at, :]
    for layer in range(2):
        rate = rates_ref[layer]
        for t in range(9):
            at = pl.ds(t, chans, stride=9)
            value = held[layer, :, t * mine : (t + 1) * mine, :].reshape(chans, chans)
            if layer == 0:
                value = value.T
            out[0, layer, at, :] = f_ref[layer, at, :] - rate * value


def xor_route(count, k):
    return [(i, i ^ k) for i in range(count)]


def swapped(value, axis, k):
    return lax.ppermute(value, axis, xor_route(lax.axis_size(axis), k))


def inputs_of(value, n_lo):
    def at(core, half, lo):
        return (core * 2 + half) * n_lo + lo

    found = []
    for k in range(n_lo - 1, -1, -1):
        route = [
            (at(core, half, lo), at(half, core, lo ^ k))
            for core in range(2)
            for half in range(2)
            for lo in range(n_lo)
            if k or core != half
        ]
        found.append(lax.ppermute(value, ("core", "half", "lo"), route))
    return found[::-1]


def fast(images, cotangent, filters, rates):
    _, chans, rows, cols = images.shape
    n_pair, n_lo = lax.axis_size("pair"), lax.axis_size("lo")
    n_image, n_band = 2 * n_pair, 2 * n_lo
    kdim = filters.shape[1]
    mine = chans // n_lo
    total = n_lo * rows
    slot = 9 * mine // n_image
    flat = (chans * rows, cols)
    bf = lambda *shape: jax.ShapeDtypeStruct(shape, BF16)
    tall, thin, wide = 3 * chans, 3 * mine, total * cols
    xs = inputs_of(images, n_lo)
    cs = inputs_of(cotangent, n_lo)
    xs = [v.reshape(flat) for v in [images] + xs]
    cs = [v.reshape(flat) for v in [cotangent] + cs]
    fh, fl, gh, gl = call(
        filter_kernel, [bf(thin, tall)] * 4, [pltpu.VMEM((2, 9, chans, chans), F32)]
    )(filters)
    (edge,) = call(edge_kernel, [(chans, cols)])(*xs)
    x_edge = swapped(edge, "core", 1)
    raw = [pltpu.VMEM((total, chans, cols), F32)]
    work = 6 * thin * tall * wide
    outs = [bf(tall, wide)] * 2 + [(thin, wide)]
    xh, xl, pre = call(
        functools.partial(rows_kernel, False), outs, raw, flops=work
    )(*xs, fh, fl)
    (edge,) = call(edge_kernel, [(chans, cols)])(*cs)
    c_edge = swapped(edge, "core", 1)
    ch, cl, back = call(
        functools.partial(rows_kernel, True), outs, raw, flops=work
    )(*cs, gh, gl)
    keep, give = call(
        functools.partial(grads_kernel, total, kdim ** (-0.5)),
        [(9 * mine, chans)] * 2,
        [
            pltpu.VMEM((2, 9 * mine, chans), F32),
            pltpu.VMEM((2, thin, wide), BF16),
            pltpu.VMEM((2, thin, wide), BF16),
        ],
        flops=2 * work,
    )(x_edge, c_edge, xh, xl, ch, cl, fh, fl, gh, gl, pre, back)
    whole = keep + swapped(give, "core", 1)
    slices = lax.all_to_all(
        whole.reshape(n_image, slot, chans), ("pair", "half"), 0, 0, tiled=True
    )
    (gram,) = call(gram_kernel, [(1, 128)])(slices)
    sums = jnp.broadcast_to(gram, (n_image * n_band, gram.shape[1]))
    sums = lax.all_to_all(sums, AXES, 0, 0, tiled=True)
    (merged,) = call(functools.partial(merge_kernel, n_band), [(slot, chans)])(
        sums, slices
    )
    pieces = [merged] + [swapped(merged, "pair", k) for k in range(1, n_pair)]
    (part,) = call(gather_kernel, [(n_pair * slot, chans)])(*pieces)
    own = [part] + [swapped(part, ("half", "lo"), k) for k in range(1, n_band)]
    others = [swapped(piece, "core", 1) for piece in own]
    return pl.pallas_call(
        functools.partial(final_kernel, n_pair, n_lo),
        out_shape=jax.ShapeDtypeStruct((1,) + filters.shape, F32),
        in_specs=[pl.BlockSpec(memory_space=pltpu.SMEM)]
        + [pl.BlockSpec(memory_space=pltpu.VMEM)] * (1 + 2 * n_band),
        scratch_shapes=[pltpu.VMEM((2, n_lo, 9 * mine, chans), F32)],
        compiler_params=pltpu.CompilerParams(vmem_limit_bytes=40 * 2**20),
    )(rates, filters, *own, *others)


def with_rims(field):
    count = lax.axis_size("band")
    forward = [(i, i + 1) for i in range(count - 1)]
    backward = [(target, source) for source, target in forward]
    low = lax.ppermute(field[:, -1:], "band", forward)
    high = lax.ppermute(field[:, :1], "band", backward)
    extended = jnp.concatenate([low, field, high], axis=1)
    return jnp.pad(extended, ((0, 0), (0, 0), (1, 1)))


def taps(padded, rows, cols, flip=False):
    chans = padded.shape[0]
    at = (2, 1, 0) if flip else (0, 1, 2)
    pieces = [padded[:, dr : dr + rows, dc : dc + cols] for dr in at for dc in at]
    return jnp.stack(pieces, axis=1).reshape(chans, 9, rows * cols)


def plain(images, cotangent, filters, rates):
    feats, cot = images[0], cotangent[0]
    chans, rows, cols = feats.shape
    scale = (9 * chans) ** (-0.5)
    patch_one = taps(with_rims(feats), rows, cols).reshape(9 * chans, rows * cols)
    pre = scale * jnp.einsum("kc,kp->cp", filters[0], patch_one, precision=HIGH)
    hidden = jax.nn.silu(pre).reshape(chans, rows, cols)
    patch_two = taps(with_rims(hidden), rows, cols).reshape(9 * chans, rows * cols)
    back = taps(with_rims(cot), rows, cols, flip=True)
    flat_cot = cot.reshape(chans, rows * cols)
    grad_two = scale * jnp.einsum("kp,cp->kc", patch_two, flat_cot, precision=HIGH)
    weight_two = filters[1].reshape(chans, 9, chans)
    dhidden = scale * jnp.einsum("itc,ctp->ip", weight_two, back, precision=HIGH)
    sig = jax.nn.sigmoid(pre)
    dpre = dhidden * sig * (1.0 + pre * (1.0 - sig))
    grad_one = scale * jnp.einsum("kp,cp->kc", patch_one, dpre, precision=HIGH)
    block = lax.psum_scatter(
        jnp.stack([grad_one, grad_two]), "band", scatter_dimension=1, tiled=True
    )
    count = lax.axis_size("image")
    for level in range(count.bit_length() - 1):
        other = lax.ppermute(block, "image", xor_route(count, 1 << level))
        inner, own_sq, other_sq = lax.psum(
            tuple(jnp.sum(v, axis=(1, 2)) for v in (block * other, block * block, other * other)),
            "band",
        )
        low = (1.0 - inner / (2.0 * (own_sq + 1e-06)))[:, None, None]
        high = (1.0 - inner / (2.0 * (other_sq + 1e-06)))[:, None, None]
        block = low * block + high * other
    height = block.shape[1]
    mine = lax.dynamic_slice_in_dim(filters, lax.axis_index("band") * height, height, 1)
    fresh = (mine - rates[:, None, None] * block)[None]
    return lax.all_gather(fresh, "band", axis=2, tiled=True)


def power_of_two(n):
    return n & (n - 1) == 0


def solution(mesh):
    n_image, n_band = mesh.shape["image"], mesh.shape["band"]

    def step(images, cotangent, filters, rates):
        chans = images.shape[1]
        if (
            4 <= n_image
            and n_image**2 <= 128
            and 4 <= n_band
            and power_of_two(n_image)
            and power_of_two(n_band)
            and (9 * chans) % (n_band // 2 * n_image * 8) == 0
        ):
            shape = (n_image // 2, 2, 2, n_band // 2)
            split = jax.sharding.Mesh(mesh.devices.reshape(shape), AXES)
            image, band = ("pair", "core"), ("half", "lo")

            def body(*args):
                return fast(*args)

        else:
            split, image, band, body = mesh, "image", "band", plain
        whole = jax.shard_map(
            body,
            mesh=split,
            in_specs=(P(image, None, band, None), P(image, None, band, None), P(), P()),
            out_specs=P(image, None, None, None),
            check_vma=False,
        )
        return whole(images, cotangent, filters, rates)

    return step
```

time: 192 us -> 69.2 us (0.36)
  waiting for transfers between devices: 75.2 us -> 12.7 us
  local copies, waits for them, and re-layouts: 28.6 us -> 1.29 us
  matrix products: 14.3 us -> 0 us
  between operations: 13.7 us -> 0.13 us
  other arithmetic: 9.83 us -> 0.04 us
  Pallas kernels: 0 us -> 7.41 us
    reduce_scatter x1 -> x0, waiting for transfers between devices: 32 us -> none  [local(): block = lax.psum_scatter(grads, 'band', scatter_dimension=1, tiled=True)]
    all_gather x1 -> x0, waiting for transfers between devices: 26.8 us -> none  [local(): return lax.all_gather(fresh, 'band', axis=2, tiled=True)]
    psum x3 -> x0, blocking collectives: 26.7 us -> none  [local(): lax.psum((jnp.sum(block * other, axis=(1, 2)), jnp.sum(block * block, axi...]
    all_to_all x0 -> x2, blocking collectives: none -> 25.4 us  [the longest x1 16 us: fast(): lax.all_to_all(whole.reshape(n_image, slot, chans), ('pair', 'half'), 0,...]
    dot_general x4 -> x0, matrix products: 14.3 us -> none  [the longest x1 5.67 us: local(): jnp.einsum('itc,ctp->ip', weight_two, back, precision=HIGH)]
    unnamed x47 -> x10, local copies, waits for them, and re-layouts: 13.5 us -> 1.28 us
    another operation x15 -> x0, local copies, waits for them, and re-layouts: 11.3 us -> none  [the longest x10 8.26 us: flipped(): return jnp.stack(pieces, axis=1).reshape(chans, 9, rows * cols)]
    pallas_call x0 -> x10, Pallas kernels: none -> 7.41 us  [the longest x1 2.45 us: fast(): call(functools.partial(grads_kernel, total, kdim ** (-0.5)), [(9 * mine,...]
  transfers between devices with their start and end apart: 11 -> 17, of which waited for: 5 -> 10; matrix products, arithmetic and copies ran while one was open for 15% -> 0% of each run, Pallas kernels for 0% -> 3%
where the time goes in v3:
time: 69.2 us; the launch traced here: 68.9 us
  blocking collectives  25.4 us (37%)
  starting transfers between devices  21.9 us (32%)
  waiting for transfers between devices  12.7 us (18%)
  Pallas kernels  7.41 us (11%)
  local copies, waits for them, and re-layouts  1.29 us (2%)
    ppermute x13, starting transfers between devices, swapped(): return lax.ppermute(value, axis, xor_route(lax.axis_size(axis), k))  17.5 us
    all_to_all x1, blocking collectives, fast(): lax.all_to_all(whole.reshape(n_image, slot, chans), ('pair', 'half'), 0,...  16 us
    all_to_all x1, blocking collectives, fast(): sums = lax.all_to_all(sums, AXES, 0, 0, tiled=True)  9.44 us
    ppermute x13, waiting for transfers between devices, swapped(): return lax.ppermute(value, axis, xor_route(lax.axis_size(axis), k))  9.14 us
    ppermute x4, starting transfers between devices, inputs_of(): found.append(lax.ppermute(value, ('core', 'half', 'lo'), route))  4.38 us
    ppermute x4, waiting for transfers between devices, inputs_of(): found.append(lax.ppermute(value, ('core', 'half', 'lo'), route))  3.59 us
    pallas_call x1, Pallas kernels, fast(): call(functools.partial(grads_kernel, total, kdim ** (-0.5)), [(9 * mine,...  2.45 us
    pallas_call x1, Pallas kernels, fast(): pl.pallas_call(functools.partial(final_kernel, n_pair, n_lo), out_shape=j...  1.91 us
  transfers between devices with their start and end apart: 17, of which 10 were waited for; matrix products, arithmetic and copies ran while one was open for 0% of the time, Pallas kernels for 3%

profile of v3, /device:TPU:0, one launch (start us, length us, event | category | flops | bytes accessed | tf_op | source)
XLA Modules:
  0.0 68.9 jit_solution(1517435381348544911)
XLA Ops:
  0.0 3.0 %collective-permute-start.1 = (f32[1,128,4,128]{3,2,1,0:T(4,128)}, f32[1,128,4,128]{3,2,1,0:T(4,128)S(1)}, u32[]{:S(2)}, u32[]{:S(2)}) collective-permute-start(f32[1,128,4,128]{3,2,1,0:T(4,128)} %param.4), channel_id=1, source_target_pairs={{0,1},{1,0},{2,5},{3,4},{4,3},{5,2},{6,7},{7,6},{8,9},{9,8},{10,13... | collective-permute-start | bytes 786440 | tf_op jit(solution)/shard_map/ppermute | solution.py:311
  3.0 0.7 collective-permute-start
  3.6 0.1 collective-permute-start.4
  3.7 0.7 collective-permute-start.3
  4.4 0.0 copy-start
  4.4 1.3 %copy-done = f32[2,1152,128]{2,1,0:T(8,128)S(1)} copy-done((f32[2,1152,128]{2,1,0:T(8,128)S(1)}, f32[2,1152,128]{2,1,0:T(8,128)}, u32[]{:S(2)}) %copy-start) | copy-done | bytes 1179672
  5.7 0.4 shard_map.48
  6.1 3.5 %collective-permute-done.1 = f32[1,128,4,128]{3,2,1,0:T(4,128)S(1)} collective-permute-done((f32[1,128,4,128]{3,2,1,0:T(4,128)}, f32[1,128,4,128]{3,2,1,0:T(4,128)S(1)}, u32[]{:S(2)}, u32[]{:S(2)}) %collective-permute-start.1) | collective-permute-done | bytes 262176 | tf_op jit(solution)/shard_map/ppermute | solution.py:311
  9.6 0.0 collective-permute-done
  9.6 0.0 copy-done.2
  9.6 5.5 %collective-permute-start.2 = (f32[128,128]{1,0:T(8,128)S(1)}, f32[128,128]{1,0:T(8,128)S(1)}, u32[]{:S(2)}, u32[]{:S(2)}) collective-permute-start(f32[128,128]{1,0:T(8,128)S(1)} %shard_map.46), channel_id=1, source_target_pairs={{0,4},{4,0},{1,5},{5,1},{2,6},{6,2},{3,7},{7,3},{8,12},{12,8},{9,1... | collective-permute-start | bytes 196616 | tf_op jit(solution)/shard_map/ppermute | solution.py:295
  15.1 0.1 collective-permute-done.4
  15.2 0.0 collective-permute-done.3
  15.2 0.0 copy-done.3
  15.2 3.4 %collective-permute-start.5 = (f32[128,128]{1,0:T(8,128)S(1)}, f32[128,128]{1,0:T(8,128)S(1)}, u32[]{:S(2)}, u32[]{:S(2)}) collective-permute-start(f32[128,128]{1,0:T(8,128)S(1)} %shard_map.47), channel_id=1, source_target_pairs={{0,4},{4,0},{1,5},{5,1},{2,6},{6,2},{3,7},{7,3},{8,12},{12,8},{9,1... | collective-permute-start | bytes 196616 | tf_op jit(solution)/shard_map/ppermute | solution.py:295
  18.6 0.9 %shard_map.49 = (bf16[384,1024]{1,0:T(8,128)(2,1)S(1)}, bf16[384,1024]{1,0:T(8,128)(2,1)S(1)}, f32[192,1024]{1,0:T(8,128)S(1)}) custom-call(f32[512,128]{1,0:T(8,128)S(1)} %bitcast.10, f32[512,128]{1,0:T(8,128)S(1)} %bitcast.18, f32[512,128]{1,0:T(8,128)S(1)} %bitcast.14, bf16[192,384]{1,0:T(8,128)(2,1)S(1)} %get-tuple-element.17.refs_2_.refs_6_, ...), custom_call_target="tpu_custom_call" | custom-call | flops 452984832 | bytes 905969 | tf_op jit(solution)/shard_map/pallas_call | solution.py:338
  19.6 0.9 %shard_map.50 = (bf16[384,1024]{1,0:T(8,128)(2,1)S(1)}, bf16[384,1024]{1,0:T(8,128)(2,1)S(1)}, f32[192,1024]{1,0:T(8,128)S(1)}) custom-call(f32[512,128]{1,0:T(8,128)S(1)} %bitcast.12, f32[512,128]{1,0:T(8,128)S(1)} %bitcast.20, f32[512,128]{1,0:T(8,128)S(1)} %bitcast.16, bf16[192,384]{1,0:T(8,128)(2,1)S(1)} %get-tuple-element.21.refs_2_.refs_8_, ...), custom_call_target="tpu_custom_call" | custom-call | flops 452984832 | bytes 905969 | tf_op jit(solution)/shard_map/pallas_call | solution.py:343
  20.5 0.0 collective-permute-done.2.refs_0_
  20.5 0.0 collective-permute-done.5.refs_1_
  20.5 2.4 %shard_map.51 = (f32[576,128]{1,0:T(8,128)S(1)}, f32[576,128]{1,0:T(8,128)S(1)}) custom-call(f32[128,128]{1,0:T(8,128)S(1)} %collective-permute-done.2.refs_0_, f32[128,128]{1,0:T(8,128)S(1)} %collective-permute-done.5.refs_1_, bf16[384,1024]{1,0:T(8,128)(2,1)S(1)} %get-tuple-element.19.refs_2_, bf16[384,1024]{1,0:T(8,128)(2,1)S(1)} %get-tuple-element.20.refs_3_, ...), custom_call_target="tpu_custom_call" | custom-call | flops 905969664 | bytes 1811939 | tf_op jit(solution)/shard_map/pallas_call | solution.py:346
  23.0 0.1 collective-permute-start.6
  23.1 1.5 %collective-permute-done.6 = f32[576,128]{1,0:T(8,128)S(1)} collective-permute-done((f32[576,128]{1,0:T(8,128)S(1)}, f32[576,128]{1,0:T(8,128)S(1)}, u32[]{:S(2)}, u32[]{:S(2)}) %collective-permute-start.6) | collective-permute-done | bytes 294944 | tf_op jit(solution)/shard_map/ppermute | solution.py:295
  24.7 16.0 %all_to_all.13.v_ref = f32[8,72,128]{2,1,0:T(8,128)S(1)} all-to-all(f32[8,72,128]{2,1,0:T(8,128)S(1)} %bitcast.23), channel_id=1, replica_groups=mesh['pair'=4,'core'=2,'half'=2,'lo'=2] {'pair','half'}, dimensions={0} | all-to-all | bytes 589824 | tf_op jit(solution)/shard_map/all_to_all | solution.py:357
  40.7 0.2 shard_map.52
  40.9 9.4 %all_to_all.14 = f32[32,1,128]{2,1,0:T(1,128)S(1)} all-to-all(f32[32,1,128]{2,1,0:T(1,128)S(1)} %broadcast_in_dim.2), channel_id=1, replica_groups=mesh['pair'=4,'core'=2,'half'=2,'lo'=2] {'pair','core','half','lo'}, dimensions={0} | all-to-all | bytes 32768 | tf_op jit(solution)/shard_map/all_to_all | solution.py:362
  50.4 0.5 shard_map.53.refs_0_
  50.9 0.6 collective-permute-start.9
  51.5 1.5 %collective-permute-start.8 = (f32[72,128]{1,0:T(8,128)S(1)}, f32[72,128]{1,0:T(8,128)S(1)}, u32[]{:S(2)}, u32[]{:S(2)}) collective-permute-start(f32[72,128]{1,0:T(8,128)S(1)} %shard_map.53.refs_0_), channel_id=1, source_target_pairs={{0,16},{8,24},{16,0},{24,8},{1,17},{9,25},{17,1},{25,9},{2,18},{10... | collective-permute-start | bytes 110600 | tf_op jit(solution)/shard_map/ppermute | solution.py:295
  53.0 2.4 %collective-permute-start.7 = (f32[72,128]{1,0:T(8,128)S(1)}, f32[72,128]{1,0:T(8,128)S(1)}, u32[]{:S(2)}, u32[]{:S(2)}) collective-permute-start(f32[72,128]{1,0:T(8,128)S(1)} %shard_map.53.refs_0_), channel_id=1, source_target_pairs={{0,8},{8,0},{16,24},{24,16},{1,9},{9,1},{17,25},{25,17},{2,10},{10... | collective-permute-start | bytes 110600 | tf_op jit(solution)/shard_map/ppermute | solution.py:295
  55.3 1.4 %collective-permute-done.9.refs_3_ = f32[72,128]{1,0:T(8,128)S(1)} collective-permute-done((f32[72,128]{1,0:T(8,128)S(1)}, f32[72,128]{1,0:T(8,128)S(1)}, u32[]{:S(2)}, u32[]{:S(2)}) %collective-permute-start.9) | collective-permute-done | bytes 36896 | tf_op jit(solution)/shard_map/ppermute | solution.py:295
  56.7 0.5 collective-permute-done.8.refs_2_
  57.2 0.2 collective-permute-done.7.refs_1_
  57.4 0.7 collective-permute-start.12
  58.1 1.4 %collective-permute-start.11 = (f32[288,128]{1,0:T(8,128)S(1)}, f32[288,128]{1,0:T(8,128)S(1)}, u32[]{:S(2)}, u32[]{:S(2)}) collective-permute-start(f32[288,128]{1,0:T(8,128)S(1)} %shard_map.54.refs_0_), channel_id=1, source_target_pairs={{0,2},{1,3},{2,0},{3,1},{4,6},{5,7},{6,4},{7,5},{8,10},{9,11},{10,... | collective-permute-start | bytes 442376 | tf_op jit(solution)/shard_map/ppermute | solution.py:295
  59.5 1.5 %collective-permute-start.10 = (f32[288,128]{1,0:T(8,128)S(1)}, f32[288,128]{1,0:T(8,128)S(1)}, u32[]{:S(2)}, u32[]{:S(2)}) collective-permute-start(f32[288,128]{1,0:T(8,128)S(1)} %shard_map.54.refs_0_), channel_id=1, source_target_pairs={{0,1},{1,0},{2,3},{3,2},{4,5},{5,4},{6,7},{7,6},{8,9},{9,8},{10,11... | collective-permute-start | bytes 442376 | tf_op jit(solution)/shard_map/ppermute | solution.py:295
  61.0 0.0 collective-permute-start.13
  61.0 3.6 %collective-permute-done.12.refs_3_ = f32[288,128]{1,0:T(8,128)S(1)} collective-permute-done((f32[288,128]{1,0:T(8,128)S(1)}, f32[288,128]{1,0:T(8,128)S(1)}, u32[]{:S(2)}, u32[]{:S(2)}) %collective-permute-start.12) | collective-permute-done | bytes 147488 | tf_op jit(solution)/shard_map/ppermute | solution.py:295
  64.6 0.0 collective-permute-start.16
  64.6 0.9 %collective-permute-done.11.refs_2_ = f32[288,128]{1,0:T(8,128)S(1)} collective-permute-done((f32[288,128]{1,0:T(8,128)S(1)}, f32[288,128]{1,0:T(8,128)S(1)}, u32[]{:S(2)}, u32[]{:S(2)}) %collective-permute-start.11) | collective-permute-done | bytes 147488 | tf_op jit(solution)/shard_map/ppermute | solution.py:295
  65.4 0.0 collective-permute-start.15
  65.4 0.0 collective-permute-done.10.refs_1_
  65.4 0.5 collective-permute-start.14
  66.0 0.0 collective-permute-done.13.refs_4_
  66.0 0.0 collective-permute-done.16.refs_7_
  66.0 0.9 %collective-permute-done.15.refs_6_ = f32[288,128]{1,0:T(8,128)S(1)} collective-permute-done((f32[288,128]{1,0:T(8,128)S(1)}, f32[288,128]{1,0:T(8,128)S(1)}, u32[]{:S(2)}, u32[]{:S(2)}) %collective-permute-start.15) | collective-permute-done | bytes 147488 | tf_op jit(solution)/shard_map/ppermute | solution.py:295
  66.8 0.2 collective-permute-done.14.refs_5_
  67.0 0.0 copy-done.4
  67.0 1.9 %shard_map.55 = f32[1,2,1152,128]{3,2,1,0:T(8,128)} custom-call(f32[2]{0:T(128)S(1)} %copy-done.4, f32[2,1152,128]{2,1,0:T(8,128)S(1)} %copy-done.1, f32[288,128]{1,0:T(8,128)S(1)} %shard_map.54.refs_0_, f32[288,128]{1,0:T(8,128)S(1)} %collective-permute-done.10.refs_1_, f32[288,128]{1,0:T(8,128)S(1)} %collective-permute-done.11.refs_2_, ...), custom_call_target="tpu_custom_call" | custom-call | tf_op jit(solution)/shard_map/pallas_call | solution.py:370
  (10 shorter events, 0.1 us)
Async XLA Ops:
  0.0 9.6 %collective-permute-start.1 = (f32[1,128,4,128]{3,2,1,0:T(4,128)}, f32[1,128,4,128]{3,2,1,0:T(4,128)S(1)}, u32[]{:S(2)}, u32[]{:S(2)}) collective-permute-start(f32[1,128,4,128]{3,2,1,0:T(4,128)} %param.4), channel_id=1, source_target_pairs={{0,1},{1,0},{2,5},{3,4},{4,3},{5,2},{6,7},{7,6},{8,9},{9,8},{10,13... | collective-permute-start | bytes 786440 | tf_op jit(solution)/shard_map/ppermute | solution.py:311
  3.0 6.6 %collective-permute-start = (f32[1,128,4,128]{3,2,1,0:T(4,128)}, f32[1,128,4,128]{3,2,1,0:T(4,128)S(1)}, u32[]{:S(2)}, u32[]{:S(2)}) collective-permute-start(f32[1,128,4,128]{3,2,1,0:T(4,128)} %param.4), channel_id=1, source_target_pairs={{2,4},{3,5},{4,2},{5,3},{10,12},{11,13},{12,10},{13,11},{18,20},{1... | collective-permute-start | bytes 786440 | tf_op jit(solution)/shard_map/ppermute | solution.py:311
  3.6 11.6 %collective-permute-start.4 = (f32[1,128,4,128]{3,2,1,0:T(4,128)}, f32[1,128,4,128]{3,2,1,0:T(4,128)S(1)}, u32[]{:S(2)}, u32[]{:S(2)}) collective-permute-start(f32[1,128,4,128]{3,2,1,0:T(4,128)} %param.5), channel_id=1, source_target_pairs={{0,1},{1,0},{2,5},{3,4},{4,3},{5,2},{6,7},{7,6},{8,9},{9,8},{10,13... | collective-permute-start | bytes 786440 | tf_op jit(solution)/shard_map/ppermute | solution.py:311
  3.7 11.5 %collective-permute-start.3 = (f32[1,128,4,128]{3,2,1,0:T(4,128)}, f32[1,128,4,128]{3,2,1,0:T(4,128)S(1)}, u32[]{:S(2)}, u32[]{:S(2)}) collective-permute-start(f32[1,128,4,128]{3,2,1,0:T(4,128)} %param.5), channel_id=1, source_target_pairs={{2,4},{3,5},{4,2},{5,3},{10,12},{11,13},{12,10},{13,11},{18,20},{1... | collective-permute-start | bytes 786440 | tf_op jit(solution)/shard_map/ppermute | solution.py:311
  4.4 1.3 %copy-start = (f32[2,1152,128]{2,1,0:T(8,128)S(1)}, f32[2,1152,128]{2,1,0:T(8,128)}, u32[]{:S(2)}) copy-start(f32[2,1152,128]{2,1,0:T(8,128)} %f_ref.3) | copy-start | bytes 3538948
  5.7 3.9 %copy-start.2 = (f32[1,128,4,128]{3,2,1,0:T(4,128)S(1)}, f32[1,128,4,128]{3,2,1,0:T(4,128)}, u32[]{:S(2)}) copy-start(f32[1,128,4,128]{3,2,1,0:T(4,128)} %param.4) | copy-start | bytes 786436
  5.7 9.5 %copy-start.3 = (f32[1,128,4,128]{3,2,1,0:T(4,128)S(1)}, f32[1,128,4,128]{3,2,1,0:T(4,128)}, u32[]{:S(2)}) copy-start(f32[1,128,4,128]{3,2,1,0:T(4,128)} %param.5) | copy-start | bytes 786436
  9.6 10.9 %collective-permute-start.2 = (f32[128,128]{1,0:T(8,128)S(1)}, f32[128,128]{1,0:T(8,128)S(1)}, u32[]{:S(2)}, u32[]{:S(2)}) collective-permute-start(f32[128,128]{1,0:T(8,128)S(1)} %shard_map.46), channel_id=1, source_target_pairs={{0,4},{4,0},{1,5},{5,1},{2,6},{6,2},{3,7},{7,3},{8,12},{12,8},{9,1... | collective-permute-start | bytes 196616 | tf_op jit(solution)/shard_map/ppermute | solution.py:295
  15.2 5.3 %collective-permute-start.5 = (f32[128,128]{1,0:T(8,128)S(1)}, f32[128,128]{1,0:T(8,128)S(1)}, u32[]{:S(2)}, u32[]{:S(2)}) collective-permute-start(f32[128,128]{1,0:T(8,128)S(1)} %shard_map.47), channel_id=1, source_target_pairs={{0,4},{4,0},{1,5},{5,1},{2,6},{6,2},{3,7},{7,3},{8,12},{12,8},{9,1... | collective-permute-start | bytes 196616 | tf_op jit(solution)/shard_map/ppermute | solution.py:295
  23.0 1.6 %collective-permute-start.6 = (f32[576,128]{1,0:T(8,128)S(1)}, f32[576,128]{1,0:T(8,128)S(1)}, u32[]{:S(2)}, u32[]{:S(2)}) collective-permute-start(f32[576,128]{1,0:T(8,128)S(1)} %get-tuple-element.28), channel_id=1, source_target_pairs={{0,4},{4,0},{1,5},{5,1},{2,6},{6,2},{3,7},{7,3},{8,12},{12,8},{9,1... | collective-permute-start | bytes 884744 | tf_op jit(solution)/shard_map/ppermute | solution.py:295
  24.6 42.4 %copy-start.1 = (f32[2,1152,128]{2,1,0:T(8,128)S(1)}, f32[2,1152,128]{2,1,0:T(8,128)}, u32[]{:S(2)}) copy-start(f32[2,1152,128]{2,1,0:T(8,128)} %f_ref.3) | copy-start | bytes 3538948
  24.6 42.4 %copy-start.4 = (f32[2]{0:T(128)S(1)}, f32[2]{0:T(128)}, u32[]{:S(2)}) copy-start(f32[2]{0:T(128)} %rates_ref.1) | copy-start | bytes 28
  50.9 5.8 %collective-permute-start.9 = (f32[72,128]{1,0:T(8,128)S(1)}, f32[72,128]{1,0:T(8,128)S(1)}, u32[]{:S(2)}, u32[]{:S(2)}) collective-permute-start(f32[72,128]{1,0:T(8,128)S(1)} %shard_map.53.refs_0_), channel_id=1, source_target_pairs={{0,24},{8,16},{16,8},{24,0},{1,25},{9,17},{17,9},{25,1},{2,26},{10... | collective-permute-start | bytes 110600 | tf_op jit(solution)/shard_map/ppermute | solution.py:295
  51.5 5.8 %collective-permute-start.8 = (f32[72,128]{1,0:T(8,128)S(1)}, f32[72,128]{1,0:T(8,128)S(1)}, u32[]{:S(2)}, u32[]{:S(2)}) collective-permute-start(f32[72,128]{1,0:T(8,128)S(1)} %shard_map.53.refs_0_), channel_id=1, source_target_pairs={{0,16},{8,24},{16,0},{24,8},{1,17},{9,25},{17,1},{25,9},{2,18},{10... | collective-permute-start | bytes 110600 | tf_op jit(solution)/shard_map/ppermute | solution.py:295
  53.0 4.4 %collective-permute-start.7 = (f32[72,128]{1,0:T(8,128)S(1)}, f32[72,128]{1,0:T(8,128)S(1)}, u32[]{:S(2)}, u32[]{:S(2)}) collective-permute-start(f32[72,128]{1,0:T(8,128)S(1)} %shard_map.53.refs_0_), channel_id=1, source_target_pairs={{0,8},{8,0},{16,24},{24,16},{1,9},{9,1},{17,25},{25,17},{2,10},{10... | collective-permute-start | bytes 110600 | tf_op jit(solution)/shard_map/ppermute | solution.py:295
  57.4 7.2 %collective-permute-start.12 = (f32[288,128]{1,0:T(8,128)S(1)}, f32[288,128]{1,0:T(8,128)S(1)}, u32[]{:S(2)}, u32[]{:S(2)}) collective-permute-start(f32[288,128]{1,0:T(8,128)S(1)} %shard_map.54.refs_0_), channel_id=1, source_target_pairs={{0,3},{1,2},{2,1},{3,0},{4,7},{5,6},{6,5},{7,4},{8,11},{9,10},{10,... | collective-permute-start | bytes 442376 | tf_op jit(solution)/shard_map/ppermute | solution.py:295
  58.1 7.3 %collective-permute-start.11 = (f32[288,128]{1,0:T(8,128)S(1)}, f32[288,128]{1,0:T(8,128)S(1)}, u32[]{:S(2)}, u32[]{:S(2)}) collective-permute-start(f32[288,128]{1,0:T(8,128)S(1)} %shard_map.54.refs_0_), channel_id=1, source_target_pairs={{0,2},{1,3},{2,0},{3,1},{4,6},{5,7},{6,4},{7,5},{8,10},{9,11},{10,... | collective-permute-start | bytes 442376 | tf_op jit(solution)/shard_map/ppermute | solution.py:295
  59.5 6.0 %collective-permute-start.10 = (f32[288,128]{1,0:T(8,128)S(1)}, f32[288,128]{1,0:T(8,128)S(1)}, u32[]{:S(2)}, u32[]{:S(2)}) collective-permute-start(f32[288,128]{1,0:T(8,128)S(1)} %shard_map.54.refs_0_), channel_id=1, source_target_pairs={{0,1},{1,0},{2,3},{3,2},{4,5},{5,4},{6,7},{7,6},{8,9},{9,8},{10,11... | collective-permute-start | bytes 442376 | tf_op jit(solution)/shard_map/ppermute | solution.py:295
  61.0 5.0 %collective-permute-start.13 = (f32[288,128]{1,0:T(8,128)S(1)}, f32[288,128]{1,0:T(8,128)S(1)}, u32[]{:S(2)}, u32[]{:S(2)}) collective-permute-start(f32[288,128]{1,0:T(8,128)S(1)} %shard_map.54.refs_0_), channel_id=1, source_target_pairs={{0,4},{4,0},{1,5},{5,1},{2,6},{6,2},{3,7},{7,3},{8,12},{12,8},{9,1... | collective-permute-start | bytes 442376 | tf_op jit(solution)/shard_map/ppermute | solution.py:295
  64.6 1.4 %collective-permute-start.16 = (f32[288,128]{1,0:T(8,128)S(1)}, f32[288,128]{1,0:T(8,128)S(1)}, u32[]{:S(2)}, u32[]{:S(2)}) collective-permute-start(f32[288,128]{1,0:T(8,128)S(1)} %collective-permute-done.12.refs_3_), channel_id=1, source_target_pairs={{0,4},{4,0},{1,5},{5,1},{2,6},{6,2},{3,7},{7,3},{8,12},{12,8},{9,1... | collective-permute-start | bytes 442376 | tf_op jit(solution)/shard_map/ppermute | solution.py:295
  65.4 1.4 %collective-permute-start.15 = (f32[288,128]{1,0:T(8,128)S(1)}, f32[288,128]{1,0:T(8,128)S(1)}, u32[]{:S(2)}, u32[]{:S(2)}) collective-permute-start(f32[288,128]{1,0:T(8,128)S(1)} %collective-permute-done.11.refs_2_), channel_id=1, source_target_pairs={{0,4},{4,0},{1,5},{5,1},{2,6},{6,2},{3,7},{7,3},{8,12},{12,8},{9,1... | collective-permute-start | bytes 442376 | tf_op jit(solution)/shard_map/ppermute | solution.py:295
  65.4 1.6 %collective-permute-start.14 = (f32[288,128]{1,0:T(8,128)S(1)}, f32[288,128]{1,0:T(8,128)S(1)}, u32[]{:S(2)}, u32[]{:S(2)}) collective-permute-start(f32[288,128]{1,0:T(8,128)S(1)} %collective-permute-done.10.refs_1_), channel_id=1, source_target_pairs={{0,4},{4,0},{1,5},{5,1},{2,6},{6,2},{3,7},{7,3},{8,12},{12,8},{9,1... | collective-permute-start | bytes 442376 | tf_op jit(solution)/shard_map/ppermute | solution.py:295

commit v4 on v3

--- a/solution.py
+++ b/solution.py
@@ -130,30 +130,57 @@
     out[...] = dot3(fh[...], fl[...], vh[...], vl[...], ((1,), (0,)))
 
 
-def grads_kernel(total, scale, *refs):
+def rims(edge, first, final, last):
+    core = lax.axis_index("core")
+    before = halves(jnp.where(core == 1, edge[...], 0.0))
+    after = halves(jnp.where(core == 0, edge[...], 0.0))
+    return {first: (0, before), final: (last, after)}
+
+
+def layer_grad(out, scale, dh, dl, vh, vl, rim_of):
+    mine = dh.shape[0] // 3
+    chans, cols = rim_of[0][1][0].shape
+    grad = dot3(dh[...], dl[...], vh[...], vl[...], ((1,), (1,)))
+    for a in range(3):
+        part = grad[:, a * chans : (a + 1) * chans]
+        if a in rim_of:
+            row, rim = rim_of[a]
+            wide = slice(row * cols, (row + 1) * cols)
+            part = part + dot3(dh[:, wide], dl[:, wide], *rim, ((1,), (1,)))
+        for b in range(3):
+            t = 3 * a + b
+            out[t * mine : (t + 1) * mine, :] = scale * part[b * mine : (b + 1) * mine, :]
+
+
+def either(wanted, scale, out, x_edge, c_edge, xh, xl, ch, cl, dh, dl, last):
+
+    @pl.when(wanted == 0)
+    def _():
+        layer_grad(out, scale, dh.at[0], dl.at[0], xh, xl, rims(x_edge, 0, 2, last))
+
+    @pl.when(wanted == 1)
+    def _():
+        layer_grad(out, scale, dh.at[1], dl.at[1], ch, cl, rims(c_edge, 2, 0, last))
+
+
+def give_kernel(total, scale, *refs):
     x_edge, c_edge, xh, xl, ch, cl, fh, fl, gh, gl, pre_ref, back_ref = refs[:12]
-    (keep_ref, give_ref), (g_ref, dh, dl) = refs[12:14], refs[14:]
+    give_ref, dh, dl = refs[12:]
     chans, cols = x_edge.shape
     mine = fh.shape[0] // 3
-    core = lax.axis_index("core")
-    last = total - 1
-    mm, nt = ((1,), (0,)), ((1,), (1,))
-    tall = [slice(k * chans, (k + 1) * chans) for k in range(3)]
+    mm = ((1,), (0,))
     part_of = [slice(k * mine, (k + 1) * mine) for k in range(3)]
 
-    def rims(edge, first, final):
-        before = halves(jnp.where(core == 1, edge[...], 0.0))
-        after = halves(jnp.where(core == 0, edge[...], 0.0))
-        return {first: (0, before), final: (last, after)}
-
-    x_rim = rims(x_edge, 0, 2)
-    c_rim = rims(c_edge, 2, 0)
-    pre_rim = {
-        row: dot3(fh[:, tall[a]], fl[:, tall[a]], *rim, mm) for a, (row, rim) in x_rim.items()
-    }
-    back_rim = {
-        row: dot3(gh[:, tall[a]], gl[:, tall[a]], *rim, mm) for a, (row, rim) in c_rim.items()
-    }
+    def rim_rows(wh, wl, rim_of):
+        return {
+            row: dot3(
+                wh[:, a * chans : (a + 1) * chans], wl[:, a * chans : (a + 1) * chans], *rim, mm
+            )
+            for a, (row, rim) in rim_of.items()
+        }
+
+    pre_rim = rim_rows(fh, fl, rims(x_edge, 0, 2, total - 1))
+    back_rim = rim_rows(gh, gl, rims(c_edge, 2, 0, total - 1))
     for row in range(total):
         wide = slice(row * cols, (row + 1) * cols)
 
@@ -178,19 +205,13 @@
             put(dh.at[0], dl.at[0], b, row, value)
         for b, value in enumerate((moved(hidden, -1), hidden, moved(hidden, 1))):
             put(dh.at[1], dl.at[1], b, row, value)
-    for layer, (vh, vl, rim_of) in enumerate(((xh, xl, x_rim), (ch, cl, c_rim))):
-        grad = dot3(dh[layer], dl[layer], vh[...], vl[...], nt)
-        for a in range(3):
-            part = grad[:, tall[a]]
-            if a in rim_of:
-                row, rim = rim_of[a]
-                wide = slice(row * cols, (row + 1) * cols)
-                part = part + dot3(dh[layer, :, wide], dl[layer, :, wide], *rim, nt)
-            for b in range(3):
-                t = 3 * a + b
-                g_ref[layer, t * mine : (t + 1) * mine, :] = scale * part[part_of[b], :]
-    keep_ref[...] = g_ref[core]
-    give_ref[...] = g_ref[1 - core]
+    wanted = 1 - lax.axis_index("core")
+    either(wanted, scale, give_ref, x_edge, c_edge, xh, xl, ch, cl, dh, dl, total - 1)
+
+
+def keep_kernel(total, scale, x_edge, c_edge, xh, xl, ch, cl, dh, dl, keep_ref):
+    wanted = lax.axis_index("core")
+    either(wanted, scale, keep_ref, x_edge, c_edge, xh, xl, ch, cl, dh, dl, total - 1)
 
 
 def gram_kernel(v_ref, out):
@@ -260,31 +281,37 @@
         out[pl.ds(start, size), :] = part[...]
 
 
-def final_kernel(n_pair, n_lo, rates_ref, f_ref, *refs):
+def final_kernel(n_pair, n_lo, swap, rates_ref, f_ref, *refs):
     n_band = 2 * n_lo
-    own, others = refs[:n_band], refs[n_band : 2 * n_band]
-    out, held = refs[2 * n_band :]
+    pieces = refs[:n_band]
+    out, held, fresh, sem = refs[-4:]
     core = lax.axis_index("core")
+    layer = 1 - core if swap else core
     band = lax.axis_index("half") * n_lo + lax.axis_index("lo")
-    size = own[0].shape[0] // n_pair
+    size = pieces[0].shape[0] // n_pair
     chans = f_ref.shape[2]
     mine = chans // n_lo
-    for k in range(n_band):
+    for k, piece in enumerate(pieces):
         place = lax.bitwise_xor(band, k)
         half, lo = place // n_lo, place % n_lo
         for p in range(n_pair):
             to = pl.ds(pl.multiple_of((2 * p + half) * size, 8), size)
-            at = slice(p * size, (p + 1) * size)
-            held[core, lo, to, :] = own[k][at, :]
-            held[1 - core, lo, to, :] = others[k][at, :]
-    for layer in range(2):
-        rate = rates_ref[layer]
-        for t in range(9):
-            at = pl.ds(t, chans, stride=9)
-            value = held[layer, :, t * mine : (t + 1) * mine, :].reshape(chans, chans)
-            if layer == 0:
-                value = value.T
-            out[0, layer, at, :] = f_ref[layer, at, :] - rate * value
+            held[lo, to, :] = piece[p * size : (p + 1) * size, :]
+    for l in range(2):
+
+        @pl.when(layer == l)
+        def _():
+            rate = rates_ref[l]
+            for t in range(9):
+                at = pl.ds(t, chans, stride=9)
+                value = held[:, t * mine : (t + 1) * mine, :].reshape(chans, chans)
+                if l == 0:
+                    value = value.T
+                fresh[at, :] = f_ref[l, at, :] - rate * value
+
+    copy = pltpu.make_async_copy(fresh, out.at[0, layer], sem)
+    copy.start()
+    copy.wait()
 
 
 def xor_route(count, k):
@@ -343,17 +370,19 @@
     ch, cl, back = call(
         functools.partial(rows_kernel, True), outs, raw, flops=work
     )(*cs, gh, gl)
-    keep, give = call(
-        functools.partial(grads_kernel, total, kdim ** (-0.5)),
-        [(9 * mine, chans)] * 2,
-        [
-            pltpu.VMEM((2, 9 * mine, chans), F32),
-            pltpu.VMEM((2, thin, wide), BF16),
-            pltpu.VMEM((2, thin, wide), BF16),
-        ],
+    scale = kdim ** (-0.5)
+    rows_of = (x_edge, c_edge, xh, xl, ch, cl)
+    part = (9 * mine, chans)
+    give, dh, dl = call(
+        functools.partial(give_kernel, total, scale),
+        [part] + [bf(2, thin, wide)] * 2,
         flops=2 * work,
-    )(x_edge, c_edge, xh, xl, ch, cl, fh, fl, gh, gl, pre, back)
-    whole = keep + swapped(give, "core", 1)
+    )(*rows_of, fh, fl, gh, gl, pre, back)
+    given = swapped(give, "core", 1)
+    (keep,) = call(
+        functools.partial(keep_kernel, total, scale), [part], flops=work
+    )(*rows_of, dh, dl)
+    whole = keep + given
     slices = lax.all_to_all(
         whole.reshape(n_image, slot, chans), ("pair", "half"), 0, 0, tiled=True
     )
@@ -364,17 +393,29 @@
         sums, slices
     )
     pieces = [merged] + [swapped(merged, "pair", k) for k in range(1, n_pair)]
-    (part,) = call(gather_kernel, [(n_pair * slot, chans)])(*pieces)
-    own = [part] + [swapped(part, ("half", "lo"), k) for k in range(1, n_band)]
+    (block,) = call(gather_kernel, [(n_pair * slot, chans)])(*pieces)
+    own = [block] + [swapped(block, ("half", "lo"), k) for k in range(1, n_band)]
     others = [swapped(piece, "core", 1) for piece in own]
-    return pl.pallas_call(
-        functools.partial(final_kernel, n_pair, n_lo),
-        out_shape=jax.ShapeDtypeStruct((1,) + filters.shape, F32),
-        in_specs=[pl.BlockSpec(memory_space=pltpu.SMEM)]
-        + [pl.BlockSpec(memory_space=pltpu.VMEM)] * (1 + 2 * n_band),
-        scratch_shapes=[pltpu.VMEM((2, n_lo, 9 * mine, chans), F32)],
-        compiler_params=pltpu.CompilerParams(vmem_limit_bytes=40 * 2**20),
-    )(rates, filters, *own, *others)
+    fresh = []
+    for swap, blocks in enumerate((own, others)):
+        fresh = [
+            pl.pallas_call(
+                functools.partial(final_kernel, n_pair, n_lo, swap),
+                out_shape=jax.ShapeDtypeStruct((1,) + filters.shape, F32),
+                in_specs=[pl.BlockSpec(memory_space=pltpu.SMEM)]
+                + [pl.BlockSpec(memory_space=pltpu.VMEM)] * (1 + n_band)
+                + [pl.BlockSpec(memory_space=pl.ANY)] * swap,
+                out_specs=pl.BlockSpec(memory_space=pl.ANY),
+                scratch_shapes=[
+                    pltpu.VMEM((n_lo,) + part, F32),
+                    pltpu.VMEM((kdim, chans), F32),
+                    pltpu.SemaphoreType.DMA,
+                ],
+                input_output_aliases={2 + n_band: 0} if swap else {},
+                compiler_params=pltpu.CompilerParams(vmem_limit_bytes=40 * 2**20),
+            )(rates, filters, *blocks, *fresh)
+        ]
+    return fresh[0]
 
 
 def with_rims(field):

time: 69.2 us -> 69 us (level)
  waiting for transfers between devices: 12.7 us -> 10.6 us
  Pallas kernels: 7.41 us -> 9.39 us
    ppermute x13, waiting for transfers between devices: 9.14 us -> 7.02 us  [swapped(): return lax.ppermute(value, axis, xor_route(lax.axis_size(axis), k))]
    pallas_call x3 -> x5, Pallas kernels: 4.38 us -> 6.37 us  [the longest x2 3.18 us: fast(): pl.pallas_call(functools.partial(final_kernel, n_pair, n_lo, swap), out_s...]
  transfers between devices with their start and end apart: 17 -> 17, of which waited for: 10 -> 8; matrix products, arithmetic and copies ran while one was open for 0% -> 0% of each run, Pallas kernels for 3% -> 7%
where the time goes in v4:
time: 69 us; the launch traced here: 68.7 us
  blocking collectives  25.3 us (37%)
  starting transfers between devices  21.9 us (32%)
  waiting for transfers between devices  10.6 us (15%)
  Pallas kernels  9.39 us (14%)
  local copies, waits for them, and re-layouts  1.3 us (2%)
    ppermute x13, starting transfers between devices, swapped(): return lax.ppermute(value, axis, xor_route(lax.axis_size(axis), k))  17.5 us
    all_to_all x1, blocking collectives, fast(): lax.all_to_all(whole.reshape(n_image, slot, chans), ('pair', 'half'), 0,...  15.9 us
    all_to_all x1, blocking collectives, fast(): sums = lax.all_to_all(sums, AXES, 0, 0, tiled=True)  9.44 us
    ppermute x13, waiting for transfers between devices, swapped(): return lax.ppermute(value, axis, xor_route(lax.axis_size(axis), k))  7.02 us
    ppermute x4, starting transfers between devices, inputs_of(): found.append(lax.ppermute(value, ('core', 'half', 'lo'), route))  4.38 us
    ppermute x4, waiting for transfers between devices, inputs_of(): found.append(lax.ppermute(value, ('core', 'half', 'lo'), route))  3.59 us
    pallas_call x2, Pallas kernels, fast(): pl.pallas_call(functools.partial(final_kernel, n_pair, n_lo, swap), out_s...  3.18 us
    pallas_call x1, Pallas kernels, fast(): call(functools.partial(give_kernel, total, scale), [part] + [bf(2, thin,...  2.14 us
  transfers between devices with their start and end apart: 17, of which 8 were waited for; matrix products, arithmetic and copies ran while one was open for 0% of the time, Pallas kernels for 7%

profile of v4, /device:TPU:0, one launch (start us, length us, event | category | flops | bytes accessed | tf_op | source)
XLA Modules:
  0.0 68.7 jit_solution(12315175839878672129)
XLA Ops:
  0.0 3.0 %collective-permute-start.1 = (f32[1,128,4,128]{3,2,1,0:T(4,128)}, f32[1,128,4,128]{3,2,1,0:T(4,128)S(1)}, u32[]{:S(2)}, u32[]{:S(2)}) collective-permute-start(f32[1,128,4,128]{3,2,1,0:T(4,128)} %param.4), channel_id=1, source_target_pairs={{0,1},{1,0},{2,5},{3,4},{4,3},{5,2},{6,7},{7,6},{8,9},{9,8},{10,13... | collective-permute-start | bytes 786440 | tf_op jit(solution)/shard_map/ppermute | solution.py:338
  3.0 0.7 collective-permute-start
  3.6 0.1 collective-permute-start.4
  3.7 0.7 collective-permute-start.3
  4.4 0.0 copy-start
  4.4 1.3 %copy-done = f32[2,1152,128]{2,1,0:T(8,128)S(1)} copy-done((f32[2,1152,128]{2,1,0:T(8,128)S(1)}, f32[2,1152,128]{2,1,0:T(8,128)}, u32[]{:S(2)}) %copy-start) | copy-done | bytes 1179672
  5.7 0.4 shard_map.48
  6.1 3.5 %collective-permute-done.1 = f32[1,128,4,128]{3,2,1,0:T(4,128)S(1)} collective-permute-done((f32[1,128,4,128]{3,2,1,0:T(4,128)}, f32[1,128,4,128]{3,2,1,0:T(4,128)S(1)}, u32[]{:S(2)}, u32[]{:S(2)}) %collective-permute-start.1) | collective-permute-done | bytes 262176 | tf_op jit(solution)/shard_map/ppermute | solution.py:338
  9.6 0.0 collective-permute-done
  9.6 5.5 %collective-permute-start.2 = (f32[128,128]{1,0:T(8,128)S(1)}, f32[128,128]{1,0:T(8,128)S(1)}, u32[]{:S(2)}, u32[]{:S(2)}) collective-permute-start(f32[128,128]{1,0:T(8,128)S(1)} %shard_map.46), channel_id=1, source_target_pairs={{0,4},{4,0},{1,5},{5,1},{2,6},{6,2},{3,7},{7,3},{8,12},{12,8},{9,1... | collective-permute-start | bytes 196616 | tf_op jit(solution)/shard_map/ppermute | solution.py:322
  15.1 0.1 collective-permute-done.4
  15.2 0.0 collective-permute-done.3
  15.2 3.4 %collective-permute-start.5 = (f32[128,128]{1,0:T(8,128)S(1)}, f32[128,128]{1,0:T(8,128)S(1)}, u32[]{:S(2)}, u32[]{:S(2)}) collective-permute-start(f32[128,128]{1,0:T(8,128)S(1)} %shard_map.47), channel_id=1, source_target_pairs={{0,4},{4,0},{1,5},{5,1},{2,6},{6,2},{3,7},{7,3},{8,12},{12,8},{9,1... | collective-permute-start | bytes 196616 | tf_op jit(solution)/shard_map/ppermute | solution.py:322
  18.6 0.9 %shard_map.49 = (bf16[384,1024]{1,0:T(8,128)(2,1)S(1)}, bf16[384,1024]{1,0:T(8,128)(2,1)S(1)}, f32[192,1024]{1,0:T(8,128)S(1)}) custom-call(f32[512,128]{1,0:T(8,128)S(1)} %bitcast.10, f32[512,128]{1,0:T(8,128)S(1)} %bitcast.18, f32[512,128]{1,0:T(8,128)S(1)} %bitcast.14, bf16[192,384]{1,0:T(8,128)(2,1)S(1)} %get-tuple-element.18.refs_2_.refs_6_, ...), custom_call_target="tpu_custom_call" | custom-call | flops 452984832 | bytes 905969 | tf_op jit(solution)/shard_map/pallas_call | solution.py:365
  19.6 0.9 %shard_map.50 = (bf16[384,1024]{1,0:T(8,128)(2,1)S(1)}, bf16[384,1024]{1,0:T(8,128)(2,1)S(1)}, f32[192,1024]{1,0:T(8,128)S(1)}) custom-call(f32[512,128]{1,0:T(8,128)S(1)} %bitcast.12, f32[512,128]{1,0:T(8,128)S(1)} %bitcast.20, f32[512,128]{1,0:T(8,128)S(1)} %bitcast.16, bf16[192,384]{1,0:T(8,128)(2,1)S(1)} %get-tuple-element.22.refs_2_.refs_8_, ...), custom_call_target="tpu_custom_call" | custom-call | flops 452984832 | bytes 905969 | tf_op jit(solution)/shard_map/pallas_call | solution.py:370
  20.5 0.0 collective-permute-done.2.refs_0_.x_edge
  20.5 0.0 collective-permute-done.5.refs_1_.c_edge
  20.5 2.1 %shard_map.51 = (f32[576,128]{1,0:T(8,128)S(1)}, bf16[2,192,1024]{2,1,0:T(8,128)(2,1)S(1)}, bf16[2,192,1024]{2,1,0:T(8,128)(2,1)S(1)}) custom-call(f32[128,128]{1,0:T(8,128)S(1)} %collective-permute-done.2.refs_0_.x_edge, f32[128,128]{1,0:T(8,128)S(1)} %collective-permute-done.5.refs_1_.c_edge, bf16[384,1024]{1,0:T(8,128)(2,1)S(1)} %get-tuple-element.20.refs_2_.xh, ...), custom_call_target="tpu_custom_call" | custom-call | flops 905969664 | bytes 1811939 | tf_op jit(solution)/shard_map/pallas_call | solution.py:376
  22.7 0.1 collective-permute-start.6
  22.8 1.0 %shard_map.52 = f32[576,128]{1,0:T(8,128)S(1)} custom-call(f32[128,128]{1,0:T(8,128)S(1)} %collective-permute-done.2.refs_0_.x_edge, f32[128,128]{1,0:T(8,128)S(1)} %collective-permute-done.5.refs_1_.c_edge, bf16[384,1024]{1,0:T(8,128)(2,1)S(1)} %get-tuple-element.20.refs_2_.xh, bf16[384,1024]{1,0:T(8,128)(2,1)S(1)} %get-tuple-element.21.refs_3_.xl, ...), custom_call_target="tpu_custom_call" | custom-call | flops 452984832 | bytes 905969 | tf_op jit(solution)/shard_map/pallas_call | solution.py:382
  23.8 0.0 copy-start.1
  23.8 0.0 copy-start.4
  23.8 0.5 collective-permute-done.6
  24.3 15.9 %all_to_all.13.v_ref = f32[8,72,128]{2,1,0:T(8,128)S(1)} all-to-all(f32[8,72,128]{2,1,0:T(8,128)S(1)} %bitcast.23), channel_id=1, replica_groups=mesh['pair'=4,'core'=2,'half'=2,'lo'=2] {'pair','half'}, dimensions={0} | all-to-all | bytes 589824 | tf_op jit(solution)/shard_map/all_to_all | solution.py:386
  40.2 0.2 shard_map.53
  40.5 9.4 %all_to_all.14 = f32[32,1,128]{2,1,0:T(1,128)S(1)} all-to-all(f32[32,1,128]{2,1,0:T(1,128)S(1)} %broadcast_in_dim.2), channel_id=1, replica_groups=mesh['pair'=4,'core'=2,'half'=2,'lo'=2] {'pair','core','half','lo'}, dimensions={0} | all-to-all | bytes 32768 | tf_op jit(solution)/shard_map/all_to_all | solution.py:391
  49.9 0.5 shard_map.54.refs_0_
  50.4 0.6 collective-permute-start.9
  51.0 1.5 %collective-permute-start.8 = (f32[72,128]{1,0:T(8,128)S(1)}, f32[72,128]{1,0:T(8,128)S(1)}, u32[]{:S(2)}, u32[]{:S(2)}) collective-permute-start(f32[72,128]{1,0:T(8,128)S(1)} %shard_map.54.refs_0_), channel_id=1, source_target_pairs={{0,16},{8,24},{16,0},{24,8},{1,17},{9,25},{17,1},{25,9},{2,18},{10... | collective-permute-start | bytes 110600 | tf_op jit(solution)/shard_map/ppermute | solution.py:322
  52.5 2.4 %collective-permute-start.7 = (f32[72,128]{1,0:T(8,128)S(1)}, f32[72,128]{1,0:T(8,128)S(1)}, u32[]{:S(2)}, u32[]{:S(2)}) collective-permute-start(f32[72,128]{1,0:T(8,128)S(1)} %shard_map.54.refs_0_), channel_id=1, source_target_pairs={{0,8},{8,0},{16,24},{24,16},{1,9},{9,1},{17,25},{25,17},{2,10},{10... | collective-permute-start | bytes 110600 | tf_op jit(solution)/shard_map/ppermute | solution.py:322
  54.9 1.4 %collective-permute-done.9.refs_3_ = f32[72,128]{1,0:T(8,128)S(1)} collective-permute-done((f32[72,128]{1,0:T(8,128)S(1)}, f32[72,128]{1,0:T(8,128)S(1)}, u32[]{:S(2)}, u32[]{:S(2)}) %collective-permute-start.9) | collective-permute-done | bytes 36896 | tf_op jit(solution)/shard_map/ppermute | solution.py:322
  56.3 0.5 collective-permute-done.8.refs_2_
  56.8 0.2 collective-permute-done.7.refs_1_
  57.0 0.7 collective-permute-start.15
  57.6 1.4 %collective-permute-start.13 = (f32[288,128]{1,0:T(8,128)S(1)}, f32[288,128]{1,0:T(8,128)S(1)}, u32[]{:S(2)}, u32[]{:S(2)}) collective-permute-start(f32[288,128]{1,0:T(8,128)S(1)} %shard_map.55.refs_0_), channel_id=1, source_target_pairs={{0,2},{1,3},{2,0},{3,1},{4,6},{5,7},{6,4},{7,5},{8,10},{9,11},{10,... | collective-permute-start | bytes 442376 | tf_op jit(solution)/shard_map/ppermute | solution.py:322
  59.0 1.5 %collective-permute-start.11 = (f32[288,128]{1,0:T(8,128)S(1)}, f32[288,128]{1,0:T(8,128)S(1)}, u32[]{:S(2)}, u32[]{:S(2)}) collective-permute-start(f32[288,128]{1,0:T(8,128)S(1)} %shard_map.55.refs_0_), channel_id=1, source_target_pairs={{0,1},{1,0},{2,3},{3,2},{4,5},{5,4},{6,7},{7,6},{8,9},{9,8},{10,11... | collective-permute-start | bytes 442376 | tf_op jit(solution)/shard_map/ppermute | solution.py:322
  60.5 0.0 collective-permute-start.10
  60.5 3.6 %collective-permute-done.15.refs_3_ = f32[288,128]{1,0:T(8,128)S(1)} collective-permute-done((f32[288,128]{1,0:T(8,128)S(1)}, f32[288,128]{1,0:T(8,128)S(1)}, u32[]{:S(2)}, u32[]{:S(2)}) %collective-permute-start.15) | collective-permute-done | bytes 147488 | tf_op jit(solution)/shard_map/ppermute | solution.py:322
  64.1 0.0 collective-permute-start.16
  64.1 0.9 %collective-permute-done.13.refs_2_ = f32[288,128]{1,0:T(8,128)S(1)} collective-permute-done((f32[288,128]{1,0:T(8,128)S(1)}, f32[288,128]{1,0:T(8,128)S(1)}, u32[]{:S(2)}, u32[]{:S(2)}) %collective-permute-start.13) | collective-permute-done | bytes 147488 | tf_op jit(solution)/shard_map/ppermute | solution.py:322
  65.0 0.0 collective-permute-start.14
  65.0 0.0 collective-permute-done.11.refs_1_
  65.0 0.5 collective-permute-start.12
  65.5 1.7 %shard_map.56.refs_4_ = f32[1,2,1152,128]{3,2,1,0:T(8,128)} custom-call(f32[2]{0:T(128)S(1)} %copy-done.4, f32[2,1152,128]{2,1,0:T(8,128)S(1)} %copy-done.1, f32[288,128]{1,0:T(8,128)S(1)} %shard_map.55.refs_0_, f32[288,128]{1,0:T(8,128)S(1)} %collective-permute-done.11.refs_1_, f32[288,128]{1,0:T(8,128)S(1)} %collective-permute-done.13.refs_2_, ...), custom_call_target="tpu_custom_call" | custom-call | tf_op jit(solution)/shard_map/pallas_call | solution.py:402
  67.2 0.0 collective-permute-done.10.refs_0_
  67.2 0.0 collective-permute-done.14.refs_2_
  67.2 0.0 collective-permute-done.12.refs_1_
  67.2 1.5 %shard_map.57 = f32[1,2,1152,128]{3,2,1,0:T(8,128)} custom-call(f32[2]{0:T(128)S(1)} %copy-done.4, f32[2,1152,128]{2,1,0:T(8,128)S(1)} %copy-done.1, f32[288,128]{1,0:T(8,128)S(1)} %collective-permute-done.10.refs_0_, f32[288,128]{1,0:T(8,128)S(1)} %collective-permute-done.12.refs_1_, ...), custom_call_target="tpu_custom_call", output_to_operand_aliasing={{}: (6, {})} | custom-call | tf_op jit(solution)/shard_map/pallas_call | solution.py:402
  (12 shorter events, 0.1 us)
Async XLA Ops:
  0.0 9.6 %collective-permute-start.1 = (f32[1,128,4,128]{3,2,1,0:T(4,128)}, f32[1,128,4,128]{3,2,1,0:T(4,128)S(1)}, u32[]{:S(2)}, u32[]{:S(2)}) collective-permute-start(f32[1,128,4,128]{3,2,1,0:T(4,128)} %param.4), channel_id=1, source_target_pairs={{0,1},{1,0},{2,5},{3,4},{4,3},{5,2},{6,7},{7,6},{8,9},{9,8},{10,13... | collective-permute-start | bytes 786440 | tf_op jit(solution)/shard_map/ppermute | solution.py:338
  3.0 6.6 %collective-permute-start = (f32[1,128,4,128]{3,2,1,0:T(4,128)}, f32[1,128,4,128]{3,2,1,0:T(4,128)S(1)}, u32[]{:S(2)}, u32[]{:S(2)}) collective-permute-start(f32[1,128,4,128]{3,2,1,0:T(4,128)} %param.4), channel_id=1, source_target_pairs={{2,4},{3,5},{4,2},{5,3},{10,12},{11,13},{12,10},{13,11},{18,20},{1... | collective-permute-start | bytes 786440 | tf_op jit(solution)/shard_map/ppermute | solution.py:338
  3.6 11.6 %collective-permute-start.4 = (f32[1,128,4,128]{3,2,1,0:T(4,128)}, f32[1,128,4,128]{3,2,1,0:T(4,128)S(1)}, u32[]{:S(2)}, u32[]{:S(2)}) collective-permute-start(f32[1,128,4,128]{3,2,1,0:T(4,128)} %param.5), channel_id=1, source_target_pairs={{0,1},{1,0},{2,5},{3,4},{4,3},{5,2},{6,7},{7,6},{8,9},{9,8},{10,13... | collective-permute-start | bytes 786440 | tf_op jit(solution)/shard_map/ppermute | solution.py:338
  3.7 11.5 %collective-permute-start.3 = (f32[1,128,4,128]{3,2,1,0:T(4,128)}, f32[1,128,4,128]{3,2,1,0:T(4,128)S(1)}, u32[]{:S(2)}, u32[]{:S(2)}) collective-permute-start(f32[1,128,4,128]{3,2,1,0:T(4,128)} %param.5), channel_id=1, source_target_pairs={{2,4},{3,5},{4,2},{5,3},{10,12},{11,13},{12,10},{13,11},{18,20},{1... | collective-permute-start | bytes 786440 | tf_op jit(solution)/shard_map/ppermute | solution.py:338
  4.4 1.3 %copy-start = (f32[2,1152,128]{2,1,0:T(8,128)S(1)}, f32[2,1152,128]{2,1,0:T(8,128)}, u32[]{:S(2)}) copy-start(f32[2,1152,128]{2,1,0:T(8,128)} %f_ref.5) | copy-start | bytes 3538948
  5.7 3.9 %copy-start.2 = (f32[1,128,4,128]{3,2,1,0:T(4,128)S(1)}, f32[1,128,4,128]{3,2,1,0:T(4,128)}, u32[]{:S(2)}) copy-start(f32[1,128,4,128]{3,2,1,0:T(4,128)} %param.4) | copy-start | bytes 786436
  5.7 9.5 %copy-start.3 = (f32[1,128,4,128]{3,2,1,0:T(4,128)S(1)}, f32[1,128,4,128]{3,2,1,0:T(4,128)}, u32[]{:S(2)}) copy-start(f32[1,128,4,128]{3,2,1,0:T(4,128)} %param.5) | copy-start | bytes 786436
  9.6 10.9 %collective-permute-start.2 = (f32[128,128]{1,0:T(8,128)S(1)}, f32[128,128]{1,0:T(8,128)S(1)}, u32[]{:S(2)}, u32[]{:S(2)}) collective-permute-start(f32[128,128]{1,0:T(8,128)S(1)} %shard_map.46), channel_id=1, source_target_pairs={{0,4},{4,0},{1,5},{5,1},{2,6},{6,2},{3,7},{7,3},{8,12},{12,8},{9,1... | collective-permute-start | bytes 196616 | tf_op jit(solution)/shard_map/ppermute | solution.py:322
  15.2 5.3 %collective-permute-start.5 = (f32[128,128]{1,0:T(8,128)S(1)}, f32[128,128]{1,0:T(8,128)S(1)}, u32[]{:S(2)}, u32[]{:S(2)}) collective-permute-start(f32[128,128]{1,0:T(8,128)S(1)} %shard_map.47), channel_id=1, source_target_pairs={{0,4},{4,0},{1,5},{5,1},{2,6},{6,2},{3,7},{7,3},{8,12},{12,8},{9,1... | collective-permute-start | bytes 196616 | tf_op jit(solution)/shard_map/ppermute | solution.py:322
  22.7 1.6 %collective-permute-start.6 = (f32[576,128]{1,0:T(8,128)S(1)}, f32[576,128]{1,0:T(8,128)S(1)}, u32[]{:S(2)}, u32[]{:S(2)}) collective-permute-start(f32[576,128]{1,0:T(8,128)S(1)} %get-tuple-element.30), channel_id=1, source_target_pairs={{0,4},{4,0},{1,5},{5,1},{2,6},{6,2},{3,7},{7,3},{8,12},{12,8},{9,1... | collective-permute-start | bytes 884744 | tf_op jit(solution)/shard_map/ppermute | solution.py:322
  23.8 41.7 %copy-start.1 = (f32[2,1152,128]{2,1,0:T(8,128)S(1)}, f32[2,1152,128]{2,1,0:T(8,128)}, u32[]{:S(2)}) copy-start(f32[2,1152,128]{2,1,0:T(8,128)} %f_ref.5) | copy-start | bytes 3538948
  23.8 41.7 %copy-start.4 = (f32[2]{0:T(128)S(1)}, f32[2]{0:T(128)}, u32[]{:S(2)}) copy-start(f32[2]{0:T(128)} %rates_ref.3) | copy-start | bytes 28
  50.4 5.8 %collective-permute-start.9 = (f32[72,128]{1,0:T(8,128)S(1)}, f32[72,128]{1,0:T(8,128)S(1)}, u32[]{:S(2)}, u32[]{:S(2)}) collective-permute-start(f32[72,128]{1,0:T(8,128)S(1)} %shard_map.54.refs_0_), channel_id=1, source_target_pairs={{0,24},{8,16},{16,8},{24,0},{1,25},{9,17},{17,9},{25,1},{2,26},{10... | collective-permute-start | bytes 110600 | tf_op jit(solution)/shard_map/ppermute | solution.py:322
  51.0 5.8 %collective-permute-start.8 = (f32[72,128]{1,0:T(8,128)S(1)}, f32[72,128]{1,0:T(8,128)S(1)}, u32[]{:S(2)}, u32[]{:S(2)}) collective-permute-start(f32[72,128]{1,0:T(8,128)S(1)} %shard_map.54.refs_0_), channel_id=1, source_target_pairs={{0,16},{8,24},{16,0},{24,8},{1,17},{9,25},{17,1},{25,9},{2,18},{10... | collective-permute-start | bytes 110600 | tf_op jit(solution)/shard_map/ppermute | solution.py:322
  52.5 4.4 %collective-permute-start.7 = (f32[72,128]{1,0:T(8,128)S(1)}, f32[72,128]{1,0:T(8,128)S(1)}, u32[]{:S(2)}, u32[]{:S(2)}) collective-permute-start(f32[72,128]{1,0:T(8,128)S(1)} %shard_map.54.refs_0_), channel_id=1, source_target_pairs={{0,8},{8,0},{16,24},{24,16},{1,9},{9,1},{17,25},{25,17},{2,10},{10... | collective-permute-start | bytes 110600 | tf_op jit(solution)/shard_map/ppermute | solution.py:322
  57.0 7.2 %collective-permute-start.15 = (f32[288,128]{1,0:T(8,128)S(1)}, f32[288,128]{1,0:T(8,128)S(1)}, u32[]{:S(2)}, u32[]{:S(2)}) collective-permute-start(f32[288,128]{1,0:T(8,128)S(1)} %shard_map.55.refs_0_), channel_id=1, source_target_pairs={{0,3},{1,2},{2,1},{3,0},{4,7},{5,6},{6,5},{7,4},{8,11},{9,10},{10,... | collective-permute-start | bytes 442376 | tf_op jit(solution)/shard_map/ppermute | solution.py:322
  57.6 7.3 %collective-permute-start.13 = (f32[288,128]{1,0:T(8,128)S(1)}, f32[288,128]{1,0:T(8,128)S(1)}, u32[]{:S(2)}, u32[]{:S(2)}) collective-permute-start(f32[288,128]{1,0:T(8,128)S(1)} %shard_map.55.refs_0_), channel_id=1, source_target_pairs={{0,2},{1,3},{2,0},{3,1},{4,6},{5,7},{6,4},{7,5},{8,10},{9,11},{10,... | collective-permute-start | bytes 442376 | tf_op jit(solution)/shard_map/ppermute | solution.py:322
  59.0 6.0 %collective-permute-start.11 = (f32[288,128]{1,0:T(8,128)S(1)}, f32[288,128]{1,0:T(8,128)S(1)}, u32[]{:S(2)}, u32[]{:S(2)}) collective-permute-start(f32[288,128]{1,0:T(8,128)S(1)} %shard_map.55.refs_0_), channel_id=1, source_target_pairs={{0,1},{1,0},{2,3},{3,2},{4,5},{5,4},{6,7},{7,6},{8,9},{9,8},{10,11... | collective-permute-start | bytes 442376 | tf_op jit(solution)/shard_map/ppermute | solution.py:322
  60.5 6.7 %collective-permute-start.10 = (f32[288,128]{1,0:T(8,128)S(1)}, f32[288,128]{1,0:T(8,128)S(1)}, u32[]{:S(2)}, u32[]{:S(2)}) collective-permute-start(f32[288,128]{1,0:T(8,128)S(1)} %shard_map.55.refs_0_), channel_id=1, source_target_pairs={{0,4},{4,0},{1,5},{5,1},{2,6},{6,2},{3,7},{7,3},{8,12},{12,8},{9,1... | collective-permute-start | bytes 442376 | tf_op jit(solution)/shard_map/ppermute | solution.py:322
  64.1 3.1 %collective-permute-start.16 = (f32[288,128]{1,0:T(8,128)S(1)}, f32[288,128]{1,0:T(8,128)S(1)}, u32[]{:S(2)}, u32[]{:S(2)}) collective-permute-start(f32[288,128]{1,0:T(8,128)S(1)} %collective-permute-done.15.refs_3_), channel_id=1, source_target_pairs={{0,4},{4,0},{1,5},{5,1},{2,6},{6,2},{3,7},{7,3},{8,12},{12,8},{9,1... | collective-permute-start | bytes 442376 | tf_op jit(solution)/shard_map/ppermute | solution.py:322
  65.0 2.2 %collective-permute-start.14 = (f32[288,128]{1,0:T(8,128)S(1)}, f32[288,128]{1,0:T(8,128)S(1)}, u32[]{:S(2)}, u32[]{:S(2)}) collective-permute-start(f32[288,128]{1,0:T(8,128)S(1)} %collective-permute-done.13.refs_2_), channel_id=1, source_target_pairs={{0,4},{4,0},{1,5},{5,1},{2,6},{6,2},{3,7},{7,3},{8,12},{12,8},{9,1... | collective-permute-start | bytes 442376 | tf_op jit(solution)/shard_map/ppermute | solution.py:322
  65.0 2.2 %collective-permute-start.12 = (f32[288,128]{1,0:T(8,128)S(1)}, f32[288,128]{1,0:T(8,128)S(1)}, u32[]{:S(2)}, u32[]{:S(2)}) collective-permute-start(f32[288,128]{1,0:T(8,128)S(1)} %collective-permute-done.11.refs_1_), channel_id=1, source_target_pairs={{0,4},{4,0},{1,5},{5,1},{2,6},{6,2},{3,7},{7,3},{8,12},{12,8},{9,1... | collective-permute-start | bytes 442376 | tf_op jit(solution)/shard_map/ppermute | solution.py:322

commit v5 on v4

--- a/solution.py
+++ b/solution.py
@@ -70,57 +70,38 @@
             put(gh, gl, b, a, taps_ref[1, t, rows, :])
 
 
-def edge_kernel(own_ref, *refs):
-    parts, out = refs[:-1], refs[-1]
-    core, lo = lax.axis_index("core"), lax.axis_index("lo")
-    kept = core == lax.axis_index("half")
-    count = len(parts)
+def sources(own, near, far):
+    core, half, lo = (lax.axis_index(name) for name in ("core", "half", "lo"))
+    kept = core == half
+    return (
+        (kept, own, lo),
+        (kept, near, 1 - lo),
+        (jnp.logical_not(kept), near, lo),
+        (jnp.logical_not(kept), far, 1 - lo),
+    )
+
+
+def edge_kernel(own_ref, near_ref, far_ref, out):
+    core = lax.axis_index("core")
     chans = out.shape[0]
     rows = own_ref.shape[0] // chans
-    place = jnp.where(core == 0, count - 1, 0)
-    for k, part in enumerate(parts):
+    for wanted, ref, block in sources(own_ref, near_ref, far_ref):
         for c, row in ((0, rows - 1), (1, 0)):
-            here = (lax.bitwise_xor(lo, k) == place) & (core == c)
-            at = pl.ds(row, chans, stride=rows)
-            if k == 0:
-
-                @pl.when(here & kept)
-                def _():
-                    out[...] = own_ref[at, :]
-
-                here = here & jnp.logical_not(kept)
-
-            @pl.when(here)
+
+            @pl.when(wanted & (core == c) & (block == 1 - c))
             def _():
-                out[...] = part[at, :]
-
-
-def rows_kernel(flip, own_ref, *refs):
-    parts, (fh, fl, vh, vl, out, raw) = refs[:-6], refs[-6:]
-    lo = lax.axis_index("lo")
-    kept = lax.axis_index("core") == lax.axis_index("half")
-    chans = raw.shape[1]
-    cols = raw.shape[2]
+                out[...] = ref[pl.ds(row, chans, stride=rows), :]
+
+
+def rows_kernel(flip, own_ref, near_ref, far_ref, fh, fl, vh, vl, out, raw):
+    total, chans, cols = raw.shape
     rows = own_ref.shape[0] // chans
-    total = raw.shape[0]
-
-    def take(ref, at):
-        for row in range(rows):
-            raw[at + row] = ref[pl.ds(row, chans, stride=rows), :]
-
-    for k, part in enumerate(parts):
-        at = lax.bitwise_xor(lo, k) * rows
-        if k:
-            take(part, at)
-            continue
-
-        @pl.when(kept)
+    for wanted, ref, block in sources(own_ref, near_ref, far_ref):
+
+        @pl.when(wanted)
         def _():
-            take(own_ref, at)
-
-        @pl.when(jnp.logical_not(kept))
-        def _():
-            take(part, at)
+            for row in range(rows):
+                raw[block * rows + row] = ref[pl.ds(row, chans, stride=rows), :]
 
     for a in range(3):
         step = 1 - a if flip else a - 1
@@ -152,66 +133,73 @@
             out[t * mine : (t + 1) * mine, :] = scale * part[b * mine : (b + 1) * mine, :]
 
 
-def either(wanted, scale, out, x_edge, c_edge, xh, xl, ch, cl, dh, dl, last):
+def row_sums(scale, wh, wl, ref, rim_of, total, flip):
+    mine = wh.shape[0] // 3
+    chans, cols = rim_of[0][1][0].shape
+    rim_row = {
+        row: dot3(
+            wh[:, a * chans : (a + 1) * chans],
+            wl[:, a * chans : (a + 1) * chans],
+            *rim,
+            ((1,), (0,)),
+        )
+        for a, (row, rim) in rim_of.items()
+    }
+    side = 1 if flip else -1
+    found = []
+    for row in range(total):
+        wide = slice(row * cols, (row + 1) * cols)
+        parts = []
+        for b in range(3):
+            value = ref[b * mine : (b + 1) * mine, wide]
+            if row in rim_row:
+                value = value + rim_row[row][b * mine : (b + 1) * mine, :]
+            parts.append(value)
+        found.append(scale * (parts[1] + moved(parts[0], side) + moved(parts[2], -side)))
+    return found
+
+
+def hidden_kernel(total, scale, edge, fh, fl, pre_ref, hh, hl, slope_ref):
+    cols = edge.shape[1]
+    for row, pre in enumerate(
+        row_sums(scale, fh, fl, pre_ref, rims(edge, 0, 2, total - 1), total, False)
+    ):
+        sig = jax.nn.sigmoid(pre)
+        hidden = pre * sig
+        slope_ref[:, row * cols : (row + 1) * cols] = sig * (1.0 + pre * (1.0 - sig))
+        for b, value in enumerate((moved(hidden, -1), hidden, moved(hidden, 1))):
+            put(hh, hl, b, row, value)
+
+
+def either(wanted, scale, out, x_edge, c_edge, xh, xl, ch, cl, hh, hl, dh, dl, last):
 
     @pl.when(wanted == 0)
     def _():
-        layer_grad(out, scale, dh.at[0], dl.at[0], xh, xl, rims(x_edge, 0, 2, last))
+        layer_grad(out, scale, dh, dl, xh, xl, rims(x_edge, 0, 2, last))
 
     @pl.when(wanted == 1)
     def _():
-        layer_grad(out, scale, dh.at[1], dl.at[1], ch, cl, rims(c_edge, 2, 0, last))
+        layer_grad(out, scale, hh, hl, ch, cl, rims(c_edge, 2, 0, last))
 
 
 def give_kernel(total, scale, *refs):
-    x_edge, c_edge, xh, xl, ch, cl, fh, fl, gh, gl, pre_ref, back_ref = refs[:12]
+    x_edge, c_edge, xh, xl, ch, cl, hh, hl, slope_ref, gh, gl, back_ref = refs[:12]
     give_ref, dh, dl = refs[12:]
-    chans, cols = x_edge.shape
-    mine = fh.shape[0] // 3
-    mm = ((1,), (0,))
-    part_of = [slice(k * mine, (k + 1) * mine) for k in range(3)]
-
-    def rim_rows(wh, wl, rim_of):
-        return {
-            row: dot3(
-                wh[:, a * chans : (a + 1) * chans], wl[:, a * chans : (a + 1) * chans], *rim, mm
-            )
-            for a, (row, rim) in rim_of.items()
-        }
-
-    pre_rim = rim_rows(fh, fl, rims(x_edge, 0, 2, total - 1))
-    back_rim = rim_rows(gh, gl, rims(c_edge, 2, 0, total - 1))
-    for row in range(total):
-        wide = slice(row * cols, (row + 1) * cols)
-
-        def summed(ref, rim, k):
-            value = ref[part_of[k], wide]
-            return value + rim[row][part_of[k], :] if row in rim else value
-
-        pre = scale * (
-            summed(pre_ref, pre_rim, 1)
-            + moved(summed(pre_ref, pre_rim, 0), -1)
-            + moved(summed(pre_ref, pre_rim, 2), 1)
-        )
-        dhidden = scale * (
-            summed(back_ref, back_rim, 1)
-            + moved(summed(back_ref, back_rim, 0), 1)
-            + moved(summed(back_ref, back_rim, 2), -1)
-        )
-        sig = jax.nn.sigmoid(pre)
-        hidden = pre * sig
-        dpre = dhidden * sig * (1.0 + pre * (1.0 - sig))
+    cols = x_edge.shape[1]
+    for row, dhidden in enumerate(
+        row_sums(scale, gh, gl, back_ref, rims(c_edge, 2, 0, total - 1), total, True)
+    ):
+        dpre = dhidden * slope_ref[:, row * cols : (row + 1) * cols]
         for b, value in enumerate((moved(dpre, 1), dpre, moved(dpre, -1))):
-            put(dh.at[0], dl.at[0], b, row, value)
-        for b, value in enumerate((moved(hidden, -1), hidden, moved(hidden, 1))):
-            put(dh.at[1], dl.at[1], b, row, value)
+            put(dh, dl, b, row, value)
     wanted = 1 - lax.axis_index("core")
-    either(wanted, scale, give_ref, x_edge, c_edge, xh, xl, ch, cl, dh, dl, total - 1)
-
-
-def keep_kernel(total, scale, x_edge, c_edge, xh, xl, ch, cl, dh, dl, keep_ref):
+    either(wanted, scale, give_ref, x_edge, c_edge, xh, xl, ch, cl, hh, hl, dh, dl, total - 1)
+
+
+def keep_kernel(total, scale, *refs):
+    x_edge, c_edge, xh, xl, ch, cl, hh, hl, dh, dl, keep_ref = refs
     wanted = lax.axis_index("core")
-    either(wanted, scale, keep_ref, x_edge, c_edge, xh, xl, ch, cl, dh, dl, total - 1)
+    either(wanted, scale, keep_ref, x_edge, c_edge, xh, xl, ch, cl, hh, hl, dh, dl, total - 1)
 
 
 def gram_kernel(v_ref, out):
@@ -281,12 +269,7 @@
         out[pl.ds(start, size), :] = part[...]
 
 
-def final_kernel(n_pair, n_lo, swap, rates_ref, f_ref, *refs):
-    n_band = 2 * n_lo
-    pieces = refs[:n_band]
-    out, held, fresh, sem = refs[-4:]
-    core = lax.axis_index("core")
-    layer = 1 - core if swap else core
+def new_layer(n_pair, n_lo, layer, rates_ref, f_ref, pieces, held, fresh):
     band = lax.axis_index("half") * n_lo + lax.axis_index("lo")
     size = pieces[0].shape[0] // n_pair
     chans = f_ref.shape[2]
@@ -309,9 +292,22 @@
                     value = value.T
                 fresh[at, :] = f_ref[l, at, :] - rate * value
 
-    copy = pltpu.make_async_copy(fresh, out.at[0, layer], sem)
-    copy.start()
-    copy.wait()
+
+def own_kernel(n_pair, n_lo, rates_ref, f_ref, *refs):
+    pieces, (fresh, held) = refs[:-2], refs[-2:]
+    new_layer(n_pair, n_lo, lax.axis_index("core"), rates_ref, f_ref, pieces, held, fresh)
+
+
+def final_kernel(n_pair, n_lo, rates_ref, f_ref, mine_ref, *refs):
+    pieces, (out, held, fresh, sems) = refs[:-4], refs[-4:]
+    core = lax.axis_index("core")
+    first = pltpu.make_async_copy(mine_ref, out.at[0, core], sems.at[0])
+    first.start()
+    new_layer(n_pair, n_lo, 1 - core, rates_ref, f_ref, pieces, held, fresh)
+    second = pltpu.make_async_copy(fresh, out.at[0, 1 - core], sems.at[1])
+    second.start()
+    first.wait()
+    second.wait()
 
 
 def xor_route(count, k):
@@ -322,21 +318,19 @@
     return lax.ppermute(value, axis, xor_route(lax.axis_size(axis), k))
 
 
-def inputs_of(value, n_lo):
+def routes():
     def at(core, half, lo):
-        return (core * 2 + half) * n_lo + lo
-
-    found = []
-    for k in range(n_lo - 1, -1, -1):
-        route = [
-            (at(core, half, lo), at(half, core, lo ^ k))
-            for core in range(2)
-            for half in range(2)
-            for lo in range(n_lo)
-            if k or core != half
-        ]
-        found.append(lax.ppermute(value, ("core", "half", "lo"), route))
-    return found[::-1]
+        return (core * 2 + half) * 2 + lo
+
+    every = [(core, half, lo) for core in range(2) for half in range(2) for lo in range(2)]
+    near = [(at(c, h, l), at(h, c, 1 - l if c == h else l)) for c, h, l in every]
+    far = [(at(c, h, l), at(h, c, 1 - l)) for c, h, l in every if c != h]
+    onward = [(at(c, h, l), at(c, h, 1 - l)) for c, h, l in every if c != h]
+    return near, far, onward
+
+
+def sent(value, route):
+    return lax.ppermute(value, ("core", "half", "lo"), route)
 
 
 def fast(images, cotangent, filters, rates):
@@ -350,10 +344,13 @@
     flat = (chans * rows, cols)
     bf = lambda *shape: jax.ShapeDtypeStruct(shape, BF16)
     tall, thin, wide = 3 * chans, 3 * mine, total * cols
-    xs = inputs_of(images, n_lo)
-    cs = inputs_of(cotangent, n_lo)
-    xs = [v.reshape(flat) for v in [images] + xs]
-    cs = [v.reshape(flat) for v in [cotangent] + cs]
+    near, far, onward = routes()
+    c_near = sent(cotangent, near)
+    x_near = sent(images, near)
+    x_far = sent(images, far)
+    c_far = sent(c_near, onward)
+    xs = [v.reshape(flat) for v in (images, x_near, x_far)]
+    cs = [v.reshape(flat) for v in (cotangent, c_near, c_far)]
     fh, fl, gh, gl = call(
         filter_kernel, [bf(thin, tall)] * 4, [pltpu.VMEM((2, 9, chans, chans), F32)]
     )(filters)
@@ -362,22 +359,19 @@
     raw = [pltpu.VMEM((total, chans, cols), F32)]
     work = 6 * thin * tall * wide
     outs = [bf(tall, wide)] * 2 + [(thin, wide)]
-    xh, xl, pre = call(
-        functools.partial(rows_kernel, False), outs, raw, flops=work
-    )(*xs, fh, fl)
+    xh, xl, pre = call(functools.partial(rows_kernel, False), outs, raw, flops=work)(*xs, fh, fl)
+    scale = kdim ** (-0.5)
+    hh, hl, slope = call(
+        functools.partial(hidden_kernel, total, scale), [bf(thin, wide)] * 2 + [(mine, wide)]
+    )(x_edge, fh, fl, pre)
     (edge,) = call(edge_kernel, [(chans, cols)])(*cs)
     c_edge = swapped(edge, "core", 1)
-    ch, cl, back = call(
-        functools.partial(rows_kernel, True), outs, raw, flops=work
-    )(*cs, gh, gl)
-    scale = kdim ** (-0.5)
-    rows_of = (x_edge, c_edge, xh, xl, ch, cl)
+    ch, cl, back = call(functools.partial(rows_kernel, True), outs, raw, flops=work)(*cs, gh, gl)
+    rows_of = (x_edge, c_edge, xh, xl, ch, cl, hh, hl)
     part = (9 * mine, chans)
     give, dh, dl = call(
-        functools.partial(give_kernel, total, scale),
-        [part] + [bf(2, thin, wide)] * 2,
-        flops=2 * work,
-    )(*rows_of, fh, fl, gh, gl, pre, back)
+        functools.partial(give_kernel, total, scale), [part] + [bf(thin, wide)] * 2, flops=2 * work
+    )(*rows_of, slope, gh, gl, back)
     given = swapped(give, "core", 1)
     (keep,) = call(
         functools.partial(keep_kernel, total, scale), [part], flops=work
@@ -389,33 +383,31 @@
     (gram,) = call(gram_kernel, [(1, 128)])(slices)
     sums = jnp.broadcast_to(gram, (n_image * n_band, gram.shape[1]))
     sums = lax.all_to_all(sums, AXES, 0, 0, tiled=True)
-    (merged,) = call(functools.partial(merge_kernel, n_band), [(slot, chans)])(
-        sums, slices
-    )
+    (merged,) = call(functools.partial(merge_kernel, n_band), [(slot, chans)])(sums, slices)
     pieces = [merged] + [swapped(merged, "pair", k) for k in range(1, n_pair)]
     (block,) = call(gather_kernel, [(n_pair * slot, chans)])(*pieces)
     own = [block] + [swapped(block, ("half", "lo"), k) for k in range(1, n_band)]
     others = [swapped(piece, "core", 1) for piece in own]
-    fresh = []
-    for swap, blocks in enumerate((own, others)):
-        fresh = [
-            pl.pallas_call(
-                functools.partial(final_kernel, n_pair, n_lo, swap),
-                out_shape=jax.ShapeDtypeStruct((1,) + filters.shape, F32),
-                in_specs=[pl.BlockSpec(memory_space=pltpu.SMEM)]
-                + [pl.BlockSpec(memory_space=pltpu.VMEM)] * (1 + n_band)
-                + [pl.BlockSpec(memory_space=pl.ANY)] * swap,
-                out_specs=pl.BlockSpec(memory_space=pl.ANY),
-                scratch_shapes=[
-                    pltpu.VMEM((n_lo,) + part, F32),
-                    pltpu.VMEM((kdim, chans), F32),
-                    pltpu.SemaphoreType.DMA,
-                ],
-                input_output_aliases={2 + n_band: 0} if swap else {},
-                compiler_params=pltpu.CompilerParams(vmem_limit_bytes=40 * 2**20),
-            )(rates, filters, *blocks, *fresh)
-        ]
-    return fresh[0]
+    layer = (kdim, chans)
+    held = pltpu.VMEM((n_lo,) + part, F32)
+    vmem, smem = (pl.BlockSpec(memory_space=m) for m in (pltpu.VMEM, pltpu.SMEM))
+    params = pltpu.CompilerParams(vmem_limit_bytes=40 * 2**20)
+    fresh = pl.pallas_call(
+        functools.partial(own_kernel, n_pair, n_lo),
+        out_shape=jax.ShapeDtypeStruct(layer, F32),
+        in_specs=[smem] + [vmem] * (1 + n_band),
+        out_specs=vmem,
+        scratch_shapes=[held],
+        compiler_params=params,
+    )(rates, filters, *own)
+    return pl.pallas_call(
+        functools.partial(final_kernel, n_pair, n_lo),
+        out_shape=jax.ShapeDtypeStruct((1,) + filters.shape, F32),
+        in_specs=[smem] + [vmem] * (2 + n_band),
+        out_specs=pl.BlockSpec(memory_space=pl.ANY),
+        scratch_shapes=[held, pltpu.VMEM(layer, F32), pltpu.SemaphoreType.DMA((2,))],
+        compiler_params=params,
+    )(rates, filters, fresh, *others)
 
 
 def with_rims(field):
@@ -482,9 +474,8 @@
         if (
             4 <= n_image
             and n_image**2 <= 128
-            and 4 <= n_band
+            and n_band == 4
             and power_of_two(n_image)
-            and power_of_two(n_band)
             and (9 * chans) % (n_band // 2 * n_image * 8) == 0
         ):
             shape = (n_image // 2, 2, 2, n_band // 2)

time: 69 us -> 67.7 us (0.981)
  starting transfers between devices: 21.9 us -> 14.7 us
  waiting for transfers between devices: 10.6 us -> 16 us
  local copies, waits for them, and re-layouts: 1.3 us -> 2.6 us
  Pallas kernels: 9.39 us -> 8.52 us
    ppermute x13, starting transfers between devices: 17.5 us -> 10.3 us  [swapped(): return lax.ppermute(value, axis, xor_route(lax.axis_size(axis), k))]
    ppermute x4, waiting for transfers between devices: 3.59 us -> 8.93 us  [sent(): return lax.ppermute(value, ('core', 'half', 'lo'), route)]
    unnamed x10 -> x12, local copies, waits for them, and re-layouts: 1.29 us -> 2.59 us
    pallas_call x3 -> x4, Pallas kernels: 5.32 us -> 4.36 us  [the longest x1 1.6 us: fast(): pl.pallas_call(functools.partial(final_kernel, n_pair, n_lo), out_shape=j...]
  transfers between devices with their start and end apart: 17 -> 17, of which waited for: 8 -> 9; matrix products, arithmetic and copies ran while one was open for 0% -> 0% of each run, Pallas kernels for 7% -> 7%
where the time goes in v5:
time: 67.7 us; the launch traced here: 67.4 us
  blocking collectives  25.3 us (37%)
  waiting for transfers between devices  16 us (24%)
  starting transfers between devices  14.7 us (22%)
  Pallas kernels  8.52 us (13%)
  local copies, waits for them, and re-layouts  2.6 us (4%)
    all_to_all x1, blocking collectives, fast(): lax.all_to_all(whole.reshape(n_image, slot, chans), ('pair', 'half'), 0,...  15.9 us
    ppermute x13, starting transfers between devices, swapped(): return lax.ppermute(value, axis, xor_route(lax.axis_size(axis), k))  10.3 us
    all_to_all x1, blocking collectives, fast(): sums = lax.all_to_all(sums, AXES, 0, 0, tiled=True)  9.41 us
    ppermute x4, waiting for transfers between devices, sent(): return lax.ppermute(value, ('core', 'half', 'lo'), route)  8.93 us
    ppermute x13, waiting for transfers between devices, swapped(): return lax.ppermute(value, axis, xor_route(lax.axis_size(axis), k))  7.08 us
    ppermute x4, starting transfers between devices, sent(): return lax.ppermute(value, ('core', 'half', 'lo'), route)  4.37 us
    unnamed x12, local copies, waits for them, and re-layouts  2.59 us
    pallas_call x1, Pallas kernels, fast(): pl.pallas_call(functools.partial(final_kernel, n_pair, n_lo), out_shape=j...  1.6 us
  transfers between devices with their start and end apart: 17, of which 9 were waited for; matrix products, arithmetic and copies ran while one was open for 0% of the time, Pallas kernels for 7%

profile of v5, /device:TPU:0, one launch (start us, length us, event | category | flops | bytes accessed | tf_op | source)
XLA Modules:
  0.0 67.4 jit_solution(9350844234339281801)
XLA Ops:
  0.0 3.0 %collective-permute-start.3 = (f32[1,128,4,128]{3,2,1,0:T(4,128)}, f32[1,128,4,128]{3,2,1,0:T(4,128)S(1)}, u32[]{:S(2)}, u32[]{:S(2)}) collective-permute-start(f32[1,128,4,128]{3,2,1,0:T(4,128)} %param.5), channel_id=1, source_target_pairs={{0,1},{1,0},{2,4},{3,5},{4,2},{5,3},{6,7},{7,6},{8,9},{9,8},{10,12... | collective-permute-start | bytes 786440 | tf_op jit(solution)/shard_map/ppermute | solution.py:333
  3.0 0.7 collective-permute-start.1
  3.6 0.1 collective-permute-start
  3.7 4.0 %collective-permute-done.3 = f32[1,128,4,128]{3,2,1,0:T(4,128)S(1)} collective-permute-done((f32[1,128,4,128]{3,2,1,0:T(4,128)}, f32[1,128,4,128]{3,2,1,0:T(4,128)S(1)}, u32[]{:S(2)}, u32[]{:S(2)}) %collective-permute-start.3) | collective-permute-done | bytes 262176 | tf_op jit(solution)/shard_map/ppermute | solution.py:333
  7.7 0.7 collective-permute-start.4
  8.4 0.0 collective-permute-done.1
  8.4 4.9 %collective-permute-done = f32[1,128,4,128]{3,2,1,0:T(4,128)S(1)} collective-permute-done((f32[1,128,4,128]{3,2,1,0:T(4,128)}, f32[1,128,4,128]{3,2,1,0:T(4,128)S(1)}, u32[]{:S(2)}, u32[]{:S(2)}) %collective-permute-start) | collective-permute-done | bytes 262176 | tf_op jit(solution)/shard_map/ppermute | solution.py:333
  13.3 0.9 %copy-done.2 = f32[1,128,4,128]{3,2,1,0:T(4,128)S(1)} copy-done((f32[1,128,4,128]{3,2,1,0:T(4,128)S(1)}, f32[1,128,4,128]{3,2,1,0:T(4,128)}, u32[]{:S(2)}) %copy-start.2) | copy-done | bytes 262168
  14.3 1.5 %collective-permute-start.2 = (f32[128,128]{1,0:T(8,128)S(1)}, f32[128,128]{1,0:T(8,128)S(1)}, u32[]{:S(2)}, u32[]{:S(2)}) collective-permute-start(f32[128,128]{1,0:T(8,128)S(1)} %shard_map.46), channel_id=1, source_target_pairs={{0,4},{4,0},{1,5},{5,1},{2,6},{6,2},{3,7},{7,3},{8,12},{12,8},{9,1... | collective-permute-start | bytes 196616 | tf_op jit(solution)/shard_map/ppermute | solution.py:318
  15.8 1.3 %copy-done = f32[2,1152,128]{2,1,0:T(8,128)S(1)} copy-done((f32[2,1152,128]{2,1,0:T(8,128)S(1)}, f32[2,1152,128]{2,1,0:T(8,128)}, u32[]{:S(2)}) %copy-start) | copy-done | bytes 1179672
  17.1 0.4 shard_map.48
  17.5 0.0 collective-permute-done.4
  17.5 0.1 shard_map.47
  17.6 0.1 collective-permute-start.5
  17.7 0.3 copy-done.3
  18.0 0.9 %shard_map.49 = (bf16[384,1024]{1,0:T(8,128)(2,1)S(1)}, bf16[384,1024]{1,0:T(8,128)(2,1)S(1)}, f32[192,1024]{1,0:T(8,128)S(1)}) custom-call(f32[512,128]{1,0:T(8,128)S(1)} %bitcast.10, f32[512,128]{1,0:T(8,128)S(1)} %bitcast.20, f32[512,128]{1,0:T(8,128)S(1)} %bitcast.18, bf16[192,384]{1,0:T(8,128)(2,1)S(1)} %get-tuple-element.21.fh, ...), custom_call_target="tpu_custom_call" | custom-call | flops 452984832 | bytes 905969 | tf_op jit(solution)/shard_map/pallas_call | solution.py:362
  18.9 0.0 collective-permute-done.2.edge.refs_0_
  19.0 0.5 shard_map.51
  19.4 0.9 %shard_map.50 = (bf16[384,1024]{1,0:T(8,128)(2,1)S(1)}, bf16[384,1024]{1,0:T(8,128)(2,1)S(1)}, f32[192,1024]{1,0:T(8,128)S(1)}) custom-call(f32[512,128]{1,0:T(8,128)S(1)} %bitcast.12, f32[512,128]{1,0:T(8,128)S(1)} %bitcast.14, f32[512,128]{1,0:T(8,128)S(1)} %bitcast.16, bf16[192,384]{1,0:T(8,128)(2,1)S(1)} %get-tuple-element.25.fh.refs_9_, ...), custom_call_target="tpu_custom_call" | custom-call | flops 452984832 | bytes 905969 | tf_op jit(solution)/shard_map/pallas_call | solution.py:369
  20.4 0.0 collective-permute-done.5.refs_1_
  20.4 1.5 %shard_map.52 = (f32[576,128]{1,0:T(8,128)S(1)}, bf16[192,1024]{1,0:T(8,128)(2,1)S(1)}, bf16[192,1024]{1,0:T(8,128)(2,1)S(1)}) custom-call(f32[128,128]{1,0:T(8,128)S(1)} %collective-permute-done.2.edge.refs_0_, f32[128,128]{1,0:T(8,128)S(1)} %collective-permute-done.5.refs_1_, bf16[384,1024]{1,0:T(8,128)(2,1)S(1)} %get-tuple-element.23.refs_2_, ...), custom_call_target="tpu_custom_call" | custom-call | flops 905969664 | bytes 1811939 | tf_op jit(solution)/shard_map/pallas_call | solution.py:372
  21.9 0.2 collective-permute-start.6
  22.1 1.0 %shard_map.53 = f32[576,128]{1,0:T(8,128)S(1)} custom-call(f32[128,128]{1,0:T(8,128)S(1)} %collective-permute-done.2.edge.refs_0_, f32[128,128]{1,0:T(8,128)S(1)} %collective-permute-done.5.refs_1_, bf16[384,1024]{1,0:T(8,128)(2,1)S(1)} %get-tuple-element.23.refs_2_, bf16[384,1024]{1,0:T(8,128)(2,1)S(1)} %get-tuple-element.24.refs_3_, ...), custom_call_target="tpu_custom_call" | custom-call | flops 452984832 | bytes 905969 | tf_op jit(solution)/shard_map/pallas_call | solution.py:376
  23.1 0.0 copy-start.1
  23.1 0.0 copy-start.5
  23.1 0.4 collective-permute-done.6
  23.5 15.9 %all_to_all.13.v_ref = f32[8,72,128]{2,1,0:T(8,128)S(1)} all-to-all(f32[8,72,128]{2,1,0:T(8,128)S(1)} %bitcast.23), channel_id=1, replica_groups=mesh['pair'=4,'core'=2,'half'=2,'lo'=2] {'pair','half'}, dimensions={0} | all-to-all | bytes 589824 | tf_op jit(solution)/shard_map/all_to_all | solution.py:380
  39.4 0.2 shard_map.54
  39.7 9.4 %all_to_all.14 = f32[32,1,128]{2,1,0:T(1,128)S(1)} all-to-all(f32[32,1,128]{2,1,0:T(1,128)S(1)} %broadcast_in_dim.2), channel_id=1, replica_groups=mesh['pair'=4,'core'=2,'half'=2,'lo'=2] {'pair','core','half','lo'}, dimensions={0} | all-to-all | bytes 32768 | tf_op jit(solution)/shard_map/all_to_all | solution.py:385
  49.1 0.5 shard_map.55.refs_0_
  49.6 0.6 collective-permute-start.9
  50.2 1.5 %collective-permute-start.8 = (f32[72,128]{1,0:T(8,128)S(1)}, f32[72,128]{1,0:T(8,128)S(1)}, u32[]{:S(2)}, u32[]{:S(2)}) collective-permute-start(f32[72,128]{1,0:T(8,128)S(1)} %shard_map.55.refs_0_), channel_id=1, source_target_pairs={{0,16},{8,24},{16,0},{24,8},{1,17},{9,25},{17,1},{25,9},{2,18},{10... | collective-permute-start | bytes 110600 | tf_op jit(solution)/shard_map/ppermute | solution.py:318
  51.7 2.4 %collective-permute-start.7 = (f32[72,128]{1,0:T(8,128)S(1)}, f32[72,128]{1,0:T(8,128)S(1)}, u32[]{:S(2)}, u32[]{:S(2)}) collective-permute-start(f32[72,128]{1,0:T(8,128)S(1)} %shard_map.55.refs_0_), channel_id=1, source_target_pairs={{0,8},{8,0},{16,24},{24,16},{1,9},{9,1},{17,25},{25,17},{2,10},{10... | collective-permute-start | bytes 110600 | tf_op jit(solution)/shard_map/ppermute | solution.py:318
  54.1 1.4 %collective-permute-done.9.refs_3_ = f32[72,128]{1,0:T(8,128)S(1)} collective-permute-done((f32[72,128]{1,0:T(8,128)S(1)}, f32[72,128]{1,0:T(8,128)S(1)}, u32[]{:S(2)}, u32[]{:S(2)}) %collective-permute-start.9) | collective-permute-done | bytes 36896 | tf_op jit(solution)/shard_map/ppermute | solution.py:318
  55.5 0.5 collective-permute-done.8.refs_2_
  56.0 0.2 collective-permute-done.7.refs_1_
  56.2 0.7 collective-permute-start.12
  56.8 1.4 %collective-permute-start.11 = (f32[288,128]{1,0:T(8,128)S(1)}, f32[288,128]{1,0:T(8,128)S(1)}, u32[]{:S(2)}, u32[]{:S(2)}) collective-permute-start(f32[288,128]{1,0:T(8,128)S(1)} %shard_map.56.refs_0_), channel_id=1, source_target_pairs={{0,2},{1,3},{2,0},{3,1},{4,6},{5,7},{6,4},{7,5},{8,10},{9,11},{10,... | collective-permute-start | bytes 442376 | tf_op jit(solution)/shard_map/ppermute | solution.py:318
  58.2 1.5 %collective-permute-start.10 = (f32[288,128]{1,0:T(8,128)S(1)}, f32[288,128]{1,0:T(8,128)S(1)}, u32[]{:S(2)}, u32[]{:S(2)}) collective-permute-start(f32[288,128]{1,0:T(8,128)S(1)} %shard_map.56.refs_0_), channel_id=1, source_target_pairs={{0,1},{1,0},{2,3},{3,2},{4,5},{5,4},{6,7},{7,6},{8,9},{9,8},{10,11... | collective-permute-start | bytes 442376 | tf_op jit(solution)/shard_map/ppermute | solution.py:318
  59.7 0.0 collective-permute-start.13
  59.7 3.6 %collective-permute-done.12.refs_3_ = f32[288,128]{1,0:T(8,128)S(1)} collective-permute-done((f32[288,128]{1,0:T(8,128)S(1)}, f32[288,128]{1,0:T(8,128)S(1)}, u32[]{:S(2)}, u32[]{:S(2)}) %collective-permute-start.12) | collective-permute-done | bytes 147488 | tf_op jit(solution)/shard_map/ppermute | solution.py:318
  63.3 0.9 %collective-permute-done.11.refs_2_ = f32[288,128]{1,0:T(8,128)S(1)} collective-permute-done((f32[288,128]{1,0:T(8,128)S(1)}, f32[288,128]{1,0:T(8,128)S(1)}, u32[]{:S(2)}, u32[]{:S(2)}) %collective-permute-start.11) | collective-permute-done | bytes 147488 | tf_op jit(solution)/shard_map/ppermute | solution.py:318
  64.2 0.5 collective-permute-start.14
  64.7 0.8 %shard_map.57.mine_ref = f32[1152,128]{1,0:T(8,128)S(1)} custom-call(f32[2]{0:T(128)S(1)} %copy-done.5, f32[2,1152,128]{2,1,0:T(8,128)S(1)} %copy-done.1, f32[288,128]{1,0:T(8,128)S(1)} %shard_map.56.refs_0_, f32[288,128]{1,0:T(8,128)S(1)} %collective-permute-done.10.refs_1_, f32[288,128]{1,0:T(8,128)S(1)} %collective-permute-done.11.refs_2_, ...), custom_call_target="tpu_custom_call" | custom-call | tf_op jit(solution)/shard_map/pallas_call | solution.py:395
  65.6 0.0 collective-permute-done.16.refs_3_
  65.6 0.0 collective-permute-done.15.refs_2_
  65.6 0.2 collective-permute-done.14.refs_1_
  65.8 1.6 %shard_map.58 = f32[1,2,1152,128]{3,2,1,0:T(8,128)} custom-call(f32[2]{0:T(128)S(1)} %copy-done.5, f32[2,1152,128]{2,1,0:T(8,128)S(1)} %copy-done.1, f32[1152,128]{1,0:T(8,128)S(1)} %shard_map.57.mine_ref, f32[288,128]{1,0:T(8,128)S(1)} %collective-permute-done.13.refs_0_, f32[288,128]{1,0:T(8,128)S(1)} %collective-permute-done.14.refs_1_, ...), custom_call_target="tpu_custom_call" | custom-call | tf_op jit(solution)/shard_map/pallas_call | solution.py:403
  (15 shorter events, 0.1 us)
Async XLA Ops:
  0.0 7.7 %collective-permute-start.3 = (f32[1,128,4,128]{3,2,1,0:T(4,128)}, f32[1,128,4,128]{3,2,1,0:T(4,128)S(1)}, u32[]{:S(2)}, u32[]{:S(2)}) collective-permute-start(f32[1,128,4,128]{3,2,1,0:T(4,128)} %param.5), channel_id=1, source_target_pairs={{0,1},{1,0},{2,4},{3,5},{4,2},{5,3},{6,7},{7,6},{8,9},{9,8},{10,12... | collective-permute-start | bytes 786440 | tf_op jit(solution)/shard_map/ppermute | solution.py:333
  3.0 5.4 %collective-permute-start.1 = (f32[1,128,4,128]{3,2,1,0:T(4,128)}, f32[1,128,4,128]{3,2,1,0:T(4,128)S(1)}, u32[]{:S(2)}, u32[]{:S(2)}) collective-permute-start(f32[1,128,4,128]{3,2,1,0:T(4,128)} %param.4), channel_id=1, source_target_pairs={{2,5},{3,4},{4,3},{5,2},{10,13},{11,12},{12,11},{13,10},{18,21},{1... | collective-permute-start | bytes 786440 | tf_op jit(solution)/shard_map/ppermute | solution.py:333
  3.6 9.7 %collective-permute-start = (f32[1,128,4,128]{3,2,1,0:T(4,128)}, f32[1,128,4,128]{3,2,1,0:T(4,128)S(1)}, u32[]{:S(2)}, u32[]{:S(2)}) collective-permute-start(f32[1,128,4,128]{3,2,1,0:T(4,128)} %param.4), channel_id=1, source_target_pairs={{0,1},{1,0},{2,4},{3,5},{4,2},{5,3},{6,7},{7,6},{8,9},{9,8},{10,12... | collective-permute-start | bytes 786440 | tf_op jit(solution)/shard_map/ppermute | solution.py:333
  7.7 9.8 %collective-permute-start.4 = (f32[1,128,4,128]{3,2,1,0:T(4,128)S(1)}, f32[1,128,4,128]{3,2,1,0:T(4,128)S(1)}, u32[]{:S(2)}, u32[]{:S(2)}) collective-permute-start(f32[1,128,4,128]{3,2,1,0:T(4,128)S(1)} %collective-permute-done.3), channel_id=1, source_target_pairs={{2,3},{3,2},{4,5},{5,4},{10,11},{11,10},{12,13},{13,12},{18,19},{1... | collective-permute-start | bytes 786440 | tf_op jit(solution)/shard_map/ppermute | solution.py:333
  13.3 0.9 %copy-start.2 = (f32[1,128,4,128]{3,2,1,0:T(4,128)S(1)}, f32[1,128,4,128]{3,2,1,0:T(4,128)}, u32[]{:S(2)}) copy-start(f32[1,128,4,128]{3,2,1,0:T(4,128)} %param.4) | copy-start | bytes 786436
  14.3 3.2 %copy-start.4 = (f32[1,128,4,128]{3,2,1,0:T(4,128)S(1)}, f32[1,128,4,128]{3,2,1,0:T(4,128)}, u32[]{:S(2)}) copy-start(f32[1,128,4,128]{3,2,1,0:T(4,128)} %param.5) | copy-start | bytes 786436
  14.3 4.6 %collective-permute-start.2 = (f32[128,128]{1,0:T(8,128)S(1)}, f32[128,128]{1,0:T(8,128)S(1)}, u32[]{:S(2)}, u32[]{:S(2)}) collective-permute-start(f32[128,128]{1,0:T(8,128)S(1)} %shard_map.46), channel_id=1, source_target_pairs={{0,4},{4,0},{1,5},{5,1},{2,6},{6,2},{3,7},{7,3},{8,12},{12,8},{9,1... | collective-permute-start | bytes 196616 | tf_op jit(solution)/shard_map/ppermute | solution.py:318
  15.8 1.3 %copy-start = (f32[2,1152,128]{2,1,0:T(8,128)S(1)}, f32[2,1152,128]{2,1,0:T(8,128)}, u32[]{:S(2)}) copy-start(f32[2,1152,128]{2,1,0:T(8,128)} %f_ref.5) | copy-start | bytes 3538948
  17.1 0.9 %copy-start.3 = (f32[1,128,4,128]{3,2,1,0:T(4,128)S(1)}, f32[1,128,4,128]{3,2,1,0:T(4,128)}, u32[]{:S(2)}) copy-start(f32[1,128,4,128]{3,2,1,0:T(4,128)} %param.4) | copy-start | bytes 786436
  17.6 2.8 %collective-permute-start.5 = (f32[128,128]{1,0:T(8,128)S(1)}, f32[128,128]{1,0:T(8,128)S(1)}, u32[]{:S(2)}, u32[]{:S(2)}) collective-permute-start(f32[128,128]{1,0:T(8,128)S(1)} %shard_map.47), channel_id=1, source_target_pairs={{0,4},{4,0},{1,5},{5,1},{2,6},{6,2},{3,7},{7,3},{8,12},{12,8},{9,1... | collective-permute-start | bytes 196616 | tf_op jit(solution)/shard_map/ppermute | solution.py:318
  21.9 1.6 %collective-permute-start.6 = (f32[576,128]{1,0:T(8,128)S(1)}, f32[576,128]{1,0:T(8,128)S(1)}, u32[]{:S(2)}, u32[]{:S(2)}) collective-permute-start(f32[576,128]{1,0:T(8,128)S(1)} %get-tuple-element.36), channel_id=1, source_target_pairs={{0,4},{4,0},{1,5},{5,1},{2,6},{6,2},{3,7},{7,3},{8,12},{12,8},{9,1... | collective-permute-start | bytes 884744 | tf_op jit(solution)/shard_map/ppermute | solution.py:318
  23.1 41.6 %copy-start.1 = (f32[2,1152,128]{2,1,0:T(8,128)S(1)}, f32[2,1152,128]{2,1,0:T(8,128)}, u32[]{:S(2)}) copy-start(f32[2,1152,128]{2,1,0:T(8,128)} %f_ref.5) | copy-start | bytes 3538948
  23.1 41.6 %copy-start.5 = (f32[2]{0:T(128)S(1)}, f32[2]{0:T(128)}, u32[]{:S(2)}) copy-start(f32[2]{0:T(128)} %rates_ref.3) | copy-start | bytes 28
  49.6 5.8 %collective-permute-start.9 = (f32[72,128]{1,0:T(8,128)S(1)}, f32[72,128]{1,0:T(8,128)S(1)}, u32[]{:S(2)}, u32[]{:S(2)}) collective-permute-start(f32[72,128]{1,0:T(8,128)S(1)} %shard_map.55.refs_0_), channel_id=1, source_target_pairs={{0,24},{8,16},{16,8},{24,0},{1,25},{9,17},{17,9},{25,1},{2,26},{10... | collective-permute-start | bytes 110600 | tf_op jit(solution)/shard_map/ppermute | solution.py:318
  50.2 5.8 %collective-permute-start.8 = (f32[72,128]{1,0:T(8,128)S(1)}, f32[72,128]{1,0:T(8,128)S(1)}, u32[]{:S(2)}, u32[]{:S(2)}) collective-permute-start(f32[72,128]{1,0:T(8,128)S(1)} %shard_map.55.refs_0_), channel_id=1, source_target_pairs={{0,16},{8,24},{16,0},{24,8},{1,17},{9,25},{17,1},{25,9},{2,18},{10... | collective-permute-start | bytes 110600 | tf_op jit(solution)/shard_map/ppermute | solution.py:318
  51.7 4.4 %collective-permute-start.7 = (f32[72,128]{1,0:T(8,128)S(1)}, f32[72,128]{1,0:T(8,128)S(1)}, u32[]{:S(2)}, u32[]{:S(2)}) collective-permute-start(f32[72,128]{1,0:T(8,128)S(1)} %shard_map.55.refs_0_), channel_id=1, source_target_pairs={{0,8},{8,0},{16,24},{24,16},{1,9},{9,1},{17,25},{25,17},{2,10},{10... | collective-permute-start | bytes 110600 | tf_op jit(solution)/shard_map/ppermute | solution.py:318
  56.2 7.2 %collective-permute-start.12 = (f32[288,128]{1,0:T(8,128)S(1)}, f32[288,128]{1,0:T(8,128)S(1)}, u32[]{:S(2)}, u32[]{:S(2)}) collective-permute-start(f32[288,128]{1,0:T(8,128)S(1)} %shard_map.56.refs_0_), channel_id=1, source_target_pairs={{0,3},{1,2},{2,1},{3,0},{4,7},{5,6},{6,5},{7,4},{8,11},{9,10},{10,... | collective-permute-start | bytes 442376 | tf_op jit(solution)/shard_map/ppermute | solution.py:318
  56.8 7.3 %collective-permute-start.11 = (f32[288,128]{1,0:T(8,128)S(1)}, f32[288,128]{1,0:T(8,128)S(1)}, u32[]{:S(2)}, u32[]{:S(2)}) collective-permute-start(f32[288,128]{1,0:T(8,128)S(1)} %shard_map.56.refs_0_), channel_id=1, source_target_pairs={{0,2},{1,3},{2,0},{3,1},{4,6},{5,7},{6,4},{7,5},{8,10},{9,11},{10,... | collective-permute-start | bytes 442376 | tf_op jit(solution)/shard_map/ppermute | solution.py:318
  58.2 6.0 %collective-permute-start.10 = (f32[288,128]{1,0:T(8,128)S(1)}, f32[288,128]{1,0:T(8,128)S(1)}, u32[]{:S(2)}, u32[]{:S(2)}) collective-permute-start(f32[288,128]{1,0:T(8,128)S(1)} %shard_map.56.refs_0_), channel_id=1, source_target_pairs={{0,1},{1,0},{2,3},{3,2},{4,5},{5,4},{6,7},{7,6},{8,9},{9,8},{10,11... | collective-permute-start | bytes 442376 | tf_op jit(solution)/shard_map/ppermute | solution.py:318
  59.7 5.8 %collective-permute-start.13 = (f32[288,128]{1,0:T(8,128)S(1)}, f32[288,128]{1,0:T(8,128)S(1)}, u32[]{:S(2)}, u32[]{:S(2)}) collective-permute-start(f32[288,128]{1,0:T(8,128)S(1)} %shard_map.56.refs_0_), channel_id=1, source_target_pairs={{0,4},{4,0},{1,5},{5,1},{2,6},{6,2},{3,7},{7,3},{8,12},{12,8},{9,1... | collective-permute-start | bytes 442376 | tf_op jit(solution)/shard_map/ppermute | solution.py:318
  63.3 2.3 %collective-permute-start.16 = (f32[288,128]{1,0:T(8,128)S(1)}, f32[288,128]{1,0:T(8,128)S(1)}, u32[]{:S(2)}, u32[]{:S(2)}) collective-permute-start(f32[288,128]{1,0:T(8,128)S(1)} %collective-permute-done.12.refs_3_), channel_id=1, source_target_pairs={{0,4},{4,0},{1,5},{5,1},{2,6},{6,2},{3,7},{7,3},{8,12},{12,8},{9,1... | collective-permute-start | bytes 442376 | tf_op jit(solution)/shard_map/ppermute | solution.py:318
  64.2 1.4 %collective-permute-start.15 = (f32[288,128]{1,0:T(8,128)S(1)}, f32[288,128]{1,0:T(8,128)S(1)}, u32[]{:S(2)}, u32[]{:S(2)}) collective-permute-start(f32[288,128]{1,0:T(8,128)S(1)} %collective-permute-done.11.refs_2_), channel_id=1, source_target_pairs={{0,4},{4,0},{1,5},{5,1},{2,6},{6,2},{3,7},{7,3},{8,12},{12,8},{9,1... | collective-permute-start | bytes 442376 | tf_op jit(solution)/shard_map/ppermute | solution.py:318
  64.2 1.6 %collective-permute-start.14 = (f32[288,128]{1,0:T(8,128)S(1)}, f32[288,128]{1,0:T(8,128)S(1)}, u32[]{:S(2)}, u32[]{:S(2)}) collective-permute-start(f32[288,128]{1,0:T(8,128)S(1)} %collective-permute-done.10.refs_1_), channel_id=1, source_target_pairs={{0,4},{4,0},{1,5},{5,1},{2,6},{6,2},{3,7},{7,3},{8,12},{12,8},{9,1... | collective-permute-start | bytes 442376 | tf_op jit(solution)/shard_map/ppermute | solution.py:318

commit v6 on v5

--- a/solution.py
+++ b/solution.py
@@ -32,11 +32,12 @@
     return high, (value - high.astype(F32)).astype(BF16)
 
 
+def product(a, b, dims=((1,), (0,))):
+    return lax.dot_general(a, b, (dims, ((), ())), preferred_element_type=F32)
+
+
 def dot3(ah, al, bh, bl, dims):
-    def one(a, b):
-        return lax.dot_general(a, b, (dims, ((), ())), preferred_element_type=F32)
-
-    return one(ah, bh) + (one(ah, bl) + one(al, bh))
+    return product(ah, bh, dims) + (product(ah, bl, dims) + product(al, bh, dims))
 
 
 def moved(value, step):
@@ -55,7 +56,9 @@
     low_ref[part] = low
 
 
-def filter_kernel(f_ref, fh, fl, gh, gl, taps_ref):
+def filter_kernel(f_ref, x_ref, c_ref, fh, fl, gh, gl, x_out, c_out, taps_ref):
+    x_out[...] = x_ref[...]
+    c_out[...] = c_ref[...]
     lo = lax.axis_index("lo")
     chans = f_ref.shape[2]
     mine = fh.shape[0] // 3
@@ -66,8 +69,12 @@
             at = pl.ds(t, chans, stride=9)
             taps_ref[0, t] = f_ref[0, at, :].T
             taps_ref[1, t] = f_ref[1, at, :]
-            put(fh, fl, b, a, taps_ref[0, t, rows, :])
-            put(gh, gl, b, a, taps_ref[1, t, rows, :])
+            to = slice(b * mine, (b + 1) * mine)
+            for layer, wh, wl in ((0, fh, fl), (1, gh, gl)):
+                high, low = halves(taps_ref[layer, t, rows, :])
+                wh[to, a * chans : (a + 1) * chans] = high
+                wh[to, (3 + a) * chans : (4 + a) * chans] = high
+                wl[to, a * chans : (a + 1) * chans] = low
 
 
 def sources(own, near, far):
@@ -93,7 +100,19 @@
                 out[...] = ref[pl.ds(row, chans, stride=rows), :]
 
 
-def rows_kernel(flip, own_ref, near_ref, far_ref, fh, fl, vh, vl, out, raw):
+def side_kernel(near_ref, far_ref, out):
+    core, lo = lax.axis_index("core"), lax.axis_index("lo")
+    chans = out.shape[0]
+    rows = near_ref.shape[0] // chans
+    for ref, block in ((near_ref, lo), (far_ref, 1 - lo)):
+        for c, row in ((0, rows - 1), (1, 0)):
+
+            @pl.when((core == c) & (block == 1 - c))
+            def _():
+                out[...] = ref[pl.ds(row, chans, stride=rows), :]
+
+
+def rows_kernel(flip, own_ref, near_ref, far_ref, fh, fl, v_ref, out, raw):
     total, chans, cols = raw.shape
     rows = own_ref.shape[0] // chans
     for wanted, ref, block in sources(own_ref, near_ref, far_ref):
@@ -103,34 +122,56 @@
             for row in range(rows):
                 raw[block * rows + row] = ref[pl.ds(row, chans, stride=rows), :]
 
-    for a in range(3):
-        step = 1 - a if flip else a - 1
-        for row in range(total):
-            value = raw[row + step] if 0 <= row + step < total else jnp.zeros((chans, cols), F32)
-            put(vh, vl, a, row, value)
-    out[...] = dot3(fh[...], fl[...], vh[...], vl[...], ((1,), (0,)))
+    for row in range(-1, total + 1):
+        inside = 0 <= row < total
+        high, low = halves(raw[row] if inside else jnp.zeros((chans, cols), F32))
+        for a in range(3):
+            to = row + a - 1 if flip else row - a + 1
+            if 0 <= to < total:
+                wide = slice(to * cols, (to + 1) * cols)
+                v_ref[a * chans : (a + 1) * chans, wide] = high
+                v_ref[(3 + a) * chans : (4 + a) * chans, wide] = low
+    out[...] = product(fh[...], v_ref[...]) + product(fl[...], v_ref[: 3 * chans, :])
 
 
 def rims(edge, first, final, last):
     core = lax.axis_index("core")
-    before = halves(jnp.where(core == 1, edge[...], 0.0))
-    after = halves(jnp.where(core == 0, edge[...], 0.0))
+    before = halves(jnp.where(core == 1, edge, 0.0))
+    after = halves(jnp.where(core == 0, edge, 0.0))
     return {first: (0, before), final: (last, after)}
 
 
-def layer_grad(out, scale, dh, dl, vh, vl, rim_of):
-    mine = dh.shape[0] // 3
+def layer_grad(out, scale, taps, dh, dl, v_ref, rim_of):
     chans, cols = rim_of[0][1][0].shape
-    grad = dot3(dh[...], dl[...], vh[...], vl[...], ((1,), (1,)))
-    for a in range(3):
-        part = grad[:, a * chans : (a + 1) * chans]
+    low = v_ref.shape[0] // 2
+    nt = ((1,), (1,))
+    first, size = taps[0] * chans, len(taps) * chans
+    high_rows = v_ref[first : first + size, :]
+    low_rows = v_ref[low + first : low + first + size, :]
+    grad = dot3(high_rows, low_rows, dh[...], dl[...], nt)
+    for at, a in enumerate(taps):
+        part = grad[at * chans : (at + 1) * chans, :]
         if a in rim_of:
             row, rim = rim_of[a]
             wide = slice(row * cols, (row + 1) * cols)
-            part = part + dot3(dh[:, wide], dl[:, wide], *rim, ((1,), (1,)))
-        for b in range(3):
-            t = 3 * a + b
-            out[t * mine : (t + 1) * mine, :] = scale * part[b * mine : (b + 1) * mine, :]
+            part = part + dot3(*rim, dh[:, wide], dl[:, wide], nt)
+        thin = part.shape[1]
+        out[at * thin : (at + 1) * thin, :] = scale * part.T
+
+
+def either(wanted, scale, taps, out, x_edge, c_edge, xv, cv, hh, hl, dh, dl, last):
+    @pl.when(wanted == 0)
+    def _():
+        layer_grad(out, scale, taps, dh, dl, xv, rims(x_edge[...], 0, 2, last))
+
+    @pl.when(wanted == 1)
+    def _():
+        layer_grad(out, scale, taps, hh, hl, cv, rims(c_edge, 2, 0, last))
+
+
+def one_of(early_ref, late_ref):
+    kept = lax.axis_index("core") == lax.axis_index("half")
+    return jnp.where(kept, late_ref[...], early_ref[...])
 
 
 def row_sums(scale, wh, wl, ref, rim_of, total, flip):
@@ -162,7 +203,7 @@
 def hidden_kernel(total, scale, edge, fh, fl, pre_ref, hh, hl, slope_ref):
     cols = edge.shape[1]
     for row, pre in enumerate(
-        row_sums(scale, fh, fl, pre_ref, rims(edge, 0, 2, total - 1), total, False)
+        row_sums(scale, fh, fl, pre_ref, rims(edge[...], 0, 2, total - 1), total, False)
     ):
         sig = jax.nn.sigmoid(pre)
         hidden = pre * sig
@@ -171,21 +212,10 @@
             put(hh, hl, b, row, value)
 
 
-def either(wanted, scale, out, x_edge, c_edge, xh, xl, ch, cl, hh, hl, dh, dl, last):
-
-    @pl.when(wanted == 0)
-    def _():
-        layer_grad(out, scale, dh, dl, xh, xl, rims(x_edge, 0, 2, last))
-
-    @pl.when(wanted == 1)
-    def _():
-        layer_grad(out, scale, hh, hl, ch, cl, rims(c_edge, 2, 0, last))
-
-
-def give_kernel(total, scale, *refs):
-    x_edge, c_edge, xh, xl, ch, cl, hh, hl, slope_ref, gh, gl, back_ref = refs[:12]
-    give_ref, dh, dl = refs[12:]
+def first_kernel(total, scale, taps, *refs):
+    x_edge, early, late, xv, cv, hh, hl, slope_ref, gh, gl, back_ref, give_ref, dh, dl = refs
     cols = x_edge.shape[1]
+    c_edge = one_of(early, late)
     for row, dhidden in enumerate(
         row_sums(scale, gh, gl, back_ref, rims(c_edge, 2, 0, total - 1), total, True)
     ):
@@ -193,13 +223,15 @@
         for b, value in enumerate((moved(dpre, 1), dpre, moved(dpre, -1))):
             put(dh, dl, b, row, value)
     wanted = 1 - lax.axis_index("core")
-    either(wanted, scale, give_ref, x_edge, c_edge, xh, xl, ch, cl, hh, hl, dh, dl, total - 1)
-
-
-def keep_kernel(total, scale, *refs):
-    x_edge, c_edge, xh, xl, ch, cl, hh, hl, dh, dl, keep_ref = refs
-    wanted = lax.axis_index("core")
-    either(wanted, scale, keep_ref, x_edge, c_edge, xh, xl, ch, cl, hh, hl, dh, dl, total - 1)
+    either(wanted, scale, taps, give_ref, x_edge, c_edge, xv, cv, hh, hl, dh, dl, total - 1)
+
+
+def grad_kernel(total, scale, taps, give, *refs):
+    x_edge, early, late, xv, cv, hh, hl, dh, dl, out = refs
+    core = lax.axis_index("core")
+    wanted = 1 - core if give else core
+    c_edge = one_of(early, late)
+    either(wanted, scale, taps, out, x_edge, c_edge, xv, cv, hh, hl, dh, dl, total - 1)
 
 
 def gram_kernel(v_ref, out):
@@ -329,6 +361,12 @@
     return near, far, onward
 
 
+def rim_routes():
+    every = [(core, half, lo) for core in range(2) for half in range(2) for lo in range(2)]
+    pairs = [(c == h, ((c * 2 + h) * 2 + l, ((1 - c) * 2 + h) * 2 + l)) for c, h, l in every]
+    return [[pair for kept, pair in pairs if kept == want] for want in (True, False)]
+
+
 def sent(value, route):
     return lax.ppermute(value, ("core", "half", "lo"), route)
 
@@ -349,34 +387,44 @@
     x_near = sent(images, near)
     x_far = sent(images, far)
     c_far = sent(c_near, onward)
-    xs = [v.reshape(flat) for v in (images, x_near, x_far)]
-    cs = [v.reshape(flat) for v in (cotangent, c_near, c_far)]
-    fh, fl, gh, gl = call(
-        filter_kernel, [bf(thin, tall)] * 4, [pltpu.VMEM((2, 9, chans, chans), F32)]
-    )(filters)
+    fh, fl, gh, gl, x_own, c_own = call(
+        filter_kernel,
+        [bf(thin, 2 * tall), bf(thin, tall)] * 2 + [flat, flat],
+        [pltpu.VMEM((2, 9, chans, chans), F32)],
+    )(filters, images.reshape(flat), cotangent.reshape(flat))
+    xs = [x_own] + [v.reshape(flat) for v in (x_near, x_far)]
+    cs = [c_own] + [v.reshape(flat) for v in (c_near, c_far)]
     (edge,) = call(edge_kernel, [(chans, cols)])(*xs)
     x_edge = swapped(edge, "core", 1)
     raw = [pltpu.VMEM((total, chans, cols), F32)]
     work = 6 * thin * tall * wide
-    outs = [bf(tall, wide)] * 2 + [(thin, wide)]
-    xh, xl, pre = call(functools.partial(rows_kernel, False), outs, raw, flops=work)(*xs, fh, fl)
+    outs = [bf(2 * tall, wide), (thin, wide)]
+    xv, pre = call(functools.partial(rows_kernel, False), outs, raw, flops=work)(*xs, fh, fl)
     scale = kdim ** (-0.5)
     hh, hl, slope = call(
         functools.partial(hidden_kernel, total, scale), [bf(thin, wide)] * 2 + [(mine, wide)]
     )(x_edge, fh, fl, pre)
-    (edge,) = call(edge_kernel, [(chans, cols)])(*cs)
-    c_edge = swapped(edge, "core", 1)
-    ch, cl, back = call(functools.partial(rows_kernel, True), outs, raw, flops=work)(*cs, gh, gl)
-    rows_of = (x_edge, c_edge, xh, xl, ch, cl, hh, hl)
+    (edge,) = call(side_kernel, [(chans, cols)])(*cs[:2])
+    early = sent(edge, rim_routes()[0])
+    (edge,) = call(side_kernel, [(chans, cols)])(*cs[1:])
+    late = sent(edge, rim_routes()[1])
+    cv, back = call(functools.partial(rows_kernel, True), outs, raw, flops=work)(*cs, gh, gl)
+    known = (x_edge, early, late, xv, cv, hh, hl)
     part = (9 * mine, chans)
     give, dh, dl = call(
-        functools.partial(give_kernel, total, scale), [part] + [bf(thin, wide)] * 2, flops=2 * work
-    )(*rows_of, slope, gh, gl, back)
-    given = swapped(give, "core", 1)
+        functools.partial(first_kernel, total, scale, (0, 1)),
+        [(2 * thin, chans)] + [bf(thin, wide)] * 2,
+        flops=work,
+    )(*known, slope, gh, gl, back)
+    given = [swapped(give, "core", 1)]
+    (give,) = call(
+        functools.partial(grad_kernel, total, scale, (2,), True), [(thin, chans)], flops=work // 3
+    )(*known, dh, dl)
+    given.append(swapped(give, "core", 1))
     (keep,) = call(
-        functools.partial(keep_kernel, total, scale), [part], flops=work
-    )(*rows_of, dh, dl)
-    whole = keep + given
+        functools.partial(grad_kernel, total, scale, (0, 1, 2), False), [part], flops=work
+    )(*known, dh, dl)
+    whole = keep + jnp.concatenate(given)
     slices = lax.all_to_all(
         whole.reshape(n_image, slot, chans), ("pair", "half"), 0, 0, tiled=True
     )

time: 67.7 us -> 70 us (1.034)
  starting transfers between devices: 14.7 us -> 19.1 us
  waiting for transfers between devices: 16 us -> 12.4 us
    ppermute x4 -> x6, waiting for transfers between devices: 8.93 us -> 3.87 us  [sent(): return lax.ppermute(value, ('core', 'half', 'lo'), route)]
    ppermute x4 -> x6, starting transfers between devices: 4.37 us -> 7.56 us  [sent(): return lax.ppermute(value, ('core', 'half', 'lo'), route)]
    ppermute x13, waiting for transfers between devices: 7.08 us -> 8.54 us  [swapped(): return lax.ppermute(value, axis, xor_route(lax.axis_size(axis), k))]
    ppermute x13, starting transfers between devices: 10.3 us -> 11.6 us  [swapped(): return lax.ppermute(value, axis, xor_route(lax.axis_size(axis), k))]
    all_to_all x1, blocking collectives: 15.9 us -> 16.9 us  [fast(): lax.all_to_all(whole.reshape(n_image, slot, chans), ('pair', 'half'), 0,...]
    unnamed x12 -> x10, local copies, waits for them, and re-layouts: 2.59 us -> 3.18 us
    pallas_call x4 -> x6, Pallas kernels: 2.98 us -> 3.46 us  [the longest x1 1.2 us: fast(): call(functools.partial(first_kernel, total, scale, (0, 1)), [(2 * thin, c...]
  transfers between devices with their start and end apart: 17 -> 19, of which waited for: 9 -> 8; matrix products, arithmetic and copies ran while one was open for 0% -> 0% of each run, Pallas kernels for 7% -> 8%
where the time goes in v6:
time: 70 us; the launch traced here: 69.7 us
  blocking collectives  25.8 us (37%)
  starting transfers between devices  19.1 us (27%)
  waiting for transfers between devices  12.4 us (18%)
  Pallas kernels  8.83 us (13%)
  local copies, waits for them, and re-layouts  3.19 us (5%)
    all_to_all x1, blocking collectives, fast(): lax.all_to_all(whole.reshape(n_image, slot, chans), ('pair', 'half'), 0,...  16.9 us
    ppermute x13, starting transfers between devices, swapped(): return lax.ppermute(value, axis, xor_route(lax.axis_size(axis), k))  11.6 us
    all_to_all x1, blocking collectives, fast(): sums = lax.all_to_all(sums, AXES, 0, 0, tiled=True)  8.96 us
    ppermute x13, waiting for transfers between devices, swapped(): return lax.ppermute(value, axis, xor_route(lax.axis_size(axis), k))  8.54 us
    ppermute x6, starting transfers between devices, sent(): return lax.ppermute(value, ('core', 'half', 'lo'), route)  7.56 us
    ppermute x6, waiting for transfers between devices, sent(): return lax.ppermute(value, ('core', 'half', 'lo'), route)  3.87 us
    unnamed x10, local copies, waits for them, and re-layouts  3.18 us
    pallas_call x1, Pallas kernels, fast(): pl.pallas_call(functools.partial(final_kernel, n_pair, n_lo), out_shape=j...  1.6 us
  transfers between devices with their start and end apart: 19, of which 8 were waited for; matrix products, arithmetic and copies ran while one was open for 0% of the time, Pallas kernels for 8%

profile of v6, /device:TPU:0, one launch (start us, length us, event | category | flops | bytes accessed | tf_op | source)
XLA Modules:
  0.0 69.7 jit_solution(11864234506267483501)
XLA Ops:
  0.0 3.0 %collective-permute-start.3 = (f32[1,128,4,128]{3,2,1,0:T(4,128)}, f32[1,128,4,128]{3,2,1,0:T(4,128)S(1)}, u32[]{:S(2)}, u32[]{:S(2)}) collective-permute-start(f32[1,128,4,128]{3,2,1,0:T(4,128)} %param.5), channel_id=1, source_target_pairs={{0,1},{1,0},{2,4},{3,5},{4,2},{5,3},{6,7},{7,6},{8,9},{9,8},{10,12... | collective-permute-start | bytes 786440 | tf_op jit(solution)/shard_map/ppermute | solution.py:371
  3.0 0.0 collective-permute-start
  3.0 0.7 collective-permute-start.1
  3.7 3.9 %collective-permute-done.3 = f32[1,128,4,128]{3,2,1,0:T(4,128)S(1)} collective-permute-done((f32[1,128,4,128]{3,2,1,0:T(4,128)}, f32[1,128,4,128]{3,2,1,0:T(4,128)S(1)}, u32[]{:S(2)}, u32[]{:S(2)}) %collective-permute-start.3) | collective-permute-done | bytes 262176 | tf_op jit(solution)/shard_map/ppermute | solution.py:371
  7.5 0.7 collective-permute-start.5
  8.2 0.0 copy-start
  8.2 1.3 %copy-done = f32[2,1152,128]{2,1,0:T(8,128)S(1)} copy-done((f32[2,1152,128]{2,1,0:T(8,128)S(1)}, f32[2,1152,128]{2,1,0:T(8,128)}, u32[]{:S(2)}) %copy-start) | copy-done | bytes 1179672
  9.5 0.9 %copy-done.2 = f32[1,128,4,128]{3,2,1,0:T(4,128)S(1)} copy-done((f32[1,128,4,128]{3,2,1,0:T(4,128)S(1)}, f32[1,128,4,128]{3,2,1,0:T(4,128)}, u32[]{:S(2)}) %copy-start.2) | copy-done | bytes 262168
  10.4 0.9 %copy-done.3 = f32[1,128,4,128]{3,2,1,0:T(4,128)S(1)} copy-done((f32[1,128,4,128]{3,2,1,0:T(4,128)S(1)}, f32[1,128,4,128]{3,2,1,0:T(4,128)}, u32[]{:S(2)}) %copy-start.3) | copy-done | bytes 262168
  11.4 0.4 shard_map.46
  11.8 0.0 collective-permute-done
  11.8 0.1 shard_map.47
  11.9 2.7 %collective-permute-start.2 = (f32[128,128]{1,0:T(8,128)S(1)}, f32[128,128]{1,0:T(8,128)S(1)}, u32[]{:S(2)}, u32[]{:S(2)}) collective-permute-start(f32[128,128]{1,0:T(8,128)S(1)} %shard_map.47), channel_id=1, source_target_pairs={{0,4},{4,0},{1,5},{5,1},{2,6},{6,2},{3,7},{7,3},{8,12},{12,8},{9,1... | collective-permute-start | bytes 196616 | tf_op jit(solution)/shard_map/ppermute | solution.py:350
  14.6 1.9 %collective-permute-start.4 = (f32[128,128]{1,0:T(8,128)S(1)}, f32[128,128]{1,0:T(8,128)S(1)}, u32[]{:S(2)}, u32[]{:S(2)}) collective-permute-start(f32[128,128]{1,0:T(8,128)S(1)} %shard_map.48), channel_id=1, source_target_pairs={{0,4},{1,5},{6,2},{7,3},{8,12},{9,13},{14,10},{15,11},{16,20},{17,... | collective-permute-start | bytes 196616 | tf_op jit(solution)/shard_map/ppermute | solution.py:371
  16.5 0.0 collective-permute-done.5
  16.6 1.3 %collective-permute-start.6 = (f32[128,128]{1,0:T(8,128)S(1)}, f32[128,128]{1,0:T(8,128)S(1)}, u32[]{:S(2)}, u32[]{:S(2)}) collective-permute-start(f32[128,128]{1,0:T(8,128)S(1)} %shard_map.49), channel_id=1, source_target_pairs={{2,6},{3,7},{4,0},{5,1},{10,14},{11,15},{12,8},{13,9},{18,22},{19,... | collective-permute-start | bytes 196616 | tf_op jit(solution)/shard_map/ppermute | solution.py:371
  17.9 0.8 %shard_map.50 = (bf16[768,1024]{1,0:T(8,128)(2,1)S(1)}, f32[192,1024]{1,0:T(8,128)S(1)}) custom-call(f32[512,128]{1,0:T(8,128)S(1)} %get-tuple-element.21.own_ref, f32[512,128]{1,0:T(8,128)S(1)} %bitcast.15, f32[512,128]{1,0:T(8,128)S(1)} %bitcast.17, bf16[192,768]{1,0:T(8,128)(2,1)S(1)} %get-tuple-element.23.fh, bf16[192,384]{1,0:T(8,128)(2,1)S(1)} %get-tuple-element.24.fl), custom_call_target="tpu_custom_call" | custom-call | flops 452984832 | bytes 905969 | tf_op jit(solution)/shard_map/pallas_call | solution.py:402
  18.7 0.5 shard_map.52
  19.2 0.8 %shard_map.51 = (bf16[768,1024]{1,0:T(8,128)(2,1)S(1)}, f32[192,1024]{1,0:T(8,128)S(1)}) custom-call(f32[512,128]{1,0:T(8,128)S(1)} %get-tuple-element.22.near_ref.own_ref, f32[512,128]{1,0:T(8,128)S(1)} %bitcast.11, f32[512,128]{1,0:T(8,128)S(1)} %bitcast.13, bf16[192,768]{1,0:T(8,128)(2,1)S(1)} %get-tuple-element.26.fh.refs_8_, ...), custom_call_target="tpu_custom_call" | custom-call | flops 452984832 | bytes 905969 | tf_op jit(solution)/shard_map/pallas_call | solution.py:411
  20.0 0.0 collective-permute-done.6.refs_2_
  20.1 1.2 %shard_map.53 = (f32[384,128]{1,0:T(8,128)S(1)}, bf16[192,1024]{1,0:T(8,128)(2,1)S(1)}, bf16[192,1024]{1,0:T(8,128)(2,1)S(1)}) custom-call(f32[128,128]{1,0:T(8,128)S(1)} %collective-permute-done.2.edge.refs_0_, f32[128,128]{1,0:T(8,128)S(1)} %collective-permute-done.4.refs_1_, f32[128,128]{1,0:T(8,128)S(1)} %collective-permute-done.6.refs_2_, ...), custom_call_target="tpu_custom_call" | custom-call | flops 452984832 | bytes 905969 | tf_op jit(solution)/shard_map/pallas_call | solution.py:414
  21.3 1.2 %collective-permute-start.7 = (f32[384,128]{1,0:T(8,128)S(1)}, f32[384,128]{1,0:T(8,128)S(1)}, u32[]{:S(2)}, u32[]{:S(2)}) collective-permute-start(f32[384,128]{1,0:T(8,128)S(1)} %get-tuple-element.36), channel_id=1, source_target_pairs={{0,4},{4,0},{1,5},{5,1},{2,6},{6,2},{3,7},{7,3},{8,12},{12,8},{9,1... | collective-permute-start | bytes 589832 | tf_op jit(solution)/shard_map/ppermute | solution.py:350
  22.5 0.7 %shard_map.55 = f32[192,128]{1,0:T(8,128)S(1)} custom-call(f32[128,128]{1,0:T(8,128)S(1)} %collective-permute-done.2.edge.refs_0_, f32[128,128]{1,0:T(8,128)S(1)} %collective-permute-done.4.refs_1_, f32[128,128]{1,0:T(8,128)S(1)} %collective-permute-done.6.refs_2_, bf16[768,1024]{1,0:T(8,128)(2,1)S(1)} %get-tuple-element.25.refs_3_, ...), custom_call_target="tpu_custom_call" | custom-call | flops 150994944 | bytes 301989 | tf_op jit(solution)/shard_map/pallas_call | solution.py:420
  23.2 0.1 collective-permute-start.8
  23.3 1.1 %shard_map.54 = f32[576,128]{1,0:T(8,128)S(1)} custom-call(f32[128,128]{1,0:T(8,128)S(1)} %collective-permute-done.2.edge.refs_0_, f32[128,128]{1,0:T(8,128)S(1)} %collective-permute-done.4.refs_1_, f32[128,128]{1,0:T(8,128)S(1)} %collective-permute-done.6.refs_2_, bf16[768,1024]{1,0:T(8,128)(2,1)S(1)} %get-tuple-element.25.refs_3_, ...), custom_call_target="tpu_custom_call" | custom-call | flops 452984832 | bytes 905969 | tf_op jit(solution)/shard_map/pallas_call | solution.py:424
  24.3 0.0 copy-start.1
  24.4 0.0 copy-start.4
  24.4 0.2 collective-permute-done.8
  24.6 16.9 %all_to_all.13.v_ref = f32[8,72,128]{2,1,0:T(8,128)S(1)} all-to-all(f32[8,72,128]{2,1,0:T(8,128)S(1)} %bitcast.22), channel_id=1, replica_groups=mesh['pair'=4,'core'=2,'half'=2,'lo'=2] {'pair','half'}, dimensions={0} | all-to-all | bytes 589824 | tf_op jit(solution)/shard_map/all_to_all | solution.py:428
  41.5 0.2 shard_map.56
  41.7 9.0 %all_to_all.14 = f32[32,1,128]{2,1,0:T(1,128)S(1)} all-to-all(f32[32,1,128]{2,1,0:T(1,128)S(1)} %broadcast_in_dim.2), channel_id=1, replica_groups=mesh['pair'=4,'core'=2,'half'=2,'lo'=2] {'pair','core','half','lo'}, dimensions={0} | all-to-all | bytes 32768 | tf_op jit(solution)/shard_map/all_to_all | solution.py:433
  50.7 0.5 shard_map.57.refs_0_
  51.2 0.7 collective-permute-start.10
  51.9 2.3 %collective-permute-start.11 = (f32[72,128]{1,0:T(8,128)S(1)}, f32[72,128]{1,0:T(8,128)S(1)}, u32[]{:S(2)}, u32[]{:S(2)}) collective-permute-start(f32[72,128]{1,0:T(8,128)S(1)} %shard_map.57.refs_0_), channel_id=1, source_target_pairs={{0,24},{8,16},{16,8},{24,0},{1,25},{9,17},{17,9},{25,1},{2,26},{10... | collective-permute-start | bytes 110600 | tf_op jit(solution)/shard_map/ppermute | solution.py:350
  54.2 0.6 collective-permute-start.9
  54.8 2.2 %collective-permute-done.10.refs_2_ = f32[72,128]{1,0:T(8,128)S(1)} collective-permute-done((f32[72,128]{1,0:T(8,128)S(1)}, f32[72,128]{1,0:T(8,128)S(1)}, u32[]{:S(2)}, u32[]{:S(2)}) %collective-permute-start.10) | collective-permute-done | bytes 36896 | tf_op jit(solution)/shard_map/ppermute | solution.py:350
  56.9 0.8 %collective-permute-done.11.refs_3_ = f32[72,128]{1,0:T(8,128)S(1)} collective-permute-done((f32[72,128]{1,0:T(8,128)S(1)}, f32[72,128]{1,0:T(8,128)S(1)}, u32[]{:S(2)}, u32[]{:S(2)}) %collective-permute-start.11) | collective-permute-done | bytes 36896 | tf_op jit(solution)/shard_map/ppermute | solution.py:350
  57.7 0.5 collective-permute-done.9.refs_1_
  58.2 0.6 collective-permute-start.12
  58.8 0.6 collective-permute-start.13
  59.4 2.3 %collective-permute-start.14 = (f32[288,128]{1,0:T(8,128)S(1)}, f32[288,128]{1,0:T(8,128)S(1)}, u32[]{:S(2)}, u32[]{:S(2)}) collective-permute-start(f32[288,128]{1,0:T(8,128)S(1)} %shard_map.58.refs_0_), channel_id=1, source_target_pairs={{0,3},{1,2},{2,1},{3,0},{4,7},{5,6},{6,5},{7,4},{8,11},{9,10},{10,... | collective-permute-start | bytes 442376 | tf_op jit(solution)/shard_map/ppermute | solution.py:350
  61.7 0.0 collective-permute-start.15
  61.7 2.8 %collective-permute-done.12.refs_1_ = f32[288,128]{1,0:T(8,128)S(1)} collective-permute-done((f32[288,128]{1,0:T(8,128)S(1)}, f32[288,128]{1,0:T(8,128)S(1)}, u32[]{:S(2)}, u32[]{:S(2)}) %collective-permute-start.12) | collective-permute-done | bytes 147488 | tf_op jit(solution)/shard_map/ppermute | solution.py:350
  64.6 1.9 %collective-permute-done.13.refs_2_ = f32[288,128]{1,0:T(8,128)S(1)} collective-permute-done((f32[288,128]{1,0:T(8,128)S(1)}, f32[288,128]{1,0:T(8,128)S(1)}, u32[]{:S(2)}, u32[]{:S(2)}) %collective-permute-start.13) | collective-permute-done | bytes 147488 | tf_op jit(solution)/shard_map/ppermute | solution.py:350
  66.5 0.5 collective-permute-start.18
  67.0 0.8 %shard_map.59.mine_ref = f32[1152,128]{1,0:T(8,128)S(1)} custom-call(f32[2]{0:T(128)S(1)} %copy-done.4, f32[2,1152,128]{2,1,0:T(8,128)S(1)} %copy-done.1, f32[288,128]{1,0:T(8,128)S(1)} %shard_map.58.refs_0_, f32[288,128]{1,0:T(8,128)S(1)} %collective-permute-done.12.refs_1_, f32[288,128]{1,0:T(8,128)S(1)} %collective-permute-done.13.refs_2_, ...), custom_call_target="tpu_custom_call" | custom-call | tf_op jit(solution)/shard_map/pallas_call | solution.py:443
  67.9 0.2 collective-permute-done.18.refs_3_
  68.1 1.6 %shard_map.60 = f32[1,2,1152,128]{3,2,1,0:T(8,128)} custom-call(f32[2]{0:T(128)S(1)} %copy-done.4, f32[2,1152,128]{2,1,0:T(8,128)S(1)} %copy-done.1, f32[1152,128]{1,0:T(8,128)S(1)} %shard_map.59.mine_ref, f32[288,128]{1,0:T(8,128)S(1)} %collective-permute-done.15.refs_0_, f32[288,128]{1,0:T(8,128)S(1)} %collective-permute-done.16.refs_1_, ...), custom_call_target="tpu_custom_call" | custom-call | tf_op jit(solution)/shard_map/pallas_call | solution.py:451
  (19 shorter events, 0.2 us)
Async XLA Ops:
  0.0 7.5 %collective-permute-start.3 = (f32[1,128,4,128]{3,2,1,0:T(4,128)}, f32[1,128,4,128]{3,2,1,0:T(4,128)S(1)}, u32[]{:S(2)}, u32[]{:S(2)}) collective-permute-start(f32[1,128,4,128]{3,2,1,0:T(4,128)} %param.5), channel_id=1, source_target_pairs={{0,1},{1,0},{2,4},{3,5},{4,2},{5,3},{6,7},{7,6},{8,9},{9,8},{10,12... | collective-permute-start | bytes 786440 | tf_op jit(solution)/shard_map/ppermute | solution.py:371
  3.0 8.9 %collective-permute-start = (f32[1,128,4,128]{3,2,1,0:T(4,128)}, f32[1,128,4,128]{3,2,1,0:T(4,128)S(1)}, u32[]{:S(2)}, u32[]{:S(2)}) collective-permute-start(f32[1,128,4,128]{3,2,1,0:T(4,128)} %param.4), channel_id=1, source_target_pairs={{0,1},{1,0},{2,4},{3,5},{4,2},{5,3},{6,7},{7,6},{8,9},{9,8},{10,12... | collective-permute-start | bytes 786440 | tf_op jit(solution)/shard_map/ppermute | solution.py:371
  3.0 8.8 %collective-permute-start.1 = (f32[1,128,4,128]{3,2,1,0:T(4,128)}, f32[1,128,4,128]{3,2,1,0:T(4,128)S(1)}, u32[]{:S(2)}, u32[]{:S(2)}) collective-permute-start(f32[1,128,4,128]{3,2,1,0:T(4,128)} %param.4), channel_id=1, source_target_pairs={{2,5},{3,4},{4,3},{5,2},{10,13},{11,12},{12,11},{13,10},{18,21},{1... | collective-permute-start | bytes 786440 | tf_op jit(solution)/shard_map/ppermute | solution.py:371
  7.5 9.0 %collective-permute-start.5 = (f32[1,128,4,128]{3,2,1,0:T(4,128)S(1)}, f32[1,128,4,128]{3,2,1,0:T(4,128)S(1)}, u32[]{:S(2)}, u32[]{:S(2)}) collective-permute-start(f32[1,128,4,128]{3,2,1,0:T(4,128)S(1)} %collective-permute-done.3), channel_id=1, source_target_pairs={{2,3},{3,2},{4,5},{5,4},{10,11},{11,10},{12,13},{13,12},{18,19},{1... | collective-permute-start | bytes 786440 | tf_op jit(solution)/shard_map/ppermute | solution.py:371
  8.2 1.3 %copy-start = (f32[2,1152,128]{2,1,0:T(8,128)S(1)}, f32[2,1152,128]{2,1,0:T(8,128)}, u32[]{:S(2)}) copy-start(f32[2,1152,128]{2,1,0:T(8,128)} %f_ref.5) | copy-start | bytes 3538948
  9.5 0.9 %copy-start.2 = (f32[1,128,4,128]{3,2,1,0:T(4,128)S(1)}, f32[1,128,4,128]{3,2,1,0:T(4,128)}, u32[]{:S(2)}) copy-start(f32[1,128,4,128]{3,2,1,0:T(4,128)} %param.5) | copy-start | bytes 786436
  10.4 0.9 %copy-start.3 = (f32[1,128,4,128]{3,2,1,0:T(4,128)S(1)}, f32[1,128,4,128]{3,2,1,0:T(4,128)}, u32[]{:S(2)}) copy-start(f32[1,128,4,128]{3,2,1,0:T(4,128)} %param.4) | copy-start | bytes 786436
  11.9 6.8 %collective-permute-start.2 = (f32[128,128]{1,0:T(8,128)S(1)}, f32[128,128]{1,0:T(8,128)S(1)}, u32[]{:S(2)}, u32[]{:S(2)}) collective-permute-start(f32[128,128]{1,0:T(8,128)S(1)} %shard_map.47), channel_id=1, source_target_pairs={{0,4},{4,0},{1,5},{5,1},{2,6},{6,2},{3,7},{7,3},{8,12},{12,8},{9,1... | collective-permute-start | bytes 196616 | tf_op jit(solution)/shard_map/ppermute | solution.py:350
  14.6 5.5 %collective-permute-start.4 = (f32[128,128]{1,0:T(8,128)S(1)}, f32[128,128]{1,0:T(8,128)S(1)}, u32[]{:S(2)}, u32[]{:S(2)}) collective-permute-start(f32[128,128]{1,0:T(8,128)S(1)} %shard_map.48), channel_id=1, source_target_pairs={{0,4},{1,5},{6,2},{7,3},{8,12},{9,13},{14,10},{15,11},{16,20},{17,... | collective-permute-start | bytes 196616 | tf_op jit(solution)/shard_map/ppermute | solution.py:371
  16.6 3.4 %collective-permute-start.6 = (f32[128,128]{1,0:T(8,128)S(1)}, f32[128,128]{1,0:T(8,128)S(1)}, u32[]{:S(2)}, u32[]{:S(2)}) collective-permute-start(f32[128,128]{1,0:T(8,128)S(1)} %shard_map.49), channel_id=1, source_target_pairs={{2,6},{3,7},{4,0},{5,1},{10,14},{11,15},{12,8},{13,9},{18,22},{19,... | collective-permute-start | bytes 196616 | tf_op jit(solution)/shard_map/ppermute | solution.py:371
  21.3 3.3 %collective-permute-start.7 = (f32[384,128]{1,0:T(8,128)S(1)}, f32[384,128]{1,0:T(8,128)S(1)}, u32[]{:S(2)}, u32[]{:S(2)}) collective-permute-start(f32[384,128]{1,0:T(8,128)S(1)} %get-tuple-element.36), channel_id=1, source_target_pairs={{0,4},{4,0},{1,5},{5,1},{2,6},{6,2},{3,7},{7,3},{8,12},{12,8},{9,1... | collective-permute-start | bytes 589832 | tf_op jit(solution)/shard_map/ppermute | solution.py:350
  23.2 1.4 %collective-permute-start.8 = (f32[192,128]{1,0:T(8,128)S(1)}, f32[192,128]{1,0:T(8,128)S(1)}, u32[]{:S(2)}, u32[]{:S(2)}) collective-permute-start(f32[192,128]{1,0:T(8,128)S(1)} %shard_map.55), channel_id=1, source_target_pairs={{0,4},{4,0},{1,5},{5,1},{2,6},{6,2},{3,7},{7,3},{8,12},{12,8},{9,1... | collective-permute-start | bytes 294920 | tf_op jit(solution)/shard_map/ppermute | solution.py:350
  24.3 42.7 %copy-start.1 = (f32[2,1152,128]{2,1,0:T(8,128)S(1)}, f32[2,1152,128]{2,1,0:T(8,128)}, u32[]{:S(2)}) copy-start(f32[2,1152,128]{2,1,0:T(8,128)} %f_ref.5) | copy-start | bytes 3538948
  24.4 42.7 %copy-start.4 = (f32[2]{0:T(128)S(1)}, f32[2]{0:T(128)}, u32[]{:S(2)}) copy-start(f32[2]{0:T(128)} %rates_ref.3) | copy-start | bytes 28
  51.2 5.7 %collective-permute-start.10 = (f32[72,128]{1,0:T(8,128)S(1)}, f32[72,128]{1,0:T(8,128)S(1)}, u32[]{:S(2)}, u32[]{:S(2)}) collective-permute-start(f32[72,128]{1,0:T(8,128)S(1)} %shard_map.57.refs_0_), channel_id=1, source_target_pairs={{0,16},{8,24},{16,0},{24,8},{1,17},{9,25},{17,1},{25,9},{2,18},{10... | collective-permute-start | bytes 110600 | tf_op jit(solution)/shard_map/ppermute | solution.py:350
  51.9 5.8 %collective-permute-start.11 = (f32[72,128]{1,0:T(8,128)S(1)}, f32[72,128]{1,0:T(8,128)S(1)}, u32[]{:S(2)}, u32[]{:S(2)}) collective-permute-start(f32[72,128]{1,0:T(8,128)S(1)} %shard_map.57.refs_0_), channel_id=1, source_target_pairs={{0,24},{8,16},{16,8},{24,0},{1,25},{9,17},{17,9},{25,1},{2,26},{10... | collective-permute-start | bytes 110600 | tf_op jit(solution)/shard_map/ppermute | solution.py:350
  54.2 4.0 %collective-permute-start.9 = (f32[72,128]{1,0:T(8,128)S(1)}, f32[72,128]{1,0:T(8,128)S(1)}, u32[]{:S(2)}, u32[]{:S(2)}) collective-permute-start(f32[72,128]{1,0:T(8,128)S(1)} %shard_map.57.refs_0_), channel_id=1, source_target_pairs={{0,8},{8,0},{16,24},{24,16},{1,9},{9,1},{17,25},{25,17},{2,10},{10... | collective-permute-start | bytes 110600 | tf_op jit(solution)/shard_map/ppermute | solution.py:350
  58.2 6.4 %collective-permute-start.12 = (f32[288,128]{1,0:T(8,128)S(1)}, f32[288,128]{1,0:T(8,128)S(1)}, u32[]{:S(2)}, u32[]{:S(2)}) collective-permute-start(f32[288,128]{1,0:T(8,128)S(1)} %shard_map.58.refs_0_), channel_id=1, source_target_pairs={{0,1},{1,0},{2,3},{3,2},{4,5},{5,4},{6,7},{7,6},{8,9},{9,8},{10,11... | collective-permute-start | bytes 442376 | tf_op jit(solution)/shard_map/ppermute | solution.py:350
  58.8 7.7 %collective-permute-start.13 = (f32[288,128]{1,0:T(8,128)S(1)}, f32[288,128]{1,0:T(8,128)S(1)}, u32[]{:S(2)}, u32[]{:S(2)}) collective-permute-start(f32[288,128]{1,0:T(8,128)S(1)} %shard_map.58.refs_0_), channel_id=1, source_target_pairs={{0,2},{1,3},{2,0},{3,1},{4,6},{5,7},{6,4},{7,5},{8,10},{9,11},{10,... | collective-permute-start | bytes 442376 | tf_op jit(solution)/shard_map/ppermute | solution.py:350
  59.4 7.1 %collective-permute-start.14 = (f32[288,128]{1,0:T(8,128)S(1)}, f32[288,128]{1,0:T(8,128)S(1)}, u32[]{:S(2)}, u32[]{:S(2)}) collective-permute-start(f32[288,128]{1,0:T(8,128)S(1)} %shard_map.58.refs_0_), channel_id=1, source_target_pairs={{0,3},{1,2},{2,1},{3,0},{4,7},{5,6},{6,5},{7,4},{8,11},{9,10},{10,... | collective-permute-start | bytes 442376 | tf_op jit(solution)/shard_map/ppermute | solution.py:350
  61.7 6.1 %collective-permute-start.15 = (f32[288,128]{1,0:T(8,128)S(1)}, f32[288,128]{1,0:T(8,128)S(1)}, u32[]{:S(2)}, u32[]{:S(2)}) collective-permute-start(f32[288,128]{1,0:T(8,128)S(1)} %shard_map.58.refs_0_), channel_id=1, source_target_pairs={{0,4},{4,0},{1,5},{5,1},{2,6},{6,2},{3,7},{7,3},{8,12},{12,8},{9,1... | collective-permute-start | bytes 442376 | tf_op jit(solution)/shard_map/ppermute | solution.py:350
  64.6 3.3 %collective-permute-start.16 = (f32[288,128]{1,0:T(8,128)S(1)}, f32[288,128]{1,0:T(8,128)S(1)}, u32[]{:S(2)}, u32[]{:S(2)}) collective-permute-start(f32[288,128]{1,0:T(8,128)S(1)} %collective-permute-done.12.refs_1_), channel_id=1, source_target_pairs={{0,4},{4,0},{1,5},{5,1},{2,6},{6,2},{3,7},{7,3},{8,12},{12,8},{9,1... | collective-permute-start | bytes 442376 | tf_op jit(solution)/shard_map/ppermute | solution.py:350
  66.5 1.4 %collective-permute-start.17 = (f32[288,128]{1,0:T(8,128)S(1)}, f32[288,128]{1,0:T(8,128)S(1)}, u32[]{:S(2)}, u32[]{:S(2)}) collective-permute-start(f32[288,128]{1,0:T(8,128)S(1)} %collective-permute-done.13.refs_2_), channel_id=1, source_target_pairs={{0,4},{4,0},{1,5},{5,1},{2,6},{6,2},{3,7},{7,3},{8,12},{12,8},{9,1... | collective-permute-start | bytes 442376 | tf_op jit(solution)/shard_map/ppermute | solution.py:350
  66.5 1.6 %collective-permute-start.18 = (f32[288,128]{1,0:T(8,128)S(1)}, f32[288,128]{1,0:T(8,128)S(1)}, u32[]{:S(2)}, u32[]{:S(2)}) collective-permute-start(f32[288,128]{1,0:T(8,128)S(1)} %collective-permute-done.14.refs_3_), channel_id=1, source_target_pairs={{0,4},{4,0},{1,5},{5,1},{2,6},{6,2},{3,7},{7,3},{8,12},{12,8},{9,1... | collective-permute-start | bytes 442376 | tf_op jit(solution)/shard_map/ppermute | solution.py:350

commit v7 on v5

--- a/solution.py
+++ b/solution.py
@@ -32,11 +32,12 @@
     return high, (value - high.astype(F32)).astype(BF16)
 
 
+def product(a, b, dims=((1,), (0,))):
+    return lax.dot_general(a, b, (dims, ((), ())), preferred_element_type=F32)
+
+
 def dot3(ah, al, bh, bl, dims):
-    def one(a, b):
-        return lax.dot_general(a, b, (dims, ((), ())), preferred_element_type=F32)
-
-    return one(ah, bh) + (one(ah, bl) + one(al, bh))
+    return product(ah, bh, dims) + (product(ah, bl, dims) + product(al, bh, dims))
 
 
 def moved(value, step):
@@ -66,8 +67,12 @@
             at = pl.ds(t, chans, stride=9)
             taps_ref[0, t] = f_ref[0, at, :].T
             taps_ref[1, t] = f_ref[1, at, :]
-            put(fh, fl, b, a, taps_ref[0, t, rows, :])
-            put(gh, gl, b, a, taps_ref[1, t, rows, :])
+            to = slice(b * mine, (b + 1) * mine)
+            for layer, wh, wl in ((0, fh, fl), (1, gh, gl)):
+                high, low = halves(taps_ref[layer, t, rows, :])
+                wh[to, a * chans : (a + 1) * chans] = high
+                wh[to, (3 + a) * chans : (4 + a) * chans] = high
+                wl[to, a * chans : (a + 1) * chans] = low
 
 
 def sources(own, near, far):
@@ -93,7 +98,7 @@
                 out[...] = ref[pl.ds(row, chans, stride=rows), :]
 
 
-def rows_kernel(flip, own_ref, near_ref, far_ref, fh, fl, vh, vl, out, raw):
+def rows_kernel(flip, own_ref, near_ref, far_ref, fh, fl, v_ref, out, raw):
     total, chans, cols = raw.shape
     rows = own_ref.shape[0] // chans
     for wanted, ref, block in sources(own_ref, near_ref, far_ref):
@@ -103,57 +108,62 @@
             for row in range(rows):
                 raw[block * rows + row] = ref[pl.ds(row, chans, stride=rows), :]
 
-    for a in range(3):
-        step = 1 - a if flip else a - 1
-        for row in range(total):
-            value = raw[row + step] if 0 <= row + step < total else jnp.zeros((chans, cols), F32)
-            put(vh, vl, a, row, value)
-    out[...] = dot3(fh[...], fl[...], vh[...], vl[...], ((1,), (0,)))
-
-
-def rims(edge, first, final, last):
+    for row in range(-1, total + 1):
+        inside = 0 <= row < total
+        high, low = halves(raw[row] if inside else jnp.zeros((chans, cols), F32))
+        for a in range(3):
+            to = row + a - 1 if flip else row - a + 1
+            if 0 <= to < total:
+                wide = slice(to * cols, (to + 1) * cols)
+                v_ref[a * chans : (a + 1) * chans, wide] = high
+                v_ref[(3 + a) * chans : (4 + a) * chans, wide] = low
+    out[...] = product(fh[...], v_ref[...]) + product(fl[...], v_ref[: 3 * chans, :])
+
+
+def rim(edge, total, flip):
     core = lax.axis_index("core")
-    before = halves(jnp.where(core == 1, edge[...], 0.0))
-    after = halves(jnp.where(core == 0, edge[...], 0.0))
-    return {first: (0, before), final: (last, after)}
-
-
-def layer_grad(out, scale, dh, dl, vh, vl, rim_of):
+    row = (total - 1) * (1 - core)
+    tap = 2 * core if flip else 2 * (1 - core)
+    return row, tap, halves(edge[...])
+
+
+def span(at, size):
+    return pl.ds(pl.multiple_of(at * size, 128), size)
+
+
+def layer_grad(out, scale, dh, dl, v_ref, edge, total, flip):
     mine = dh.shape[0] // 3
-    chans, cols = rim_of[0][1][0].shape
-    grad = dot3(dh[...], dl[...], vh[...], vl[...], ((1,), (1,)))
+    chans, cols = edge.shape
+    low = v_ref.shape[0] // 2
+    nt = ((1,), (1,))
+    row, tap, (eh, el) = rim(edge, total, flip)
+    wide = span(row, cols)
+    grad = dot3(dh[...], dl[...], v_ref[:low, :], v_ref[low:, :], nt)
+    extra = dot3(dh[:, wide], dl[:, wide], eh, el, nt)
     for a in range(3):
         part = grad[:, a * chans : (a + 1) * chans]
-        if a in rim_of:
-            row, rim = rim_of[a]
-            wide = slice(row * cols, (row + 1) * cols)
-            part = part + dot3(dh[:, wide], dl[:, wide], *rim, ((1,), (1,)))
+        if a != 1:
+            part = part + jnp.where(tap == a, extra, 0.0)
         for b in range(3):
             t = 3 * a + b
             out[t * mine : (t + 1) * mine, :] = scale * part[b * mine : (b + 1) * mine, :]
 
 
-def row_sums(scale, wh, wl, ref, rim_of, total, flip):
+def row_sums(scale, wh, wl, ref, edge, total, flip):
     mine = wh.shape[0] // 3
-    chans, cols = rim_of[0][1][0].shape
-    rim_row = {
-        row: dot3(
-            wh[:, a * chans : (a + 1) * chans],
-            wl[:, a * chans : (a + 1) * chans],
-            *rim,
-            ((1,), (0,)),
-        )
-        for a, (row, rim) in rim_of.items()
-    }
+    chans, cols = edge.shape
+    row, tap, (eh, el) = rim(edge, total, flip)
+    deep = span(tap, chans)
+    extra = dot3(wh[:, deep], wl[:, deep], eh, el, ((1,), (0,)))
     side = 1 if flip else -1
     found = []
-    for row in range(total):
-        wide = slice(row * cols, (row + 1) * cols)
+    for at in range(total):
+        wide = slice(at * cols, (at + 1) * cols)
         parts = []
         for b in range(3):
             value = ref[b * mine : (b + 1) * mine, wide]
-            if row in rim_row:
-                value = value + rim_row[row][b * mine : (b + 1) * mine, :]
+            if at in (0, total - 1):
+                value = value + jnp.where(row == at, extra[b * mine : (b + 1) * mine, :], 0.0)
             parts.append(value)
         found.append(scale * (parts[1] + moved(parts[0], side) + moved(parts[2], -side)))
     return found
@@ -161,9 +171,7 @@
 
 def hidden_kernel(total, scale, edge, fh, fl, pre_ref, hh, hl, slope_ref):
     cols = edge.shape[1]
-    for row, pre in enumerate(
-        row_sums(scale, fh, fl, pre_ref, rims(edge, 0, 2, total - 1), total, False)
-    ):
+    for row, pre in enumerate(row_sums(scale, fh, fl, pre_ref, edge, total, False)):
         sig = jax.nn.sigmoid(pre)
         hidden = pre * sig
         slope_ref[:, row * cols : (row + 1) * cols] = sig * (1.0 + pre * (1.0 - sig))
@@ -171,35 +179,31 @@
             put(hh, hl, b, row, value)
 
 
-def either(wanted, scale, out, x_edge, c_edge, xh, xl, ch, cl, hh, hl, dh, dl, last):
+def either(wanted, scale, out, x_edge, c_edge, xv, cv, hh, hl, dh, dl, total):
 
     @pl.when(wanted == 0)
     def _():
-        layer_grad(out, scale, dh, dl, xh, xl, rims(x_edge, 0, 2, last))
+        layer_grad(out, scale, dh, dl, xv, x_edge, total, False)
 
     @pl.when(wanted == 1)
     def _():
-        layer_grad(out, scale, hh, hl, ch, cl, rims(c_edge, 2, 0, last))
+        layer_grad(out, scale, hh, hl, cv, c_edge, total, True)
 
 
 def give_kernel(total, scale, *refs):
-    x_edge, c_edge, xh, xl, ch, cl, hh, hl, slope_ref, gh, gl, back_ref = refs[:12]
-    give_ref, dh, dl = refs[12:]
+    x_edge, c_edge, xv, cv, hh, hl, slope_ref, gh, gl, back_ref, give_ref, dh, dl = refs
     cols = x_edge.shape[1]
-    for row, dhidden in enumerate(
-        row_sums(scale, gh, gl, back_ref, rims(c_edge, 2, 0, total - 1), total, True)
-    ):
+    for row, dhidden in enumerate(row_sums(scale, gh, gl, back_ref, c_edge, total, True)):
         dpre = dhidden * slope_ref[:, row * cols : (row + 1) * cols]
         for b, value in enumerate((moved(dpre, 1), dpre, moved(dpre, -1))):
             put(dh, dl, b, row, value)
     wanted = 1 - lax.axis_index("core")
-    either(wanted, scale, give_ref, x_edge, c_edge, xh, xl, ch, cl, hh, hl, dh, dl, total - 1)
-
-
-def keep_kernel(total, scale, *refs):
-    x_edge, c_edge, xh, xl, ch, cl, hh, hl, dh, dl, keep_ref = refs
+    either(wanted, scale, give_ref, x_edge, c_edge, xv, cv, hh, hl, dh, dl, total)
+
+
+def keep_kernel(total, scale, x_edge, c_edge, xv, cv, hh, hl, dh, dl, keep_ref):
     wanted = lax.axis_index("core")
-    either(wanted, scale, keep_ref, x_edge, c_edge, xh, xl, ch, cl, hh, hl, dh, dl, total - 1)
+    either(wanted, scale, keep_ref, x_edge, c_edge, xv, cv, hh, hl, dh, dl, total)
 
 
 def gram_kernel(v_ref, out):
@@ -352,22 +356,24 @@
     xs = [v.reshape(flat) for v in (images, x_near, x_far)]
     cs = [v.reshape(flat) for v in (cotangent, c_near, c_far)]
     fh, fl, gh, gl = call(
-        filter_kernel, [bf(thin, tall)] * 4, [pltpu.VMEM((2, 9, chans, chans), F32)]
+        filter_kernel,
+        [bf(thin, 2 * tall), bf(thin, tall)] * 2,
+        [pltpu.VMEM((2, 9, chans, chans), F32)],
     )(filters)
     (edge,) = call(edge_kernel, [(chans, cols)])(*xs)
     x_edge = swapped(edge, "core", 1)
     raw = [pltpu.VMEM((total, chans, cols), F32)]
     work = 6 * thin * tall * wide
-    outs = [bf(tall, wide)] * 2 + [(thin, wide)]
-    xh, xl, pre = call(functools.partial(rows_kernel, False), outs, raw, flops=work)(*xs, fh, fl)
+    outs = [bf(2 * tall, wide), (thin, wide)]
+    xv, pre = call(functools.partial(rows_kernel, False), outs, raw, flops=work)(*xs, fh, fl)
     scale = kdim ** (-0.5)
     hh, hl, slope = call(
         functools.partial(hidden_kernel, total, scale), [bf(thin, wide)] * 2 + [(mine, wide)]
     )(x_edge, fh, fl, pre)
     (edge,) = call(edge_kernel, [(chans, cols)])(*cs)
     c_edge = swapped(edge, "core", 1)
-    ch, cl, back = call(functools.partial(rows_kernel, True), outs, raw, flops=work)(*cs, gh, gl)
-    rows_of = (x_edge, c_edge, xh, xl, ch, cl, hh, hl)
+    cv, back = call(functools.partial(rows_kernel, True), outs, raw, flops=work)(*cs, gh, gl)
+    rows_of = (x_edge, c_edge, xv, cv, hh, hl)
     part = (9 * mine, chans)
     give, dh, dl = call(
         functools.partial(give_kernel, total, scale), [part] + [bf(thin, wide)] * 2, flops=2 * work

time: 67.7 us -> 67.2 us (level)
  no operation moved by 1% of the time
where the time goes in v7:
time: 67.2 us; the launch traced here: 67 us
  blocking collectives  25.4 us (38%)
  waiting for transfers between devices  15.8 us (24%)
  starting transfers between devices  15 us (22%)
  Pallas kernels  8.18 us (12%)
  local copies, waits for them, and re-layouts  2.25 us (3%)
    all_to_all x1, blocking collectives, fast(): lax.all_to_all(whole.reshape(n_image, slot, chans), ('pair', 'half'), 0,...  16 us
    ppermute x13, starting transfers between devices, swapped(): return lax.ppermute(value, axis, xor_route(lax.axis_size(axis), k))  10.7 us
    all_to_all x1, blocking collectives, fast(): sums = lax.all_to_all(sums, AXES, 0, 0, tiled=True)  9.41 us
    ppermute x4, waiting for transfers between devices, sent(): return lax.ppermute(value, ('core', 'half', 'lo'), route)  8.93 us
    ppermute x13, waiting for transfers between devices, swapped(): return lax.ppermute(value, axis, xor_route(lax.axis_size(axis), k))  6.91 us
    ppermute x4, starting transfers between devices, sent(): return lax.ppermute(value, ('core', 'half', 'lo'), route)  4.37 us
    unnamed x12, local copies, waits for them, and re-layouts  2.24 us
    pallas_call x1, Pallas kernels, fast(): pl.pallas_call(functools.partial(final_kernel, n_pair, n_lo), out_shape=j...  1.6 us
  transfers between devices with their start and end apart: 17, of which 9 were waited for; matrix products, arithmetic and copies ran while one was open for 0% of the time, Pallas kernels for 7%

profile of v7, /device:TPU:0, one launch (start us, length us, event | category | flops | bytes accessed | tf_op | source)
XLA Modules:
  0.0 67.0 jit_solution(9321801249935024579)
XLA Ops:
  0.0 3.0 %collective-permute-start.3 = (f32[1,128,4,128]{3,2,1,0:T(4,128)}, f32[1,128,4,128]{3,2,1,0:T(4,128)S(1)}, u32[]{:S(2)}, u32[]{:S(2)}) collective-permute-start(f32[1,128,4,128]{3,2,1,0:T(4,128)} %param.5), channel_id=1, source_target_pairs={{0,1},{1,0},{2,4},{3,5},{4,2},{5,3},{6,7},{7,6},{8,9},{9,8},{10,12... | collective-permute-start | bytes 786440 | tf_op jit(solution)/shard_map/ppermute | solution.py:337
  3.0 0.7 collective-permute-start.1
  3.6 0.1 collective-permute-start
  3.7 4.0 %collective-permute-done.3 = f32[1,128,4,128]{3,2,1,0:T(4,128)S(1)} collective-permute-done((f32[1,128,4,128]{3,2,1,0:T(4,128)}, f32[1,128,4,128]{3,2,1,0:T(4,128)S(1)}, u32[]{:S(2)}, u32[]{:S(2)}) %collective-permute-start.3) | collective-permute-done | bytes 262176 | tf_op jit(solution)/shard_map/ppermute | solution.py:337
  7.7 0.7 collective-permute-start.4
  8.4 0.0 collective-permute-done.1
  8.4 4.9 %collective-permute-done = f32[1,128,4,128]{3,2,1,0:T(4,128)S(1)} collective-permute-done((f32[1,128,4,128]{3,2,1,0:T(4,128)}, f32[1,128,4,128]{3,2,1,0:T(4,128)S(1)}, u32[]{:S(2)}, u32[]{:S(2)}) %collective-permute-start) | collective-permute-done | bytes 262176 | tf_op jit(solution)/shard_map/ppermute | solution.py:337
  13.3 0.9 %copy-done.2 = f32[1,128,4,128]{3,2,1,0:T(4,128)S(1)} copy-done((f32[1,128,4,128]{3,2,1,0:T(4,128)S(1)}, f32[1,128,4,128]{3,2,1,0:T(4,128)}, u32[]{:S(2)}) %copy-start.2) | copy-done | bytes 262168
  14.3 1.5 %collective-permute-start.2 = (f32[128,128]{1,0:T(8,128)S(1)}, f32[128,128]{1,0:T(8,128)S(1)}, u32[]{:S(2)}, u32[]{:S(2)}) collective-permute-start(f32[128,128]{1,0:T(8,128)S(1)} %shard_map.46), channel_id=1, source_target_pairs={{0,4},{4,0},{1,5},{5,1},{2,6},{6,2},{3,7},{7,3},{8,12},{12,8},{9,1... | collective-permute-start | bytes 196616 | tf_op jit(solution)/shard_map/ppermute | solution.py:322
  15.8 1.3 %copy-done = f32[2,1152,128]{2,1,0:T(8,128)S(1)} copy-done((f32[2,1152,128]{2,1,0:T(8,128)S(1)}, f32[2,1152,128]{2,1,0:T(8,128)}, u32[]{:S(2)}) %copy-start) | copy-done | bytes 1179672
  17.1 0.4 shard_map.48
  17.5 0.0 collective-permute-done.4
  17.5 0.1 shard_map.47
  17.6 0.1 collective-permute-start.5
  17.7 0.8 %shard_map.49 = (bf16[768,1024]{1,0:T(8,128)(2,1)S(1)}, f32[192,1024]{1,0:T(8,128)S(1)}) custom-call(f32[512,128]{1,0:T(8,128)S(1)} %bitcast.10, f32[512,128]{1,0:T(8,128)S(1)} %bitcast.20, f32[512,128]{1,0:T(8,128)S(1)} %bitcast.18, bf16[192,768]{1,0:T(8,128)(2,1)S(1)} %get-tuple-element.19.fh, bf16[192,384]{1,0:T(8,128)(2,1)S(1)} %get-tuple-element.20.fl), custom_call_target="tpu_custom_call" | custom-call | flops 452984832 | bytes 905969 | tf_op jit(solution)/shard_map/pallas_call | solution.py:368
  18.6 0.0 collective-permute-done.2.edge.refs_0_.x_edge
  18.6 0.4 shard_map.51
  19.0 0.8 %shard_map.50 = (bf16[768,1024]{1,0:T(8,128)(2,1)S(1)}, f32[192,1024]{1,0:T(8,128)S(1)}) custom-call(f32[512,128]{1,0:T(8,128)S(1)} %bitcast.12, f32[512,128]{1,0:T(8,128)S(1)} %bitcast.14, f32[512,128]{1,0:T(8,128)S(1)} %bitcast.16, bf16[192,768]{1,0:T(8,128)(2,1)S(1)} %get-tuple-element.22.fh.refs_7_, bf16[192,384]{1,0:T(8,128)(2,1)S(1)} %get-tuple-element.23.fl.refs_8_), custom_call_target="tpu_custom_call" | custom-call | flops 452984832 | bytes 905969 | tf_op jit(solution)/shard_map/pallas_call | solution.py:375
  19.9 0.0 collective-permute-done.5.refs_1_.c_edge
  19.9 1.4 %shard_map.52 = (f32[576,128]{1,0:T(8,128)S(1)}, bf16[192,1024]{1,0:T(8,128)(2,1)S(1)}, bf16[192,1024]{1,0:T(8,128)(2,1)S(1)}) custom-call(f32[128,128]{1,0:T(8,128)S(1)} %collective-permute-done.2.edge.refs_0_.x_edge, f32[128,128]{1,0:T(8,128)S(1)} %collective-permute-done.5.refs_1_.c_edge, bf16[768,1024]{1,0:T(8,128)(2,1)S(1)} %get-tuple-element.21.refs_2_.xv, ...), custom_call_target="tpu_custom_call" | custom-call | flops 905969664 | bytes 1811939 | tf_op jit(solution)/shard_map/pallas_call | solution.py:378
  21.3 0.5 collective-permute-start.6
  21.8 1.0 %shard_map.53 = f32[576,128]{1,0:T(8,128)S(1)} custom-call(f32[128,128]{1,0:T(8,128)S(1)} %collective-permute-done.2.edge.refs_0_.x_edge, f32[128,128]{1,0:T(8,128)S(1)} %collective-permute-done.5.refs_1_.c_edge, bf16[768,1024]{1,0:T(8,128)(2,1)S(1)} %get-tuple-element.21.refs_2_.xv, bf16[768,1024]{1,0:T(8,128)(2,1)S(1)} %get-tuple-element.24.refs_3_.cv, ...), custom_call_target="tpu_custom_call" | custom-call | flops 452984832 | bytes 905969 | tf_op jit(solution)/shard_map/pallas_call | solution.py:382
  22.8 0.0 copy-start.1
  22.8 0.0 copy-start.5
  22.8 0.2 collective-permute-done.6
  23.0 16.0 %all_to_all.13.v_ref = f32[8,72,128]{2,1,0:T(8,128)S(1)} all-to-all(f32[8,72,128]{2,1,0:T(8,128)S(1)} %bitcast.23), channel_id=1, replica_groups=mesh['pair'=4,'core'=2,'half'=2,'lo'=2] {'pair','half'}, dimensions={0} | all-to-all | bytes 589824 | tf_op jit(solution)/shard_map/all_to_all | solution.py:386
  39.0 0.2 shard_map.54
  39.3 9.4 %all_to_all.14 = f32[32,1,128]{2,1,0:T(1,128)S(1)} all-to-all(f32[32,1,128]{2,1,0:T(1,128)S(1)} %broadcast_in_dim.2), channel_id=1, replica_groups=mesh['pair'=4,'core'=2,'half'=2,'lo'=2] {'pair','core','half','lo'}, dimensions={0} | all-to-all | bytes 32768 | tf_op jit(solution)/shard_map/all_to_all | solution.py:391
  48.7 0.5 shard_map.55.refs_0_
  49.2 0.6 collective-permute-start.9
  49.8 1.5 %collective-permute-start.8 = (f32[72,128]{1,0:T(8,128)S(1)}, f32[72,128]{1,0:T(8,128)S(1)}, u32[]{:S(2)}, u32[]{:S(2)}) collective-permute-start(f32[72,128]{1,0:T(8,128)S(1)} %shard_map.55.refs_0_), channel_id=1, source_target_pairs={{0,16},{8,24},{16,0},{24,8},{1,17},{9,25},{17,1},{25,9},{2,18},{10... | collective-permute-start | bytes 110600 | tf_op jit(solution)/shard_map/ppermute | solution.py:322
  51.3 2.4 %collective-permute-start.7 = (f32[72,128]{1,0:T(8,128)S(1)}, f32[72,128]{1,0:T(8,128)S(1)}, u32[]{:S(2)}, u32[]{:S(2)}) collective-permute-start(f32[72,128]{1,0:T(8,128)S(1)} %shard_map.55.refs_0_), channel_id=1, source_target_pairs={{0,8},{8,0},{16,24},{24,16},{1,9},{9,1},{17,25},{25,17},{2,10},{10... | collective-permute-start | bytes 110600 | tf_op jit(solution)/shard_map/ppermute | solution.py:322
  53.7 1.4 %collective-permute-done.9.refs_3_ = f32[72,128]{1,0:T(8,128)S(1)} collective-permute-done((f32[72,128]{1,0:T(8,128)S(1)}, f32[72,128]{1,0:T(8,128)S(1)}, u32[]{:S(2)}, u32[]{:S(2)}) %collective-permute-start.9) | collective-permute-done | bytes 36896 | tf_op jit(solution)/shard_map/ppermute | solution.py:322
  55.1 0.5 collective-permute-done.8.refs_2_
  55.6 0.2 collective-permute-done.7.refs_1_
  55.8 0.7 %collective-permute-start.12 = (f32[288,128]{1,0:T(8,128)S(1)}, f32[288,128]{1,0:T(8,128)S(1)}, u32[]{:S(2)}, u32[]{:S(2)}) collective-permute-start(f32[288,128]{1,0:T(8,128)S(1)} %shard_map.56.refs_0_), channel_id=1, source_target_pairs={{0,3},{1,2},{2,1},{3,0},{4,7},{5,6},{6,5},{7,4},{8,11},{9,10},{10,... | collective-permute-start | bytes 442376 | tf_op jit(solution)/shard_map/ppermute | solution.py:322
  56.4 1.4 %collective-permute-start.11 = (f32[288,128]{1,0:T(8,128)S(1)}, f32[288,128]{1,0:T(8,128)S(1)}, u32[]{:S(2)}, u32[]{:S(2)}) collective-permute-start(f32[288,128]{1,0:T(8,128)S(1)} %shard_map.56.refs_0_), channel_id=1, source_target_pairs={{0,2},{1,3},{2,0},{3,1},{4,6},{5,7},{6,4},{7,5},{8,10},{9,11},{10,... | collective-permute-start | bytes 442376 | tf_op jit(solution)/shard_map/ppermute | solution.py:322
  57.8 1.5 %collective-permute-start.10 = (f32[288,128]{1,0:T(8,128)S(1)}, f32[288,128]{1,0:T(8,128)S(1)}, u32[]{:S(2)}, u32[]{:S(2)}) collective-permute-start(f32[288,128]{1,0:T(8,128)S(1)} %shard_map.56.refs_0_), channel_id=1, source_target_pairs={{0,1},{1,0},{2,3},{3,2},{4,5},{5,4},{6,7},{7,6},{8,9},{9,8},{10,11... | collective-permute-start | bytes 442376 | tf_op jit(solution)/shard_map/ppermute | solution.py:322
  59.3 0.0 collective-permute-start.13
  59.3 3.6 %collective-permute-done.12.refs_3_ = f32[288,128]{1,0:T(8,128)S(1)} collective-permute-done((f32[288,128]{1,0:T(8,128)S(1)}, f32[288,128]{1,0:T(8,128)S(1)}, u32[]{:S(2)}, u32[]{:S(2)}) %collective-permute-start.12) | collective-permute-done | bytes 147488 | tf_op jit(solution)/shard_map/ppermute | solution.py:322
  62.9 0.0 collective-permute-start.16
  62.9 0.9 %collective-permute-done.11.refs_2_ = f32[288,128]{1,0:T(8,128)S(1)} collective-permute-done((f32[288,128]{1,0:T(8,128)S(1)}, f32[288,128]{1,0:T(8,128)S(1)}, u32[]{:S(2)}, u32[]{:S(2)}) %collective-permute-start.11) | collective-permute-done | bytes 147488 | tf_op jit(solution)/shard_map/ppermute | solution.py:322
  63.8 0.0 collective-permute-start.15
  63.8 0.5 collective-permute-start.14
  64.3 0.8 %shard_map.57.mine_ref = f32[1152,128]{1,0:T(8,128)S(1)} custom-call(f32[2]{0:T(128)S(1)} %copy-done.5, f32[2,1152,128]{2,1,0:T(8,128)S(1)} %copy-done.1, f32[288,128]{1,0:T(8,128)S(1)} %shard_map.56.refs_0_, f32[288,128]{1,0:T(8,128)S(1)} %collective-permute-done.10.refs_1_, f32[288,128]{1,0:T(8,128)S(1)} %collective-permute-done.11.refs_2_, ...), custom_call_target="tpu_custom_call" | custom-call | tf_op jit(solution)/shard_map/pallas_call | solution.py:401
  65.2 0.0 collective-permute-done.15.refs_2_
  65.2 0.2 collective-permute-done.14.refs_1_
  65.4 1.6 %shard_map.58 = f32[1,2,1152,128]{3,2,1,0:T(8,128)} custom-call(f32[2]{0:T(128)S(1)} %copy-done.5, f32[2,1152,128]{2,1,0:T(8,128)S(1)} %copy-done.1, f32[1152,128]{1,0:T(8,128)S(1)} %shard_map.57.mine_ref, f32[288,128]{1,0:T(8,128)S(1)} %collective-permute-done.13.refs_0_, f32[288,128]{1,0:T(8,128)S(1)} %collective-permute-done.14.refs_1_, ...), custom_call_target="tpu_custom_call" | custom-call | tf_op jit(solution)/shard_map/pallas_call | solution.py:409
  (15 shorter events, 0.1 us)
Async XLA Ops:
  0.0 7.7 %collective-permute-start.3 = (f32[1,128,4,128]{3,2,1,0:T(4,128)}, f32[1,128,4,128]{3,2,1,0:T(4,128)S(1)}, u32[]{:S(2)}, u32[]{:S(2)}) collective-permute-start(f32[1,128,4,128]{3,2,1,0:T(4,128)} %param.5), channel_id=1, source_target_pairs={{0,1},{1,0},{2,4},{3,5},{4,2},{5,3},{6,7},{7,6},{8,9},{9,8},{10,12... | collective-permute-start | bytes 786440 | tf_op jit(solution)/shard_map/ppermute | solution.py:337
  3.0 5.4 %collective-permute-start.1 = (f32[1,128,4,128]{3,2,1,0:T(4,128)}, f32[1,128,4,128]{3,2,1,0:T(4,128)S(1)}, u32[]{:S(2)}, u32[]{:S(2)}) collective-permute-start(f32[1,128,4,128]{3,2,1,0:T(4,128)} %param.4), channel_id=1, source_target_pairs={{2,5},{3,4},{4,3},{5,2},{10,13},{11,12},{12,11},{13,10},{18,21},{1... | collective-permute-start | bytes 786440 | tf_op jit(solution)/shard_map/ppermute | solution.py:337
  3.6 9.7 %collective-permute-start = (f32[1,128,4,128]{3,2,1,0:T(4,128)}, f32[1,128,4,128]{3,2,1,0:T(4,128)S(1)}, u32[]{:S(2)}, u32[]{:S(2)}) collective-permute-start(f32[1,128,4,128]{3,2,1,0:T(4,128)} %param.4), channel_id=1, source_target_pairs={{0,1},{1,0},{2,4},{3,5},{4,2},{5,3},{6,7},{7,6},{8,9},{9,8},{10,12... | collective-permute-start | bytes 786440 | tf_op jit(solution)/shard_map/ppermute | solution.py:337
  7.7 9.8 %collective-permute-start.4 = (f32[1,128,4,128]{3,2,1,0:T(4,128)S(1)}, f32[1,128,4,128]{3,2,1,0:T(4,128)S(1)}, u32[]{:S(2)}, u32[]{:S(2)}) collective-permute-start(f32[1,128,4,128]{3,2,1,0:T(4,128)S(1)} %collective-permute-done.3), channel_id=1, source_target_pairs={{2,3},{3,2},{4,5},{5,4},{10,11},{11,10},{12,13},{13,12},{18,19},{1... | collective-permute-start | bytes 786440 | tf_op jit(solution)/shard_map/ppermute | solution.py:337
  13.3 0.9 %copy-start.2 = (f32[1,128,4,128]{3,2,1,0:T(4,128)S(1)}, f32[1,128,4,128]{3,2,1,0:T(4,128)}, u32[]{:S(2)}) copy-start(f32[1,128,4,128]{3,2,1,0:T(4,128)} %param.4) | copy-start | bytes 786436
  14.3 3.3 %copy-start.4 = (f32[1,128,4,128]{3,2,1,0:T(4,128)S(1)}, f32[1,128,4,128]{3,2,1,0:T(4,128)}, u32[]{:S(2)}) copy-start(f32[1,128,4,128]{3,2,1,0:T(4,128)} %param.5) | copy-start | bytes 786436
  14.3 3.5 %copy-start.3 = (f32[1,128,4,128]{3,2,1,0:T(4,128)S(1)}, f32[1,128,4,128]{3,2,1,0:T(4,128)}, u32[]{:S(2)}) copy-start(f32[1,128,4,128]{3,2,1,0:T(4,128)} %param.4) | copy-start | bytes 786436
  14.3 4.2 %collective-permute-start.2 = (f32[128,128]{1,0:T(8,128)S(1)}, f32[128,128]{1,0:T(8,128)S(1)}, u32[]{:S(2)}, u32[]{:S(2)}) collective-permute-start(f32[128,128]{1,0:T(8,128)S(1)} %shard_map.46), channel_id=1, source_target_pairs={{0,4},{4,0},{1,5},{5,1},{2,6},{6,2},{3,7},{7,3},{8,12},{12,8},{9,1... | collective-permute-start | bytes 196616 | tf_op jit(solution)/shard_map/ppermute | solution.py:322
  15.8 1.3 %copy-start = (f32[2,1152,128]{2,1,0:T(8,128)S(1)}, f32[2,1152,128]{2,1,0:T(8,128)}, u32[]{:S(2)}) copy-start(f32[2,1152,128]{2,1,0:T(8,128)} %f_ref.5) | copy-start | bytes 3538948
  17.6 2.2 %collective-permute-start.5 = (f32[128,128]{1,0:T(8,128)S(1)}, f32[128,128]{1,0:T(8,128)S(1)}, u32[]{:S(2)}, u32[]{:S(2)}) collective-permute-start(f32[128,128]{1,0:T(8,128)S(1)} %shard_map.47), channel_id=1, source_target_pairs={{0,4},{4,0},{1,5},{5,1},{2,6},{6,2},{3,7},{7,3},{8,12},{12,8},{9,1... | collective-permute-start | bytes 196616 | tf_op jit(solution)/shard_map/ppermute | solution.py:322
  21.3 1.7 %collective-permute-start.6 = (f32[576,128]{1,0:T(8,128)S(1)}, f32[576,128]{1,0:T(8,128)S(1)}, u32[]{:S(2)}, u32[]{:S(2)}) collective-permute-start(f32[576,128]{1,0:T(8,128)S(1)} %get-tuple-element.32), channel_id=1, source_target_pairs={{0,4},{4,0},{1,5},{5,1},{2,6},{6,2},{3,7},{7,3},{8,12},{12,8},{9,1... | collective-permute-start | bytes 884744 | tf_op jit(solution)/shard_map/ppermute | solution.py:322
  22.8 41.5 %copy-start.1 = (f32[2,1152,128]{2,1,0:T(8,128)S(1)}, f32[2,1152,128]{2,1,0:T(8,128)}, u32[]{:S(2)}) copy-start(f32[2,1152,128]{2,1,0:T(8,128)} %f_ref.5) | copy-start | bytes 3538948
  22.8 41.5 %copy-start.5 = (f32[2]{0:T(128)S(1)}, f32[2]{0:T(128)}, u32[]{:S(2)}) copy-start(f32[2]{0:T(128)} %rates_ref.3) | copy-start | bytes 28
  49.2 5.8 %collective-permute-start.9 = (f32[72,128]{1,0:T(8,128)S(1)}, f32[72,128]{1,0:T(8,128)S(1)}, u32[]{:S(2)}, u32[]{:S(2)}) collective-permute-start(f32[72,128]{1,0:T(8,128)S(1)} %shard_map.55.refs_0_), channel_id=1, source_target_pairs={{0,24},{8,16},{16,8},{24,0},{1,25},{9,17},{17,9},{25,1},{2,26},{10... | collective-permute-start | bytes 110600 | tf_op jit(solution)/shard_map/ppermute | solution.py:322
  49.8 5.8 %collective-permute-start.8 = (f32[72,128]{1,0:T(8,128)S(1)}, f32[72,128]{1,0:T(8,128)S(1)}, u32[]{:S(2)}, u32[]{:S(2)}) collective-permute-start(f32[72,128]{1,0:T(8,128)S(1)} %shard_map.55.refs_0_), channel_id=1, source_target_pairs={{0,16},{8,24},{16,0},{24,8},{1,17},{9,25},{17,1},{25,9},{2,18},{10... | collective-permute-start | bytes 110600 | tf_op jit(solution)/shard_map/ppermute | solution.py:322
  51.3 4.4 %collective-permute-start.7 = (f32[72,128]{1,0:T(8,128)S(1)}, f32[72,128]{1,0:T(8,128)S(1)}, u32[]{:S(2)}, u32[]{:S(2)}) collective-permute-start(f32[72,128]{1,0:T(8,128)S(1)} %shard_map.55.refs_0_), channel_id=1, source_target_pairs={{0,8},{8,0},{16,24},{24,16},{1,9},{9,1},{17,25},{25,17},{2,10},{10... | collective-permute-start | bytes 110600 | tf_op jit(solution)/shard_map/ppermute | solution.py:322
  55.8 7.2 %collective-permute-start.12 = (f32[288,128]{1,0:T(8,128)S(1)}, f32[288,128]{1,0:T(8,128)S(1)}, u32[]{:S(2)}, u32[]{:S(2)}) collective-permute-start(f32[288,128]{1,0:T(8,128)S(1)} %shard_map.56.refs_0_), channel_id=1, source_target_pairs={{0,3},{1,2},{2,1},{3,0},{4,7},{5,6},{6,5},{7,4},{8,11},{9,10},{10,... | collective-permute-start | bytes 442376 | tf_op jit(solution)/shard_map/ppermute | solution.py:322
  56.4 7.3 %collective-permute-start.11 = (f32[288,128]{1,0:T(8,128)S(1)}, f32[288,128]{1,0:T(8,128)S(1)}, u32[]{:S(2)}, u32[]{:S(2)}) collective-permute-start(f32[288,128]{1,0:T(8,128)S(1)} %shard_map.56.refs_0_), channel_id=1, source_target_pairs={{0,2},{1,3},{2,0},{3,1},{4,6},{5,7},{6,4},{7,5},{8,10},{9,11},{10,... | collective-permute-start | bytes 442376 | tf_op jit(solution)/shard_map/ppermute | solution.py:322
  57.8 6.0 %collective-permute-start.10 = (f32[288,128]{1,0:T(8,128)S(1)}, f32[288,128]{1,0:T(8,128)S(1)}, u32[]{:S(2)}, u32[]{:S(2)}) collective-permute-start(f32[288,128]{1,0:T(8,128)S(1)} %shard_map.56.refs_0_), channel_id=1, source_target_pairs={{0,1},{1,0},{2,3},{3,2},{4,5},{5,4},{6,7},{7,6},{8,9},{9,8},{10,11... | collective-permute-start | bytes 442376 | tf_op jit(solution)/shard_map/ppermute | solution.py:322
  59.3 5.8 %collective-permute-start.13 = (f32[288,128]{1,0:T(8,128)S(1)}, f32[288,128]{1,0:T(8,128)S(1)}, u32[]{:S(2)}, u32[]{:S(2)}) collective-permute-start(f32[288,128]{1,0:T(8,128)S(1)} %shard_map.56.refs_0_), channel_id=1, source_target_pairs={{0,4},{4,0},{1,5},{5,1},{2,6},{6,2},{3,7},{7,3},{8,12},{12,8},{9,1... | collective-permute-start | bytes 442376 | tf_op jit(solution)/shard_map/ppermute | solution.py:322
  62.9 2.3 %collective-permute-start.16 = (f32[288,128]{1,0:T(8,128)S(1)}, f32[288,128]{1,0:T(8,128)S(1)}, u32[]{:S(2)}, u32[]{:S(2)}) collective-permute-start(f32[288,128]{1,0:T(8,128)S(1)} %collective-permute-done.12.refs_3_), channel_id=1, source_target_pairs={{0,4},{4,0},{1,5},{5,1},{2,6},{6,2},{3,7},{7,3},{8,12},{12,8},{9,1... | collective-permute-start | bytes 442376 | tf_op jit(solution)/shard_map/ppermute | solution.py:322
  63.8 1.4 %collective-permute-start.15 = (f32[288,128]{1,0:T(8,128)S(1)}, f32[288,128]{1,0:T(8,128)S(1)}, u32[]{:S(2)}, u32[]{:S(2)}) collective-permute-start(f32[288,128]{1,0:T(8,128)S(1)} %collective-permute-done.11.refs_2_), channel_id=1, source_target_pairs={{0,4},{4,0},{1,5},{5,1},{2,6},{6,2},{3,7},{7,3},{8,12},{12,8},{9,1... | collective-permute-start | bytes 442376 | tf_op jit(solution)/shard_map/ppermute | solution.py:322
  63.8 1.6 %collective-permute-start.14 = (f32[288,128]{1,0:T(8,128)S(1)}, f32[288,128]{1,0:T(8,128)S(1)}, u32[]{:S(2)}, u32[]{:S(2)}) collective-permute-start(f32[288,128]{1,0:T(8,128)S(1)} %collective-permute-done.10.refs_1_), channel_id=1, source_target_pairs={{0,4},{4,0},{1,5},{5,1},{2,6},{6,2},{3,7},{7,3},{8,12},{12,8},{9,1... | collective-permute-start | bytes 442376 | tf_op jit(solution)/shard_map/ppermute | solution.py:322

commit v8 on v5

--- a/solution.py
+++ b/solution.py
@@ -55,7 +55,7 @@
     low_ref[part] = low
 
 
-def filter_kernel(f_ref, fh, fl, gh, gl, taps_ref):
+def filter_kernel(f_ref, fh, fl, gh, gl, part_ref, taps_ref):
     lo = lax.axis_index("lo")
     chans = f_ref.shape[2]
     mine = fh.shape[0] // 3
@@ -68,6 +68,8 @@
             taps_ref[1, t] = f_ref[1, at, :]
             put(fh, fl, b, a, taps_ref[0, t, rows, :])
             put(gh, gl, b, a, taps_ref[1, t, rows, :])
+            for layer in range(2):
+                part_ref[layer, t * mine : (t + 1) * mine, :] = taps_ref[layer, t, rows, :]
 
 
 def sources(own, near, far):
@@ -213,7 +215,7 @@
     out[...] = total
 
 
-def merge_kernel(n_band, sums_ref, v_ref, out):
+def merge_kernel(n_band, rates_ref, sums_ref, v_ref, f_ref, out):
     core = lax.axis_index("core")
     count = v_ref.shape[0]
     sums = sums_ref[...]
@@ -257,7 +259,10 @@
     total = jnp.zeros(out.shape, F32)
     for i in range(count):
         total = total + weight[i : i + 1, :] * v_ref[i]
-    out[...] = total
+    size = out.shape[0]
+    slot = 2 * lax.axis_index("pair") + lax.axis_index("half")
+    mine = f_ref[core, pl.ds(pl.multiple_of(slot * size, 8), size), :]
+    out[...] = mine - rates_ref[core] * total
 
 
 def gather_kernel(*refs):
@@ -269,10 +274,10 @@
         out[pl.ds(start, size), :] = part[...]
 
 
-def new_layer(n_pair, n_lo, layer, rates_ref, f_ref, pieces, held, fresh):
+def new_layer(n_pair, n_lo, layer, pieces, held, fresh):
     band = lax.axis_index("half") * n_lo + lax.axis_index("lo")
     size = pieces[0].shape[0] // n_pair
-    chans = f_ref.shape[2]
+    chans = fresh.shape[1]
     mine = chans // n_lo
     for k, piece in enumerate(pieces):
         place = lax.bitwise_xor(band, k)
@@ -284,26 +289,25 @@
 
         @pl.when(layer == l)
         def _():
-            rate = rates_ref[l]
             for t in range(9):
                 at = pl.ds(t, chans, stride=9)
                 value = held[:, t * mine : (t + 1) * mine, :].reshape(chans, chans)
                 if l == 0:
                     value = value.T
-                fresh[at, :] = f_ref[l, at, :] - rate * value
-
-
-def own_kernel(n_pair, n_lo, rates_ref, f_ref, *refs):
+                fresh[at, :] = value
+
+
+def own_kernel(n_pair, n_lo, *refs):
     pieces, (fresh, held) = refs[:-2], refs[-2:]
-    new_layer(n_pair, n_lo, lax.axis_index("core"), rates_ref, f_ref, pieces, held, fresh)
-
-
-def final_kernel(n_pair, n_lo, rates_ref, f_ref, mine_ref, *refs):
+    new_layer(n_pair, n_lo, lax.axis_index("core"), pieces, held, fresh)
+
+
+def final_kernel(n_pair, n_lo, mine_ref, *refs):
     pieces, (out, held, fresh, sems) = refs[:-4], refs[-4:]
     core = lax.axis_index("core")
     first = pltpu.make_async_copy(mine_ref, out.at[0, core], sems.at[0])
     first.start()
-    new_layer(n_pair, n_lo, 1 - core, rates_ref, f_ref, pieces, held, fresh)
+    new_layer(n_pair, n_lo, 1 - core, pieces, held, fresh)
     second = pltpu.make_async_copy(fresh, out.at[0, 1 - core], sems.at[1])
     second.start()
     first.wait()
@@ -351,8 +355,10 @@
     c_far = sent(c_near, onward)
     xs = [v.reshape(flat) for v in (images, x_near, x_far)]
     cs = [v.reshape(flat) for v in (cotangent, c_near, c_far)]
-    fh, fl, gh, gl = call(
-        filter_kernel, [bf(thin, tall)] * 4, [pltpu.VMEM((2, 9, chans, chans), F32)]
+    fh, fl, gh, gl, tapped = call(
+        filter_kernel,
+        [bf(thin, tall)] * 4 + [(2, 9 * mine, chans)],
+        [pltpu.VMEM((2, 9, chans, chans), F32)],
     )(filters)
     (edge,) = call(edge_kernel, [(chans, cols)])(*xs)
     x_edge = swapped(edge, "core", 1)
@@ -383,31 +389,37 @@
     (gram,) = call(gram_kernel, [(1, 128)])(slices)
     sums = jnp.broadcast_to(gram, (n_image * n_band, gram.shape[1]))
     sums = lax.all_to_all(sums, AXES, 0, 0, tiled=True)
-    (merged,) = call(functools.partial(merge_kernel, n_band), [(slot, chans)])(sums, slices)
+    vmem, smem = (pl.BlockSpec(memory_space=m) for m in (pltpu.VMEM, pltpu.SMEM))
+    params = pltpu.CompilerParams(vmem_limit_bytes=40 * 2**20)
+    merged = pl.pallas_call(
+        functools.partial(merge_kernel, n_band),
+        out_shape=jax.ShapeDtypeStruct((slot, chans), F32),
+        in_specs=[smem] + [vmem] * 3,
+        out_specs=vmem,
+        compiler_params=params,
+    )(rates, sums, slices, tapped)
     pieces = [merged] + [swapped(merged, "pair", k) for k in range(1, n_pair)]
     (block,) = call(gather_kernel, [(n_pair * slot, chans)])(*pieces)
     own = [block] + [swapped(block, ("half", "lo"), k) for k in range(1, n_band)]
     others = [swapped(piece, "core", 1) for piece in own]
     layer = (kdim, chans)
     held = pltpu.VMEM((n_lo,) + part, F32)
-    vmem, smem = (pl.BlockSpec(memory_space=m) for m in (pltpu.VMEM, pltpu.SMEM))
-    params = pltpu.CompilerParams(vmem_limit_bytes=40 * 2**20)
     fresh = pl.pallas_call(
         functools.partial(own_kernel, n_pair, n_lo),
         out_shape=jax.ShapeDtypeStruct(layer, F32),
-        in_specs=[smem] + [vmem] * (1 + n_band),
+        in_specs=[vmem] * n_band,
         out_specs=vmem,
         scratch_shapes=[held],
         compiler_params=params,
-    )(rates, filters, *own)
+    )(*own)
     return pl.pallas_call(
         functools.partial(final_kernel, n_pair, n_lo),
         out_shape=jax.ShapeDtypeStruct((1,) + filters.shape, F32),
-        in_specs=[smem] + [vmem] * (2 + n_band),
+        in_specs=[vmem] * (1 + n_band),
         out_specs=pl.BlockSpec(memory_space=pl.ANY),
         scratch_shapes=[held, pltpu.VMEM(layer, F32), pltpu.SemaphoreType.DMA((2,))],
         compiler_params=params,
-    )(rates, filters, fresh, *others)
+    )(fresh, *others)
 
 
 def with_rims(field):

time: 67.7 us -> 67.6 us (level)
    unnamed x12 -> x10, local copies, waits for them, and re-layouts: 2.59 us -> 2.56 us
  transfers between devices with their start and end apart: 17 -> 17, of which waited for: 9 -> 10; matrix products, arithmetic and copies ran while one was open for 0% -> 0% of each run, Pallas kernels for 7% -> 6%
where the time goes in v8:
time: 67.6 us; the launch traced here: 67.4 us
  blocking collectives  25.3 us (37%)
  waiting for transfers between devices  16.6 us (25%)
  starting transfers between devices  14.7 us (22%)
  Pallas kernels  7.99 us (12%)
  local copies, waits for them, and re-layouts  2.57 us (4%)
    all_to_all x1, blocking collectives, fast(): lax.all_to_all(whole.reshape(n_image, slot, chans), ('pair', 'half'), 0,...  15.9 us
    ppermute x13, starting transfers between devices, swapped(): return lax.ppermute(value, axis, xor_route(lax.axis_size(axis), k))  10.3 us
    all_to_all x1, blocking collectives, fast(): sums = lax.all_to_all(sums, AXES, 0, 0, tiled=True)  9.41 us
    ppermute x4, waiting for transfers between devices, sent(): return lax.ppermute(value, ('core', 'half', 'lo'), route)  8.93 us
    ppermute x13, waiting for transfers between devices, swapped(): return lax.ppermute(value, axis, xor_route(lax.axis_size(axis), k))  7.65 us
    ppermute x4, starting transfers between devices, sent(): return lax.ppermute(value, ('core', 'half', 'lo'), route)  4.37 us
    unnamed x10, local copies, waits for them, and re-layouts  2.56 us
    pallas_call x1, Pallas kernels, fast(): call(functools.partial(give_kernel, total, scale), [part] + [bf(thin, wid...  1.46 us
  transfers between devices with their start and end apart: 17, of which 10 were waited for; matrix products, arithmetic and copies ran while one was open for 0% of the time, Pallas kernels for 6%

profile of v8, /device:TPU:0, one launch (start us, length us, event | category | flops | bytes accessed | tf_op | source)
XLA Modules:
  0.0 67.4 jit_solution(3798238923236224860)
XLA Ops:
  0.0 3.0 %collective-permute-start.3 = (f32[1,128,4,128]{3,2,1,0:T(4,128)}, f32[1,128,4,128]{3,2,1,0:T(4,128)S(1)}, u32[]{:S(2)}, u32[]{:S(2)}) collective-permute-start(f32[1,128,4,128]{3,2,1,0:T(4,128)} %param.5), channel_id=1, source_target_pairs={{0,1},{1,0},{2,4},{3,5},{4,2},{5,3},{6,7},{7,6},{8,9},{9,8},{10,12... | collective-permute-start | bytes 786440 | tf_op jit(solution)/shard_map/ppermute | solution.py:337
  3.0 0.7 collective-permute-start.1
  3.6 0.1 collective-permute-start
  3.7 4.0 %collective-permute-done.3 = f32[1,128,4,128]{3,2,1,0:T(4,128)S(1)} collective-permute-done((f32[1,128,4,128]{3,2,1,0:T(4,128)}, f32[1,128,4,128]{3,2,1,0:T(4,128)S(1)}, u32[]{:S(2)}, u32[]{:S(2)}) %collective-permute-start.3) | collective-permute-done | bytes 262176 | tf_op jit(solution)/shard_map/ppermute | solution.py:337
  7.7 0.7 collective-permute-start.4
  8.4 0.0 collective-permute-done.1
  8.4 4.9 %collective-permute-done = f32[1,128,4,128]{3,2,1,0:T(4,128)S(1)} collective-permute-done((f32[1,128,4,128]{3,2,1,0:T(4,128)}, f32[1,128,4,128]{3,2,1,0:T(4,128)S(1)}, u32[]{:S(2)}, u32[]{:S(2)}) %collective-permute-start) | collective-permute-done | bytes 262176 | tf_op jit(solution)/shard_map/ppermute | solution.py:337
  13.3 0.9 %copy-done.1 = f32[1,128,4,128]{3,2,1,0:T(4,128)S(1)} copy-done((f32[1,128,4,128]{3,2,1,0:T(4,128)S(1)}, f32[1,128,4,128]{3,2,1,0:T(4,128)}, u32[]{:S(2)}) %copy-start.1) | copy-done | bytes 262168
  14.3 1.5 %collective-permute-start.2 = (f32[128,128]{1,0:T(8,128)S(1)}, f32[128,128]{1,0:T(8,128)S(1)}, u32[]{:S(2)}, u32[]{:S(2)}) collective-permute-start(f32[128,128]{1,0:T(8,128)S(1)} %shard_map.46), channel_id=1, source_target_pairs={{0,4},{4,0},{1,5},{5,1},{2,6},{6,2},{3,7},{7,3},{8,12},{12,8},{9,1... | collective-permute-start | bytes 196616 | tf_op jit(solution)/shard_map/ppermute | solution.py:322
  15.8 1.3 %copy-done = f32[2,1152,128]{2,1,0:T(8,128)S(1)} copy-done((f32[2,1152,128]{2,1,0:T(8,128)S(1)}, f32[2,1152,128]{2,1,0:T(8,128)}, u32[]{:S(2)}) %copy-start) | copy-done | bytes 1179672
  17.1 0.4 shard_map.48
  17.5 0.0 collective-permute-done.4
  17.5 0.1 shard_map.47
  17.6 0.1 collective-permute-start.5
  17.7 0.3 copy-done.2
  18.0 0.9 %shard_map.49 = (bf16[384,1024]{1,0:T(8,128)(2,1)S(1)}, bf16[384,1024]{1,0:T(8,128)(2,1)S(1)}, f32[192,1024]{1,0:T(8,128)S(1)}) custom-call(f32[512,128]{1,0:T(8,128)S(1)} %bitcast.10, f32[512,128]{1,0:T(8,128)S(1)} %bitcast.20, f32[512,128]{1,0:T(8,128)S(1)} %bitcast.18, bf16[192,384]{1,0:T(8,128)(2,1)S(1)} %get-tuple-element.22.fh, ...), custom_call_target="tpu_custom_call" | custom-call | flops 452984832 | bytes 905969 | tf_op jit(solution)/shard_map/pallas_call | solution.py:368
  18.9 0.0 collective-permute-done.2.edge.refs_0_
  19.0 0.5 shard_map.51
  19.4 0.9 %shard_map.50 = (bf16[384,1024]{1,0:T(8,128)(2,1)S(1)}, bf16[384,1024]{1,0:T(8,128)(2,1)S(1)}, f32[192,1024]{1,0:T(8,128)S(1)}) custom-call(f32[512,128]{1,0:T(8,128)S(1)} %bitcast.12, f32[512,128]{1,0:T(8,128)S(1)} %bitcast.14, f32[512,128]{1,0:T(8,128)S(1)} %bitcast.16, bf16[192,384]{1,0:T(8,128)(2,1)S(1)} %get-tuple-element.26.fh.refs_9_, ...), custom_call_target="tpu_custom_call" | custom-call | flops 452984832 | bytes 905969 | tf_op jit(solution)/shard_map/pallas_call | solution.py:375
  20.4 1.5 %shard_map.52 = (f32[576,128]{1,0:T(8,128)S(1)}, bf16[192,1024]{1,0:T(8,128)(2,1)S(1)}, bf16[192,1024]{1,0:T(8,128)(2,1)S(1)}) custom-call(f32[128,128]{1,0:T(8,128)S(1)} %collective-permute-done.2.edge.refs_0_, f32[128,128]{1,0:T(8,128)S(1)} %collective-permute-done.5.refs_1_, bf16[384,1024]{1,0:T(8,128)(2,1)S(1)} %get-tuple-element.24.refs_2_, ...), custom_call_target="tpu_custom_call" | custom-call | flops 905969664 | bytes 1811939 | tf_op jit(solution)/shard_map/pallas_call | solution.py:378
  21.9 0.2 collective-permute-start.6
  22.1 1.0 %shard_map.53 = f32[576,128]{1,0:T(8,128)S(1)} custom-call(f32[128,128]{1,0:T(8,128)S(1)} %collective-permute-done.2.edge.refs_0_, f32[128,128]{1,0:T(8,128)S(1)} %collective-permute-done.5.refs_1_, bf16[384,1024]{1,0:T(8,128)(2,1)S(1)} %get-tuple-element.24.refs_2_, bf16[384,1024]{1,0:T(8,128)(2,1)S(1)} %get-tuple-element.25.refs_3_, ...), custom_call_target="tpu_custom_call" | custom-call | flops 452984832 | bytes 905969 | tf_op jit(solution)/shard_map/pallas_call | solution.py:382
  23.1 0.0 copy-start.4
  23.1 0.4 collective-permute-done.6
  23.5 15.9 %all_to_all.13.v_ref = f32[8,72,128]{2,1,0:T(8,128)S(1)} all-to-all(f32[8,72,128]{2,1,0:T(8,128)S(1)} %bitcast.23), channel_id=1, replica_groups=mesh['pair'=4,'core'=2,'half'=2,'lo'=2] {'pair','half'}, dimensions={0} | all-to-all | bytes 589824 | tf_op jit(solution)/shard_map/all_to_all | solution.py:386
  39.4 0.2 shard_map.54
  39.7 9.4 %all_to_all.14 = f32[32,1,128]{2,1,0:T(1,128)S(1)} all-to-all(f32[32,1,128]{2,1,0:T(1,128)S(1)} %broadcast_in_dim.2), channel_id=1, replica_groups=mesh['pair'=4,'core'=2,'half'=2,'lo'=2] {'pair','core','half','lo'}, dimensions={0} | all-to-all | bytes 32768 | tf_op jit(solution)/shard_map/all_to_all | solution.py:391
  49.1 1.1 %shard_map.55.refs_0_ = f32[72,128]{1,0:T(8,128)S(1)} custom-call(f32[2]{0:T(128)S(1)} %copy-done.4, f32[32,128]{1,0:T(8,128)S(1)} %bitcast.21, f32[8,72,128]{2,1,0:T(8,128)S(1)} %all_to_all.13.v_ref, f32[2,576,128]{2,1,0:T(8,128)S(1)} %get-tuple-element.38.f_ref), custom_call_target="tpu_custom_call" | custom-call | tf_op jit(solution)/shard_map/pallas_call | solution.py:394
  50.2 0.6 collective-permute-start.9
  50.8 1.5 %collective-permute-start.8 = (f32[72,128]{1,0:T(8,128)S(1)}, f32[72,128]{1,0:T(8,128)S(1)}, u32[]{:S(2)}, u32[]{:S(2)}) collective-permute-start(f32[72,128]{1,0:T(8,128)S(1)} %shard_map.55.refs_0_), channel_id=1, source_target_pairs={{0,16},{8,24},{16,0},{24,8},{1,17},{9,25},{17,1},{25,9},{2,18},{10... | collective-permute-start | bytes 110600 | tf_op jit(solution)/shard_map/ppermute | solution.py:322
  52.3 2.4 %collective-permute-start.7 = (f32[72,128]{1,0:T(8,128)S(1)}, f32[72,128]{1,0:T(8,128)S(1)}, u32[]{:S(2)}, u32[]{:S(2)}) collective-permute-start(f32[72,128]{1,0:T(8,128)S(1)} %shard_map.55.refs_0_), channel_id=1, source_target_pairs={{0,8},{8,0},{16,24},{24,16},{1,9},{9,1},{17,25},{25,17},{2,10},{10... | collective-permute-start | bytes 110600 | tf_op jit(solution)/shard_map/ppermute | solution.py:322
  54.6 1.4 %collective-permute-done.9.refs_3_ = f32[72,128]{1,0:T(8,128)S(1)} collective-permute-done((f32[72,128]{1,0:T(8,128)S(1)}, f32[72,128]{1,0:T(8,128)S(1)}, u32[]{:S(2)}, u32[]{:S(2)}) %collective-permute-start.9) | collective-permute-done | bytes 36896 | tf_op jit(solution)/shard_map/ppermute | solution.py:322
  56.0 0.5 collective-permute-done.8.refs_2_
  56.5 0.2 collective-permute-done.7.refs_1_
  56.7 0.7 collective-permute-start.12
  57.4 1.4 %collective-permute-start.11 = (f32[288,128]{1,0:T(8,128)S(1)}, f32[288,128]{1,0:T(8,128)S(1)}, u32[]{:S(2)}, u32[]{:S(2)}) collective-permute-start(f32[288,128]{1,0:T(8,128)S(1)} %shard_map.56.refs_0_), channel_id=1, source_target_pairs={{0,2},{1,3},{2,0},{3,1},{4,6},{5,7},{6,4},{7,5},{8,10},{9,11},{10,... | collective-permute-start | bytes 442376 | tf_op jit(solution)/shard_map/ppermute | solution.py:322
  58.7 1.5 %collective-permute-start.10 = (f32[288,128]{1,0:T(8,128)S(1)}, f32[288,128]{1,0:T(8,128)S(1)}, u32[]{:S(2)}, u32[]{:S(2)}) collective-permute-start(f32[288,128]{1,0:T(8,128)S(1)} %shard_map.56.refs_0_), channel_id=1, source_target_pairs={{0,1},{1,0},{2,3},{3,2},{4,5},{5,4},{6,7},{7,6},{8,9},{9,8},{10,11... | collective-permute-start | bytes 442376 | tf_op jit(solution)/shard_map/ppermute | solution.py:322
  60.3 0.0 collective-permute-start.13
  60.3 3.6 %collective-permute-done.12.refs_3_ = f32[288,128]{1,0:T(8,128)S(1)} collective-permute-done((f32[288,128]{1,0:T(8,128)S(1)}, f32[288,128]{1,0:T(8,128)S(1)}, u32[]{:S(2)}, u32[]{:S(2)}) %collective-permute-start.12) | collective-permute-done | bytes 147488 | tf_op jit(solution)/shard_map/ppermute | solution.py:322
  63.9 0.9 %collective-permute-done.11.refs_2_ = f32[288,128]{1,0:T(8,128)S(1)} collective-permute-done((f32[288,128]{1,0:T(8,128)S(1)}, f32[288,128]{1,0:T(8,128)S(1)}, u32[]{:S(2)}, u32[]{:S(2)}) %collective-permute-start.11) | collective-permute-done | bytes 147488 | tf_op jit(solution)/shard_map/ppermute | solution.py:322
  64.7 0.0 collective-permute-start.15
  64.7 0.5 collective-permute-start.14
  65.2 0.3 shard_map.57.mine_ref
  65.5 0.0 collective-permute-done.13.refs_0_
  65.6 0.0 collective-permute-done.16.refs_3_
  65.6 0.5 collective-permute-done.15.refs_2_
  66.1 0.2 collective-permute-done.14.refs_1_
  66.3 1.1 %shard_map.58 = f32[1,2,1152,128]{3,2,1,0:T(8,128)} custom-call(f32[1152,128]{1,0:T(8,128)S(1)} %shard_map.57.mine_ref, f32[288,128]{1,0:T(8,128)S(1)} %collective-permute-done.13.refs_0_, f32[288,128]{1,0:T(8,128)S(1)} %collective-permute-done.14.refs_1_, f32[288,128]{1,0:T(8,128)S(1)} %collective-permute-done.15.refs_2_, ...), custom_call_target="tpu_custom_call" | custom-call | tf_op jit(solution)/shard_map/pallas_call | solution.py:415
  (13 shorter events, 0.1 us)
Async XLA Ops:
  0.0 7.7 %collective-permute-start.3 = (f32[1,128,4,128]{3,2,1,0:T(4,128)}, f32[1,128,4,128]{3,2,1,0:T(4,128)S(1)}, u32[]{:S(2)}, u32[]{:S(2)}) collective-permute-start(f32[1,128,4,128]{3,2,1,0:T(4,128)} %param.5), channel_id=1, source_target_pairs={{0,1},{1,0},{2,4},{3,5},{4,2},{5,3},{6,7},{7,6},{8,9},{9,8},{10,12... | collective-permute-start | bytes 786440 | tf_op jit(solution)/shard_map/ppermute | solution.py:337
  3.0 5.4 %collective-permute-start.1 = (f32[1,128,4,128]{3,2,1,0:T(4,128)}, f32[1,128,4,128]{3,2,1,0:T(4,128)S(1)}, u32[]{:S(2)}, u32[]{:S(2)}) collective-permute-start(f32[1,128,4,128]{3,2,1,0:T(4,128)} %param.4), channel_id=1, source_target_pairs={{2,5},{3,4},{4,3},{5,2},{10,13},{11,12},{12,11},{13,10},{18,21},{1... | collective-permute-start | bytes 786440 | tf_op jit(solution)/shard_map/ppermute | solution.py:337
  3.6 9.7 %collective-permute-start = (f32[1,128,4,128]{3,2,1,0:T(4,128)}, f32[1,128,4,128]{3,2,1,0:T(4,128)S(1)}, u32[]{:S(2)}, u32[]{:S(2)}) collective-permute-start(f32[1,128,4,128]{3,2,1,0:T(4,128)} %param.4), channel_id=1, source_target_pairs={{0,1},{1,0},{2,4},{3,5},{4,2},{5,3},{6,7},{7,6},{8,9},{9,8},{10,12... | collective-permute-start | bytes 786440 | tf_op jit(solution)/shard_map/ppermute | solution.py:337
  7.7 9.8 %collective-permute-start.4 = (f32[1,128,4,128]{3,2,1,0:T(4,128)S(1)}, f32[1,128,4,128]{3,2,1,0:T(4,128)S(1)}, u32[]{:S(2)}, u32[]{:S(2)}) collective-permute-start(f32[1,128,4,128]{3,2,1,0:T(4,128)S(1)} %collective-permute-done.3), channel_id=1, source_target_pairs={{2,3},{3,2},{4,5},{5,4},{10,11},{11,10},{12,13},{13,12},{18,19},{1... | collective-permute-start | bytes 786440 | tf_op jit(solution)/shard_map/ppermute | solution.py:337
  13.3 0.9 %copy-start.1 = (f32[1,128,4,128]{3,2,1,0:T(4,128)S(1)}, f32[1,128,4,128]{3,2,1,0:T(4,128)}, u32[]{:S(2)}) copy-start(f32[1,128,4,128]{3,2,1,0:T(4,128)} %param.4) | copy-start | bytes 786436
  14.3 3.3 %copy-start.3 = (f32[1,128,4,128]{3,2,1,0:T(4,128)S(1)}, f32[1,128,4,128]{3,2,1,0:T(4,128)}, u32[]{:S(2)}) copy-start(f32[1,128,4,128]{3,2,1,0:T(4,128)} %param.5) | copy-start | bytes 786436
  14.3 4.6 %collective-permute-start.2 = (f32[128,128]{1,0:T(8,128)S(1)}, f32[128,128]{1,0:T(8,128)S(1)}, u32[]{:S(2)}, u32[]{:S(2)}) collective-permute-start(f32[128,128]{1,0:T(8,128)S(1)} %shard_map.46), channel_id=1, source_target_pairs={{0,4},{4,0},{1,5},{5,1},{2,6},{6,2},{3,7},{7,3},{8,12},{12,8},{9,1... | collective-permute-start | bytes 196616 | tf_op jit(solution)/shard_map/ppermute | solution.py:322
  15.8 1.3 %copy-start = (f32[2,1152,128]{2,1,0:T(8,128)S(1)}, f32[2,1152,128]{2,1,0:T(8,128)}, u32[]{:S(2)}) copy-start(f32[2,1152,128]{2,1,0:T(8,128)} %f_ref.1) | copy-start | bytes 3538948
  17.1 0.9 %copy-start.2 = (f32[1,128,4,128]{3,2,1,0:T(4,128)S(1)}, f32[1,128,4,128]{3,2,1,0:T(4,128)}, u32[]{:S(2)}) copy-start(f32[1,128,4,128]{3,2,1,0:T(4,128)} %param.4) | copy-start | bytes 786436
  17.6 2.8 %collective-permute-start.5 = (f32[128,128]{1,0:T(8,128)S(1)}, f32[128,128]{1,0:T(8,128)S(1)}, u32[]{:S(2)}, u32[]{:S(2)}) collective-permute-start(f32[128,128]{1,0:T(8,128)S(1)} %shard_map.47), channel_id=1, source_target_pairs={{0,4},{4,0},{1,5},{5,1},{2,6},{6,2},{3,7},{7,3},{8,12},{12,8},{9,1... | collective-permute-start | bytes 196616 | tf_op jit(solution)/shard_map/ppermute | solution.py:322
  21.9 1.6 %collective-permute-start.6 = (f32[576,128]{1,0:T(8,128)S(1)}, f32[576,128]{1,0:T(8,128)S(1)}, u32[]{:S(2)}, u32[]{:S(2)}) collective-permute-start(f32[576,128]{1,0:T(8,128)S(1)} %get-tuple-element.37), channel_id=1, source_target_pairs={{0,4},{4,0},{1,5},{5,1},{2,6},{6,2},{3,7},{7,3},{8,12},{12,8},{9,1... | collective-permute-start | bytes 884744 | tf_op jit(solution)/shard_map/ppermute | solution.py:322
  23.1 26.0 %copy-start.4 = (f32[2]{0:T(128)S(1)}, f32[2]{0:T(128)}, u32[]{:S(2)}) copy-start(f32[2]{0:T(128)} %rates_ref.1) | copy-start | bytes 28
  50.2 5.8 %collective-permute-start.9 = (f32[72,128]{1,0:T(8,128)S(1)}, f32[72,128]{1,0:T(8,128)S(1)}, u32[]{:S(2)}, u32[]{:S(2)}) collective-permute-start(f32[72,128]{1,0:T(8,128)S(1)} %shard_map.55.refs_0_), channel_id=1, source_target_pairs={{0,24},{8,16},{16,8},{24,0},{1,25},{9,17},{17,9},{25,1},{2,26},{10... | collective-permute-start | bytes 110600 | tf_op jit(solution)/shard_map/ppermute | solution.py:322
  50.8 5.8 %collective-permute-start.8 = (f32[72,128]{1,0:T(8,128)S(1)}, f32[72,128]{1,0:T(8,128)S(1)}, u32[]{:S(2)}, u32[]{:S(2)}) collective-permute-start(f32[72,128]{1,0:T(8,128)S(1)} %shard_map.55.refs_0_), channel_id=1, source_target_pairs={{0,16},{8,24},{16,0},{24,8},{1,17},{9,25},{17,1},{25,9},{2,18},{10... | collective-permute-start | bytes 110600 | tf_op jit(solution)/shard_map/ppermute | solution.py:322
  52.3 4.4 %collective-permute-start.7 = (f32[72,128]{1,0:T(8,128)S(1)}, f32[72,128]{1,0:T(8,128)S(1)}, u32[]{:S(2)}, u32[]{:S(2)}) collective-permute-start(f32[72,128]{1,0:T(8,128)S(1)} %shard_map.55.refs_0_), channel_id=1, source_target_pairs={{0,8},{8,0},{16,24},{24,16},{1,9},{9,1},{17,25},{25,17},{2,10},{10... | collective-permute-start | bytes 110600 | tf_op jit(solution)/shard_map/ppermute | solution.py:322
  56.7 7.2 %collective-permute-start.12 = (f32[288,128]{1,0:T(8,128)S(1)}, f32[288,128]{1,0:T(8,128)S(1)}, u32[]{:S(2)}, u32[]{:S(2)}) collective-permute-start(f32[288,128]{1,0:T(8,128)S(1)} %shard_map.56.refs_0_), channel_id=1, source_target_pairs={{0,3},{1,2},{2,1},{3,0},{4,7},{5,6},{6,5},{7,4},{8,11},{9,10},{10,... | collective-permute-start | bytes 442376 | tf_op jit(solution)/shard_map/ppermute | solution.py:322
  57.4 7.3 %collective-permute-start.11 = (f32[288,128]{1,0:T(8,128)S(1)}, f32[288,128]{1,0:T(8,128)S(1)}, u32[]{:S(2)}, u32[]{:S(2)}) collective-permute-start(f32[288,128]{1,0:T(8,128)S(1)} %shard_map.56.refs_0_), channel_id=1, source_target_pairs={{0,2},{1,3},{2,0},{3,1},{4,6},{5,7},{6,4},{7,5},{8,10},{9,11},{10,... | collective-permute-start | bytes 442376 | tf_op jit(solution)/shard_map/ppermute | solution.py:322
  58.7 6.0 %collective-permute-start.10 = (f32[288,128]{1,0:T(8,128)S(1)}, f32[288,128]{1,0:T(8,128)S(1)}, u32[]{:S(2)}, u32[]{:S(2)}) collective-permute-start(f32[288,128]{1,0:T(8,128)S(1)} %shard_map.56.refs_0_), channel_id=1, source_target_pairs={{0,1},{1,0},{2,3},{3,2},{4,5},{5,4},{6,7},{7,6},{8,9},{9,8},{10,11... | collective-permute-start | bytes 442376 | tf_op jit(solution)/shard_map/ppermute | solution.py:322
  60.3 5.3 %collective-permute-start.13 = (f32[288,128]{1,0:T(8,128)S(1)}, f32[288,128]{1,0:T(8,128)S(1)}, u32[]{:S(2)}, u32[]{:S(2)}) collective-permute-start(f32[288,128]{1,0:T(8,128)S(1)} %shard_map.56.refs_0_), channel_id=1, source_target_pairs={{0,4},{4,0},{1,5},{5,1},{2,6},{6,2},{3,7},{7,3},{8,12},{12,8},{9,1... | collective-permute-start | bytes 442376 | tf_op jit(solution)/shard_map/ppermute | solution.py:322
  63.9 1.7 %collective-permute-start.16 = (f32[288,128]{1,0:T(8,128)S(1)}, f32[288,128]{1,0:T(8,128)S(1)}, u32[]{:S(2)}, u32[]{:S(2)}) collective-permute-start(f32[288,128]{1,0:T(8,128)S(1)} %collective-permute-done.12.refs_3_), channel_id=1, source_target_pairs={{0,4},{4,0},{1,5},{5,1},{2,6},{6,2},{3,7},{7,3},{8,12},{12,8},{9,1... | collective-permute-start | bytes 442376 | tf_op jit(solution)/shard_map/ppermute | solution.py:322
  64.7 1.4 %collective-permute-start.15 = (f32[288,128]{1,0:T(8,128)S(1)}, f32[288,128]{1,0:T(8,128)S(1)}, u32[]{:S(2)}, u32[]{:S(2)}) collective-permute-start(f32[288,128]{1,0:T(8,128)S(1)} %collective-permute-done.11.refs_2_), channel_id=1, source_target_pairs={{0,4},{4,0},{1,5},{5,1},{2,6},{6,2},{3,7},{7,3},{8,12},{12,8},{9,1... | collective-permute-start | bytes 442376 | tf_op jit(solution)/shard_map/ppermute | solution.py:322
  64.7 1.6 %collective-permute-start.14 = (f32[288,128]{1,0:T(8,128)S(1)}, f32[288,128]{1,0:T(8,128)S(1)}, u32[]{:S(2)}, u32[]{:S(2)}) collective-permute-start(f32[288,128]{1,0:T(8,128)S(1)} %collective-permute-done.10.refs_1_), channel_id=1, source_target_pairs={{0,4},{4,0},{1,5},{5,1},{2,6},{6,2},{3,7},{7,3},{8,12},{12,8},{9,1... | collective-permute-start | bytes 442376 | tf_op jit(solution)/shard_map/ppermute | solution.py:322

commit v9 on v8

--- a/solution.py
+++ b/solution.py
@@ -55,7 +55,7 @@
     low_ref[part] = low
 
 
-def filter_kernel(f_ref, fh, fl, gh, gl, part_ref, taps_ref):
+def filter_kernel(rates_ref, f_ref, fh, fl, gh, gl, slice_ref, rate_ref, taps_ref, part_ref):
     lo = lax.axis_index("lo")
     chans = f_ref.shape[2]
     mine = fh.shape[0] // 3
@@ -70,6 +70,11 @@
             put(gh, gl, b, a, taps_ref[1, t, rows, :])
             for layer in range(2):
                 part_ref[layer, t * mine : (t + 1) * mine, :] = taps_ref[layer, t, rows, :]
+    core = lax.axis_index("core")
+    size = slice_ref.shape[0]
+    slot = 2 * lax.axis_index("pair") + lax.axis_index("half")
+    slice_ref[...] = part_ref[core, pl.ds(pl.multiple_of(slot * size, 8), size), :]
+    rate_ref[...] = jnp.full(rate_ref.shape, rates_ref[core], F32)
 
 
 def sources(own, near, far):
@@ -215,7 +220,7 @@
     out[...] = total
 
 
-def merge_kernel(n_band, rates_ref, sums_ref, v_ref, f_ref, out):
+def merge_kernel(n_band, sums_ref, v_ref, f_ref, rate_ref, out):
     core = lax.axis_index("core")
     count = v_ref.shape[0]
     sums = sums_ref[...]
@@ -259,10 +264,7 @@
     total = jnp.zeros(out.shape, F32)
     for i in range(count):
         total = total + weight[i : i + 1, :] * v_ref[i]
-    size = out.shape[0]
-    slot = 2 * lax.axis_index("pair") + lax.axis_index("half")
-    mine = f_ref[core, pl.ds(pl.multiple_of(slot * size, 8), size), :]
-    out[...] = mine - rates_ref[core] * total
+    out[...] = f_ref[...] - rate_ref[...] * total
 
 
 def gather_kernel(*refs):
@@ -355,11 +357,20 @@
     c_far = sent(c_near, onward)
     xs = [v.reshape(flat) for v in (images, x_near, x_far)]
     cs = [v.reshape(flat) for v in (cotangent, c_near, c_far)]
-    fh, fl, gh, gl, tapped = call(
+    vmem, smem = (pl.BlockSpec(memory_space=m) for m in (pltpu.VMEM, pltpu.SMEM))
+    params = pltpu.CompilerParams(vmem_limit_bytes=40 * 2**20)
+    like = lambda *shape: jax.ShapeDtypeStruct(shape, F32)
+    fh, fl, gh, gl, tapped, rate = pl.pallas_call(
         filter_kernel,
-        [bf(thin, tall)] * 4 + [(2, 9 * mine, chans)],
-        [pltpu.VMEM((2, 9, chans, chans), F32)],
-    )(filters)
+        out_shape=[bf(thin, tall)] * 4 + [like(slot, chans), like(1, chans)],
+        in_specs=[smem, vmem],
+        out_specs=[vmem] * 6,
+        scratch_shapes=[
+            pltpu.VMEM((2, 9, chans, chans), F32),
+            pltpu.VMEM((2, 9 * mine, chans), F32),
+        ],
+        compiler_params=params,
+    )(rates, filters)
     (edge,) = call(edge_kernel, [(chans, cols)])(*xs)
     x_edge = swapped(edge, "core", 1)
     raw = [pltpu.VMEM((total, chans, cols), F32)]
@@ -389,15 +400,9 @@
     (gram,) = call(gram_kernel, [(1, 128)])(slices)
     sums = jnp.broadcast_to(gram, (n_image * n_band, gram.shape[1]))
     sums = lax.all_to_all(sums, AXES, 0, 0, tiled=True)
-    vmem, smem = (pl.BlockSpec(memory_space=m) for m in (pltpu.VMEM, pltpu.SMEM))
-    params = pltpu.CompilerParams(vmem_limit_bytes=40 * 2**20)
-    merged = pl.pallas_call(
-        functools.partial(merge_kernel, n_band),
-        out_shape=jax.ShapeDtypeStruct((slot, chans), F32),
-        in_specs=[smem] + [vmem] * 3,
-        out_specs=vmem,
-        compiler_params=params,
-    )(rates, sums, slices, tapped)
+    (merged,) = call(functools.partial(merge_kernel, n_band), [(slot, chans)])(
+        sums, slices, tapped, rate
+    )
     pieces = [merged] + [swapped(merged, "pair", k) for k in range(1, n_pair)]
     (block,) = call(gather_kernel, [(n_pair * slot, chans)])(*pieces)
     own = [block] + [swapped(block, ("half", "lo"), k) for k in range(1, n_band)]

time: 67.6 us -> 68.1 us (level)
  transfers between devices with their start and end apart: 17 -> 17, of which waited for: 10 -> 10; matrix products, arithmetic and copies ran while one was open for 0% -> 0% of each run, Pallas kernels for 6% -> 7%
where the time goes in v9:
time: 68.1 us; the launch traced here: 67.8 us
  blocking collectives  25.3 us (37%)
  waiting for transfers between devices  16.4 us (24%)
  starting transfers between devices  15 us (22%)
  Pallas kernels  7.99 us (12%)
  local copies, waits for them, and re-layouts  2.89 us (4%)
    all_to_all x1, blocking collectives, fast(): lax.all_to_all(whole.reshape(n_image, slot, chans), ('pair', 'half'), 0,...  15.9 us
    ppermute x13, starting transfers between devices, swapped(): return lax.ppermute(value, axis, xor_route(lax.axis_size(axis), k))  10.6 us
    all_to_all x1, blocking collectives, fast(): sums = lax.all_to_all(sums, AXES, 0, 0, tiled=True)  9.41 us
    ppermute x4, waiting for transfers between devices, sent(): return lax.ppermute(value, ('core', 'half', 'lo'), route)  8.93 us
    ppermute x13, waiting for transfers between devices, swapped(): return lax.ppermute(value, axis, xor_route(lax.axis_size(axis), k))  7.45 us
    ppermute x4, starting transfers between devices, sent(): return lax.ppermute(value, ('core', 'half', 'lo'), route)  4.37 us
    unnamed x10, local copies, waits for them, and re-layouts  2.88 us
    pallas_call x1, Pallas kernels, fast(): call(functools.partial(give_kernel, total, scale), [part] + [bf(thin, wid...  1.46 us
  transfers between devices with their start and end apart: 17, of which 10 were waited for; matrix products, arithmetic and copies ran while one was open for 0% of the time, Pallas kernels for 7%

profile of v9, /device:TPU:0, one launch (start us, length us, event | category | flops | bytes accessed | tf_op | source)
XLA Modules:
  0.0 67.8 jit_solution(8303219174551429188)
XLA Ops:
  0.0 3.0 %collective-permute-start.3 = (f32[1,128,4,128]{3,2,1,0:T(4,128)}, f32[1,128,4,128]{3,2,1,0:T(4,128)S(1)}, u32[]{:S(2)}, u32[]{:S(2)}) collective-permute-start(f32[1,128,4,128]{3,2,1,0:T(4,128)} %param.5), channel_id=1, source_target_pairs={{0,1},{1,0},{2,4},{3,5},{4,2},{5,3},{6,7},{7,6},{8,9},{9,8},{10,12... | collective-permute-start | bytes 786440 | tf_op jit(solution)/shard_map/ppermute | solution.py:339
  3.0 0.7 collective-permute-start.1
  3.6 0.1 collective-permute-start
  3.7 4.0 %collective-permute-done.3 = f32[1,128,4,128]{3,2,1,0:T(4,128)S(1)} collective-permute-done((f32[1,128,4,128]{3,2,1,0:T(4,128)}, f32[1,128,4,128]{3,2,1,0:T(4,128)S(1)}, u32[]{:S(2)}, u32[]{:S(2)}) %collective-permute-start.3) | collective-permute-done | bytes 262176 | tf_op jit(solution)/shard_map/ppermute | solution.py:339
  7.7 0.7 collective-permute-start.4
  8.4 0.0 collective-permute-done.1
  8.4 4.9 %collective-permute-done = f32[1,128,4,128]{3,2,1,0:T(4,128)S(1)} collective-permute-done((f32[1,128,4,128]{3,2,1,0:T(4,128)}, f32[1,128,4,128]{3,2,1,0:T(4,128)S(1)}, u32[]{:S(2)}, u32[]{:S(2)}) %collective-permute-start) | collective-permute-done | bytes 262176 | tf_op jit(solution)/shard_map/ppermute | solution.py:339
  13.3 0.9 %copy-done.1 = f32[1,128,4,128]{3,2,1,0:T(4,128)S(1)} copy-done((f32[1,128,4,128]{3,2,1,0:T(4,128)S(1)}, f32[1,128,4,128]{3,2,1,0:T(4,128)}, u32[]{:S(2)}) %copy-start.1) | copy-done | bytes 262168
  14.3 1.5 %collective-permute-start.2 = (f32[128,128]{1,0:T(8,128)S(1)}, f32[128,128]{1,0:T(8,128)S(1)}, u32[]{:S(2)}, u32[]{:S(2)}) collective-permute-start(f32[128,128]{1,0:T(8,128)S(1)} %shard_map.46), channel_id=1, source_target_pairs={{0,4},{4,0},{1,5},{5,1},{2,6},{6,2},{3,7},{7,3},{8,12},{12,8},{9,1... | collective-permute-start | bytes 196616 | tf_op jit(solution)/shard_map/ppermute | solution.py:324
  15.8 1.3 %copy-done = f32[2,1152,128]{2,1,0:T(8,128)S(1)} copy-done((f32[2,1152,128]{2,1,0:T(8,128)S(1)}, f32[2,1152,128]{2,1,0:T(8,128)}, u32[]{:S(2)}) %copy-start) | copy-done | bytes 1179672
  17.1 0.7 copy-done.4
  17.7 1.0 %shard_map.48 = (bf16[192,384]{1,0:T(8,128)(2,1)S(1)}, bf16[192,384]{1,0:T(8,128)(2,1)S(1)}, bf16[192,384]{1,0:T(8,128)(2,1)S(1)}, bf16[192,384]{1,0:T(8,128)(2,...) custom-call(f32[2]{0:T(128)S(1)} %copy-done.4, f32[2,1152,128]{2,1,0:T(8,128)S(1)} %copy-done), custom_call_target="tpu_custom_call" | custom-call | tf_op jit(solution)/shard_map/pallas_call | solution.py:363
  18.7 0.0 collective-permute-done.4
  18.7 0.1 shard_map.47
  18.8 0.1 collective-permute-start.5
  18.9 0.9 %shard_map.49 = (bf16[384,1024]{1,0:T(8,128)(2,1)S(1)}, bf16[384,1024]{1,0:T(8,128)(2,1)S(1)}, f32[192,1024]{1,0:T(8,128)S(1)}) custom-call(f32[512,128]{1,0:T(8,128)S(1)} %bitcast.10, f32[512,128]{1,0:T(8,128)S(1)} %bitcast.20, f32[512,128]{1,0:T(8,128)S(1)} %bitcast.18, bf16[192,384]{1,0:T(8,128)(2,1)S(1)} %get-tuple-element.23.fh, ...), custom_call_target="tpu_custom_call" | custom-call | flops 452984832 | bytes 905969 | tf_op jit(solution)/shard_map/pallas_call | solution.py:379
  19.8 0.0 collective-permute-done.2.edge.refs_0_
  19.8 0.5 shard_map.51
  20.3 0.9 %shard_map.50 = (bf16[384,1024]{1,0:T(8,128)(2,1)S(1)}, bf16[384,1024]{1,0:T(8,128)(2,1)S(1)}, f32[192,1024]{1,0:T(8,128)S(1)}) custom-call(f32[512,128]{1,0:T(8,128)S(1)} %bitcast.12, f32[512,128]{1,0:T(8,128)S(1)} %bitcast.14, f32[512,128]{1,0:T(8,128)S(1)} %bitcast.16, bf16[192,384]{1,0:T(8,128)(2,1)S(1)} %get-tuple-element.27.fh.refs_9_, ...), custom_call_target="tpu_custom_call" | custom-call | flops 452984832 | bytes 905969 | tf_op jit(solution)/shard_map/pallas_call | solution.py:386
  21.3 0.0 collective-permute-done.5.refs_1_
  21.3 1.5 %shard_map.52 = (f32[576,128]{1,0:T(8,128)S(1)}, bf16[192,1024]{1,0:T(8,128)(2,1)S(1)}, bf16[192,1024]{1,0:T(8,128)(2,1)S(1)}) custom-call(f32[128,128]{1,0:T(8,128)S(1)} %collective-permute-done.2.edge.refs_0_, f32[128,128]{1,0:T(8,128)S(1)} %collective-permute-done.5.refs_1_, bf16[384,1024]{1,0:T(8,128)(2,1)S(1)} %get-tuple-element.25.refs_2_, ...), custom_call_target="tpu_custom_call" | custom-call | flops 905969664 | bytes 1811939 | tf_op jit(solution)/shard_map/pallas_call | solution.py:389
  22.7 0.5 collective-permute-start.6
  23.3 1.0 %shard_map.53 = f32[576,128]{1,0:T(8,128)S(1)} custom-call(f32[128,128]{1,0:T(8,128)S(1)} %collective-permute-done.2.edge.refs_0_, f32[128,128]{1,0:T(8,128)S(1)} %collective-permute-done.5.refs_1_, bf16[384,1024]{1,0:T(8,128)(2,1)S(1)} %get-tuple-element.25.refs_2_, bf16[384,1024]{1,0:T(8,128)(2,1)S(1)} %get-tuple-element.26.refs_3_, ...), custom_call_target="tpu_custom_call" | custom-call | flops 452984832 | bytes 905969 | tf_op jit(solution)/shard_map/pallas_call | solution.py:393
  24.3 0.2 collective-permute-done.6
  24.5 15.9 %all_to_all.13.v_ref = f32[8,72,128]{2,1,0:T(8,128)S(1)} all-to-all(f32[8,72,128]{2,1,0:T(8,128)S(1)} %bitcast.23), channel_id=1, replica_groups=mesh['pair'=4,'core'=2,'half'=2,'lo'=2] {'pair','half'}, dimensions={0} | all-to-all | bytes 589824 | tf_op jit(solution)/shard_map/all_to_all | solution.py:397
  40.4 0.2 shard_map.54
  40.7 9.4 %all_to_all.14 = f32[32,1,128]{2,1,0:T(1,128)S(1)} all-to-all(f32[32,1,128]{2,1,0:T(1,128)S(1)} %broadcast_in_dim.2), channel_id=1, replica_groups=mesh['pair'=4,'core'=2,'half'=2,'lo'=2] {'pair','core','half','lo'}, dimensions={0} | all-to-all | bytes 32768 | tf_op jit(solution)/shard_map/all_to_all | solution.py:402
  50.1 0.5 shard_map.55.refs_0_
  50.6 0.6 collective-permute-start.9
  51.2 1.5 %collective-permute-start.8 = (f32[72,128]{1,0:T(8,128)S(1)}, f32[72,128]{1,0:T(8,128)S(1)}, u32[]{:S(2)}, u32[]{:S(2)}) collective-permute-start(f32[72,128]{1,0:T(8,128)S(1)} %shard_map.55.refs_0_), channel_id=1, source_target_pairs={{0,16},{8,24},{16,0},{24,8},{1,17},{9,25},{17,1},{25,9},{2,18},{10... | collective-permute-start | bytes 110600 | tf_op jit(solution)/shard_map/ppermute | solution.py:324
  52.7 2.4 %collective-permute-start.7 = (f32[72,128]{1,0:T(8,128)S(1)}, f32[72,128]{1,0:T(8,128)S(1)}, u32[]{:S(2)}, u32[]{:S(2)}) collective-permute-start(f32[72,128]{1,0:T(8,128)S(1)} %shard_map.55.refs_0_), channel_id=1, source_target_pairs={{0,8},{8,0},{16,24},{24,16},{1,9},{9,1},{17,25},{25,17},{2,10},{10... | collective-permute-start | bytes 110600 | tf_op jit(solution)/shard_map/ppermute | solution.py:324
  55.1 1.4 %collective-permute-done.9.refs_3_ = f32[72,128]{1,0:T(8,128)S(1)} collective-permute-done((f32[72,128]{1,0:T(8,128)S(1)}, f32[72,128]{1,0:T(8,128)S(1)}, u32[]{:S(2)}, u32[]{:S(2)}) %collective-permute-start.9) | collective-permute-done | bytes 36896 | tf_op jit(solution)/shard_map/ppermute | solution.py:324
  56.4 0.5 collective-permute-done.8.refs_2_
  57.0 0.2 collective-permute-done.7.refs_1_
  57.1 0.7 collective-permute-start.12
  57.8 1.4 %collective-permute-start.11 = (f32[288,128]{1,0:T(8,128)S(1)}, f32[288,128]{1,0:T(8,128)S(1)}, u32[]{:S(2)}, u32[]{:S(2)}) collective-permute-start(f32[288,128]{1,0:T(8,128)S(1)} %shard_map.56.refs_0_), channel_id=1, source_target_pairs={{0,2},{1,3},{2,0},{3,1},{4,6},{5,7},{6,4},{7,5},{8,10},{9,11},{10,... | collective-permute-start | bytes 442376 | tf_op jit(solution)/shard_map/ppermute | solution.py:324
  59.2 1.5 %collective-permute-start.10 = (f32[288,128]{1,0:T(8,128)S(1)}, f32[288,128]{1,0:T(8,128)S(1)}, u32[]{:S(2)}, u32[]{:S(2)}) collective-permute-start(f32[288,128]{1,0:T(8,128)S(1)} %shard_map.56.refs_0_), channel_id=1, source_target_pairs={{0,1},{1,0},{2,3},{3,2},{4,5},{5,4},{6,7},{7,6},{8,9},{9,8},{10,11... | collective-permute-start | bytes 442376 | tf_op jit(solution)/shard_map/ppermute | solution.py:324
  60.7 0.0 collective-permute-start.13
  60.7 3.6 %collective-permute-done.12.refs_3_ = f32[288,128]{1,0:T(8,128)S(1)} collective-permute-done((f32[288,128]{1,0:T(8,128)S(1)}, f32[288,128]{1,0:T(8,128)S(1)}, u32[]{:S(2)}, u32[]{:S(2)}) %collective-permute-start.12) | collective-permute-done | bytes 147488 | tf_op jit(solution)/shard_map/ppermute | solution.py:324
  64.3 0.0 collective-permute-start.16
  64.3 0.9 %collective-permute-done.11.refs_2_ = f32[288,128]{1,0:T(8,128)S(1)} collective-permute-done((f32[288,128]{1,0:T(8,128)S(1)}, f32[288,128]{1,0:T(8,128)S(1)}, u32[]{:S(2)}, u32[]{:S(2)}) %collective-permute-start.11) | collective-permute-done | bytes 147488 | tf_op jit(solution)/shard_map/ppermute | solution.py:324
  65.2 0.5 collective-permute-start.14
  65.7 0.3 shard_map.57.mine_ref
  66.0 0.0 collective-permute-done.13.refs_0_
  66.0 0.0 collective-permute-done.16.refs_3_
  66.0 0.5 collective-permute-done.15.refs_2_
  66.5 0.2 collective-permute-done.14.refs_1_
  66.8 1.1 %shard_map.58 = f32[1,2,1152,128]{3,2,1,0:T(8,128)} custom-call(f32[1152,128]{1,0:T(8,128)S(1)} %shard_map.57.mine_ref, f32[288,128]{1,0:T(8,128)S(1)} %collective-permute-done.13.refs_0_, f32[288,128]{1,0:T(8,128)S(1)} %collective-permute-done.14.refs_1_, f32[288,128]{1,0:T(8,128)S(1)} %collective-permute-done.15.refs_2_, ...), custom_call_target="tpu_custom_call" | custom-call | tf_op jit(solution)/shard_map/pallas_call | solution.py:420
  (13 shorter events, 0.1 us)
Async XLA Ops:
  0.0 7.7 %collective-permute-start.3 = (f32[1,128,4,128]{3,2,1,0:T(4,128)}, f32[1,128,4,128]{3,2,1,0:T(4,128)S(1)}, u32[]{:S(2)}, u32[]{:S(2)}) collective-permute-start(f32[1,128,4,128]{3,2,1,0:T(4,128)} %param.5), channel_id=1, source_target_pairs={{0,1},{1,0},{2,4},{3,5},{4,2},{5,3},{6,7},{7,6},{8,9},{9,8},{10,12... | collective-permute-start | bytes 786440 | tf_op jit(solution)/shard_map/ppermute | solution.py:339
  3.0 5.4 %collective-permute-start.1 = (f32[1,128,4,128]{3,2,1,0:T(4,128)}, f32[1,128,4,128]{3,2,1,0:T(4,128)S(1)}, u32[]{:S(2)}, u32[]{:S(2)}) collective-permute-start(f32[1,128,4,128]{3,2,1,0:T(4,128)} %param.4), channel_id=1, source_target_pairs={{2,5},{3,4},{4,3},{5,2},{10,13},{11,12},{12,11},{13,10},{18,21},{1... | collective-permute-start | bytes 786440 | tf_op jit(solution)/shard_map/ppermute | solution.py:339
  3.6 9.7 %collective-permute-start = (f32[1,128,4,128]{3,2,1,0:T(4,128)}, f32[1,128,4,128]{3,2,1,0:T(4,128)S(1)}, u32[]{:S(2)}, u32[]{:S(2)}) collective-permute-start(f32[1,128,4,128]{3,2,1,0:T(4,128)} %param.4), channel_id=1, source_target_pairs={{0,1},{1,0},{2,4},{3,5},{4,2},{5,3},{6,7},{7,6},{8,9},{9,8},{10,12... | collective-permute-start | bytes 786440 | tf_op jit(solution)/shard_map/ppermute | solution.py:339
  7.7 11.0 %collective-permute-start.4 = (f32[1,128,4,128]{3,2,1,0:T(4,128)S(1)}, f32[1,128,4,128]{3,2,1,0:T(4,128)S(1)}, u32[]{:S(2)}, u32[]{:S(2)}) collective-permute-start(f32[1,128,4,128]{3,2,1,0:T(4,128)S(1)} %collective-permute-done.3), channel_id=1, source_target_pairs={{2,3},{3,2},{4,5},{5,4},{10,11},{11,10},{12,13},{13,12},{18,19},{1... | collective-permute-start | bytes 786440 | tf_op jit(solution)/shard_map/ppermute | solution.py:339
  13.3 0.9 %copy-start.1 = (f32[1,128,4,128]{3,2,1,0:T(4,128)S(1)}, f32[1,128,4,128]{3,2,1,0:T(4,128)}, u32[]{:S(2)}) copy-start(f32[1,128,4,128]{3,2,1,0:T(4,128)} %param.4) | copy-start | bytes 786436
  14.3 4.5 %copy-start.3 = (f32[1,128,4,128]{3,2,1,0:T(4,128)S(1)}, f32[1,128,4,128]{3,2,1,0:T(4,128)}, u32[]{:S(2)}) copy-start(f32[1,128,4,128]{3,2,1,0:T(4,128)} %param.5) | copy-start | bytes 786436
  14.3 5.5 %collective-permute-start.2 = (f32[128,128]{1,0:T(8,128)S(1)}, f32[128,128]{1,0:T(8,128)S(1)}, u32[]{:S(2)}, u32[]{:S(2)}) collective-permute-start(f32[128,128]{1,0:T(8,128)S(1)} %shard_map.46), channel_id=1, source_target_pairs={{0,4},{4,0},{1,5},{5,1},{2,6},{6,2},{3,7},{7,3},{8,12},{12,8},{9,1... | collective-permute-start | bytes 196616 | tf_op jit(solution)/shard_map/ppermute | solution.py:324
  15.8 1.3 %copy-start = (f32[2,1152,128]{2,1,0:T(8,128)S(1)}, f32[2,1152,128]{2,1,0:T(8,128)}, u32[]{:S(2)}) copy-start(f32[2,1152,128]{2,1,0:T(8,128)} %f_ref.1) | copy-start | bytes 3538948
  17.1 0.7 copy-start.4
  17.7 1.2 %copy-start.2 = (f32[1,128,4,128]{3,2,1,0:T(4,128)S(1)}, f32[1,128,4,128]{3,2,1,0:T(4,128)}, u32[]{:S(2)}) copy-start(f32[1,128,4,128]{3,2,1,0:T(4,128)} %param.4) | copy-start | bytes 786436
  18.8 2.4 %collective-permute-start.5 = (f32[128,128]{1,0:T(8,128)S(1)}, f32[128,128]{1,0:T(8,128)S(1)}, u32[]{:S(2)}, u32[]{:S(2)}) collective-permute-start(f32[128,128]{1,0:T(8,128)S(1)} %shard_map.47), channel_id=1, source_target_pairs={{0,4},{4,0},{1,5},{5,1},{2,6},{6,2},{3,7},{7,3},{8,12},{12,8},{9,1... | collective-permute-start | bytes 196616 | tf_op jit(solution)/shard_map/ppermute | solution.py:324
  22.7 1.7 %collective-permute-start.6 = (f32[576,128]{1,0:T(8,128)S(1)}, f32[576,128]{1,0:T(8,128)S(1)}, u32[]{:S(2)}, u32[]{:S(2)}) collective-permute-start(f32[576,128]{1,0:T(8,128)S(1)} %get-tuple-element.38), channel_id=1, source_target_pairs={{0,4},{4,0},{1,5},{5,1},{2,6},{6,2},{3,7},{7,3},{8,12},{12,8},{9,1... | collective-permute-start | bytes 884744 | tf_op jit(solution)/shard_map/ppermute | solution.py:324
  50.6 5.8 %collective-permute-start.9 = (f32[72,128]{1,0:T(8,128)S(1)}, f32[72,128]{1,0:T(8,128)S(1)}, u32[]{:S(2)}, u32[]{:S(2)}) collective-permute-start(f32[72,128]{1,0:T(8,128)S(1)} %shard_map.55.refs_0_), channel_id=1, source_target_pairs={{0,24},{8,16},{16,8},{24,0},{1,25},{9,17},{17,9},{25,1},{2,26},{10... | collective-permute-start | bytes 110600 | tf_op jit(solution)/shard_map/ppermute | solution.py:324
  51.2 5.8 %collective-permute-start.8 = (f32[72,128]{1,0:T(8,128)S(1)}, f32[72,128]{1,0:T(8,128)S(1)}, u32[]{:S(2)}, u32[]{:S(2)}) collective-permute-start(f32[72,128]{1,0:T(8,128)S(1)} %shard_map.55.refs_0_), channel_id=1, source_target_pairs={{0,16},{8,24},{16,0},{24,8},{1,17},{9,25},{17,1},{25,9},{2,18},{10... | collective-permute-start | bytes 110600 | tf_op jit(solution)/shard_map/ppermute | solution.py:324
  52.7 4.4 %collective-permute-start.7 = (f32[72,128]{1,0:T(8,128)S(1)}, f32[72,128]{1,0:T(8,128)S(1)}, u32[]{:S(2)}, u32[]{:S(2)}) collective-permute-start(f32[72,128]{1,0:T(8,128)S(1)} %shard_map.55.refs_0_), channel_id=1, source_target_pairs={{0,8},{8,0},{16,24},{24,16},{1,9},{9,1},{17,25},{25,17},{2,10},{10... | collective-permute-start | bytes 110600 | tf_op jit(solution)/shard_map/ppermute | solution.py:324
  57.1 7.2 %collective-permute-start.12 = (f32[288,128]{1,0:T(8,128)S(1)}, f32[288,128]{1,0:T(8,128)S(1)}, u32[]{:S(2)}, u32[]{:S(2)}) collective-permute-start(f32[288,128]{1,0:T(8,128)S(1)} %shard_map.56.refs_0_), channel_id=1, source_target_pairs={{0,3},{1,2},{2,1},{3,0},{4,7},{5,6},{6,5},{7,4},{8,11},{9,10},{10,... | collective-permute-start | bytes 442376 | tf_op jit(solution)/shard_map/ppermute | solution.py:324
  57.8 7.3 %collective-permute-start.11 = (f32[288,128]{1,0:T(8,128)S(1)}, f32[288,128]{1,0:T(8,128)S(1)}, u32[]{:S(2)}, u32[]{:S(2)}) collective-permute-start(f32[288,128]{1,0:T(8,128)S(1)} %shard_map.56.refs_0_), channel_id=1, source_target_pairs={{0,2},{1,3},{2,0},{3,1},{4,6},{5,7},{6,4},{7,5},{8,10},{9,11},{10,... | collective-permute-start | bytes 442376 | tf_op jit(solution)/shard_map/ppermute | solution.py:324
  59.2 6.0 %collective-permute-start.10 = (f32[288,128]{1,0:T(8,128)S(1)}, f32[288,128]{1,0:T(8,128)S(1)}, u32[]{:S(2)}, u32[]{:S(2)}) collective-permute-start(f32[288,128]{1,0:T(8,128)S(1)} %shard_map.56.refs_0_), channel_id=1, source_target_pairs={{0,1},{1,0},{2,3},{3,2},{4,5},{5,4},{6,7},{7,6},{8,9},{9,8},{10,11... | collective-permute-start | bytes 442376 | tf_op jit(solution)/shard_map/ppermute | solution.py:324
  60.7 5.3 %collective-permute-start.13 = (f32[288,128]{1,0:T(8,128)S(1)}, f32[288,128]{1,0:T(8,128)S(1)}, u32[]{:S(2)}, u32[]{:S(2)}) collective-permute-start(f32[288,128]{1,0:T(8,128)S(1)} %shard_map.56.refs_0_), channel_id=1, source_target_pairs={{0,4},{4,0},{1,5},{5,1},{2,6},{6,2},{3,7},{7,3},{8,12},{12,8},{9,1... | collective-permute-start | bytes 442376 | tf_op jit(solution)/shard_map/ppermute | solution.py:324
  64.3 1.7 %collective-permute-start.16 = (f32[288,128]{1,0:T(8,128)S(1)}, f32[288,128]{1,0:T(8,128)S(1)}, u32[]{:S(2)}, u32[]{:S(2)}) collective-permute-start(f32[288,128]{1,0:T(8,128)S(1)} %collective-permute-done.12.refs_3_), channel_id=1, source_target_pairs={{0,4},{4,0},{1,5},{5,1},{2,6},{6,2},{3,7},{7,3},{8,12},{12,8},{9,1... | collective-permute-start | bytes 442376 | tf_op jit(solution)/shard_map/ppermute | solution.py:324
  65.2 1.4 %collective-permute-start.15 = (f32[288,128]{1,0:T(8,128)S(1)}, f32[288,128]{1,0:T(8,128)S(1)}, u32[]{:S(2)}, u32[]{:S(2)}) collective-permute-start(f32[288,128]{1,0:T(8,128)S(1)} %collective-permute-done.11.refs_2_), channel_id=1, source_target_pairs={{0,4},{4,0},{1,5},{5,1},{2,6},{6,2},{3,7},{7,3},{8,12},{12,8},{9,1... | collective-permute-start | bytes 442376 | tf_op jit(solution)/shard_map/ppermute | solution.py:324
  65.2 1.6 %collective-permute-start.14 = (f32[288,128]{1,0:T(8,128)S(1)}, f32[288,128]{1,0:T(8,128)S(1)}, u32[]{:S(2)}, u32[]{:S(2)}) collective-permute-start(f32[288,128]{1,0:T(8,128)S(1)} %collective-permute-done.10.refs_1_), channel_id=1, source_target_pairs={{0,4},{4,0},{1,5},{5,1},{2,6},{6,2},{3,7},{7,3},{8,12},{12,8},{9,1... | collective-permute-start | bytes 442376 | tf_op jit(solution)/shard_map/ppermute | solution.py:324
